TPU v7x, 256 devices: a whole 4x4x8 slice. The times are simulated.
256 devices in a mesh: tm: 64 (over x, z, core), col: 4 (over y).
Axes of the slice: x: 4, y: 4, z: 8, core: 2. Of those that a mesh axis runs over, the one named last changes fastest.
Arguments:
- observations: float32 [1024, 64, 256], P('tm', 'col'), may hold values from -6 to 6
- band_index: int32 [1024], P('tm'), may hold values from 0 to 3
- obs_mask: int32 [1024], P('tm'), may hold values 0 or 1
- diffusivity: float32 [4, 256], replicated, may hold values from 0.005 to 0.05
- mode_correction_factors: float32 [4, 256, 256], replicated, may hold values from -0.01 to 0.06
- mode_backward_factors: float32 [4, 256, 256], replicated, may hold values from -0.01 to 1.01
- initial_mean: float32 [256], replicated, may hold values from -6 to 6
Outputs:
- filtered: float32 [1024, 64, 256], P('tm', 'col')
- smoothed: float32 [1024, 64, 256], P('tm', 'col')
All inputs are finite; a program needn't handle non-finite values. No bound on the sum of `obs_mask` on one device may be relied on, other than what follows from the above.
Results may differ from a plain program's by a relative error of at most 0.0003.
Values sent between devices are 32-bit elements; how exact they have to be, the bound alone decides.
A program may use at most 64 MiB of HBM per device.

v0:
```python
import jax
import jax.numpy as jnp
from jax import lax
from jax.sharding import PartitionSpec as P

GRID = 16


def entering(value, axis, combine, identity, reverse):
    peers, index = (lax.axis_size(axis), lax.axis_index(axis))
    everything = jax.tree.map(lambda part: lax.all_gather(part, axis), value)
    start = jax.tree.map(
        lambda part, zero: jnp.broadcast_to(jnp.asarray(zero, part.dtype), part.shape),
        value,
        identity,
    )

    def lap(k, before):
        at = peers - 1 - k if reverse else k
        reached = at > index if reverse else at < index
        new = combine(before, jax.tree.map(lambda part: part[at], everything))
        return jax.tree.map(lambda a, b: jnp.where(reached, a, b), new, before)

    return lax.fori_loop(0, peers, lap, start)


def passed_along(block, axis, distance):
    devices = range(lax.axis_size(axis))
    route = [(i - distance, i) for i in devices if i - distance in devices]
    return lax.ppermute(block, axis, route)


def accurate_matmul_result(first_factor, second_factor):
    return jnp.dot(first_factor, second_factor, precision=lax.Precision.HIGHEST)


def apply_flipped_matrix(first_factor, second_factor):
    return lax.dot_general(
        first_factor, second_factor, (((1,), (1,)), ((), ())), precision=lax.Precision.HIGHEST
    )


def diffusion_matrices(diffusivity, side_cells):
    cell_count = side_cells * side_cells
    cell_ids = jnp.arange(cell_count)
    cell_row = cell_ids // side_cells
    cell_col = cell_ids % side_cells
    adjacent = (
        jnp.abs(cell_row[:, None] - cell_row[None, :])
        + jnp.abs(cell_col[:, None] - cell_col[None, :])
        == 1
    )
    coupling = (
        0.5 * (diffusivity[:, :, None] + diffusivity[:, None, :]) * adjacent.astype(jnp.float32)
    )
    keeping = 1.0 - jnp.sum(coupling, axis=2)
    return coupling + keeping[:, :, None] * jnp.eye(cell_count, dtype=jnp.float32)


def compose_pair(earlier, later):
    return (
        accurate_matmul_result(earlier[0], later[0]),
        accurate_matmul_result(earlier[1], later[0]) + later[1],
    )


def shards(
    observations,
    band_index,
    obs_mask,
    diffusivity,
    mode_correction_factors,
    mode_backward_factors,
    initial_mean,
):
    steps_dev = observations.shape[0]
    record_rows = observations.shape[1]
    states = initial_mean.shape[0]
    column_share = states // lax.axis_size("col")
    column_index = lax.axis_index("col")
    time_devices = lax.axis_size("tm")
    time_index = lax.axis_index("tm")
    dynamics_operator_matrix = diffusion_matrices(diffusivity, GRID)
    corrected = dynamics_operator_matrix - jax.vmap(apply_flipped_matrix)(
        dynamics_operator_matrix, mode_correction_factors
    )
    tables = jnp.stack([dynamics_operator_matrix, corrected], axis=1)
    identity = jnp.eye(states, dtype=jnp.float32)
    own_identity = lax.dynamic_slice_in_dim(identity, column_index * column_share, column_share, 0)
    blank_records = jnp.zeros((record_rows, states), jnp.float32)
    blank_columns = jnp.zeros((column_share, states), jnp.float32)
    initial_rows = jnp.concatenate([own_identity, blank_records], axis=0)
    final_here = (time_index == time_devices - 1) & (jnp.arange(steps_dev) == steps_dev - 1)
    live_flags = 1.0 - final_here.astype(jnp.float32)

    def compose_filter(element_rows, argument_entries):
        entry_measurement, current_strip, current_measured_flag = argument_entries
        source = current_measured_flag.astype(jnp.float32) * apply_flipped_matrix(
            entry_measurement, mode_correction_factors[current_strip]
        )
        element_rows = accurate_matmul_result(
            element_rows, tables[current_strip, current_measured_flag]
        ) + jnp.concatenate([blank_columns, source], axis=0)
        return (element_rows, None)

    forward_rows, _ = lax.scan(compose_filter, initial_rows, (observations, band_index, obs_mask))
    whole_matrix = lax.all_gather(forward_rows[:column_share], "col", axis=0, tiled=True)
    prefix_matrix, prefix_records = entering(
        (whole_matrix, forward_rows[column_share:]),
        "tm",
        compose_pair,
        (identity, blank_records),
        False,
    )
    start_rows = accurate_matmul_result(initial_mean[None, :], prefix_matrix) + prefix_records

    def filter_step(current_hidden_vector, argument_entries):
        entry_measurement, current_strip, current_measured_flag = argument_entries
        projected_field_vector = accurate_matmul_result(
            current_hidden_vector, dynamics_operator_matrix[current_strip]
        )
        corrected_hidden_vector = projected_field_vector + current_measured_flag.astype(
            jnp.float32
        ) * apply_flipped_matrix(
            entry_measurement - projected_field_vector, mode_correction_factors[current_strip]
        )
        return (corrected_hidden_vector, (corrected_hidden_vector, projected_field_vector))

    _, (filtered, predicted) = lax.scan(
        filter_step, start_rows, (observations, band_index, obs_mask)
    )
    following = passed_along(predicted[0], "tm", -1)
    next_predicted = jnp.concatenate([predicted[1:], following[None]], axis=0)

    def compose_smoother(element_rows, argument_entries):
        current_average, projected_field_vector, current_strip, current_active_flag = (
            argument_entries
        )
        current_correction_factor = mode_backward_factors[current_strip] * current_active_flag
        beginning_shift_amount = current_average - apply_flipped_matrix(
            projected_field_vector, current_correction_factor
        )
        element_rows = apply_flipped_matrix(
            element_rows, current_correction_factor
        ) + jnp.concatenate([blank_columns, beginning_shift_amount], axis=0)
        return (element_rows, beginning_shift_amount)

    backward_rows, offsets = lax.scan(
        compose_smoother,
        initial_rows,
        (filtered, next_predicted, band_index, live_flags),
        reverse=True,
    )
    whole_back = lax.all_gather(backward_rows[:column_share], "col", axis=0, tiled=True)
    suffix_matrix, after_records = entering(
        (whole_back, backward_rows[column_share:]),
        "tm",
        compose_pair,
        (identity, blank_records),
        True,
    )

    def smooth_step(following_lines, argument_entries):
        current_strip, current_active_flag, beginning_shift_amount = argument_entries
        current_refined_estimate = (
            apply_flipped_matrix(
                following_lines, mode_backward_factors[current_strip] * current_active_flag
            )
            + beginning_shift_amount
        )
        return (current_refined_estimate, current_refined_estimate)

    _, smoothed = lax.scan(
        smooth_step, after_records, (band_index, live_flags, offsets), reverse=True
    )
    return (filtered, smoothed)


def solution(mesh):
    return jax.shard_map(
        shards,
        mesh=mesh,
        in_specs=(P("tm", "col", None), P("tm"), P("tm"), P(), P(), P(), P()),
        out_specs=(P("tm", "col", None), P("tm", "col", None)),
        check_vma=False,
    )
```

profile of v0, /device:TPU:1, one launch (start us, length us, event | category | flops | bytes accessed | tf_op | source)
XLA Modules:
  0.0 1077.7 jit_solution(15576919279618056153)
XLA Ops:
  8.7 2.1 multiply_add_fusion.1
  10.8 2.6 fusion.56
  13.7 2.8 pad_maximum_fusion
  16.5 153.7 %while.88 = (s32[]{:T(128)}, f32[80,256]{1,0:T(8,128)S(1)}, s32[16]{0:T(128)}, s32[16]{0:T(128)}, f32[4,2,256,256]{3,2,0,1:T(8,128)}, /*index=5*/f32[16,16,256]{...) while((s32[]{:T(128)}, f32[80,256]{1,0:T(8,128)S(1)}, ...), condition=%wide.region_2.3_spmd, body=%wide.region_1.2_spmd.sunk | while | flops 75522056 | bytes 901857 | solution.py:106
  170.9 11.9 %all_gather.30 = f32[256,256]{1,0:T(8,128)} all-gather(f32[64,256]{1,0:T(8,128)S(1)} %slice.18), channel_id=1, replica_groups=mesh['tm'=64,'col'=4] {'col'}, dimensions={0}, use_global_device_ids=true | all-gather | bytes 327680 | tf_op jit(solution)/shard_map/all_gather | solution.py:107
  184.0 67.5 %all-gather.11.cloned.1.call-done = f32[1024,256]{1,0:T(8,128)} async-done(((f32[16,256]{1,0:T(8,128)}), f32[1024,256]{1,0:T(8,128)}) %all-gather.11.cloned.1.call-update) | async-done | bytes 1048592 | tf_op jit(solution)/shard_map/all_gather | solution.py:11
  251.6 100.2 %all-gather.9.cloned.1.call-done = f32[16384,256]{1,0:T(8,128)} async-done(((f32[256,256]{1,0:T(8,128)}), f32[16384,256]{1,0:T(8,128)}) %all-gather.9.cloned.1.call-update) | async-done | bytes 16777232 | tf_op jit(solution)/shard_map/all_gather | solution.py:11
  351.8 181.6 %while.92 = (s32[]{:T(128)}, f32[256,256]{0,1:T(8,128)S(1)}, f32[16,256]{1,0:T(8,128)S(1)}, s32[]{:T(128)}, f32[64,256,256]{2,1,0:T(8,128)}, /*index=5*/f32[64,16,256]{2,1,0:T(8,128)}, s32[]{:T(128)}, s32[]{:T(128)}) while((s32[]{:T(128)}, f32[256,256]{0,1:T(8,128)S(1)}, f32[16,256]{1,0:T(8,128)S(1)}, s32[]{:T(128)}, ...), condition=%wide.region_4.5_spmd.clone, body=%wide.region_3.4_spmd.clone.sunk | while | flops 213991424 | bytes 1936488 | solution.py:24
  353.0 1.6 fusion.105
  358.7 1.6 fusion.105
  361.5 1.6 fusion.105
  367.2 1.6 fusion.105
  370.0 1.6 fusion.105
  372.9 1.6 fusion.105
  375.7 1.6 fusion.105
  378.6 1.6 fusion.105
  381.4 1.6 fusion.105
  384.2 1.6 fusion.105
  387.1 1.6 fusion.105
  389.9 1.6 fusion.105
  392.7 1.6 fusion.105
  395.6 1.6 fusion.105
  401.3 1.6 fusion.105
  404.1 1.6 fusion.105
  406.9 1.6 fusion.105
  409.8 1.6 fusion.105
  412.6 1.6 fusion.105
  418.3 1.6 fusion.105
  421.1 1.6 fusion.105
  426.8 1.6 fusion.105
  429.6 1.6 fusion.105
  435.3 1.6 fusion.105
  438.2 1.6 fusion.105
  443.8 1.6 fusion.105
  446.7 1.6 fusion.105
  452.3 1.6 fusion.105
  455.2 1.6 fusion.105
  460.9 1.6 fusion.105
  463.7 1.6 fusion.105
  469.4 1.6 fusion.105
  472.2 1.6 fusion.105
  477.9 1.6 fusion.105
  480.7 1.6 fusion.105
  486.4 1.6 fusion.105
  489.2 1.6 fusion.105
  494.9 1.6 fusion.105
  497.7 1.6 fusion.105
  503.4 1.6 fusion.105
  506.3 1.6 fusion.105
  511.9 1.6 fusion.105
  514.8 1.6 fusion.105
  520.4 1.6 fusion.105
  523.3 1.6 fusion.105
  529.0 1.6 fusion.105
  531.8 1.6 fusion.105
  533.8 106.6 %while.89 = (s32[]{:T(128)}, f32[16,256]{1,0:T(8,128)S(1)}, f32[16,16,256]{2,1,0:T(8,128)S(1)}, f32[16,16,256]{2,1,0:T(8,128)S(1)}, s32[16]{0:T(128)}, /*index=5...) while((s32[]{:T(128)}, f32[16,256]{1,0:T(8,128)S(1)}, ...), condition=%wide.region_6.7_spmd, body=%wide.region_5.6_spmd.sunk | while | flops 25178116 | bytes 657091 | solution.py:129
  640.4 2.2 collective-permute-start
  642.6 2.9 collective-permute-done
  645.5 93.1 %while.90 = (s32[]{:T(128)}, f32[80,256]{1,0:T(8,128)S(1)}, f32[16,16,256]{2,1,0:T(8,128)S(1)}, s32[16]{0:T(128)}, f32[4,256,256]{2,1,0:T(8,128)S(1)}, /*index=5...) while((s32[]{:T(128)}, f32[80,256]{1,0:T(8,128)S(1)}, ...), condition=%wide.region_8.9_spmd, body=%wide.region_7.8_spmd.sunk | while | flops 75653128 | bytes 935623 | solution.py:148
  739.4 10.9 %all_gather.35 = f32[256,256]{1,0:T(8,128)} all-gather(f32[64,256]{1,0:T(8,128)S(1)} %slice.22), channel_id=1, replica_groups=mesh['tm'=64,'col'=4] {'col'}, dimensions={0}, use_global_device_ids=true | all-gather | bytes 327680 | tf_op jit(solution)/shard_map/all_gather | solution.py:154
  750.3 63.5 %all-gather.15.cloned.1.call-done = f32[1024,256]{1,0:T(8,128)} async-done(((f32[16,256]{1,0:T(8,128)}), f32[1024,256]{1,0:T(8,128)}) %all-gather.15.cloned.1.call-update) | async-done | bytes 1048592 | tf_op jit(solution)/shard_map/all_gather | solution.py:11
  813.8 100.1 %all-gather.13.cloned.1.call-done = f32[16384,256]{1,0:T(8,128)} async-done(((f32[256,256]{1,0:T(8,128)}), f32[16384,256]{1,0:T(8,128)}) %all-gather.13.cloned.1.call-update) | async-done | bytes 16777232 | tf_op jit(solution)/shard_map/all_gather | solution.py:11
  913.9 80.5 %while.93 = (s32[]{:T(128)}, f32[16,256]{1,0:T(8,128)S(1)}, s32[]{:T(128)}, f32[64,256,256]{2,1,0:T(8,128)}, f32[64,16,256]{2,1,0:T(8,128)}, /*index=5*/s32[]{:T(128)}, s32[]{:T(128)}, s32[]{:T(128)}, s32[]{:T(128)}) while((s32[]{:T(128)}, f32[16,256]{1,0:T(8,128)S(1)}, s32[]{:T(128)}, f32[64,256,256]{2,1,0:T(8,128)}, ...), condition=%wide.region_10.11_spmd.clone, body=%wide.region_9.10_spmd.clone.sunk | while | flops 12599304 | bytes 363165 | solution.py:24
  994.4 76.0 %while.91 = (s32[]{:T(128)}, f32[16,256]{1,0:T(8,128)S(1)}, f32[16,16,256]{2,1,0:T(8,128)S(1)}, s32[16]{0:T(128)}, f32[4,256,256]{2,1,0:T(8,128)S(1)}, /*index=5...) while((s32[]{:T(128)}, f32[16,256]{1,0:T(8,128)S(1)}, ...), condition=%wide.region_12.13_spmd, body=%wide.region_11.12_spmd.sunk | while | flops 12652550 | bytes 360639 | solution.py:173
  (668 shorter events, 439.4 us)
Async XLA Ops:
  7.2 526.2 %copy-start = (f32[256]{0:T(256)S(1)}, f32[256]{0:T(256)}, u32[]{:S(2)}) copy-start(f32[256]{0:T(256)} %param.25) | copy-start | bytes 3076
  7.2 638.3 %copy-start.1 = (f32[4,256,256]{2,1,0:T(8,128)S(1)}, f32[4,256,256]{2,1,0:T(8,128)}, u32[]{:S(2)}) copy-start(f32[4,256,256]{2,1,0:T(8,128)} %param.24) | copy-start | bytes 3145732
  7.2 244.4 %all-gather.11.cloned.1.call-start = ((), (), s32[]{:S(2)}) async-start(), calls=%async_computation.1 | async-start | bytes 1064960 | tf_op jit(solution)/shard_map/all_gather | solution.py:11
  170.8 180.9 %all-gather.9.cloned.1.call-start = ((), (), s32[]{:S(2)}) async-start(), calls=%async_computation | async-start | bytes 17039360 | tf_op jit(solution)/shard_map/all_gather | solution.py:11
  182.9 631.0 %all-gather.15.cloned.1.call-start = ((), (), s32[]{:S(2)}) async-start(), calls=%async_computation.3 | async-start | bytes 1064960 | tf_op jit(solution)/shard_map/all_gather | solution.py:11
  640.4 5.1 collective-permute-start
  738.6 331.9 %copy-start.2 = (f32[16,16,256]{2,1,0:T(8,128)}, f32[16,16,256]{2,1,0:T(8,128)S(1)}, u32[]{:S(2)}) copy-start(f32[16,16,256]{2,1,0:T(8,128)S(1)} %get-tuple-element.1261) | copy-start | bytes 786436
  739.3 174.6 %all-gather.13.cloned.1.call-start = ((), (), s32[]{:S(2)}) async-start(), calls=%async_computation.2 | async-start | bytes 17039360 | tf_op jit(solution)/shard_map/all_gather | solution.py:11
  1070.4 0.8 copy-start.3
Sparse Core Ops, SparseCore 0:
  171.0 80.5 all-gather.10
  254.3 97.3 all-gather.8
  739.4 74.3 all-gather.14
  816.5 97.3 all-gather.12
where the time goes:
time: 1090 us; the launch traced here: 1080 us
  matrix products  368 us (34%)
  waiting for transfers between devices  334 us (31%)
  loops' own time  185 us (17%)
  local copies, waits for them, and re-layouts  144 us (13%)
  blocking collectives  22.9 us (2%)
  between operations  14.1 us (1%)
    all_gather x4, waiting for transfers between devices, entering(): everything = jax.tree.map(lambda part: lax.all_gather(part, axis), value)  331 us
    dot_general x225, matrix products, accurate_matmul_result(): return jnp.dot(first_factor, second_factor, precision=lax.Precision.HIGHEST)  278 us
    dynamic_slice x96, local copies, waits for them, and re-layouts, shards(): lax.scan(compose_filter, initial_rows, (observations, band_index, obs_mask))  120 us
    dot_general x81, matrix products, apply_flipped_matrix(): lax.dot_general(first_factor, second_factor, (((1,), (1,)), ((), ())), pr...  90.2 us
    another operation x1, loops' own time, shards(): lax.scan(compose_filter, initial_rows, (observations, band_index, obs_mask))  73.1 us
    another operation x1, loops' own time, shards(): lax.scan(filter_step, start_rows, (observations, band_index, obs_mask))  42.3 us
    another operation x1, loops' own time, shards(): lax.scan(compose_smoother, initial_rows, (filtered, next_predicted, band_...  31.6 us
    another operation x1, loops' own time, shards(): lax.scan(smooth_step, after_records, (band_index, live_flags, offsets), r...  31.3 us
  transfers between devices with their start and end apart: 5, of which 5 were waited for; matrix products, arithmetic and copies ran while one was open for 0% of the time, Pallas kernels for 0%

commit v1 on v0

--- a/solution.py
+++ b/solution.py
@@ -6,28 +6,26 @@
 GRID = 16
 
 
-def entering(value, axis, combine, identity, reverse):
-    peers, index = (lax.axis_size(axis), lax.axis_index(axis))
-    everything = jax.tree.map(lambda part: lax.all_gather(part, axis), value)
-    start = jax.tree.map(
-        lambda part, zero: jnp.broadcast_to(jnp.asarray(zero, part.dtype), part.shape),
-        value,
-        identity,
-    )
-
-    def lap(k, before):
-        at = peers - 1 - k if reverse else k
-        reached = at > index if reverse else at < index
-        new = combine(before, jax.tree.map(lambda part: part[at], everything))
-        return jax.tree.map(lambda a, b: jnp.where(reached, a, b), new, before)
-
-    return lax.fori_loop(0, peers, lap, start)
-
-
 def passed_along(block, axis, distance):
     devices = range(lax.axis_size(axis))
     route = [(i - distance, i) for i in devices if i - distance in devices]
     return lax.ppermute(block, axis, route)
+
+
+def doubling_scan(matrix, records, axis, reverse):
+    peers, index = (lax.axis_size(axis), lax.axis_index(axis))
+    distance = 1
+    while distance < peers:
+        step = -distance if reverse else distance
+        reached = index + distance < peers if reverse else index >= distance
+        got_records = passed_along(records, axis, step)
+        new_records = accurate_matmul_result(got_records, matrix) + records
+        if 2 * distance < peers:
+            got_matrix = passed_along(matrix, axis, step)
+            matrix = jnp.where(reached, accurate_matmul_result(got_matrix, matrix), matrix)
+        records = jnp.where(reached, new_records, records)
+        distance *= 2
+    return records
 
 
 def accurate_matmul_result(first_factor, second_factor):
@@ -105,14 +103,18 @@
 
     forward_rows, _ = lax.scan(compose_filter, initial_rows, (observations, band_index, obs_mask))
     whole_matrix = lax.all_gather(forward_rows[:column_share], "col", axis=0, tiled=True)
-    prefix_matrix, prefix_records = entering(
-        (whole_matrix, forward_rows[column_share:]),
-        "tm",
-        compose_pair,
-        (identity, blank_records),
-        False,
+    first_block = time_index == 0
+    block_records = forward_rows[column_share:]
+    folded_records = jnp.where(
+        first_block, accurate_matmul_result(initial_mean[None, :], whole_matrix) + block_records, block_records
     )
-    start_rows = accurate_matmul_result(initial_mean[None, :], prefix_matrix) + prefix_records
+    folded_matrix = jnp.where(first_block, jnp.zeros_like(whole_matrix), whole_matrix)
+    ending_records = doubling_scan(folded_matrix, folded_records, "tm", False)
+    start_rows = jnp.where(
+        first_block,
+        jnp.broadcast_to(initial_mean[None, :], blank_records.shape),
+        passed_along(ending_records, "tm", 1),
+    )
 
     def filter_step(current_hidden_vector, argument_entries):
         entry_measurement, current_strip, current_measured_flag = argument_entries
@@ -152,13 +154,8 @@
         reverse=True,
     )
     whole_back = lax.all_gather(backward_rows[:column_share], "col", axis=0, tiled=True)
-    suffix_matrix, after_records = entering(
-        (whole_back, backward_rows[column_share:]),
-        "tm",
-        compose_pair,
-        (identity, blank_records),
-        True,
-    )
+    opening_records = doubling_scan(whole_back, backward_rows[column_share:], "tm", True)
+    after_records = passed_along(opening_records, "tm", -1)
 
     def smooth_step(following_lines, argument_entries):
         current_strip, current_active_flag, beginning_shift_amount = argument_entries

time: 1090 us -> 581 us (0.53)
  waiting for transfers between devices: 334 us -> 82.2 us
  matrix products: 368 us -> 127 us
  starting transfers between devices: 2.32 us -> 89.5 us
  local copies, waits for them, and re-layouts: 144 us -> 76.9 us
  loops' own time: 185 us -> 167 us
  between operations: 14.1 us -> 1.63 us
    all_gather x4 -> x0, waiting for transfers between devices: 331 us -> none  [entering(): everything = jax.tree.map(lambda part: lax.all_gather(part, axis), value)]
    dot_general x225 -> x55, matrix products: 278 us -> 30 us  [accurate_matmul_result(): return jnp.dot(first_factor, second_factor, precision=lax.Precision.HIGHEST)]
    ppermute x1 -> x25, starting transfers between devices: 2.16 us -> 89.5 us  [passed_along(): return lax.ppermute(block, axis, route)]
    ppermute x1 -> x25, waiting for transfers between devices: 2.85 us -> 82.2 us  [passed_along(): return lax.ppermute(block, axis, route)]
    dynamic_slice x96, local copies, waits for them, and re-layouts: 120 us -> 56.4 us  [shards(): lax.scan(compose_filter, initial_rows, (observations, band_index, obs_mask))]
  transfers between devices with their start and end apart: 5 -> 25, of which waited for: 5 -> 19; matrix products, arithmetic and copies ran while one was open for 0% -> 1% of each run, Pallas kernels for 0% -> 0%
where the time goes in v1:
time: 581 us; the launch traced here: 572 us
  loops' own time  167 us (29%)
  matrix products  127 us (22%)
  starting transfers between devices  89.5 us (15%)
  waiting for transfers between devices  82.2 us (14%)
  local copies, waits for them, and re-layouts  76.9 us (13%)
  blocking collectives  20.8 us (4%)
  other arithmetic  6.65 us (1%)
    dot_general x81, matrix products, apply_flipped_matrix(): lax.dot_general(first_factor, second_factor, (((1,), (1,)), ((), ())), pr...  97.4 us
    ppermute x25, starting transfers between devices, passed_along(): return lax.ppermute(block, axis, route)  89.5 us
    ppermute x25, waiting for transfers between devices, passed_along(): return lax.ppermute(block, axis, route)  82.2 us
    another operation x1, loops' own time, shards(): lax.scan(compose_filter, initial_rows, (observations, band_index, obs_mask))  73.9 us
    dynamic_slice x96, local copies, waits for them, and re-layouts, shards(): lax.scan(compose_filter, initial_rows, (observations, band_index, obs_mask))  56.4 us
    another operation x1, loops' own time, shards(): lax.scan(filter_step, start_rows, (observations, band_index, obs_mask))  36.9 us
    dot_general x55, matrix products, accurate_matmul_result(): return jnp.dot(first_factor, second_factor, precision=lax.Precision.HIGHEST)  30 us
    another operation x1, loops' own time, shards(): lax.scan(compose_smoother, initial_rows, (filtered, next_predicted, band_...  28.6 us
  transfers between devices with their start and end apart: 25, of which 19 were waited for; matrix products, arithmetic and copies ran while one was open for 1% of the time, Pallas kernels for 0%

profile of v1, /device:TPU:1, one launch (start us, length us, event | category | flops | bytes accessed | tf_op | source)
XLA Modules:
  0.0 572.0 jit_solution(13419827064083312169)
XLA Ops:
  2.1 2.1 multiply_add_fusion.1
  5.5 2.8 pad_maximum_fusion
  8.3 128.7 %while.56 = (s32[]{:T(128)}, f32[80,256]{1,0:T(8,128)S(1)}, s32[16]{0:T(128)S(1)}, s32[16]{0:T(128)S(1)}, f32[4,2,256,256]{3,2,0,1:T(8,128)}, /*index=5*/f32[16,...) while((s32[]{:T(128)}, f32[80,256]{1,0:T(8,128)S(1)}, ...), condition=%wide.region_2.3_spmd, body=%wide.region_1.2_spmd.sunk | while | flops 75522056 | bytes 901857 | solution.py:104
  137.1 11.2 %all_gather.6 = f32[256,256]{1,0:T(8,128)S(1)} all-gather(f32[64,256]{1,0:T(8,128)S(1)} %slice.18), channel_id=1, replica_groups=mesh['tm'=64,'col'=4] {'col'}, dimensions={0}, use_global_device_ids=true | all-gather | bytes 327680 | tf_op jit(solution)/shard_map/all_gather | solution.py:105
  148.4 6.5 %collective-permute-start.2 = (f32[256,256]{1,0:T(8,128)S(1)}, f32[256,256]{1,0:T(8,128)S(1)}, u32[]{:S(2)}, u32[]{:S(2)}) collective-permute-start(f32[256,256]{1,0:T(8,128)S(1)} %broadcast_select_fusion), channel_id=1, source_target_pairs={{0,4},{4,8},{8,12},{12,16},{16,20},{20,24},{24,28},{28,32},{32,36}... | collective-permute-start | bytes 786440 | tf_op jit(solution)/shard_map/ppermute | solution.py:12
  154.9 3.3 collective-permute-done.2
  158.5 3.6 collective-permute-start.4
  162.3 4.4 collective-permute-done.4
  167.1 7.4 %collective-permute-start.6 = (f32[256,256]{1,0:T(8,128)S(1)}, f32[256,256]{1,0:T(8,128)S(1)}, u32[]{:S(2)}, u32[]{:S(2)}) collective-permute-start(f32[256,256]{1,0:T(8,128)S(1)} %convolution_select_fusion.8), channel_id=1, source_target_pairs={{0,16},{4,20},{8,24},{12,28},{16,32},{20,36},{24,40},{28,44},{32,4... | collective-permute-start | bytes 786440 | tf_op jit(solution)/shard_map/ppermute | solution.py:12
  174.5 4.9 collective-permute-start
  179.4 6.4 %collective-permute-done = f32[16,256]{1,0:T(8,128)S(1)} collective-permute-done((f32[16,256]{1,0:T(8,128)S(1)}, f32[16,256]{1,0:T(8,128)S(1)}, u32[]{:S(2)}, u32[]{:S(2)}) %collective-permute-start) | collective-permute-done | bytes 16416 | tf_op jit(solution)/shard_map/ppermute | solution.py:12
  186.0 4.2 collective-permute-start.1
  192.2 2.5 collective-permute-start.3
  195.8 15.2 %collective-permute-start.5 = (f32[16,256]{1,0:T(8,128)S(1)}, f32[16,256]{1,0:T(8,128)S(1)}, u32[]{:S(2)}, u32[]{:S(2)}) collective-permute-start(f32[16,256]{1,0:T(8,128)S(1)} %fusion.44), channel_id=1, source_target_pairs={{0,32},{4,36},{8,40},{12,44},{16,48},{20,52},{24,56},{28,60},{32,6... | collective-permute-start | bytes 49160 | tf_op jit(solution)/shard_map/ppermute | solution.py:12
  211.4 2.8 collective-permute-start.10
  214.5 2.6 collective-permute-start.7
  218.2 7.8 %collective-permute-start.9 = (f32[16,256]{1,0:T(8,128)S(1)}, f32[16,256]{1,0:T(8,128)S(1)}, u32[]{:S(2)}, u32[]{:S(2)}) collective-permute-start(f32[16,256]{1,0:T(8,128)S(1)} %fusion.42), channel_id=1, source_target_pairs={{0,128},{4,132},{8,136},{12,140},{16,144},{20,148},{24,152},{28,15... | collective-permute-start | bytes 49160 | tf_op jit(solution)/shard_map/ppermute | solution.py:12
  227.1 9.9 %collective-permute-start.11 = (f32[16,256]{1,0:T(8,128)S(1)}, f32[16,256]{1,0:T(8,128)S(1)}, u32[]{:S(2)}, u32[]{:S(2)}) collective-permute-start(f32[16,256]{1,0:T(8,128)S(1)} %fusion.41), channel_id=1, source_target_pairs={{0,4},{4,8},{8,12},{12,16},{16,20},{20,24},{24,28},{28,32},{32,36}... | collective-permute-start | bytes 49160 | tf_op jit(solution)/shard_map/ppermute | solution.py:12
  238.6 85.6 %while.57 = (s32[]{:T(128)}, f32[16,256]{1,0:T(8,128)S(1)}, f32[16,16,256]{2,1,0:T(8,128)}, f32[16,16,256]{2,1,0:T(8,128)S(1)}, s32[16]{0:T(128)S(1)}, /*index=5...) while((s32[]{:T(128)}, f32[16,256]{1,0:T(8,128)S(1)}, ...), condition=%wide.region_4.5_spmd, body=%wide.region_3.4_spmd.sunk | while | flops 25178116 | bytes 657091 | solution.py:131
  242.3 1.7 bitcast_dynamic-update-slice_fusion.9
  247.7 1.7 bitcast_dynamic-update-slice_fusion.9
  253.0 1.7 bitcast_dynamic-update-slice_fusion.9
  258.4 1.7 bitcast_dynamic-update-slice_fusion.9
  263.7 1.7 bitcast_dynamic-update-slice_fusion.9
  269.1 1.7 bitcast_dynamic-update-slice_fusion.9
  274.4 1.7 bitcast_dynamic-update-slice_fusion.9
  279.8 1.7 bitcast_dynamic-update-slice_fusion.9
  285.1 1.7 bitcast_dynamic-update-slice_fusion.9
  290.5 1.7 bitcast_dynamic-update-slice_fusion.9
  295.8 1.7 bitcast_dynamic-update-slice_fusion.9
  301.2 1.7 bitcast_dynamic-update-slice_fusion.9
  306.5 1.7 bitcast_dynamic-update-slice_fusion.9
  311.9 1.7 bitcast_dynamic-update-slice_fusion.9
  317.2 1.7 bitcast_dynamic-update-slice_fusion.9
  322.6 1.7 bitcast_dynamic-update-slice_fusion.9
  324.2 1.9 collective-permute-start.12
  326.2 3.7 collective-permute-done.12
  329.9 87.4 %while.58 = (s32[]{:T(128)}, f32[80,256]{1,0:T(8,128)S(1)}, f32[16,16,256]{2,1,0:T(8,128)S(1)}, s32[16]{0:T(128)S(1)}, f32[4,256,256]{2,1,0:T(8,128)S(1)}, /*ind...) while((s32[]{:T(128)}, f32[80,256]{1,0:T(8,128)S(1)}, ...), condition=%wide.region_6.7_spmd, body=%wide.region_5.6_spmd.sunk | while | flops 75653128 | bytes 935623 | solution.py:150
  332.8 1.6 bitcast_dynamic-update-slice_fusion.10
  338.2 1.6 bitcast_dynamic-update-slice_fusion.10
  349.2 1.6 bitcast_dynamic-update-slice_fusion.10
  354.6 1.6 bitcast_dynamic-update-slice_fusion.10
  360.1 1.6 bitcast_dynamic-update-slice_fusion.10
  365.6 1.6 bitcast_dynamic-update-slice_fusion.10
  371.0 1.6 bitcast_dynamic-update-slice_fusion.10
  376.5 1.6 bitcast_dynamic-update-slice_fusion.10
  392.9 1.6 bitcast_dynamic-update-slice_fusion.10
  398.3 1.6 bitcast_dynamic-update-slice_fusion.10
  417.3 9.5 %all_gather.7 = f32[256,256]{1,0:T(8,128)S(1)} all-gather(f32[64,256]{1,0:T(8,128)S(1)} %slice.23), channel_id=1, replica_groups=mesh['tm'=64,'col'=4] {'col'}, dimensions={0}, use_global_device_ids=true | all-gather | bytes 327680 | tf_op jit(solution)/shard_map/all_gather | solution.py:156
  426.8 2.3 collective-permute-start.15
  429.1 6.4 %collective-permute-done.15 = f32[256,256]{1,0:T(8,128)S(1)} collective-permute-done((f32[256,256]{1,0:T(8,128)S(1)}, f32[256,256]{1,0:T(8,128)S(1)}, u32[]{:S(2)}, u32[]{:S(2)}) %collective-permute-start.15) | collective-permute-done | bytes 262176 | tf_op jit(solution)/shard_map/ppermute | solution.py:12
  437.2 7.3 %collective-permute-done.17 = f32[256,256]{1,0:T(8,128)S(1)} collective-permute-done((f32[256,256]{1,0:T(8,128)S(1)}, f32[256,256]{1,0:T(8,128)S(1)}, u32[]{:S(2)}, u32[]{:S(2)}) %collective-permute-start.17) | collective-permute-done | bytes 262176 | tf_op jit(solution)/shard_map/ppermute | solution.py:12
  446.2 1.9 collective-permute-start.13
  448.2 4.5 collective-permute-done.13
  454.2 7.1 %collective-permute-done.19 = f32[256,256]{1,0:T(8,128)S(1)} collective-permute-done((f32[256,256]{1,0:T(8,128)S(1)}, f32[256,256]{1,0:T(8,128)S(1)}, u32[]{:S(2)}, u32[]{:S(2)}) %collective-permute-start.19) | collective-permute-done | bytes 262176 | tf_op jit(solution)/shard_map/ppermute | solution.py:12
  463.0 1.8 collective-permute-done.14
  466.4 5.0 collective-permute-done.16
  472.9 3.5 collective-permute-done.21
  478.1 5.7 %collective-permute-done.18 = f32[16,256]{1,0:T(8,128)S(1)} collective-permute-done((f32[16,256]{1,0:T(8,128)S(1)}, f32[16,256]{1,0:T(8,128)S(1)}, u32[]{:S(2)}, u32[]{:S(2)}) %collective-permute-start.18) | collective-permute-done | bytes 16416 | tf_op jit(solution)/shard_map/ppermute | solution.py:12
  485.4 11.7 %collective-permute-done.20 = f32[16,256]{1,0:T(8,128)S(1)} collective-permute-done((f32[16,256]{1,0:T(8,128)S(1)}, f32[16,256]{1,0:T(8,128)S(1)}, u32[]{:S(2)}, u32[]{:S(2)}) %collective-permute-start.20) | collective-permute-done | bytes 16416 | tf_op jit(solution)/shard_map/ppermute | solution.py:12
  499.0 4.3 collective-permute-done.22
  503.5 3.2 collective-permute-start.24
  506.7 4.3 collective-permute-done.24
  511.1 60.2 %while.59 = (s32[]{:T(128)}, f32[16,256]{1,0:T(8,128)S(1)}, f32[16,16,256]{2,1,0:T(8,128)S(1)}, s32[16]{0:T(128)S(1)}, f32[4,256,256]{2,1,0:T(8,128)S(1)}, /*ind...) while((s32[]{:T(128)}, f32[16,256]{1,0:T(8,128)S(1)}, ...), condition=%wide.region_8.9_spmd, body=%wide.region_7.8_spmd.sunk | while | flops 12652550 | bytes 360639 | solution.py:170
  (343 shorter events, 179.6 us)
Async XLA Ops:
  0.6 3.5 copy-start.2
  0.6 3.5 copy-start.1
  5.5 2.8 copy-start.5
  5.5 2.8 copy-start.6
  8.3 153.8 %copy-start.4 = (f32[256]{0:T(256)S(1)}, f32[256]{0:T(256)}, u32[]{:S(2)}) copy-start(f32[256]{0:T(256)} %param.21) | copy-start | bytes 3076
  148.4 9.8 %collective-permute-start.2 = (f32[256,256]{1,0:T(8,128)S(1)}, f32[256,256]{1,0:T(8,128)S(1)}, u32[]{:S(2)}, u32[]{:S(2)}) collective-permute-start(f32[256,256]{1,0:T(8,128)S(1)} %broadcast_select_fusion), channel_id=1, source_target_pairs={{0,4},{4,8},{8,12},{12,16},{16,20},{20,24},{24,28},{28,32},{32,36}... | collective-permute-start | bytes 786440 | tf_op jit(solution)/shard_map/ppermute | solution.py:12
  158.5 8.2 %collective-permute-start.4 = (f32[256,256]{1,0:T(8,128)S(1)}, f32[256,256]{1,0:T(8,128)S(1)}, u32[]{:S(2)}, u32[]{:S(2)}) collective-permute-start(f32[256,256]{1,0:T(8,128)S(1)} %convolution_select_fusion.9), channel_id=1, source_target_pairs={{0,8},{4,12},{8,16},{12,20},{16,24},{20,28},{24,32},{28,36},{32,40... | collective-permute-start | bytes 786440 | tf_op jit(solution)/shard_map/ppermute | solution.py:12
  167.1 23.2 %collective-permute-start.6 = (f32[256,256]{1,0:T(8,128)S(1)}, f32[256,256]{1,0:T(8,128)S(1)}, u32[]{:S(2)}, u32[]{:S(2)}) collective-permute-start(f32[256,256]{1,0:T(8,128)S(1)} %convolution_select_fusion.8), channel_id=1, source_target_pairs={{0,16},{4,20},{8,24},{12,28},{16,32},{20,36},{24,40},{28,44},{32,4... | collective-permute-start | bytes 786440 | tf_op jit(solution)/shard_map/ppermute | solution.py:12
  174.5 11.3 %collective-permute-start = (f32[16,256]{1,0:T(8,128)S(1)}, f32[16,256]{1,0:T(8,128)S(1)}, u32[]{:S(2)}, u32[]{:S(2)}) collective-permute-start(f32[16,256]{1,0:T(8,128)S(1)} %add_select_fusion), channel_id=1, source_target_pairs={{0,4},{4,8},{8,12},{12,16},{16,20},{20,24},{24,28},{28,32},{32,36}... | collective-permute-start | bytes 49160 | tf_op jit(solution)/shard_map/ppermute | solution.py:12
  186.0 6.0 %collective-permute-start.1 = (f32[16,256]{1,0:T(8,128)S(1)}, f32[16,256]{1,0:T(8,128)S(1)}, u32[]{:S(2)}, u32[]{:S(2)}) collective-permute-start(f32[16,256]{1,0:T(8,128)S(1)} %fusion.46), channel_id=1, source_target_pairs={{0,8},{4,12},{8,16},{12,20},{16,24},{20,28},{24,32},{28,36},{32,40... | collective-permute-start | bytes 49160 | tf_op jit(solution)/shard_map/ppermute | solution.py:12
  190.7 20.3 %collective-permute-start.8 = (f32[256,256]{1,0:T(8,128)S(1)}, f32[256,256]{1,0:T(8,128)S(1)}, u32[]{:S(2)}, u32[]{:S(2)}) collective-permute-start(f32[256,256]{1,0:T(8,128)S(1)} %convolution_select_fusion.7), channel_id=1, source_target_pairs={{0,32},{4,36},{8,40},{12,44},{16,48},{20,52},{24,56},{28,60},{32,6... | collective-permute-start | bytes 786440 | tf_op jit(solution)/shard_map/ppermute | solution.py:12
  192.2 3.3 collective-permute-start.3
  195.8 18.4 %collective-permute-start.5 = (f32[16,256]{1,0:T(8,128)S(1)}, f32[16,256]{1,0:T(8,128)S(1)}, u32[]{:S(2)}, u32[]{:S(2)}) collective-permute-start(f32[16,256]{1,0:T(8,128)S(1)} %fusion.44), channel_id=1, source_target_pairs={{0,32},{4,36},{8,40},{12,44},{16,48},{20,52},{24,56},{28,60},{32,6... | collective-permute-start | bytes 49160 | tf_op jit(solution)/shard_map/ppermute | solution.py:12
  211.4 14.5 %collective-permute-start.10 = (f32[256,256]{1,0:T(8,128)S(1)}, f32[256,256]{1,0:T(8,128)S(1)}, u32[]{:S(2)}, u32[]{:S(2)}) collective-permute-start(f32[256,256]{1,0:T(8,128)S(1)} %convolution_select_fusion.6), channel_id=1, source_target_pairs={{0,64},{4,68},{8,72},{12,76},{16,80},{20,84},{24,88},{28,92},{32,9... | collective-permute-start | bytes 786440 | tf_op jit(solution)/shard_map/ppermute | solution.py:12
  214.5 3.4 collective-permute-start.7
  218.2 8.7 %collective-permute-start.9 = (f32[16,256]{1,0:T(8,128)S(1)}, f32[16,256]{1,0:T(8,128)S(1)}, u32[]{:S(2)}, u32[]{:S(2)}) collective-permute-start(f32[16,256]{1,0:T(8,128)S(1)} %fusion.42), channel_id=1, source_target_pairs={{0,128},{4,132},{8,136},{12,140},{16,144},{20,148},{24,152},{28,15... | collective-permute-start | bytes 49160 | tf_op jit(solution)/shard_map/ppermute | solution.py:12
  227.1 10.8 %collective-permute-start.11 = (f32[16,256]{1,0:T(8,128)S(1)}, f32[16,256]{1,0:T(8,128)S(1)}, u32[]{:S(2)}, u32[]{:S(2)}) collective-permute-start(f32[16,256]{1,0:T(8,128)S(1)} %fusion.41), channel_id=1, source_target_pairs={{0,4},{4,8},{8,12},{12,16},{16,20},{20,24},{24,28},{28,32},{32,36}... | collective-permute-start | bytes 49160 | tf_op jit(solution)/shard_map/ppermute | solution.py:12
  238.6 91.3 %copy-start = (f32[4,256,256]{2,1,0:T(8,128)S(1)}, f32[4,256,256]{2,1,0:T(8,128)}, u32[]{:S(2)}) copy-start(f32[4,256,256]{2,1,0:T(8,128)} %param.20) | copy-start | bytes 3145732
  324.2 5.6 collective-permute-start.12
  426.8 8.7 %collective-permute-start.15 = (f32[256,256]{1,0:T(8,128)S(1)}, f32[256,256]{1,0:T(8,128)S(1)}, u32[]{:S(2)}, u32[]{:S(2)}) collective-permute-start(f32[256,256]{1,0:T(8,128)S(1)} %all_gather.7), channel_id=1, source_target_pairs={{4,0},{8,4},{12,8},{16,12},{20,16},{24,20},{28,24},{32,28},{36,32}... | collective-permute-start | bytes 786440 | tf_op jit(solution)/shard_map/ppermute | solution.py:12
  435.9 8.6 %collective-permute-start.17 = (f32[256,256]{1,0:T(8,128)S(1)}, f32[256,256]{1,0:T(8,128)S(1)}, u32[]{:S(2)}, u32[]{:S(2)}) collective-permute-start(f32[256,256]{1,0:T(8,128)S(1)} %convolution_select_fusion.4), channel_id=1, source_target_pairs={{8,0},{12,4},{16,8},{20,12},{24,16},{28,20},{32,24},{36,28},{40,32... | collective-permute-start | bytes 786440 | tf_op jit(solution)/shard_map/ppermute | solution.py:12
  444.9 16.4 %collective-permute-start.19 = (f32[256,256]{1,0:T(8,128)S(1)}, f32[256,256]{1,0:T(8,128)S(1)}, u32[]{:S(2)}, u32[]{:S(2)}) collective-permute-start(f32[256,256]{1,0:T(8,128)S(1)} %convolution_select_fusion.3), channel_id=1, source_target_pairs={{16,0},{20,4},{24,8},{28,12},{32,16},{36,20},{40,24},{44,28},{48,3... | collective-permute-start | bytes 786440 | tf_op jit(solution)/shard_map/ppermute | solution.py:12
  446.2 6.4 %collective-permute-start.13 = (f32[16,256]{1,0:T(8,128)S(1)}, f32[16,256]{1,0:T(8,128)S(1)}, u32[]{:S(2)}, u32[]{:S(2)}) collective-permute-start(f32[16,256]{1,0:T(8,128)S(1)} %slice.22), channel_id=1, source_target_pairs={{4,0},{8,4},{12,8},{16,12},{20,16},{24,20},{28,24},{32,28},{36,32}... | collective-permute-start | bytes 49160 | tf_op jit(solution)/shard_map/ppermute | solution.py:12
  452.9 11.9 %collective-permute-start.14 = (f32[16,256]{1,0:T(8,128)S(1)}, f32[16,256]{1,0:T(8,128)S(1)}, u32[]{:S(2)}, u32[]{:S(2)}) collective-permute-start(f32[16,256]{1,0:T(8,128)S(1)} %fusion.40), channel_id=1, source_target_pairs={{8,0},{12,4},{16,8},{20,12},{24,16},{28,20},{32,24},{36,28},{40,32... | collective-permute-start | bytes 49160 | tf_op jit(solution)/shard_map/ppermute | solution.py:12
  461.7 14.7 %collective-permute-start.21 = (f32[256,256]{1,0:T(8,128)S(1)}, f32[256,256]{1,0:T(8,128)S(1)}, u32[]{:S(2)}, u32[]{:S(2)}) collective-permute-start(f32[256,256]{1,0:T(8,128)S(1)} %convolution_select_fusion.2), channel_id=1, source_target_pairs={{32,0},{36,4},{40,8},{44,12},{48,16},{52,20},{56,24},{60,28},{64,3... | collective-permute-start | bytes 786440 | tf_op jit(solution)/shard_map/ppermute | solution.py:12
  465.1 6.4 %collective-permute-start.16 = (f32[16,256]{1,0:T(8,128)S(1)}, f32[16,256]{1,0:T(8,128)S(1)}, u32[]{:S(2)}, u32[]{:S(2)}) collective-permute-start(f32[16,256]{1,0:T(8,128)S(1)} %fusion.39), channel_id=1, source_target_pairs={{16,0},{20,4},{24,8},{28,12},{32,16},{36,20},{40,24},{44,28},{48,3... | collective-permute-start | bytes 49160 | tf_op jit(solution)/shard_map/ppermute | solution.py:12
  471.6 12.2 %collective-permute-start.18 = (f32[16,256]{1,0:T(8,128)S(1)}, f32[16,256]{1,0:T(8,128)S(1)}, u32[]{:S(2)}, u32[]{:S(2)}) collective-permute-start(f32[16,256]{1,0:T(8,128)S(1)} %fusion.38), channel_id=1, source_target_pairs={{32,0},{36,4},{40,8},{44,12},{48,16},{52,20},{56,24},{60,28},{64,3... | collective-permute-start | bytes 49160 | tf_op jit(solution)/shard_map/ppermute | solution.py:12
  476.8 21.8 %collective-permute-start.23 = (f32[256,256]{1,0:T(8,128)S(1)}, f32[256,256]{1,0:T(8,128)S(1)}, u32[]{:S(2)}, u32[]{:S(2)}) collective-permute-start(f32[256,256]{1,0:T(8,128)S(1)} %convolution_select_fusion.1), channel_id=1, source_target_pairs={{64,0},{68,4},{72,8},{76,12},{80,16},{84,20},{88,24},{92,28},{96,3... | collective-permute-start | bytes 786440 | tf_op jit(solution)/shard_map/ppermute | solution.py:12
  484.1 13.0 %collective-permute-start.20 = (f32[16,256]{1,0:T(8,128)S(1)}, f32[16,256]{1,0:T(8,128)S(1)}, u32[]{:S(2)}, u32[]{:S(2)}) collective-permute-start(f32[16,256]{1,0:T(8,128)S(1)} %fusion.37), channel_id=1, source_target_pairs={{64,0},{68,4},{72,8},{76,12},{80,16},{84,20},{88,24},{92,28},{96,3... | collective-permute-start | bytes 49160 | tf_op jit(solution)/shard_map/ppermute | solution.py:12
  497.3 6.0 %collective-permute-start.22 = (f32[16,256]{1,0:T(8,128)S(1)}, f32[16,256]{1,0:T(8,128)S(1)}, u32[]{:S(2)}, u32[]{:S(2)}) collective-permute-start(f32[16,256]{1,0:T(8,128)S(1)} %fusion.36), channel_id=1, source_target_pairs={{128,0},{132,4},{136,8},{140,12},{144,16},{148,20},{152,24},{156,2... | collective-permute-start | bytes 49160 | tf_op jit(solution)/shard_map/ppermute | solution.py:12
  503.5 7.5 %collective-permute-start.24 = (f32[16,256]{1,0:T(8,128)S(1)}, f32[16,256]{1,0:T(8,128)S(1)}, u32[]{:S(2)}, u32[]{:S(2)}) collective-permute-start(f32[16,256]{1,0:T(8,128)S(1)} %fusion.35), channel_id=1, source_target_pairs={{4,0},{8,4},{12,8},{16,12},{20,16},{24,20},{28,24},{32,28},{36,32}... | collective-permute-start | bytes 49160 | tf_op jit(solution)/shard_map/ppermute | solution.py:12
  571.3 0.8 copy-start.3

commit v2 on v1

v2 whole, which is shorter than its diff:
```python
import functools

import jax
import jax.numpy as jnp
from jax import lax
from jax.experimental import pallas as pl
from jax.experimental.pallas import tpu as pltpu
from jax.sharding import PartitionSpec as P

GRID = 16


def passed_along(block, axis, distance):
    devices = range(lax.axis_size(axis))
    route = [(i - distance, i) for i in devices if i - distance in devices]
    return lax.ppermute(block, axis, route)


def accurate_matmul_result(first_factor, second_factor):
    return jnp.dot(first_factor, second_factor, precision=lax.Precision.HIGHEST)


def doubling_scan(matrix, records, axis, reverse):
    peers, index = (lax.axis_size(axis), lax.axis_index(axis))
    distance = 1
    while distance < peers:
        step = -distance if reverse else distance
        reached = index + distance < peers if reverse else index >= distance
        got_records = passed_along(records, axis, step)
        new_records = accurate_matmul_result(got_records, matrix) + records
        if 2 * distance < peers:
            got_matrix = passed_along(matrix, axis, step)
            matrix = jnp.where(reached, accurate_matmul_result(got_matrix, matrix), matrix)
        records = jnp.where(reached, new_records, records)
        distance *= 2
    return records


def diffusion_matrices(diffusivity, side_cells):
    cell_count = side_cells * side_cells
    cell_ids = jnp.arange(cell_count)
    cell_row = cell_ids // side_cells
    cell_col = cell_ids % side_cells
    adjacent = (
        jnp.abs(cell_row[:, None] - cell_row[None, :])
        + jnp.abs(cell_col[:, None] - cell_col[None, :])
        == 1
    )
    coupling = (
        0.5 * (diffusivity[:, :, None] + diffusivity[:, None, :]) * adjacent.astype(jnp.float32)
    )
    keeping = 1.0 - jnp.sum(coupling, axis=2)
    return coupling + keeping[:, :, None] * jnp.eye(cell_count, dtype=jnp.float32)


def recurrence_kernel(*refs, steps, reverse, store_all, side):
    if side:
        pick_ref, side_pick_ref, start_ref, table_ref, side_ref, source_ref, out_ref, side_out_ref = refs
    else:
        pick_ref, start_ref, table_ref, source_ref, out_ref = refs
    rows = start_ref[...]
    order = range(steps - 1, -1, -1) if reverse else range(steps)
    for t in order:
        if side:
            side_out_ref[t] = jnp.dot(
                rows,
                side_ref[side_pick_ref[t]],
                precision=lax.Precision.HIGHEST,
                preferred_element_type=jnp.float32,
            )
        rows = (
            jnp.dot(
                rows,
                table_ref[pick_ref[t]],
                precision=lax.Precision.HIGHEST,
                preferred_element_type=jnp.float32,
            )
            + source_ref[t]
        )
        if store_all:
            out_ref[t] = rows
    if not store_all:
        out_ref[...] = rows


def recurrence(pick, start, table, source, reverse, store_all, side=None):
    steps = source.shape[0]
    smem = pl.BlockSpec(memory_space=pltpu.SMEM)
    vmem = pl.BlockSpec(memory_space=pltpu.VMEM)
    out_shape = jax.ShapeDtypeStruct(source.shape if store_all else start.shape, jnp.float32)
    if side is None:
        operands = (pick, start, table, source)
        in_specs = [smem, vmem, vmem, vmem]
        out_specs = vmem
    else:
        side_pick, side_table = side
        operands = (pick, side_pick, start, table, side_table, source)
        in_specs = [smem, smem, vmem, vmem, vmem, vmem]
        out_shape = (out_shape, jax.ShapeDtypeStruct(source.shape, jnp.float32))
        out_specs = (vmem, vmem)
    return pl.pallas_call(
        functools.partial(
            recurrence_kernel,
            steps=steps,
            reverse=reverse,
            store_all=store_all,
            side=side is not None,
        ),
        out_shape=out_shape,
        in_specs=in_specs,
        out_specs=out_specs,
    )(*operands)


def per_band_products(lines, factors, weights):
    steps, rows, states = lines.shape
    bands = factors.shape[0]
    every = accurate_matmul_result(
        lines.reshape(steps * rows, states),
        jnp.transpose(factors, (1, 0, 2)).reshape(states, bands * states),
    ).reshape(steps, rows, bands, states)
    return jnp.sum(every * weights[:, None, :, None], axis=2)


def shards(
    observations,
    band_index,
    obs_mask,
    diffusivity,
    mode_correction_factors,
    mode_backward_factors,
    initial_mean,
):
    steps_dev = observations.shape[0]
    record_rows = observations.shape[1]
    states = initial_mean.shape[0]
    bands = diffusivity.shape[0]
    column_share = states // lax.axis_size("col")
    column_index = lax.axis_index("col")
    time_devices = lax.axis_size("tm")
    time_index = lax.axis_index("tm")
    dynamics = diffusion_matrices(diffusivity, GRID)
    gain = jnp.transpose(mode_correction_factors, (0, 2, 1))
    corrected = dynamics - jnp.einsum(
        "bij,bjk->bik", dynamics, gain, precision=lax.Precision.HIGHEST
    )
    forward_table = jnp.stack([dynamics, corrected], axis=1).reshape(2 * bands, states, states)
    forward_pick = 2 * band_index + obs_mask
    identity = jnp.eye(states, dtype=jnp.float32)
    own_identity = lax.dynamic_slice_in_dim(identity, column_index * column_share, column_share, 0)
    blank_columns = jnp.zeros((steps_dev, column_share, states), jnp.float32)
    initial_rows = jnp.concatenate(
        [own_identity, jnp.zeros((record_rows, states), jnp.float32)], axis=0
    )
    band_weights = (band_index[:, None] == jnp.arange(bands)[None, :]).astype(jnp.float32)
    observed_weights = band_weights * obs_mask.astype(jnp.float32)[:, None]
    measured = per_band_products(observations, gain, observed_weights)

    forward_rows = recurrence(
        forward_pick,
        initial_rows,
        forward_table,
        jnp.concatenate([blank_columns, measured], axis=1),
        False,
        False,
    )
    whole_matrix = lax.all_gather(forward_rows[:column_share], "col", axis=0, tiled=True)
    first_block = time_index == 0
    block_records = forward_rows[column_share:]
    folded_records = jnp.where(
        first_block,
        accurate_matmul_result(initial_mean[None, :], whole_matrix) + block_records,
        block_records,
    )
    folded_matrix = jnp.where(first_block, jnp.zeros_like(whole_matrix), whole_matrix)
    ending_records = doubling_scan(folded_matrix, folded_records, "tm", False)
    start_rows = jnp.where(
        first_block,
        jnp.broadcast_to(initial_mean[None, :], (record_rows, states)),
        passed_along(ending_records, "tm", 1),
    )

    filtered, predicted = recurrence(
        forward_pick,
        start_rows,
        forward_table,
        measured,
        False,
        True,
        side=(band_index, dynamics),
    )
    following = passed_along(predicted[0], "tm", -1)
    next_predicted = jnp.concatenate([predicted[1:], following[None]], axis=0)

    final_here = (time_index == time_devices - 1) & (jnp.arange(steps_dev) == steps_dev - 1)
    backward = jnp.transpose(mode_backward_factors, (0, 2, 1))
    backward_table = jnp.concatenate([backward, jnp.zeros_like(backward[:1])], axis=0)
    backward_pick = jnp.where(final_here, bands, band_index)
    live_weights = band_weights * (1.0 - final_here.astype(jnp.float32))[:, None]
    shift = filtered - per_band_products(next_predicted, backward, live_weights)

    backward_rows = recurrence(
        backward_pick,
        initial_rows,
        backward_table,
        jnp.concatenate([blank_columns, shift], axis=1),
        True,
        False,
    )
    whole_back = lax.all_gather(backward_rows[:column_share], "col", axis=0, tiled=True)
    opening_records = doubling_scan(whole_back, backward_rows[column_share:], "tm", True)
    after_records = passed_along(opening_records, "tm", -1)

    smoothed = recurrence(backward_pick, after_records, backward_table, shift, True, True)
    return (filtered, smoothed)


def solution(mesh):
    return jax.shard_map(
        shards,
        mesh=mesh,
        in_specs=(P("tm", "col", None), P("tm"), P("tm"), P(), P(), P(), P()),
        out_specs=(P("tm", "col", None), P("tm", "col", None)),
        check_vma=False,
    )
```

time: 581 us -> 248 us (0.43); the launches traced: 572 us -> 246 us
  loops' own time: 167 us -> 0 us
  matrix products: 127 us -> 10.6 us
  local copies, waits for them, and re-layouts: 76.9 us -> 9.93 us
  Pallas kernels: 0 us -> 29.1 us
  waiting for transfers between devices: 82.2 us -> 75.9 us
    another operation x4 -> x0, loops' own time: 167 us -> none  [the longest x1 73.9 us: shards(): lax.scan(compose_filter, initial_rows, (observations, band_index, obs_mask))]
    dot_general x81 -> x1, matrix products: 97.4 us -> 1.32 us  [shards(): jnp.einsum('bij,bjk->bik', dynamics, gain, precision=lax.Precision.HIGHEST)]
    dynamic_slice x128 -> x0, local copies, waits for them, and re-layouts: 75 us -> none  [the longest x96 56.4 us: shards(): lax.scan(compose_filter, initial_rows, (observations, band_index, obs_mask))]
    pallas_call x0 -> x4, Pallas kernels: none -> 29.1 us  [recurrence(): pl.pallas_call(functools.partial(recurrence_kernel, steps=steps, reverse=...]
    dot_general x55 -> x25, matrix products: 30 us -> 9.24 us  [accurate_matmul_result(): return jnp.dot(first_factor, second_factor, precision=lax.Precision.HIGHEST)]
    ppermute x25, waiting for transfers between devices: 82.2 us -> 75.9 us  [passed_along(): return lax.ppermute(block, axis, route)]
  transfers between devices with their start and end apart: 25 -> 25, of which waited for: 19 -> 18; matrix products, arithmetic and copies ran while one was open for 1% -> 4% of each run, Pallas kernels for 0% -> 0%
where the time goes in v2:
time: 248 us; the launch traced here: 246 us
  starting transfers between devices  92.2 us (37%)
  waiting for transfers between devices  75.9 us (31%)
  Pallas kernels  29.1 us (12%)
  blocking collectives  21 us (8%)
  matrix products  10.6 us (4%)
  local copies, waits for them, and re-layouts  9.93 us (4%)
  other arithmetic  5.98 us (2%)
    ppermute x25, starting transfers between devices, passed_along(): return lax.ppermute(block, axis, route)  92.2 us
    ppermute x25, waiting for transfers between devices, passed_along(): return lax.ppermute(block, axis, route)  75.9 us
    pallas_call x4, Pallas kernels, recurrence(): pl.pallas_call(functools.partial(recurrence_kernel, steps=steps, reverse=...  29.1 us
    all_gather x1, blocking collectives, shards(): lax.all_gather(forward_rows[:column_share], 'col', axis=0, tiled=True)  11.2 us
    all_gather x1, blocking collectives, shards(): lax.all_gather(backward_rows[:column_share], 'col', axis=0, tiled=True)  9.77 us
    dot_general x25, matrix products, accurate_matmul_result(): return jnp.dot(first_factor, second_factor, precision=lax.Precision.HIGHEST)  9.24 us
  transfers between devices with their start and end apart: 25, of which 18 were waited for; matrix products, arithmetic and copies ran while one was open for 4% of the time, Pallas kernels for 0%

profile of v2, /device:TPU:1, one launch (start us, length us, event | category | flops | bytes accessed | tf_op | source)
XLA Modules:
  0.0 246.3 jit_solution(14512496863521838126)
XLA Ops:
  0.9 1.2 fusion.17
  2.1 1.1 multiply_add_fusion.1
  3.2 1.3 fusion
  4.7 1.5 copy.10
  7.5 1.1 fusion.1.refs_5_
  8.6 1.2 concatenate.16.refs_3_
  9.8 7.4 %shard_map.86 = f32[80,256]{1,0:T(8,128)} custom-call(s32[16]{0:T(128)} %get-tuple-element.9.refs_0_, f32[80,256]{1,0:T(8,128)} %concatenate.15.refs_1_, f32[8,256,256]{2,1,0:T(8,128)} %bitcast.86, f32[16,80,256]{2,1,0:T(8,128)} %concatenate.16.refs_3_), custom_call_target="tpu_custom_call" | custom-call | tf_op jit(solution)/shard_map/pallas_call | solution.py:101
  17.2 0.8 slice.24
  18.0 11.2 %all_gather.6 = f32[256,256]{1,0:T(8,128)S(1)} all-gather(f32[64,256]{1,0:T(8,128)S(1)} %slice.24), channel_id=1, replica_groups=mesh['tm'=64,'col'=4] {'col'}, dimensions={0}, use_global_device_ids=true | all-gather | bytes 327680 | tf_op jit(solution)/shard_map/all_gather | solution.py:167
  29.3 6.5 %collective-permute-start.2 = (f32[256,256]{1,0:T(8,128)S(1)}, f32[256,256]{1,0:T(8,128)S(1)}, u32[]{:S(2)}, u32[]{:S(2)}) collective-permute-start(f32[256,256]{1,0:T(8,128)S(1)} %broadcast_select_fusion), channel_id=1, source_target_pairs={{0,4},{4,8},{8,12},{12,16},{16,20},{20,24},{24,28},{28,32},{32,36}... | collective-permute-start | bytes 786440 | tf_op jit(solution)/shard_map/ppermute | solution.py:16
  35.8 3.3 %collective-permute-done.2 = f32[256,256]{1,0:T(8,128)S(1)} collective-permute-done((f32[256,256]{1,0:T(8,128)S(1)}, f32[256,256]{1,0:T(8,128)S(1)}, u32[]{:S(2)}, u32[]{:S(2)}) %collective-permute-start.2) | collective-permute-done | bytes 262176 | tf_op jit(solution)/shard_map/ppermute | solution.py:16
  39.5 3.6 %collective-permute-start.4 = (f32[256,256]{1,0:T(8,128)S(1)}, f32[256,256]{1,0:T(8,128)S(1)}, u32[]{:S(2)}, u32[]{:S(2)}) collective-permute-start(f32[256,256]{1,0:T(8,128)S(1)} %convolution_select_fusion.9), channel_id=1, source_target_pairs={{0,8},{4,12},{8,16},{12,20},{16,24},{20,28},{24,32},{28,36},{32,40... | collective-permute-start | bytes 786440 | tf_op jit(solution)/shard_map/ppermute | solution.py:16
  43.3 4.4 %collective-permute-done.4 = f32[256,256]{1,0:T(8,128)S(1)} collective-permute-done((f32[256,256]{1,0:T(8,128)S(1)}, f32[256,256]{1,0:T(8,128)S(1)}, u32[]{:S(2)}, u32[]{:S(2)}) %collective-permute-start.4) | collective-permute-done | bytes 262176 | tf_op jit(solution)/shard_map/ppermute | solution.py:16
  48.0 7.4 %collective-permute-start.6 = (f32[256,256]{1,0:T(8,128)S(1)}, f32[256,256]{1,0:T(8,128)S(1)}, u32[]{:S(2)}, u32[]{:S(2)}) collective-permute-start(f32[256,256]{1,0:T(8,128)S(1)} %convolution_select_fusion.8), channel_id=1, source_target_pairs={{0,16},{4,20},{8,24},{12,28},{16,32},{20,36},{24,40},{28,44},{32,4... | collective-permute-start | bytes 786440 | tf_op jit(solution)/shard_map/ppermute | solution.py:16
  55.4 0.7 add_select_fusion
  56.1 4.9 %collective-permute-start = (f32[16,256]{1,0:T(8,128)S(1)}, f32[16,256]{1,0:T(8,128)S(1)}, u32[]{:S(2)}, u32[]{:S(2)}) collective-permute-start(f32[16,256]{1,0:T(8,128)S(1)} %add_select_fusion), channel_id=1, source_target_pairs={{0,4},{4,8},{8,12},{12,16},{16,20},{20,24},{24,28},{28,32},{32,36}... | collective-permute-start | bytes 49160 | tf_op jit(solution)/shard_map/ppermute | solution.py:16
  61.0 5.7 %collective-permute-done = f32[16,256]{1,0:T(8,128)S(1)} collective-permute-done((f32[16,256]{1,0:T(8,128)S(1)}, f32[16,256]{1,0:T(8,128)S(1)}, u32[]{:S(2)}, u32[]{:S(2)}) %collective-permute-start) | collective-permute-done | bytes 16416 | tf_op jit(solution)/shard_map/ppermute | solution.py:16
  66.9 4.2 %collective-permute-start.1 = (f32[16,256]{1,0:T(8,128)S(1)}, f32[16,256]{1,0:T(8,128)S(1)}, u32[]{:S(2)}, u32[]{:S(2)}) collective-permute-start(f32[16,256]{1,0:T(8,128)S(1)} %fusion.14), channel_id=1, source_target_pairs={{0,8},{4,12},{8,16},{12,20},{16,24},{20,28},{24,32},{28,36},{32,40... | collective-permute-start | bytes 49160 | tf_op jit(solution)/shard_map/ppermute | solution.py:16
  71.6 1.3 collective-permute-start.8
  73.2 2.5 %collective-permute-start.3 = (f32[16,256]{1,0:T(8,128)S(1)}, f32[16,256]{1,0:T(8,128)S(1)}, u32[]{:S(2)}, u32[]{:S(2)}) collective-permute-start(f32[16,256]{1,0:T(8,128)S(1)} %fusion.13), channel_id=1, source_target_pairs={{0,16},{4,20},{8,24},{12,28},{16,32},{20,36},{24,40},{28,44},{32,4... | collective-permute-start | bytes 49160 | tf_op jit(solution)/shard_map/ppermute | solution.py:16
  75.6 0.8 collective-permute-done.3
  76.7 15.0 %collective-permute-start.5 = (f32[16,256]{1,0:T(8,128)S(1)}, f32[16,256]{1,0:T(8,128)S(1)}, u32[]{:S(2)}, u32[]{:S(2)}) collective-permute-start(f32[16,256]{1,0:T(8,128)S(1)} %fusion.12), channel_id=1, source_target_pairs={{0,32},{4,36},{8,40},{12,44},{16,48},{20,52},{24,56},{28,60},{32,6... | collective-permute-start | bytes 49160 | tf_op jit(solution)/shard_map/ppermute | solution.py:16
  92.1 3.0 %collective-permute-start.10 = (f32[256,256]{1,0:T(8,128)S(1)}, f32[256,256]{1,0:T(8,128)S(1)}, u32[]{:S(2)}, u32[]{:S(2)}) collective-permute-start(f32[256,256]{1,0:T(8,128)S(1)} %convolution_select_fusion.6), channel_id=1, source_target_pairs={{0,64},{4,68},{8,72},{12,76},{16,80},{20,84},{24,88},{28,92},{32,9... | collective-permute-start | bytes 786440 | tf_op jit(solution)/shard_map/ppermute | solution.py:16
  95.4 2.6 %collective-permute-start.7 = (f32[16,256]{1,0:T(8,128)S(1)}, f32[16,256]{1,0:T(8,128)S(1)}, u32[]{:S(2)}, u32[]{:S(2)}) collective-permute-start(f32[16,256]{1,0:T(8,128)S(1)} %fusion.11), channel_id=1, source_target_pairs={{0,64},{4,68},{8,72},{12,76},{16,80},{20,84},{24,88},{28,92},{32,9... | collective-permute-start | bytes 49160 | tf_op jit(solution)/shard_map/ppermute | solution.py:16
  98.0 0.8 collective-permute-done.7
  99.1 7.7 %collective-permute-start.9 = (f32[16,256]{1,0:T(8,128)S(1)}, f32[16,256]{1,0:T(8,128)S(1)}, u32[]{:S(2)}, u32[]{:S(2)}) collective-permute-start(f32[16,256]{1,0:T(8,128)S(1)} %fusion.10), channel_id=1, source_target_pairs={{0,128},{4,132},{8,136},{12,140},{16,144},{20,148},{24,152},{28,15... | collective-permute-start | bytes 49160 | tf_op jit(solution)/shard_map/ppermute | solution.py:16
  107.9 10.1 %collective-permute-start.11 = (f32[16,256]{1,0:T(8,128)S(1)}, f32[16,256]{1,0:T(8,128)S(1)}, u32[]{:S(2)}, u32[]{:S(2)}) collective-permute-start(f32[16,256]{1,0:T(8,128)S(1)} %fusion.9), channel_id=1, source_target_pairs={{0,4},{4,8},{8,12},{12,16},{16,20},{20,24},{24,28},{28,32},{32,36}... | collective-permute-start | bytes 49160 | tf_op jit(solution)/shard_map/ppermute | solution.py:16
  118.1 1.3 multiply_add_fusion.refs_4_
  120.0 7.9 %shard_map.87 = (f32[16,16,256]{2,1,0:T(8,128)}, f32[16,16,256]{2,1,0:T(8,128)}) custom-call(s32[16]{0:T(128)} %get-tuple-element.9.refs_0_, s32[16]{0:T(128)} %refs_1_.1, f32[16,256]{1,0:T(8,128)} %broadcast_select_fusion.1.refs_2_, f32[8,256,256]{2,1,0:T(8,128)} %bitcast.87, f32[4,256,256]{2,1,0:T(8,128)} %multiply_add_fusion.refs_4_, f32[16,16,256]{2,1,0:T(8,128)} %copy-done.3), custom_call_target="tpu_custom_call" | custom-call | tf_op jit(solution)/shard_map/pallas_call | solution.py:101
  127.9 0.7 slice_bitcast_fusion
  128.6 2.0 collective-permute-start.12
  131.1 1.2 concatenate.17.refs_2_
  132.3 1.5 collective-permute-done.12
  133.8 1.1 fusion.2
  135.0 1.2 concatenate.19.refs_3_
  136.2 7.1 %shard_map.88 = f32[80,256]{1,0:T(8,128)} custom-call(s32[16]{0:T(128)} %get-tuple-element.8.refs_0_, f32[80,256]{1,0:T(8,128)} %concatenate.15.refs_1_, f32[5,256,256]{2,1,0:T(8,128)} %concatenate.17.refs_2_, f32[16,80,256]{2,1,0:T(8,128)} %concatenate.19.refs_3_), custom_call_target="tpu_custom_call" | custom-call | tf_op jit(solution)/shard_map/pallas_call | solution.py:101
  143.3 0.8 slice.27
  144.1 9.8 %all_gather.7 = f32[256,256]{1,0:T(8,128)S(1)} all-gather(f32[64,256]{1,0:T(8,128)S(1)} %slice.27), channel_id=1, replica_groups=mesh['tm'=64,'col'=4] {'col'}, dimensions={0}, use_global_device_ids=true | all-gather | bytes 327680 | tf_op jit(solution)/shard_map/all_gather | solution.py:210
  153.9 2.5 %collective-permute-start.15 = (f32[256,256]{1,0:T(8,128)S(1)}, f32[256,256]{1,0:T(8,128)S(1)}, u32[]{:S(2)}, u32[]{:S(2)}) collective-permute-start(f32[256,256]{1,0:T(8,128)S(1)} %all_gather.7), channel_id=1, source_target_pairs={{4,0},{8,4},{12,8},{16,12},{20,16},{24,20},{28,24},{32,28},{36,32}... | collective-permute-start | bytes 786440 | tf_op jit(solution)/shard_map/ppermute | solution.py:16
  156.4 6.1 %collective-permute-done.15 = f32[256,256]{1,0:T(8,128)S(1)} collective-permute-done((f32[256,256]{1,0:T(8,128)S(1)}, f32[256,256]{1,0:T(8,128)S(1)}, u32[]{:S(2)}, u32[]{:S(2)}) %collective-permute-start.15) | collective-permute-done | bytes 262176 | tf_op jit(solution)/shard_map/ppermute | solution.py:16
  162.9 1.3 collective-permute-start.17
  164.2 7.3 %collective-permute-done.17 = f32[256,256]{1,0:T(8,128)S(1)} collective-permute-done((f32[256,256]{1,0:T(8,128)S(1)}, f32[256,256]{1,0:T(8,128)S(1)}, u32[]{:S(2)}, u32[]{:S(2)}) %collective-permute-start.17) | collective-permute-done | bytes 262176 | tf_op jit(solution)/shard_map/ppermute | solution.py:16
  171.9 1.3 collective-permute-start.19
  173.2 0.7 slice.26
  174.0 1.9 collective-permute-start.13
  175.9 3.8 %collective-permute-done.13 = f32[16,256]{1,0:T(8,128)S(1)} collective-permute-done((f32[16,256]{1,0:T(8,128)S(1)}, f32[16,256]{1,0:T(8,128)S(1)}, u32[]{:S(2)}, u32[]{:S(2)}) %collective-permute-start.13) | collective-permute-done | bytes 16416 | tf_op jit(solution)/shard_map/ppermute | solution.py:16
  179.6 0.9 fusion.8
  180.6 1.3 collective-permute-start.14
  181.9 6.4 %collective-permute-done.19 = f32[256,256]{1,0:T(8,128)S(1)} collective-permute-done((f32[256,256]{1,0:T(8,128)S(1)}, f32[256,256]{1,0:T(8,128)S(1)}, u32[]{:S(2)}, u32[]{:S(2)}) %collective-permute-start.19) | collective-permute-done | bytes 262176 | tf_op jit(solution)/shard_map/ppermute | solution.py:16
  188.7 1.3 collective-permute-start.21
  190.0 2.5 %collective-permute-done.14 = f32[16,256]{1,0:T(8,128)S(1)} collective-permute-done((f32[16,256]{1,0:T(8,128)S(1)}, f32[16,256]{1,0:T(8,128)S(1)}, u32[]{:S(2)}, u32[]{:S(2)}) %collective-permute-start.14) | collective-permute-done | bytes 16416 | tf_op jit(solution)/shard_map/ppermute | solution.py:16
  192.8 1.3 collective-permute-start.16
  194.1 5.0 %collective-permute-done.16 = f32[16,256]{1,0:T(8,128)S(1)} collective-permute-done((f32[16,256]{1,0:T(8,128)S(1)}, f32[16,256]{1,0:T(8,128)S(1)}, u32[]{:S(2)}, u32[]{:S(2)}) %collective-permute-start.16) | collective-permute-done | bytes 16416 | tf_op jit(solution)/shard_map/ppermute | solution.py:16
  199.3 1.5 collective-permute-start.18
  200.8 2.6 %collective-permute-done.21 = f32[256,256]{1,0:T(8,128)S(1)} collective-permute-done((f32[256,256]{1,0:T(8,128)S(1)}, f32[256,256]{1,0:T(8,128)S(1)}, u32[]{:S(2)}, u32[]{:S(2)}) %collective-permute-start.21) | collective-permute-done | bytes 262176 | tf_op jit(solution)/shard_map/ppermute | solution.py:16
  203.8 1.3 collective-permute-start.23
  205.1 6.4 %collective-permute-done.18 = f32[16,256]{1,0:T(8,128)S(1)} collective-permute-done((f32[16,256]{1,0:T(8,128)S(1)}, f32[16,256]{1,0:T(8,128)S(1)}, u32[]{:S(2)}, u32[]{:S(2)}) %collective-permute-start.18) | collective-permute-done | bytes 16416 | tf_op jit(solution)/shard_map/ppermute | solution.py:16
  211.7 1.3 collective-permute-start.20
  213.0 8.6 %collective-permute-done.20 = f32[16,256]{1,0:T(8,128)S(1)} collective-permute-done((f32[16,256]{1,0:T(8,128)S(1)}, f32[16,256]{1,0:T(8,128)S(1)}, u32[]{:S(2)}, u32[]{:S(2)}) %collective-permute-start.20) | collective-permute-done | bytes 16416 | tf_op jit(solution)/shard_map/ppermute | solution.py:16
  221.9 1.3 collective-permute-start.22
  223.6 8.6 %collective-permute-done.22 = f32[16,256]{1,0:T(8,128)S(1)} collective-permute-done((f32[16,256]{1,0:T(8,128)S(1)}, f32[16,256]{1,0:T(8,128)S(1)}, u32[]{:S(2)}, u32[]{:S(2)}) %collective-permute-start.22) | collective-permute-done | bytes 16416 | tf_op jit(solution)/shard_map/ppermute | solution.py:16
  232.4 5.1 %collective-permute-start.24 = (f32[16,256]{1,0:T(8,128)S(1)}, f32[16,256]{1,0:T(8,128)S(1)}, u32[]{:S(2)}, u32[]{:S(2)}) collective-permute-start(f32[16,256]{1,0:T(8,128)S(1)} %fusion.3), channel_id=1, source_target_pairs={{4,0},{8,4},{12,8},{16,12},{20,16},{24,20},{28,24},{32,28},{36,32}... | collective-permute-start | bytes 49160 | tf_op jit(solution)/shard_map/ppermute | solution.py:16
  237.4 1.5 collective-permute-done.24.refs_1_
  239.5 6.7 %shard_map.89 = f32[16,16,256]{2,1,0:T(8,128)} custom-call(s32[16]{0:T(128)} %get-tuple-element.8.refs_0_, f32[16,256]{1,0:T(8,128)} %copy-done.8, f32[5,256,256]{2,1,0:T(8,128)} %concatenate.17.refs_2_, f32[16,16,256]{2,1,0:T(8,128)} %copy-done.2), custom_call_target="tpu_custom_call" | custom-call | tf_op jit(solution)/shard_map/pallas_call | solution.py:101
  (69 shorter events, 10.0 us)
Async XLA Ops:
  0.6 2.6 %copy-start = (f32[4,256,256]{2,1,0:T(8,128)S(1)}, f32[4,256,256]{2,1,0:T(8,128)}, u32[]{:S(2)}) copy-start(f32[4,256,256]{2,1,0:T(8,128)} %param.11) | copy-start | bytes 3145732
  0.6 2.6 %copy-start.4 = (f32[4,256]{1,0:T(4,128)S(1)}, f32[4,256]{1,0:T(4,128)}, u32[]{:S(2)}) copy-start(f32[4,256]{1,0:T(4,128)} %param.10) | copy-start | bytes 12292
  4.7 1.6 copy-start.9
  4.7 1.5 copy-start.11
  4.7 2.8 %copy-start.7 = (f32[16,16,256]{2,1,0:T(8,128)S(1)}, f32[16,16,256]{2,1,0:T(8,128)}, u32[]{:S(2)}) copy-start(f32[16,16,256]{2,1,0:T(8,128)} %param.7) | copy-start | bytes 786436
  8.6 8.6 %copy-start.3 = (f32[16,16,256]{2,1,0:T(8,128)}, f32[16,16,256]{2,1,0:T(8,128)S(1)}, u32[]{:S(2)}) copy-start(f32[16,16,256]{2,1,0:T(8,128)S(1)} %fusion.1.refs_5_) | copy-start | bytes 786436
  9.8 33.2 %copy-start.10 = (f32[256]{0:T(256)S(1)}, f32[256]{0:T(256)}, u32[]{:S(2)}) copy-start(f32[256]{0:T(256)} %param.13) | copy-start | bytes 3076
  29.3 9.8 %collective-permute-start.2 = (f32[256,256]{1,0:T(8,128)S(1)}, f32[256,256]{1,0:T(8,128)S(1)}, u32[]{:S(2)}, u32[]{:S(2)}) collective-permute-start(f32[256,256]{1,0:T(8,128)S(1)} %broadcast_select_fusion), channel_id=1, source_target_pairs={{0,4},{4,8},{8,12},{12,16},{16,20},{20,24},{24,28},{28,32},{32,36}... | collective-permute-start | bytes 786440 | tf_op jit(solution)/shard_map/ppermute | solution.py:16
  39.5 8.2 %collective-permute-start.4 = (f32[256,256]{1,0:T(8,128)S(1)}, f32[256,256]{1,0:T(8,128)S(1)}, u32[]{:S(2)}, u32[]{:S(2)}) collective-permute-start(f32[256,256]{1,0:T(8,128)S(1)} %convolution_select_fusion.9), channel_id=1, source_target_pairs={{0,8},{4,12},{8,16},{12,20},{16,24},{20,28},{24,32},{28,36},{32,40... | collective-permute-start | bytes 786440 | tf_op jit(solution)/shard_map/ppermute | solution.py:16
  48.0 23.2 %collective-permute-start.6 = (f32[256,256]{1,0:T(8,128)S(1)}, f32[256,256]{1,0:T(8,128)S(1)}, u32[]{:S(2)}, u32[]{:S(2)}) collective-permute-start(f32[256,256]{1,0:T(8,128)S(1)} %convolution_select_fusion.8), channel_id=1, source_target_pairs={{0,16},{4,20},{8,24},{12,28},{16,32},{20,36},{24,40},{28,44},{32,4... | collective-permute-start | bytes 786440 | tf_op jit(solution)/shard_map/ppermute | solution.py:16
  56.1 10.6 %collective-permute-start = (f32[16,256]{1,0:T(8,128)S(1)}, f32[16,256]{1,0:T(8,128)S(1)}, u32[]{:S(2)}, u32[]{:S(2)}) collective-permute-start(f32[16,256]{1,0:T(8,128)S(1)} %add_select_fusion), channel_id=1, source_target_pairs={{0,4},{4,8},{8,12},{12,16},{16,20},{20,24},{24,28},{28,32},{32,36}... | collective-permute-start | bytes 49160 | tf_op jit(solution)/shard_map/ppermute | solution.py:16
  66.9 6.0 %collective-permute-start.1 = (f32[16,256]{1,0:T(8,128)S(1)}, f32[16,256]{1,0:T(8,128)S(1)}, u32[]{:S(2)}, u32[]{:S(2)}) collective-permute-start(f32[16,256]{1,0:T(8,128)S(1)} %fusion.14), channel_id=1, source_target_pairs={{0,8},{4,12},{8,16},{12,20},{16,24},{20,28},{24,32},{28,36},{32,40... | collective-permute-start | bytes 49160 | tf_op jit(solution)/shard_map/ppermute | solution.py:16
  71.6 20.1 %collective-permute-start.8 = (f32[256,256]{1,0:T(8,128)S(1)}, f32[256,256]{1,0:T(8,128)S(1)}, u32[]{:S(2)}, u32[]{:S(2)}) collective-permute-start(f32[256,256]{1,0:T(8,128)S(1)} %convolution_select_fusion.7), channel_id=1, source_target_pairs={{0,32},{4,36},{8,40},{12,44},{16,48},{20,52},{24,56},{28,60},{32,6... | collective-permute-start | bytes 786440 | tf_op jit(solution)/shard_map/ppermute | solution.py:16
  73.2 3.3 %collective-permute-start.3 = (f32[16,256]{1,0:T(8,128)S(1)}, f32[16,256]{1,0:T(8,128)S(1)}, u32[]{:S(2)}, u32[]{:S(2)}) collective-permute-start(f32[16,256]{1,0:T(8,128)S(1)} %fusion.13), channel_id=1, source_target_pairs={{0,16},{4,20},{8,24},{12,28},{16,32},{20,36},{24,40},{28,44},{32,4... | collective-permute-start | bytes 49160 | tf_op jit(solution)/shard_map/ppermute | solution.py:16
  76.7 18.4 %collective-permute-start.5 = (f32[16,256]{1,0:T(8,128)S(1)}, f32[16,256]{1,0:T(8,128)S(1)}, u32[]{:S(2)}, u32[]{:S(2)}) collective-permute-start(f32[16,256]{1,0:T(8,128)S(1)} %fusion.12), channel_id=1, source_target_pairs={{0,32},{4,36},{8,40},{12,44},{16,48},{20,52},{24,56},{28,60},{32,6... | collective-permute-start | bytes 49160 | tf_op jit(solution)/shard_map/ppermute | solution.py:16
  92.1 14.7 %collective-permute-start.10 = (f32[256,256]{1,0:T(8,128)S(1)}, f32[256,256]{1,0:T(8,128)S(1)}, u32[]{:S(2)}, u32[]{:S(2)}) collective-permute-start(f32[256,256]{1,0:T(8,128)S(1)} %convolution_select_fusion.6), channel_id=1, source_target_pairs={{0,64},{4,68},{8,72},{12,76},{16,80},{20,84},{24,88},{28,92},{32,9... | collective-permute-start | bytes 786440 | tf_op jit(solution)/shard_map/ppermute | solution.py:16
  95.4 3.4 %collective-permute-start.7 = (f32[16,256]{1,0:T(8,128)S(1)}, f32[16,256]{1,0:T(8,128)S(1)}, u32[]{:S(2)}, u32[]{:S(2)}) collective-permute-start(f32[16,256]{1,0:T(8,128)S(1)} %fusion.11), channel_id=1, source_target_pairs={{0,64},{4,68},{8,72},{12,76},{16,80},{20,84},{24,88},{28,92},{32,9... | collective-permute-start | bytes 49160 | tf_op jit(solution)/shard_map/ppermute | solution.py:16
  99.1 8.7 %collective-permute-start.9 = (f32[16,256]{1,0:T(8,128)S(1)}, f32[16,256]{1,0:T(8,128)S(1)}, u32[]{:S(2)}, u32[]{:S(2)}) collective-permute-start(f32[16,256]{1,0:T(8,128)S(1)} %fusion.10), channel_id=1, source_target_pairs={{0,128},{4,132},{8,136},{12,140},{16,144},{20,148},{24,152},{28,15... | collective-permute-start | bytes 49160 | tf_op jit(solution)/shard_map/ppermute | solution.py:16
  107.9 11.5 %collective-permute-start.11 = (f32[16,256]{1,0:T(8,128)S(1)}, f32[16,256]{1,0:T(8,128)S(1)}, u32[]{:S(2)}, u32[]{:S(2)}) collective-permute-start(f32[16,256]{1,0:T(8,128)S(1)} %fusion.9), channel_id=1, source_target_pairs={{0,4},{4,8},{8,12},{12,16},{16,20},{20,24},{24,28},{28,32},{32,36}... | collective-permute-start | bytes 49160 | tf_op jit(solution)/shard_map/ppermute | solution.py:16
  119.4 11.3 %copy-start.1 = (f32[4,256,256]{2,1,0:T(8,128)S(1)}, f32[4,256,256]{2,1,0:T(8,128)}, u32[]{:S(2)}) copy-start(f32[4,256,256]{2,1,0:T(8,128)} %param.12) | copy-start | bytes 3145732
  128.6 3.6 %copy-start.6 = (f32[16,16,256]{2,1,0:T(8,128)S(1)}, f32[16,16,256]{2,1,0:T(8,128)}, u32[]{:S(2)}) copy-start(f32[16,16,256]{2,1,0:T(8,128)} %get-tuple-element.5) | copy-start | bytes 786436
  128.6 5.2 %collective-permute-start.12 = (f32[16,256]{1,0:T(8,128)S(1)}, f32[16,256]{1,0:T(8,128)S(1)}, u32[]{:S(2)}, u32[]{:S(2)}) collective-permute-start(f32[16,256]{1,0:T(8,128)S(1)} %slice_bitcast_fusion), channel_id=1, source_target_pairs={{4,0},{8,4},{12,8},{16,12},{20,16},{24,20},{28,24},{32,28},{36,32}... | collective-permute-start | bytes 49160 | tf_op jit(solution)/shard_map/ppermute | solution.py:16
  131.0 3.9 %copy-start.5 = (f32[16,16,256]{2,1,0:T(8,128)S(1)}, f32[16,16,256]{2,1,0:T(8,128)}, u32[]{:S(2)}) copy-start(f32[16,16,256]{2,1,0:T(8,128)} %get-tuple-element.2) | copy-start | bytes 786436
  134.9 8.3 %copy-start.2 = (f32[16,16,256]{2,1,0:T(8,128)}, f32[16,16,256]{2,1,0:T(8,128)S(1)}, u32[]{:S(2)}) copy-start(f32[16,16,256]{2,1,0:T(8,128)S(1)} %sub.88.refs_3_) | copy-start | bytes 786436
  153.9 8.7 %collective-permute-start.15 = (f32[256,256]{1,0:T(8,128)S(1)}, f32[256,256]{1,0:T(8,128)S(1)}, u32[]{:S(2)}, u32[]{:S(2)}) collective-permute-start(f32[256,256]{1,0:T(8,128)S(1)} %all_gather.7), channel_id=1, source_target_pairs={{4,0},{8,4},{12,8},{16,12},{20,16},{24,20},{28,24},{32,28},{36,32}... | collective-permute-start | bytes 786440 | tf_op jit(solution)/shard_map/ppermute | solution.py:16
  162.9 8.6 %collective-permute-start.17 = (f32[256,256]{1,0:T(8,128)S(1)}, f32[256,256]{1,0:T(8,128)S(1)}, u32[]{:S(2)}, u32[]{:S(2)}) collective-permute-start(f32[256,256]{1,0:T(8,128)S(1)} %convolution_select_fusion.4), channel_id=1, source_target_pairs={{8,0},{12,4},{16,8},{20,12},{24,16},{28,20},{32,24},{36,28},{40,32... | collective-permute-start | bytes 786440 | tf_op jit(solution)/shard_map/ppermute | solution.py:16
  171.9 16.4 %collective-permute-start.19 = (f32[256,256]{1,0:T(8,128)S(1)}, f32[256,256]{1,0:T(8,128)S(1)}, u32[]{:S(2)}, u32[]{:S(2)}) collective-permute-start(f32[256,256]{1,0:T(8,128)S(1)} %convolution_select_fusion.3), channel_id=1, source_target_pairs={{16,0},{20,4},{24,8},{28,12},{32,16},{36,20},{40,24},{44,28},{48,3... | collective-permute-start | bytes 786440 | tf_op jit(solution)/shard_map/ppermute | solution.py:16
  174.0 5.7 %collective-permute-start.13 = (f32[16,256]{1,0:T(8,128)S(1)}, f32[16,256]{1,0:T(8,128)S(1)}, u32[]{:S(2)}, u32[]{:S(2)}) collective-permute-start(f32[16,256]{1,0:T(8,128)S(1)} %slice.26), channel_id=1, source_target_pairs={{4,0},{8,4},{12,8},{16,12},{20,16},{24,20},{28,24},{32,28},{36,32}... | collective-permute-start | bytes 49160 | tf_op jit(solution)/shard_map/ppermute | solution.py:16
  180.6 11.9 %collective-permute-start.14 = (f32[16,256]{1,0:T(8,128)S(1)}, f32[16,256]{1,0:T(8,128)S(1)}, u32[]{:S(2)}, u32[]{:S(2)}) collective-permute-start(f32[16,256]{1,0:T(8,128)S(1)} %fusion.8), channel_id=1, source_target_pairs={{8,0},{12,4},{16,8},{20,12},{24,16},{28,20},{32,24},{36,28},{40,32... | collective-permute-start | bytes 49160 | tf_op jit(solution)/shard_map/ppermute | solution.py:16
  188.7 14.7 %collective-permute-start.21 = (f32[256,256]{1,0:T(8,128)S(1)}, f32[256,256]{1,0:T(8,128)S(1)}, u32[]{:S(2)}, u32[]{:S(2)}) collective-permute-start(f32[256,256]{1,0:T(8,128)S(1)} %convolution_select_fusion.2), channel_id=1, source_target_pairs={{32,0},{36,4},{40,8},{44,12},{48,16},{52,20},{56,24},{60,28},{64,3... | collective-permute-start | bytes 786440 | tf_op jit(solution)/shard_map/ppermute | solution.py:16
  192.8 6.3 %collective-permute-start.16 = (f32[16,256]{1,0:T(8,128)S(1)}, f32[16,256]{1,0:T(8,128)S(1)}, u32[]{:S(2)}, u32[]{:S(2)}) collective-permute-start(f32[16,256]{1,0:T(8,128)S(1)} %fusion.7), channel_id=1, source_target_pairs={{16,0},{20,4},{24,8},{28,12},{32,16},{36,20},{40,24},{44,28},{48,3... | collective-permute-start | bytes 49160 | tf_op jit(solution)/shard_map/ppermute | solution.py:16
  199.3 12.2 %collective-permute-start.18 = (f32[16,256]{1,0:T(8,128)S(1)}, f32[16,256]{1,0:T(8,128)S(1)}, u32[]{:S(2)}, u32[]{:S(2)}) collective-permute-start(f32[16,256]{1,0:T(8,128)S(1)} %fusion.6), channel_id=1, source_target_pairs={{32,0},{36,4},{40,8},{44,12},{48,16},{52,20},{56,24},{60,28},{64,3... | collective-permute-start | bytes 49160 | tf_op jit(solution)/shard_map/ppermute | solution.py:16
  203.8 19.4 %collective-permute-start.23 = (f32[256,256]{1,0:T(8,128)S(1)}, f32[256,256]{1,0:T(8,128)S(1)}, u32[]{:S(2)}, u32[]{:S(2)}) collective-permute-start(f32[256,256]{1,0:T(8,128)S(1)} %convolution_select_fusion.1), channel_id=1, source_target_pairs={{64,0},{68,4},{72,8},{76,12},{80,16},{84,20},{88,24},{92,28},{96,3... | collective-permute-start | bytes 786440 | tf_op jit(solution)/shard_map/ppermute | solution.py:16
  211.7 9.9 %collective-permute-start.20 = (f32[16,256]{1,0:T(8,128)S(1)}, f32[16,256]{1,0:T(8,128)S(1)}, u32[]{:S(2)}, u32[]{:S(2)}) collective-permute-start(f32[16,256]{1,0:T(8,128)S(1)} %fusion.5), channel_id=1, source_target_pairs={{64,0},{68,4},{72,8},{76,12},{80,16},{84,20},{88,24},{92,28},{96,3... | collective-permute-start | bytes 49160 | tf_op jit(solution)/shard_map/ppermute | solution.py:16
  221.9 10.3 %collective-permute-start.22 = (f32[16,256]{1,0:T(8,128)S(1)}, f32[16,256]{1,0:T(8,128)S(1)}, u32[]{:S(2)}, u32[]{:S(2)}) collective-permute-start(f32[16,256]{1,0:T(8,128)S(1)} %fusion.4), channel_id=1, source_target_pairs={{128,0},{132,4},{136,8},{140,12},{144,16},{148,20},{152,24},{156,2... | collective-permute-start | bytes 49160 | tf_op jit(solution)/shard_map/ppermute | solution.py:16
  232.4 6.6 %collective-permute-start.24 = (f32[16,256]{1,0:T(8,128)S(1)}, f32[16,256]{1,0:T(8,128)S(1)}, u32[]{:S(2)}, u32[]{:S(2)}) collective-permute-start(f32[16,256]{1,0:T(8,128)S(1)} %fusion.3), channel_id=1, source_target_pairs={{4,0},{8,4},{12,8},{16,12},{20,16},{24,20},{28,24},{32,28},{36,32}... | collective-permute-start | bytes 49160 | tf_op jit(solution)/shard_map/ppermute | solution.py:16
  238.9 0.6 copy-start.8

commit v3 on v2

--- a/solution.py
+++ b/solution.py
@@ -20,18 +20,30 @@
     return jnp.dot(first_factor, second_factor, precision=lax.Precision.HIGHEST)
 
 
-def doubling_scan(matrix, records, axis, reverse):
+def doubling_maps(matrix, axis, reverse):
+    peers, index = (lax.axis_size(axis), lax.axis_index(axis))
+    maps = [matrix]
+    distance = 1
+    while 2 * distance < peers:
+        step = -distance if reverse else distance
+        reached = index + distance < peers if reverse else index >= distance
+        got_matrix = passed_along(matrix, axis, step)
+        matrix = jnp.where(reached, accurate_matmul_result(got_matrix, matrix), matrix)
+        maps.append(matrix)
+        distance *= 2
+    return maps
+
+
+def doubling_records(maps, records, axis, reverse):
     peers, index = (lax.axis_size(axis), lax.axis_index(axis))
     distance = 1
-    while distance < peers:
+    for matrix in maps:
         step = -distance if reverse else distance
         reached = index + distance < peers if reverse else index >= distance
         got_records = passed_along(records, axis, step)
-        new_records = accurate_matmul_result(got_records, matrix) + records
-        if 2 * distance < peers:
-            got_matrix = passed_along(matrix, axis, step)
-            matrix = jnp.where(reached, accurate_matmul_result(got_matrix, matrix), matrix)
-        records = jnp.where(reached, new_records, records)
+        records = jnp.where(
+            reached, accurate_matmul_result(got_records, matrix) + records, records
+        )
         distance *= 2
     return records
 
@@ -149,31 +161,39 @@
     identity = jnp.eye(states, dtype=jnp.float32)
     own_identity = lax.dynamic_slice_in_dim(identity, column_index * column_share, column_share, 0)
     blank_columns = jnp.zeros((steps_dev, column_share, states), jnp.float32)
-    initial_rows = jnp.concatenate(
-        [own_identity, jnp.zeros((record_rows, states), jnp.float32)], axis=0
-    )
     band_weights = (band_index[:, None] == jnp.arange(bands)[None, :]).astype(jnp.float32)
     observed_weights = band_weights * obs_mask.astype(jnp.float32)[:, None]
     measured = per_band_products(observations, gain, observed_weights)
 
+    blank_records = jnp.zeros((record_rows, states), jnp.float32)
     forward_rows = recurrence(
-        forward_pick,
-        initial_rows,
-        forward_table,
-        jnp.concatenate([blank_columns, measured], axis=1),
-        False,
-        False,
-    )
-    whole_matrix = lax.all_gather(forward_rows[:column_share], "col", axis=0, tiled=True)
+        forward_pick, own_identity, forward_table, blank_columns, False, False
+    )
+    whole_matrix = lax.all_gather(forward_rows, "col", axis=0, tiled=True)
     first_block = time_index == 0
-    block_records = forward_rows[column_share:]
+    forward_maps = doubling_maps(
+        jnp.where(first_block, jnp.zeros_like(whole_matrix), whole_matrix), "tm", False
+    )
+
+    final_here = (time_index == time_devices - 1) & (jnp.arange(steps_dev) == steps_dev - 1)
+    backward = jnp.transpose(mode_backward_factors, (0, 2, 1))
+    backward_table = jnp.concatenate([backward, jnp.zeros_like(backward[:1])], axis=0)
+    backward_pick = jnp.where(final_here, bands, band_index)
+    backward_rows = recurrence(
+        backward_pick, own_identity, backward_table, blank_columns, True, False
+    )
+    whole_back = lax.all_gather(backward_rows, "col", axis=0, tiled=True)
+    backward_maps = doubling_maps(whole_back, "tm", True)
+
+    block_records = recurrence(
+        forward_pick, blank_records, forward_table, measured, False, False
+    )
     folded_records = jnp.where(
         first_block,
         accurate_matmul_result(initial_mean[None, :], whole_matrix) + block_records,
         block_records,
     )
-    folded_matrix = jnp.where(first_block, jnp.zeros_like(whole_matrix), whole_matrix)
-    ending_records = doubling_scan(folded_matrix, folded_records, "tm", False)
+    ending_records = doubling_records(forward_maps, folded_records, "tm", False)
     start_rows = jnp.where(
         first_block,
         jnp.broadcast_to(initial_mean[None, :], (record_rows, states)),
@@ -192,23 +212,11 @@
     following = passed_along(predicted[0], "tm", -1)
     next_predicted = jnp.concatenate([predicted[1:], following[None]], axis=0)
 
-    final_here = (time_index == time_devices - 1) & (jnp.arange(steps_dev) == steps_dev - 1)
-    backward = jnp.transpose(mode_backward_factors, (0, 2, 1))
-    backward_table = jnp.concatenate([backward, jnp.zeros_like(backward[:1])], axis=0)
-    backward_pick = jnp.where(final_here, bands, band_index)
     live_weights = band_weights * (1.0 - final_here.astype(jnp.float32))[:, None]
     shift = filtered - per_band_products(next_predicted, backward, live_weights)
 
-    backward_rows = recurrence(
-        backward_pick,
-        initial_rows,
-        backward_table,
-        jnp.concatenate([blank_columns, shift], axis=1),
-        True,
-        False,
-    )
-    whole_back = lax.all_gather(backward_rows[:column_share], "col", axis=0, tiled=True)
-    opening_records = doubling_scan(whole_back, backward_rows[column_share:], "tm", True)
+    back_records = recurrence(backward_pick, blank_records, backward_table, shift, True, False)
+    opening_records = doubling_records(backward_maps, back_records, "tm", True)
     after_records = passed_along(opening_records, "tm", -1)
 
     smoothed = recurrence(backward_pick, after_records, backward_table, shift, True, True)

time: 248 us -> 215 us (0.87)
  waiting for transfers between devices: 75.9 us -> 47 us
  starting transfers between devices: 92.2 us -> 74.6 us
  Pallas kernels: 29.1 us -> 42.5 us
    ppermute x25, waiting for transfers between devices: 75.9 us -> 47 us  [passed_along(): return lax.ppermute(block, axis, route)]
    ppermute x25, starting transfers between devices: 92.2 us -> 74.6 us  [passed_along(): return lax.ppermute(block, axis, route)]
    pallas_call x4 -> x6, Pallas kernels: 29.1 us -> 42.5 us  [recurrence(): pl.pallas_call(functools.partial(recurrence_kernel, steps=steps, reverse=...]
    concatenate x3 -> x0, local copies, waits for them, and re-layouts: 3.07 us -> none  [the longest x1 1.22 us: shards(): jnp.concatenate([blank_columns, measured], axis=1)]
  transfers between devices with their start and end apart: 25 -> 25, of which waited for: 18 -> 11; matrix products, arithmetic and copies ran while one was open for 4% -> 8% of each run, Pallas kernels for 0% -> 13%
where the time goes in v3:
time: 215 us; the launch traced here: 214 us
  starting transfers between devices  74.6 us (35%)
  waiting for transfers between devices  47 us (22%)
  Pallas kernels  42.5 us (20%)
  blocking collectives  21 us (10%)
  matrix products  11.3 us (5%)
  local copies, waits for them, and re-layouts  8.94 us (4%)
  other arithmetic  6.67 us (3%)
    ppermute x25, starting transfers between devices, passed_along(): return lax.ppermute(block, axis, route)  74.6 us
    ppermute x25, waiting for transfers between devices, passed_along(): return lax.ppermute(block, axis, route)  47 us
    pallas_call x6, Pallas kernels, recurrence(): pl.pallas_call(functools.partial(recurrence_kernel, steps=steps, reverse=...  42.5 us
    all_gather x1, blocking collectives, shards(): whole_matrix = lax.all_gather(forward_rows, 'col', axis=0, tiled=True)  11.4 us
    dot_general x25, matrix products, accurate_matmul_result(): return jnp.dot(first_factor, second_factor, precision=lax.Precision.HIGHEST)  9.98 us
    all_gather x1, blocking collectives, shards(): whole_back = lax.all_gather(backward_rows, 'col', axis=0, tiled=True)  9.58 us
  transfers between devices with their start and end apart: 25, of which 11 were waited for; matrix products, arithmetic and copies ran while one was open for 8% of the time, Pallas kernels for 13%

profile of v3, /device:TPU:1, one launch (start us, length us, event | category | flops | bytes accessed | tf_op | source)
XLA Modules:
  0.0 213.7 jit_solution(6571900345188524242)
XLA Ops:
  0.9 1.2 fusion.17
  2.1 1.1 multiply_add_fusion.1
  3.2 1.4 fusion
  4.7 1.5 copy.10
  6.2 0.6 constant_dynamic-slice_fusion.refs_1_
  6.9 0.6 broadcast_select_fusion.2
  7.4 1.1 broadcast_in_dim.12.refs_3_
  8.5 7.4 %shard_map.86 = f32[64,256]{1,0:T(8,128)} custom-call(s32[16]{0:T(128)} %get-tuple-element.9.refs_0_, f32[64,256]{1,0:T(8,128)} %constant_dynamic-slice_fusion.refs_1_, f32[8,256,256]{2,1,0:T(8,128)} %bitcast.86, f32[16,64,256]{2,1,0:T(8,128)} %broadcast_in_dim.12.refs_3_), custom_call_target="tpu_custom_call" | custom-call | tf_op jit(solution)/shard_map/pallas_call | solution.py:113
  15.9 11.4 %all_gather.6 = f32[256,256]{1,0:T(8,128)S(1)} all-gather(f32[64,256]{1,0:T(8,128)} %shard_map.86), channel_id=1, replica_groups=mesh['tm'=64,'col'=4] {'col'}, dimensions={0}, use_global_device_ids=true | all-gather | bytes 327680 | tf_op jit(solution)/shard_map/all_gather | solution.py:172
  27.4 6.5 %collective-permute-start.2 = (f32[256,256]{1,0:T(8,128)S(1)}, f32[256,256]{1,0:T(8,128)S(1)}, u32[]{:S(2)}, u32[]{:S(2)}) collective-permute-start(f32[256,256]{1,0:T(8,128)S(1)} %broadcast_select_fusion), channel_id=1, source_target_pairs={{0,4},{4,8},{8,12},{12,16},{16,20},{20,24},{24,28},{28,32},{32,36}... | collective-permute-start | bytes 786440 | tf_op jit(solution)/shard_map/ppermute | solution.py:16
  33.9 1.8 fusion.1.refs_3_.refs_5_
  35.7 0.6 broadcast_in_dim.13.refs_1_
  36.3 6.9 %shard_map.87 = f32[16,256]{1,0:T(8,128)} custom-call(s32[16]{0:T(128)} %get-tuple-element.9.refs_0_, f32[16,256]{1,0:T(8,128)} %broadcast_in_dim.13.refs_1_, f32[8,256,256]{2,1,0:T(8,128)} %bitcast.87, f32[16,16,256]{2,1,0:T(8,128)} %fusion.1.refs_3_.refs_5_), custom_call_target="tpu_custom_call" | custom-call | tf_op jit(solution)/shard_map/pallas_call | solution.py:113
  43.4 0.4 convolution_select_fusion.9
  43.8 3.6 %collective-permute-start.4 = (f32[256,256]{1,0:T(8,128)S(1)}, f32[256,256]{1,0:T(8,128)S(1)}, u32[]{:S(2)}, u32[]{:S(2)}) collective-permute-start(f32[256,256]{1,0:T(8,128)S(1)} %convolution_select_fusion.9), channel_id=1, source_target_pairs={{0,8},{4,12},{8,16},{12,20},{16,24},{20,28},{24,32},{28,36},{32,40... | collective-permute-start | bytes 786440 | tf_op jit(solution)/shard_map/ppermute | solution.py:16
  47.4 0.7 add_select_fusion
  48.1 2.2 %collective-permute-start = (f32[16,256]{1,0:T(8,128)S(1)}, f32[16,256]{1,0:T(8,128)S(1)}, u32[]{:S(2)}, u32[]{:S(2)}) collective-permute-start(f32[16,256]{1,0:T(8,128)S(1)} %add_select_fusion), channel_id=1, source_target_pairs={{0,4},{4,8},{8,12},{12,16},{16,20},{20,24},{24,28},{28,32},{32,36}... | collective-permute-start | bytes 49160 | tf_op jit(solution)/shard_map/ppermute | solution.py:16
  50.3 2.3 %collective-permute-done = f32[16,256]{1,0:T(8,128)S(1)} collective-permute-done((f32[16,256]{1,0:T(8,128)S(1)}, f32[16,256]{1,0:T(8,128)S(1)}, u32[]{:S(2)}, u32[]{:S(2)}) %collective-permute-start) | collective-permute-done | bytes 16416 | tf_op jit(solution)/shard_map/ppermute | solution.py:16
  52.8 3.5 %collective-permute-start.1 = (f32[16,256]{1,0:T(8,128)S(1)}, f32[16,256]{1,0:T(8,128)S(1)}, u32[]{:S(2)}, u32[]{:S(2)}) collective-permute-start(f32[16,256]{1,0:T(8,128)S(1)} %fusion.14), channel_id=1, source_target_pairs={{0,8},{4,12},{8,16},{12,20},{16,24},{20,28},{24,32},{28,36},{32,40... | collective-permute-start | bytes 49160 | tf_op jit(solution)/shard_map/ppermute | solution.py:16
  56.8 6.2 %collective-permute-start.6 = (f32[256,256]{1,0:T(8,128)S(1)}, f32[256,256]{1,0:T(8,128)S(1)}, u32[]{:S(2)}, u32[]{:S(2)}) collective-permute-start(f32[256,256]{1,0:T(8,128)S(1)} %convolution_select_fusion.8), channel_id=1, source_target_pairs={{0,16},{4,20},{8,24},{12,28},{16,32},{20,36},{24,40},{28,44},{32,4... | collective-permute-start | bytes 786440 | tf_op jit(solution)/shard_map/ppermute | solution.py:16
  63.2 3.3 %collective-permute-start.3 = (f32[16,256]{1,0:T(8,128)S(1)}, f32[16,256]{1,0:T(8,128)S(1)}, u32[]{:S(2)}, u32[]{:S(2)}) collective-permute-start(f32[16,256]{1,0:T(8,128)S(1)} %fusion.13), channel_id=1, source_target_pairs={{0,16},{4,20},{8,24},{12,28},{16,32},{20,36},{24,40},{28,44},{32,4... | collective-permute-start | bytes 49160 | tf_op jit(solution)/shard_map/ppermute | solution.py:16
  66.5 1.6 copy.11
  68.0 1.2 concatenate.6.refs_2_
  69.2 7.1 %shard_map.90 = f32[64,256]{1,0:T(8,128)} custom-call(s32[16]{0:T(128)} %get-tuple-element.8.refs_0_, f32[64,256]{1,0:T(8,128)} %constant_dynamic-slice_fusion.refs_1_, f32[5,256,256]{2,1,0:T(8,128)} %concatenate.6.refs_2_, f32[16,64,256]{2,1,0:T(8,128)} %broadcast_in_dim.12.refs_3_), custom_call_target="tpu_custom_call" | custom-call | tf_op jit(solution)/shard_map/pallas_call | solution.py:113
  76.5 3.1 %collective-permute-start.5 = (f32[16,256]{1,0:T(8,128)S(1)}, f32[16,256]{1,0:T(8,128)S(1)}, u32[]{:S(2)}, u32[]{:S(2)}) collective-permute-start(f32[16,256]{1,0:T(8,128)S(1)} %fusion.12), channel_id=1, source_target_pairs={{0,32},{4,36},{8,40},{12,44},{16,48},{20,52},{24,56},{28,60},{32,6... | collective-permute-start | bytes 49160 | tf_op jit(solution)/shard_map/ppermute | solution.py:16
  80.0 7.1 %collective-permute-start.8 = (f32[256,256]{1,0:T(8,128)S(1)}, f32[256,256]{1,0:T(8,128)S(1)}, u32[]{:S(2)}, u32[]{:S(2)}) collective-permute-start(f32[256,256]{1,0:T(8,128)S(1)} %convolution_select_fusion.7), channel_id=1, source_target_pairs={{0,32},{4,36},{8,40},{12,44},{16,48},{20,52},{24,56},{28,60},{32,6... | collective-permute-start | bytes 786440 | tf_op jit(solution)/shard_map/ppermute | solution.py:16
  87.1 9.6 %all_gather.7 = f32[256,256]{1,0:T(8,128)S(1)} all-gather(f32[64,256]{1,0:T(8,128)} %shard_map.90), channel_id=1, replica_groups=mesh['tm'=64,'col'=4] {'col'}, dimensions={0}, use_global_device_ids=true | all-gather | bytes 327680 | tf_op jit(solution)/shard_map/all_gather | solution.py:185
  96.7 8.2 %collective-permute-start.15 = (f32[256,256]{1,0:T(8,128)S(1)}, f32[256,256]{1,0:T(8,128)S(1)}, u32[]{:S(2)}, u32[]{:S(2)}) collective-permute-start(f32[256,256]{1,0:T(8,128)S(1)} %all_gather.7), channel_id=1, source_target_pairs={{4,0},{8,4},{12,8},{16,12},{20,16},{24,20},{28,24},{32,28},{36,32}... | collective-permute-start | bytes 786440 | tf_op jit(solution)/shard_map/ppermute | solution.py:16
  105.1 3.1 %collective-permute-start.7 = (f32[16,256]{1,0:T(8,128)S(1)}, f32[16,256]{1,0:T(8,128)S(1)}, u32[]{:S(2)}, u32[]{:S(2)}) collective-permute-start(f32[16,256]{1,0:T(8,128)S(1)} %fusion.11), channel_id=1, source_target_pairs={{0,64},{4,68},{8,72},{12,76},{16,80},{20,84},{24,88},{28,92},{32,9... | collective-permute-start | bytes 49160 | tf_op jit(solution)/shard_map/ppermute | solution.py:16
  108.6 2.8 %collective-permute-start.10 = (f32[256,256]{1,0:T(8,128)S(1)}, f32[256,256]{1,0:T(8,128)S(1)}, u32[]{:S(2)}, u32[]{:S(2)}) collective-permute-start(f32[256,256]{1,0:T(8,128)S(1)} %convolution_select_fusion.6), channel_id=1, source_target_pairs={{0,64},{4,68},{8,72},{12,76},{16,80},{20,84},{24,88},{28,92},{32,9... | collective-permute-start | bytes 786440 | tf_op jit(solution)/shard_map/ppermute | solution.py:16
  111.5 1.3 multiply_add_fusion.refs_4_
  113.0 2.2 %collective-permute-start.9 = (f32[16,256]{1,0:T(8,128)S(1)}, f32[16,256]{1,0:T(8,128)S(1)}, u32[]{:S(2)}, u32[]{:S(2)}) collective-permute-start(f32[16,256]{1,0:T(8,128)S(1)} %fusion.10), channel_id=1, source_target_pairs={{0,128},{4,132},{8,136},{12,140},{16,144},{20,148},{24,152},{28,15... | collective-permute-start | bytes 49160 | tf_op jit(solution)/shard_map/ppermute | solution.py:16
  115.3 1.6 collective-permute-done.10
  117.5 3.8 %collective-permute-start.11 = (f32[16,256]{1,0:T(8,128)S(1)}, f32[16,256]{1,0:T(8,128)S(1)}, u32[]{:S(2)}, u32[]{:S(2)}) collective-permute-start(f32[16,256]{1,0:T(8,128)S(1)} %fusion.9), channel_id=1, source_target_pairs={{0,4},{4,8},{8,12},{12,16},{16,20},{20,24},{24,28},{28,32},{32,36}... | collective-permute-start | bytes 49160 | tf_op jit(solution)/shard_map/ppermute | solution.py:16
  121.7 1.3 collective-permute-start.17
  123.0 0.6 broadcast_select_fusion.1.refs_2_
  123.6 7.9 %shard_map.88 = (f32[16,16,256]{2,1,0:T(8,128)}, f32[16,16,256]{2,1,0:T(8,128)}) custom-call(s32[16]{0:T(128)} %get-tuple-element.9.refs_0_, s32[16]{0:T(128)} %refs_1_.1, f32[16,256]{1,0:T(8,128)} %broadcast_select_fusion.1.refs_2_, f32[8,256,256]{2,1,0:T(8,128)} %bitcast.88, f32[4,256,256]{2,1,0:T(8,128)} %multiply_add_fusion.refs_4_, ...), custom_call_target="tpu_custom_call" | custom-call | tf_op jit(solution)/shard_map/pallas_call | solution.py:113
  131.5 0.8 slice_bitcast_fusion
  132.3 1.9 collective-permute-start.12
  134.6 1.5 collective-permute-start.19
  136.1 1.0 slice.6
  137.3 1.1 fusion.2
  138.4 0.7 sub.88.refs_3_
  139.1 6.6 %shard_map.89 = f32[16,256]{1,0:T(8,128)} custom-call(s32[16]{0:T(128)} %get-tuple-element.8.refs_0_, f32[16,256]{1,0:T(8,128)} %broadcast_in_dim.13.refs_1_, f32[5,256,256]{2,1,0:T(8,128)} %concatenate.6.refs_2_, f32[16,16,256]{2,1,0:T(8,128)} %sub.88.refs_3_), custom_call_target="tpu_custom_call" | custom-call | tf_op jit(solution)/shard_map/pallas_call | solution.py:113
  145.8 1.9 collective-permute-start.13
  147.7 5.1 %collective-permute-done.13 = f32[16,256]{1,0:T(8,128)S(1)} collective-permute-done((f32[16,256]{1,0:T(8,128)}, f32[16,256]{1,0:T(8,128)S(1)}, u32[]{:S(2)}, u32[]{:S(2)}) %collective-permute-start.13) | collective-permute-done | bytes 16416 | tf_op jit(solution)/shard_map/ppermute | solution.py:16
  152.8 0.9 fusion.8
  153.7 1.3 collective-permute-start.14
  155.4 1.3 collective-permute-start.21
  156.7 1.5 collective-permute-done.14
  158.4 1.3 collective-permute-start.16
  159.7 5.7 %collective-permute-done.16 = f32[16,256]{1,0:T(8,128)S(1)} collective-permute-done((f32[16,256]{1,0:T(8,128)S(1)}, f32[16,256]{1,0:T(8,128)S(1)}, u32[]{:S(2)}, u32[]{:S(2)}) %collective-permute-start.16) | collective-permute-done | bytes 16416 | tf_op jit(solution)/shard_map/ppermute | solution.py:16
  165.7 1.3 collective-permute-start.18
  167.0 2.8 %collective-permute-done.21 = f32[256,256]{1,0:T(8,128)S(1)} collective-permute-done((f32[256,256]{1,0:T(8,128)S(1)}, f32[256,256]{1,0:T(8,128)S(1)}, u32[]{:S(2)}, u32[]{:S(2)}) %collective-permute-start.21) | collective-permute-done | bytes 262176 | tf_op jit(solution)/shard_map/ppermute | solution.py:16
  170.2 1.3 collective-permute-start.23
  171.5 5.8 %collective-permute-done.18 = f32[16,256]{1,0:T(8,128)S(1)} collective-permute-done((f32[16,256]{1,0:T(8,128)S(1)}, f32[16,256]{1,0:T(8,128)S(1)}, u32[]{:S(2)}, u32[]{:S(2)}) %collective-permute-start.18) | collective-permute-done | bytes 16416 | tf_op jit(solution)/shard_map/ppermute | solution.py:16
  177.5 1.3 collective-permute-start.20
  178.8 13.2 %collective-permute-done.20 = f32[16,256]{1,0:T(8,128)S(1)} collective-permute-done((f32[16,256]{1,0:T(8,128)S(1)}, f32[16,256]{1,0:T(8,128)S(1)}, u32[]{:S(2)}, u32[]{:S(2)}) %collective-permute-start.20) | collective-permute-done | bytes 16416 | tf_op jit(solution)/shard_map/ppermute | solution.py:16
  192.2 1.3 collective-permute-start.22
  194.0 7.1 %collective-permute-done.22 = f32[16,256]{1,0:T(8,128)S(1)} collective-permute-done((f32[16,256]{1,0:T(8,128)S(1)}, f32[16,256]{1,0:T(8,128)S(1)}, u32[]{:S(2)}, u32[]{:S(2)}) %collective-permute-start.22) | collective-permute-done | bytes 16416 | tf_op jit(solution)/shard_map/ppermute | solution.py:16
  201.3 3.4 %collective-permute-start.24 = (f32[16,256]{1,0:T(8,128)S(1)}, f32[16,256]{1,0:T(8,128)S(1)}, u32[]{:S(2)}, u32[]{:S(2)}) collective-permute-start(f32[16,256]{1,0:T(8,128)S(1)} %fusion.3), channel_id=1, source_target_pairs={{4,0},{8,4},{12,8},{16,12},{20,16},{24,20},{28,24},{32,28},{36,32}... | collective-permute-start | bytes 49160 | tf_op jit(solution)/shard_map/ppermute | solution.py:16
  204.8 1.6 collective-permute-done.24.refs_1_
  206.4 0.6 copy-done.5
  207.0 6.7 %shard_map.91 = f32[16,16,256]{2,1,0:T(8,128)} custom-call(s32[16]{0:T(128)} %get-tuple-element.8.refs_0_, f32[16,256]{1,0:T(8,128)} %copy-done.5, f32[5,256,256]{2,1,0:T(8,128)} %concatenate.6.refs_2_, f32[16,16,256]{2,1,0:T(8,128)} %sub.88.refs_3_), custom_call_target="tpu_custom_call" | custom-call | tf_op jit(solution)/shard_map/pallas_call | solution.py:113
  (61 shorter events, 6.6 us)
Async XLA Ops:
  0.6 2.5 %copy-start = (f32[4,256,256]{2,1,0:T(8,128)S(1)}, f32[4,256,256]{2,1,0:T(8,128)}, u32[]{:S(2)}) copy-start(f32[4,256,256]{2,1,0:T(8,128)} %param.11) | copy-start | bytes 3145732
  0.6 2.5 %copy-start.2 = (f32[4,256]{1,0:T(4,128)S(1)}, f32[4,256]{1,0:T(4,128)}, u32[]{:S(2)}) copy-start(f32[4,256]{1,0:T(4,128)} %param.10) | copy-start | bytes 12292
  4.7 2.1 %copy-start.6 = (s32[16]{0:T(128)S(1)}, s32[16]{0:T(128)}, u32[]{:S(2)}) copy-start(s32[16]{0:T(128)} %refs_1_.1) | copy-start | bytes 196
  4.7 2.1 %copy-start.8 = (s32[16]{0:T(128)S(1)}, s32[16]{0:T(128)}, u32[]{:S(2)}) copy-start(s32[16]{0:T(128)} %param.9) | copy-start | bytes 196
  8.5 25.4 %copy-start.4 = (f32[16,16,256]{2,1,0:T(8,128)S(1)}, f32[16,16,256]{2,1,0:T(8,128)}, u32[]{:S(2)}) copy-start(f32[16,16,256]{2,1,0:T(8,128)} %param.7) | copy-start | bytes 786436
  27.4 15.8 %copy-start.7 = (f32[256]{0:T(256)S(1)}, f32[256]{0:T(256)}, u32[]{:S(2)}) copy-start(f32[256]{0:T(256)} %param.13) | copy-start | bytes 3076
  27.4 16.0 %collective-permute-start.2 = (f32[256,256]{1,0:T(8,128)S(1)}, f32[256,256]{1,0:T(8,128)S(1)}, u32[]{:S(2)}, u32[]{:S(2)}) collective-permute-start(f32[256,256]{1,0:T(8,128)S(1)} %broadcast_select_fusion), channel_id=1, source_target_pairs={{0,4},{4,8},{8,12},{12,16},{16,20},{20,24},{24,28},{28,32},{32,36}... | collective-permute-start | bytes 786440 | tf_op jit(solution)/shard_map/ppermute | solution.py:16
  43.8 12.6 %collective-permute-start.4 = (f32[256,256]{1,0:T(8,128)S(1)}, f32[256,256]{1,0:T(8,128)S(1)}, u32[]{:S(2)}, u32[]{:S(2)}) collective-permute-start(f32[256,256]{1,0:T(8,128)S(1)} %convolution_select_fusion.9), channel_id=1, source_target_pairs={{0,8},{4,12},{8,16},{12,20},{16,24},{20,28},{24,32},{28,36},{32,40... | collective-permute-start | bytes 786440 | tf_op jit(solution)/shard_map/ppermute | solution.py:16
  48.1 4.5 %collective-permute-start = (f32[16,256]{1,0:T(8,128)S(1)}, f32[16,256]{1,0:T(8,128)S(1)}, u32[]{:S(2)}, u32[]{:S(2)}) collective-permute-start(f32[16,256]{1,0:T(8,128)S(1)} %add_select_fusion), channel_id=1, source_target_pairs={{0,4},{4,8},{8,12},{12,16},{16,20},{20,24},{24,28},{28,32},{32,36}... | collective-permute-start | bytes 49160 | tf_op jit(solution)/shard_map/ppermute | solution.py:16
  52.8 10.1 %collective-permute-start.1 = (f32[16,256]{1,0:T(8,128)S(1)}, f32[16,256]{1,0:T(8,128)S(1)}, u32[]{:S(2)}, u32[]{:S(2)}) collective-permute-start(f32[16,256]{1,0:T(8,128)S(1)} %fusion.14), channel_id=1, source_target_pairs={{0,8},{4,12},{8,16},{12,20},{16,24},{20,28},{24,32},{28,36},{32,40... | collective-permute-start | bytes 49160 | tf_op jit(solution)/shard_map/ppermute | solution.py:16
  56.8 22.8 %collective-permute-start.6 = (f32[256,256]{1,0:T(8,128)S(1)}, f32[256,256]{1,0:T(8,128)S(1)}, u32[]{:S(2)}, u32[]{:S(2)}) collective-permute-start(f32[256,256]{1,0:T(8,128)S(1)} %convolution_select_fusion.8), channel_id=1, source_target_pairs={{0,16},{4,20},{8,24},{12,28},{16,32},{20,36},{24,40},{28,44},{32,4... | collective-permute-start | bytes 786440 | tf_op jit(solution)/shard_map/ppermute | solution.py:16
  63.2 13.1 %collective-permute-start.3 = (f32[16,256]{1,0:T(8,128)S(1)}, f32[16,256]{1,0:T(8,128)S(1)}, u32[]{:S(2)}, u32[]{:S(2)}) collective-permute-start(f32[16,256]{1,0:T(8,128)S(1)} %fusion.13), channel_id=1, source_target_pairs={{0,16},{4,20},{8,24},{12,28},{16,32},{20,36},{24,40},{28,44},{32,4... | collective-permute-start | bytes 49160 | tf_op jit(solution)/shard_map/ppermute | solution.py:16
  76.5 28.3 %collective-permute-start.5 = (f32[16,256]{1,0:T(8,128)S(1)}, f32[16,256]{1,0:T(8,128)S(1)}, u32[]{:S(2)}, u32[]{:S(2)}) collective-permute-start(f32[16,256]{1,0:T(8,128)S(1)} %fusion.12), channel_id=1, source_target_pairs={{0,32},{4,36},{8,40},{12,44},{16,48},{20,52},{24,56},{28,60},{32,6... | collective-permute-start | bytes 49160 | tf_op jit(solution)/shard_map/ppermute | solution.py:16
  80.0 28.2 %collective-permute-start.8 = (f32[256,256]{1,0:T(8,128)S(1)}, f32[256,256]{1,0:T(8,128)S(1)}, u32[]{:S(2)}, u32[]{:S(2)}) collective-permute-start(f32[256,256]{1,0:T(8,128)S(1)} %convolution_select_fusion.7), channel_id=1, source_target_pairs={{0,32},{4,36},{8,40},{12,44},{16,48},{20,52},{24,56},{28,60},{32,6... | collective-permute-start | bytes 786440 | tf_op jit(solution)/shard_map/ppermute | solution.py:16
  96.7 24.6 %collective-permute-start.15 = (f32[256,256]{1,0:T(8,128)S(1)}, f32[256,256]{1,0:T(8,128)S(1)}, u32[]{:S(2)}, u32[]{:S(2)}) collective-permute-start(f32[256,256]{1,0:T(8,128)S(1)} %all_gather.7), channel_id=1, source_target_pairs={{4,0},{8,4},{12,8},{16,12},{20,16},{24,20},{28,24},{32,28},{36,32}... | collective-permute-start | bytes 786440 | tf_op jit(solution)/shard_map/ppermute | solution.py:16
  105.1 7.7 %collective-permute-start.7 = (f32[16,256]{1,0:T(8,128)S(1)}, f32[16,256]{1,0:T(8,128)S(1)}, u32[]{:S(2)}, u32[]{:S(2)}) collective-permute-start(f32[16,256]{1,0:T(8,128)S(1)} %fusion.11), channel_id=1, source_target_pairs={{0,64},{4,68},{8,72},{12,76},{16,80},{20,84},{24,88},{28,92},{32,9... | collective-permute-start | bytes 49160 | tf_op jit(solution)/shard_map/ppermute | solution.py:16
  108.6 8.2 %collective-permute-start.10 = (f32[256,256]{1,0:T(8,128)S(1)}, f32[256,256]{1,0:T(8,128)S(1)}, u32[]{:S(2)}, u32[]{:S(2)}) collective-permute-start(f32[256,256]{1,0:T(8,128)S(1)} %convolution_select_fusion.6), channel_id=1, source_target_pairs={{0,64},{4,68},{8,72},{12,76},{16,80},{20,84},{24,88},{28,92},{32,9... | collective-permute-start | bytes 786440 | tf_op jit(solution)/shard_map/ppermute | solution.py:16
  113.0 4.2 %collective-permute-start.9 = (f32[16,256]{1,0:T(8,128)S(1)}, f32[16,256]{1,0:T(8,128)S(1)}, u32[]{:S(2)}, u32[]{:S(2)}) collective-permute-start(f32[16,256]{1,0:T(8,128)S(1)} %fusion.10), channel_id=1, source_target_pairs={{0,128},{4,132},{8,136},{12,140},{16,144},{20,148},{24,152},{28,15... | collective-permute-start | bytes 49160 | tf_op jit(solution)/shard_map/ppermute | solution.py:16
  117.5 5.5 %collective-permute-start.11 = (f32[16,256]{1,0:T(8,128)S(1)}, f32[16,256]{1,0:T(8,128)S(1)}, u32[]{:S(2)}, u32[]{:S(2)}) collective-permute-start(f32[16,256]{1,0:T(8,128)S(1)} %fusion.9), channel_id=1, source_target_pairs={{0,4},{4,8},{8,12},{12,16},{16,20},{20,24},{24,28},{28,32},{32,36}... | collective-permute-start | bytes 49160 | tf_op jit(solution)/shard_map/ppermute | solution.py:16
  121.7 12.5 %collective-permute-start.17 = (f32[256,256]{1,0:T(8,128)S(1)}, f32[256,256]{1,0:T(8,128)S(1)}, u32[]{:S(2)}, u32[]{:S(2)}) collective-permute-start(f32[256,256]{1,0:T(8,128)S(1)} %convolution_select_fusion.4), channel_id=1, source_target_pairs={{8,0},{12,4},{16,8},{20,12},{24,16},{28,20},{32,24},{36,28},{40,32... | collective-permute-start | bytes 786440 | tf_op jit(solution)/shard_map/ppermute | solution.py:16
  123.6 13.7 %copy-start.1 = (f32[4,256,256]{2,1,0:T(8,128)S(1)}, f32[4,256,256]{2,1,0:T(8,128)}, u32[]{:S(2)}) copy-start(f32[4,256,256]{2,1,0:T(8,128)} %param.12) | copy-start | bytes 3145732
  131.5 6.9 %copy-start.3 = (f32[16,16,256]{2,1,0:T(8,128)S(1)}, f32[16,16,256]{2,1,0:T(8,128)}, u32[]{:S(2)}) copy-start(f32[16,16,256]{2,1,0:T(8,128)} %get-tuple-element.2) | copy-start | bytes 786436
  132.3 5.0 %collective-permute-start.12 = (f32[16,256]{1,0:T(8,128)S(1)}, f32[16,256]{1,0:T(8,128)S(1)}, u32[]{:S(2)}, u32[]{:S(2)}) collective-permute-start(f32[16,256]{1,0:T(8,128)S(1)} %slice_bitcast_fusion), channel_id=1, source_target_pairs={{4,0},{8,4},{12,8},{16,12},{20,16},{24,20},{28,24},{32,28},{36,32}... | collective-permute-start | bytes 49160 | tf_op jit(solution)/shard_map/ppermute | solution.py:16
  134.6 20.5 %collective-permute-start.19 = (f32[256,256]{1,0:T(8,128)S(1)}, f32[256,256]{1,0:T(8,128)S(1)}, u32[]{:S(2)}, u32[]{:S(2)}) collective-permute-start(f32[256,256]{1,0:T(8,128)S(1)} %convolution_select_fusion.3), channel_id=1, source_target_pairs={{16,0},{20,4},{24,8},{28,12},{32,16},{36,20},{40,24},{44,28},{48,3... | collective-permute-start | bytes 786440 | tf_op jit(solution)/shard_map/ppermute | solution.py:16
  145.8 7.0 %collective-permute-start.13 = (f32[16,256]{1,0:T(8,128)}, f32[16,256]{1,0:T(8,128)S(1)}, u32[]{:S(2)}, u32[]{:S(2)}) collective-permute-start(f32[16,256]{1,0:T(8,128)} %shard_map.89), channel_id=1, source_target_pairs={{4,0},{8,4},{12,8},{16,12},{20,16},{24,20},{28,24},{32,28},{36,32}... | collective-permute-start | bytes 49160 | tf_op jit(solution)/shard_map/ppermute | solution.py:16
  153.7 4.5 %collective-permute-start.14 = (f32[16,256]{1,0:T(8,128)S(1)}, f32[16,256]{1,0:T(8,128)S(1)}, u32[]{:S(2)}, u32[]{:S(2)}) collective-permute-start(f32[16,256]{1,0:T(8,128)S(1)} %fusion.8), channel_id=1, source_target_pairs={{8,0},{12,4},{16,8},{20,12},{24,16},{28,20},{32,24},{36,28},{40,32... | collective-permute-start | bytes 49160 | tf_op jit(solution)/shard_map/ppermute | solution.py:16
  155.4 14.3 %collective-permute-start.21 = (f32[256,256]{1,0:T(8,128)S(1)}, f32[256,256]{1,0:T(8,128)S(1)}, u32[]{:S(2)}, u32[]{:S(2)}) collective-permute-start(f32[256,256]{1,0:T(8,128)S(1)} %convolution_select_fusion.2), channel_id=1, source_target_pairs={{32,0},{36,4},{40,8},{44,12},{48,16},{52,20},{56,24},{60,28},{64,3... | collective-permute-start | bytes 786440 | tf_op jit(solution)/shard_map/ppermute | solution.py:16
  158.4 7.0 %collective-permute-start.16 = (f32[16,256]{1,0:T(8,128)S(1)}, f32[16,256]{1,0:T(8,128)S(1)}, u32[]{:S(2)}, u32[]{:S(2)}) collective-permute-start(f32[16,256]{1,0:T(8,128)S(1)} %fusion.7), channel_id=1, source_target_pairs={{16,0},{20,4},{24,8},{28,12},{32,16},{36,20},{40,24},{44,28},{48,3... | collective-permute-start | bytes 49160 | tf_op jit(solution)/shard_map/ppermute | solution.py:16
  165.7 11.6 %collective-permute-start.18 = (f32[16,256]{1,0:T(8,128)S(1)}, f32[16,256]{1,0:T(8,128)S(1)}, u32[]{:S(2)}, u32[]{:S(2)}) collective-permute-start(f32[16,256]{1,0:T(8,128)S(1)} %fusion.6), channel_id=1, source_target_pairs={{32,0},{36,4},{40,8},{44,12},{48,16},{52,20},{56,24},{60,28},{64,3... | collective-permute-start | bytes 49160 | tf_op jit(solution)/shard_map/ppermute | solution.py:16
  170.2 23.4 %collective-permute-start.23 = (f32[256,256]{1,0:T(8,128)S(1)}, f32[256,256]{1,0:T(8,128)S(1)}, u32[]{:S(2)}, u32[]{:S(2)}) collective-permute-start(f32[256,256]{1,0:T(8,128)S(1)} %convolution_select_fusion.1), channel_id=1, source_target_pairs={{64,0},{68,4},{72,8},{76,12},{80,16},{84,20},{88,24},{92,28},{96,3... | collective-permute-start | bytes 786440 | tf_op jit(solution)/shard_map/ppermute | solution.py:16
  177.5 14.5 %collective-permute-start.20 = (f32[16,256]{1,0:T(8,128)S(1)}, f32[16,256]{1,0:T(8,128)S(1)}, u32[]{:S(2)}, u32[]{:S(2)}) collective-permute-start(f32[16,256]{1,0:T(8,128)S(1)} %fusion.5), channel_id=1, source_target_pairs={{64,0},{68,4},{72,8},{76,12},{80,16},{84,20},{88,24},{92,28},{96,3... | collective-permute-start | bytes 49160 | tf_op jit(solution)/shard_map/ppermute | solution.py:16
  192.2 8.8 %collective-permute-start.22 = (f32[16,256]{1,0:T(8,128)S(1)}, f32[16,256]{1,0:T(8,128)S(1)}, u32[]{:S(2)}, u32[]{:S(2)}) collective-permute-start(f32[16,256]{1,0:T(8,128)S(1)} %fusion.4), channel_id=1, source_target_pairs={{128,0},{132,4},{136,8},{140,12},{144,16},{148,20},{152,24},{156,2... | collective-permute-start | bytes 49160 | tf_op jit(solution)/shard_map/ppermute | solution.py:16
  201.3 5.1 %collective-permute-start.24 = (f32[16,256]{1,0:T(8,128)S(1)}, f32[16,256]{1,0:T(8,128)S(1)}, u32[]{:S(2)}, u32[]{:S(2)}) collective-permute-start(f32[16,256]{1,0:T(8,128)S(1)} %fusion.3), channel_id=1, source_target_pairs={{4,0},{8,4},{12,8},{16,12},{20,16},{24,20},{28,24},{32,28},{36,32}... | collective-permute-start | bytes 49160 | tf_op jit(solution)/shard_map/ppermute | solution.py:16
  206.4 0.6 copy-start.5

commit v4 on v3

--- a/solution.py
+++ b/solution.py
@@ -8,12 +8,27 @@
 from jax.sharding import PartitionSpec as P
 
 GRID = 16
+UNROLL = 4
 
 
 def passed_along(block, axis, distance):
     devices = range(lax.axis_size(axis))
     route = [(i - distance, i) for i in devices if i - distance in devices]
     return lax.ppermute(block, axis, route)
+
+
+def gathered_rows(part, axis):
+    peers, index = (lax.axis_size(axis), lax.axis_index(axis))
+    rows = part.shape[0]
+    whole = jnp.zeros((peers * rows,) + part.shape[1:], part.dtype)
+    for shift in range(peers):
+        if shift == 0:
+            got = part
+        else:
+            got = lax.ppermute(part, axis, [(i, (i + shift) % peers) for i in range(peers)])
+        owner = lax.rem(index - shift + peers, peers)
+        whole = lax.dynamic_update_slice_in_dim(whole, got, owner * rows, 0)
+    return whole
 
 
 def accurate_matmul_result(first_factor, second_factor):
@@ -70,9 +85,8 @@
         pick_ref, side_pick_ref, start_ref, table_ref, side_ref, source_ref, out_ref, side_out_ref = refs
     else:
         pick_ref, start_ref, table_ref, source_ref, out_ref = refs
-    rows = start_ref[...]
-    order = range(steps - 1, -1, -1) if reverse else range(steps)
-    for t in order:
+    def advance(i, rows):
+        t = steps - 1 - i if reverse else i
         if side:
             side_out_ref[t] = jnp.dot(
                 rows,
@@ -91,6 +105,9 @@
         )
         if store_all:
             out_ref[t] = rows
+        return rows
+
+    rows = lax.fori_loop(0, steps, advance, start_ref[...], unroll=UNROLL)
     if not store_all:
         out_ref[...] = rows
 
@@ -169,7 +186,7 @@
     forward_rows = recurrence(
         forward_pick, own_identity, forward_table, blank_columns, False, False
     )
-    whole_matrix = lax.all_gather(forward_rows, "col", axis=0, tiled=True)
+    whole_matrix = gathered_rows(forward_rows, "col")
     first_block = time_index == 0
     forward_maps = doubling_maps(
         jnp.where(first_block, jnp.zeros_like(whole_matrix), whole_matrix), "tm", False
@@ -182,7 +199,7 @@
     backward_rows = recurrence(
         backward_pick, own_identity, backward_table, blank_columns, True, False
     )
-    whole_back = lax.all_gather(backward_rows, "col", axis=0, tiled=True)
+    whole_back = gathered_rows(backward_rows, "col")
     backward_maps = doubling_maps(whole_back, "tm", True)
 
     block_records = recurrence(

time: 215 us -> 215 us (level)
  blocking collectives: 21 us -> 0 us
  starting transfers between devices: 74.6 us -> 95 us
    all_gather x2 -> x0, blocking collectives: 21 us -> none  [the longest x1 11.4 us: shards(): whole_matrix = lax.all_gather(forward_rows, 'col', axis=0, tiled=True)]
    ppermute x25, starting transfers between devices: 74.6 us -> 86.3 us  [passed_along(): return lax.ppermute(block, axis, route)]
    ppermute x0 -> x6, starting transfers between devices: none -> 8.69 us  [gathered_rows(): lax.ppermute(part, axis, [(i, (i + shift) % peers) for i in range(peers)])]
  transfers between devices with their start and end apart: 25 -> 31, of which waited for: 11 -> 12; matrix products, arithmetic and copies ran while one was open for 8% -> 9% of each run, Pallas kernels for 13% -> 13%
where the time goes in v4:
time: 215 us; the launch traced here: 214 us
  starting transfers between devices  95 us (44%)
  waiting for transfers between devices  47.2 us (22%)
  Pallas kernels  43.2 us (20%)
  matrix products  11.3 us (5%)
  local copies, waits for them, and re-layouts  9.06 us (4%)
  other arithmetic  6.72 us (3%)
    ppermute x25, starting transfers between devices, passed_along(): return lax.ppermute(block, axis, route)  86.3 us
    ppermute x25, waiting for transfers between devices, passed_along(): return lax.ppermute(block, axis, route)  47.2 us
    pallas_call x6, Pallas kernels, recurrence(): pl.pallas_call(functools.partial(recurrence_kernel, steps=steps, reverse=...  43.2 us
    dot_general x25, matrix products, accurate_matmul_result(): return jnp.dot(first_factor, second_factor, precision=lax.Precision.HIGHEST)  9.98 us
    ppermute x6, starting transfers between devices, gathered_rows(): lax.ppermute(part, axis, [(i, (i + shift) % peers) for i in range(peers)])  8.69 us
  transfers between devices with their start and end apart: 31, of which 12 were waited for; matrix products, arithmetic and copies ran while one was open for 9% of the time, Pallas kernels for 13%

profile of v4, /device:TPU:1, one launch (start us, length us, event | category | flops | bytes accessed | tf_op | source)
XLA Modules:
  0.0 214.2 jit_solution(10523804303336834628)
XLA Ops:
  0.9 1.2 fusion.17
  2.1 1.1 multiply_add_fusion.1
  3.2 1.4 fusion
  4.7 1.5 copy.10
  6.2 0.6 constant_dynamic-slice_fusion.refs_1_
  6.9 0.6 broadcast_select_fusion.2
  7.5 1.1 broadcast_in_dim.12.refs_3_
  8.6 7.5 %shard_map.86 = f32[64,256]{1,0:T(8,128)} custom-call(s32[16]{0:T(128)} %get-tuple-element.9.refs_0_, f32[64,256]{1,0:T(8,128)} %constant_dynamic-slice_fusion.refs_1_, f32[8,256,256]{2,1,0:T(8,128)} %bitcast.86, f32[16,64,256]{2,1,0:T(8,128)} %broadcast_in_dim.12.refs_3_), custom_call_target="tpu_custom_call" | custom-call | tf_op jit(solution)/shard_map/pallas_call | solution.py:130
  16.0 2.1 collective-permute-start
  18.2 2.6 %collective-permute-start.1 = (f32[64,256]{1,0:T(8,128)}, f32[64,256]{1,0:T(8,128)S(1)}, u32[]{:S(2)}, u32[]{:S(2)}) collective-permute-start(f32[64,256]{1,0:T(8,128)} %shard_map.86), channel_id=1, source_target_pairs={{0,2},{1,3},{2,0},{3,1},{4,6},{5,7},{6,4},{7,5},{8,10},{9,11},{10,... | collective-permute-start | bytes 196616 | tf_op jit(solution)/shard_map/ppermute | solution.py:28
  20.8 1.1 collective-permute-start.2
  21.8 1.6 copy.11
  23.4 1.2 concatenate.6.refs_2_
  24.6 7.2 %shard_map.90 = f32[64,256]{1,0:T(8,128)} custom-call(s32[16]{0:T(128)} %get-tuple-element.8.refs_0_, f32[64,256]{1,0:T(8,128)} %constant_dynamic-slice_fusion.refs_1_, f32[5,256,256]{2,1,0:T(8,128)} %concatenate.6.refs_2_, f32[16,64,256]{2,1,0:T(8,128)} %broadcast_in_dim.12.refs_3_), custom_call_target="tpu_custom_call" | custom-call | tf_op jit(solution)/shard_map/pallas_call | solution.py:130
  32.2 0.8 collective-permute-start.18
  33.1 1.8 fusion.1.refs_3_.refs_5_
  34.9 0.6 broadcast_in_dim.13.refs_1_
  35.5 7.0 %shard_map.87 = f32[16,256]{1,0:T(8,128)} custom-call(s32[16]{0:T(128)} %get-tuple-element.9.refs_0_, f32[16,256]{1,0:T(8,128)} %broadcast_in_dim.13.refs_1_, f32[8,256,256]{2,1,0:T(8,128)} %bitcast.87, f32[16,16,256]{2,1,0:T(8,128)} %fusion.1.refs_3_.refs_5_), custom_call_target="tpu_custom_call" | custom-call | tf_op jit(solution)/shard_map/pallas_call | solution.py:130
  42.5 1.7 collective-permute-start.19
  44.6 0.7 add_select_fusion
  45.3 5.5 %collective-permute-start.3 = (f32[16,256]{1,0:T(8,128)S(1)}, f32[16,256]{1,0:T(8,128)S(1)}, u32[]{:S(2)}, u32[]{:S(2)}) collective-permute-start(f32[16,256]{1,0:T(8,128)S(1)} %add_select_fusion), channel_id=1, source_target_pairs={{0,4},{4,8},{8,12},{12,16},{16,20},{20,24},{24,28},{28,32},{32,36}... | collective-permute-start | bytes 49160 | tf_op jit(solution)/shard_map/ppermute | solution.py:17
  50.8 1.9 collective-permute-start.5
  52.7 1.3 multiply_add_fusion.refs_4_
  54.3 3.5 %collective-permute-start.4 = (f32[16,256]{1,0:T(8,128)S(1)}, f32[16,256]{1,0:T(8,128)S(1)}, u32[]{:S(2)}, u32[]{:S(2)}) collective-permute-start(f32[16,256]{1,0:T(8,128)S(1)} %fusion.14), channel_id=1, source_target_pairs={{0,8},{4,12},{8,16},{12,20},{16,24},{20,28},{24,32},{28,36},{32,40... | collective-permute-start | bytes 49160 | tf_op jit(solution)/shard_map/ppermute | solution.py:17
  58.2 3.6 %collective-permute-start.7 = (f32[256,256]{1,0:T(8,128)S(1)}, f32[256,256]{1,0:T(8,128)S(1)}, u32[]{:S(2)}, u32[]{:S(2)}) collective-permute-start(f32[256,256]{1,0:T(8,128)S(1)} %convolution_select_fusion.9), channel_id=1, source_target_pairs={{0,8},{4,12},{8,16},{12,20},{16,24},{20,28},{24,32},{28,36},{32,40... | collective-permute-start | bytes 786440 | tf_op jit(solution)/shard_map/ppermute | solution.py:17
  62.1 5.2 %collective-permute-start.6 = (f32[16,256]{1,0:T(8,128)S(1)}, f32[16,256]{1,0:T(8,128)S(1)}, u32[]{:S(2)}, u32[]{:S(2)}) collective-permute-start(f32[16,256]{1,0:T(8,128)S(1)} %fusion.13), channel_id=1, source_target_pairs={{0,16},{4,20},{8,24},{12,28},{16,32},{20,36},{24,40},{28,44},{32,4... | collective-permute-start | bytes 49160 | tf_op jit(solution)/shard_map/ppermute | solution.py:17
  67.7 6.1 %collective-permute-start.9 = (f32[256,256]{1,0:T(8,128)S(1)}, f32[256,256]{1,0:T(8,128)S(1)}, u32[]{:S(2)}, u32[]{:S(2)}) collective-permute-start(f32[256,256]{1,0:T(8,128)S(1)} %convolution_select_fusion.8), channel_id=1, source_target_pairs={{0,16},{4,20},{8,24},{12,28},{16,32},{20,36},{24,40},{28,44},{32,4... | collective-permute-start | bytes 786440 | tf_op jit(solution)/shard_map/ppermute | solution.py:17
  74.1 2.5 %collective-permute-start.8 = (f32[16,256]{1,0:T(8,128)S(1)}, f32[16,256]{1,0:T(8,128)S(1)}, u32[]{:S(2)}, u32[]{:S(2)}) collective-permute-start(f32[16,256]{1,0:T(8,128)S(1)} %fusion.12), channel_id=1, source_target_pairs={{0,32},{4,36},{8,40},{12,44},{16,48},{20,52},{24,56},{28,60},{32,6... | collective-permute-start | bytes 49160 | tf_op jit(solution)/shard_map/ppermute | solution.py:17
  76.6 3.5 %collective-permute-done.9 = f32[256,256]{1,0:T(8,128)S(1)} collective-permute-done((f32[256,256]{1,0:T(8,128)S(1)}, f32[256,256]{1,0:T(8,128)S(1)}, u32[]{:S(2)}, u32[]{:S(2)}) %collective-permute-start.9) | collective-permute-done | bytes 262176 | tf_op jit(solution)/shard_map/ppermute | solution.py:17
  80.5 5.6 %collective-permute-start.11 = (f32[256,256]{1,0:T(8,128)S(1)}, f32[256,256]{1,0:T(8,128)S(1)}, u32[]{:S(2)}, u32[]{:S(2)}) collective-permute-start(f32[256,256]{1,0:T(8,128)S(1)} %convolution_select_fusion.7), channel_id=1, source_target_pairs={{0,32},{4,36},{8,40},{12,44},{16,48},{20,52},{24,56},{28,60},{32,6... | collective-permute-start | bytes 786440 | tf_op jit(solution)/shard_map/ppermute | solution.py:17
  86.3 3.1 %collective-permute-start.10 = (f32[16,256]{1,0:T(8,128)S(1)}, f32[16,256]{1,0:T(8,128)S(1)}, u32[]{:S(2)}, u32[]{:S(2)}) collective-permute-start(f32[16,256]{1,0:T(8,128)S(1)} %fusion.11), channel_id=1, source_target_pairs={{0,64},{4,68},{8,72},{12,76},{16,80},{20,84},{24,88},{28,92},{32,9... | collective-permute-start | bytes 49160 | tf_op jit(solution)/shard_map/ppermute | solution.py:17
  89.9 8.7 %collective-permute-start.13 = (f32[256,256]{1,0:T(8,128)S(1)}, f32[256,256]{1,0:T(8,128)S(1)}, u32[]{:S(2)}, u32[]{:S(2)}) collective-permute-start(f32[256,256]{1,0:T(8,128)S(1)} %convolution_select_fusion.6), channel_id=1, source_target_pairs={{0,64},{4,68},{8,72},{12,76},{16,80},{20,84},{24,88},{28,92},{32,9... | collective-permute-start | bytes 786440 | tf_op jit(solution)/shard_map/ppermute | solution.py:17
  98.6 11.3 %collective-permute-start.21 = (f32[256,256]{1,0:T(8,128)S(1)}, f32[256,256]{1,0:T(8,128)S(1)}, u32[]{:S(2)}, u32[]{:S(2)}) collective-permute-start(f32[256,256]{1,0:T(8,128)S(1)} %constant_dynamic-update-slice_fusion), channel_id=1, source_target_pairs={{4,0},{8,4},{12,8},{16,12},{20,16},{24,20},{28,24},{32,28},{36,32}... | collective-permute-start | bytes 786440 | tf_op jit(solution)/shard_map/ppermute | solution.py:17
  110.2 3.8 %collective-permute-start.12 = (f32[16,256]{1,0:T(8,128)S(1)}, f32[16,256]{1,0:T(8,128)S(1)}, u32[]{:S(2)}, u32[]{:S(2)}) collective-permute-start(f32[16,256]{1,0:T(8,128)S(1)} %fusion.10), channel_id=1, source_target_pairs={{0,128},{4,132},{8,136},{12,140},{16,144},{20,148},{24,152},{28,15... | collective-permute-start | bytes 49160 | tf_op jit(solution)/shard_map/ppermute | solution.py:17
  115.1 7.8 %collective-permute-start.14 = (f32[16,256]{1,0:T(8,128)S(1)}, f32[16,256]{1,0:T(8,128)S(1)}, u32[]{:S(2)}, u32[]{:S(2)}) collective-permute-start(f32[16,256]{1,0:T(8,128)S(1)} %fusion.9), channel_id=1, source_target_pairs={{0,4},{4,8},{8,12},{12,16},{16,20},{20,24},{24,28},{28,32},{32,36}... | collective-permute-start | bytes 49160 | tf_op jit(solution)/shard_map/ppermute | solution.py:17
  123.3 1.3 collective-permute-start.23
  124.6 0.6 broadcast_select_fusion.1.refs_2_
  125.2 7.9 %shard_map.88 = (f32[16,16,256]{2,1,0:T(8,128)}, f32[16,16,256]{2,1,0:T(8,128)}) custom-call(s32[16]{0:T(128)} %get-tuple-element.9.refs_0_, s32[16]{0:T(128)} %refs_1_.1, f32[16,256]{1,0:T(8,128)} %broadcast_select_fusion.1.refs_2_, f32[8,256,256]{2,1,0:T(8,128)} %bitcast.88, f32[4,256,256]{2,1,0:T(8,128)} %multiply_add_fusion.refs_4_, ...), custom_call_target="tpu_custom_call" | custom-call | tf_op jit(solution)/shard_map/pallas_call | solution.py:130
  133.1 0.8 slice_bitcast_fusion
  133.9 1.9 collective-permute-start.15
  136.2 1.3 collective-permute-start.25
  137.5 1.0 slice.6
  138.9 1.1 fusion.2
  140.0 0.7 sub.94.refs_3_
  140.7 6.8 %shard_map.89 = f32[16,256]{1,0:T(8,128)} custom-call(s32[16]{0:T(128)} %get-tuple-element.8.refs_0_, f32[16,256]{1,0:T(8,128)} %broadcast_in_dim.13.refs_1_, f32[5,256,256]{2,1,0:T(8,128)} %concatenate.6.refs_2_, f32[16,16,256]{2,1,0:T(8,128)} %sub.94.refs_3_), custom_call_target="tpu_custom_call" | custom-call | tf_op jit(solution)/shard_map/pallas_call | solution.py:130
  147.5 1.9 collective-permute-start.16
  149.4 3.9 %collective-permute-done.16 = f32[16,256]{1,0:T(8,128)S(1)} collective-permute-done((f32[16,256]{1,0:T(8,128)}, f32[16,256]{1,0:T(8,128)S(1)}, u32[]{:S(2)}, u32[]{:S(2)}) %collective-permute-start.16) | collective-permute-done | bytes 16416 | tf_op jit(solution)/shard_map/ppermute | solution.py:17
  153.4 0.9 fusion.8
  154.3 1.3 collective-permute-start.20
  156.0 1.3 collective-permute-start.27
  157.3 2.2 %collective-permute-done.20 = f32[16,256]{1,0:T(8,128)S(1)} collective-permute-done((f32[16,256]{1,0:T(8,128)S(1)}, f32[16,256]{1,0:T(8,128)S(1)}, u32[]{:S(2)}, u32[]{:S(2)}) %collective-permute-start.20) | collective-permute-done | bytes 16416 | tf_op jit(solution)/shard_map/ppermute | solution.py:17
  159.7 1.3 collective-permute-start.22
  161.0 6.5 %collective-permute-done.22 = f32[16,256]{1,0:T(8,128)S(1)} collective-permute-done((f32[16,256]{1,0:T(8,128)S(1)}, f32[16,256]{1,0:T(8,128)S(1)}, u32[]{:S(2)}, u32[]{:S(2)}) %collective-permute-start.22) | collective-permute-done | bytes 16416 | tf_op jit(solution)/shard_map/ppermute | solution.py:17
  167.8 1.3 collective-permute-start.24
  169.1 2.5 %collective-permute-done.27 = f32[256,256]{1,0:T(8,128)S(1)} collective-permute-done((f32[256,256]{1,0:T(8,128)S(1)}, f32[256,256]{1,0:T(8,128)S(1)}, u32[]{:S(2)}, u32[]{:S(2)}) %collective-permute-start.27) | collective-permute-done | bytes 262176 | tf_op jit(solution)/shard_map/ppermute | solution.py:17
  172.0 1.3 collective-permute-start.29
  173.3 5.6 %collective-permute-done.24 = f32[16,256]{1,0:T(8,128)S(1)} collective-permute-done((f32[16,256]{1,0:T(8,128)S(1)}, f32[16,256]{1,0:T(8,128)S(1)}, u32[]{:S(2)}, u32[]{:S(2)}) %collective-permute-start.24) | collective-permute-done | bytes 16416 | tf_op jit(solution)/shard_map/ppermute | solution.py:17
  179.1 1.3 collective-permute-start.26
  180.4 12.5 %collective-permute-done.26 = f32[16,256]{1,0:T(8,128)S(1)} collective-permute-done((f32[16,256]{1,0:T(8,128)S(1)}, f32[16,256]{1,0:T(8,128)S(1)}, u32[]{:S(2)}, u32[]{:S(2)}) %collective-permute-start.26) | collective-permute-done | bytes 16416 | tf_op jit(solution)/shard_map/ppermute | solution.py:17
  193.2 1.3 collective-permute-start.28
  194.9 4.3 %collective-permute-done.28 = f32[16,256]{1,0:T(8,128)S(1)} collective-permute-done((f32[16,256]{1,0:T(8,128)S(1)}, f32[16,256]{1,0:T(8,128)S(1)}, u32[]{:S(2)}, u32[]{:S(2)}) %collective-permute-start.28) | collective-permute-done | bytes 16416 | tf_op jit(solution)/shard_map/ppermute | solution.py:17
  199.4 2.2 %collective-permute-start.30 = (f32[16,256]{1,0:T(8,128)S(1)}, f32[16,256]{1,0:T(8,128)S(1)}, u32[]{:S(2)}, u32[]{:S(2)}) collective-permute-start(f32[16,256]{1,0:T(8,128)S(1)} %fusion.3), channel_id=1, source_target_pairs={{4,0},{8,4},{12,8},{16,12},{20,16},{24,20},{28,24},{32,28},{36,32}... | collective-permute-start | bytes 49160 | tf_op jit(solution)/shard_map/ppermute | solution.py:17
  201.6 5.1 %collective-permute-done.30.refs_1_ = f32[16,256]{1,0:T(8,128)S(1)} collective-permute-done((f32[16,256]{1,0:T(8,128)S(1)}, f32[16,256]{1,0:T(8,128)S(1)}, u32[]{:S(2)}, u32[]{:S(2)}) %collective-permute-start.30) | collective-permute-done | bytes 16416 | tf_op jit(solution)/shard_map/ppermute | solution.py:17
  207.3 6.9 %shard_map.91 = f32[16,16,256]{2,1,0:T(8,128)} custom-call(s32[16]{0:T(128)} %get-tuple-element.8.refs_0_, f32[16,256]{1,0:T(8,128)} %copy-done.7, f32[5,256,256]{2,1,0:T(8,128)} %concatenate.6.refs_2_, f32[16,16,256]{2,1,0:T(8,128)} %sub.94.refs_3_), custom_call_target="tpu_custom_call" | custom-call | tf_op jit(solution)/shard_map/pallas_call | solution.py:130
  (85 shorter events, 8.9 us)
Async XLA Ops:
  0.6 2.5 %copy-start = (f32[4,256,256]{2,1,0:T(8,128)S(1)}, f32[4,256,256]{2,1,0:T(8,128)}, u32[]{:S(2)}) copy-start(f32[4,256,256]{2,1,0:T(8,128)} %param.11) | copy-start | bytes 3145732
  0.6 2.5 %copy-start.2 = (f32[4,256]{1,0:T(4,128)S(1)}, f32[4,256]{1,0:T(4,128)}, u32[]{:S(2)}) copy-start(f32[4,256]{1,0:T(4,128)} %param.10) | copy-start | bytes 12292
  4.7 2.2 %copy-start.8 = (s32[16]{0:T(128)S(1)}, s32[16]{0:T(128)}, u32[]{:S(2)}) copy-start(s32[16]{0:T(128)} %refs_1_.1) | copy-start | bytes 196
  4.7 2.2 %copy-start.10 = (s32[16]{0:T(128)S(1)}, s32[16]{0:T(128)}, u32[]{:S(2)}) copy-start(s32[16]{0:T(128)} %param.9) | copy-start | bytes 196
  16.0 26.5 %collective-permute-start = (f32[64,256]{1,0:T(8,128)}, f32[64,256]{1,0:T(8,128)S(1)}, u32[]{:S(2)}, u32[]{:S(2)}) collective-permute-start(f32[64,256]{1,0:T(8,128)} %shard_map.86), channel_id=1, source_target_pairs={{0,1},{1,2},{2,3},{3,0},{4,5},{5,6},{6,7},{7,4},{8,9},{9,10},{10,1... | collective-permute-start | bytes 196616 | tf_op jit(solution)/shard_map/ppermute | solution.py:28
  18.2 26.1 %collective-permute-start.1 = (f32[64,256]{1,0:T(8,128)}, f32[64,256]{1,0:T(8,128)S(1)}, u32[]{:S(2)}, u32[]{:S(2)}) collective-permute-start(f32[64,256]{1,0:T(8,128)} %shard_map.86), channel_id=1, source_target_pairs={{0,2},{1,3},{2,0},{3,1},{4,6},{5,7},{6,4},{7,5},{8,10},{9,11},{10,... | collective-permute-start | bytes 196616 | tf_op jit(solution)/shard_map/ppermute | solution.py:28
  20.8 23.5 %collective-permute-start.2 = (f32[64,256]{1,0:T(8,128)}, f32[64,256]{1,0:T(8,128)S(1)}, u32[]{:S(2)}, u32[]{:S(2)}) collective-permute-start(f32[64,256]{1,0:T(8,128)} %shard_map.86), channel_id=1, source_target_pairs={{0,3},{1,0},{2,1},{3,2},{4,7},{5,4},{6,5},{7,6},{8,11},{9,8},{10,9... | collective-permute-start | bytes 196616 | tf_op jit(solution)/shard_map/ppermute | solution.py:28
  23.4 9.7 %copy-start.6 = (f32[16,16,256]{2,1,0:T(8,128)S(1)}, f32[16,16,256]{2,1,0:T(8,128)}, u32[]{:S(2)}) copy-start(f32[16,16,256]{2,1,0:T(8,128)} %param.7) | copy-start | bytes 786436
  31.8 42.1 %collective-permute-start.17 = (f32[64,256]{1,0:T(8,128)}, f32[64,256]{1,0:T(8,128)S(1)}, u32[]{:S(2)}, u32[]{:S(2)}) collective-permute-start(f32[64,256]{1,0:T(8,128)} %shard_map.90), channel_id=1, source_target_pairs={{0,1},{1,2},{2,3},{3,0},{4,5},{5,6},{6,7},{7,4},{8,9},{9,10},{10,1... | collective-permute-start | bytes 196616 | tf_op jit(solution)/shard_map/ppermute | solution.py:28
  32.2 53.9 %collective-permute-start.18 = (f32[64,256]{1,0:T(8,128)}, f32[64,256]{1,0:T(8,128)S(1)}, u32[]{:S(2)}, u32[]{:S(2)}) collective-permute-start(f32[64,256]{1,0:T(8,128)} %shard_map.90), channel_id=1, source_target_pairs={{0,2},{1,3},{2,0},{3,1},{4,6},{5,7},{6,4},{7,5},{8,10},{9,11},{10,... | collective-permute-start | bytes 196616 | tf_op jit(solution)/shard_map/ppermute | solution.py:28
  33.1 9.4 %copy-start.5 = (f32[64,256]{1,0:T(8,128)S(1)}, f32[64,256]{1,0:T(8,128)}, u32[]{:S(2)}) copy-start(f32[64,256]{1,0:T(8,128)} %shard_map.86) | copy-start | bytes 196612
  33.1 9.4 %copy-start.4 = (f32[64,256]{1,0:T(8,128)S(1)}, f32[64,256]{1,0:T(8,128)}, u32[]{:S(2)}) copy-start(f32[64,256]{1,0:T(8,128)} %shard_map.90) | copy-start | bytes 196612
  33.1 11.2 %copy-start.9 = (f32[256]{0:T(256)S(1)}, f32[256]{0:T(256)}, u32[]{:S(2)}) copy-start(f32[256]{0:T(256)} %param.13) | copy-start | bytes 3076
  42.5 56.0 %collective-permute-start.19 = (f32[64,256]{1,0:T(8,128)S(1)}, f32[64,256]{1,0:T(8,128)S(1)}, u32[]{:S(2)}, u32[]{:S(2)}) collective-permute-start(f32[64,256]{1,0:T(8,128)S(1)} %copy-done.4), channel_id=1, source_target_pairs={{0,3},{1,0},{2,1},{3,2},{4,7},{5,4},{6,5},{7,6},{8,11},{9,8},{10,9... | collective-permute-start | bytes 196616 | tf_op jit(solution)/shard_map/ppermute | solution.py:28
  45.3 8.8 %collective-permute-start.3 = (f32[16,256]{1,0:T(8,128)S(1)}, f32[16,256]{1,0:T(8,128)S(1)}, u32[]{:S(2)}, u32[]{:S(2)}) collective-permute-start(f32[16,256]{1,0:T(8,128)S(1)} %add_select_fusion), channel_id=1, source_target_pairs={{0,4},{4,8},{8,12},{12,16},{16,20},{20,24},{24,28},{28,32},{32,36}... | collective-permute-start | bytes 49160 | tf_op jit(solution)/shard_map/ppermute | solution.py:17
  50.8 7.0 %collective-permute-start.5 = (f32[256,256]{1,0:T(8,128)S(1)}, f32[256,256]{1,0:T(8,128)S(1)}, u32[]{:S(2)}, u32[]{:S(2)}) collective-permute-start(f32[256,256]{1,0:T(8,128)S(1)} %broadcast_select_fusion), channel_id=1, source_target_pairs={{0,4},{4,8},{8,12},{12,16},{16,20},{20,24},{24,28},{28,32},{32,36}... | collective-permute-start | bytes 786440 | tf_op jit(solution)/shard_map/ppermute | solution.py:17
  54.3 7.6 %collective-permute-start.4 = (f32[16,256]{1,0:T(8,128)S(1)}, f32[16,256]{1,0:T(8,128)S(1)}, u32[]{:S(2)}, u32[]{:S(2)}) collective-permute-start(f32[16,256]{1,0:T(8,128)S(1)} %fusion.14), channel_id=1, source_target_pairs={{0,8},{4,12},{8,16},{12,20},{16,24},{20,28},{24,32},{28,36},{32,40... | collective-permute-start | bytes 49160 | tf_op jit(solution)/shard_map/ppermute | solution.py:17
  58.2 9.1 %collective-permute-start.7 = (f32[256,256]{1,0:T(8,128)S(1)}, f32[256,256]{1,0:T(8,128)S(1)}, u32[]{:S(2)}, u32[]{:S(2)}) collective-permute-start(f32[256,256]{1,0:T(8,128)S(1)} %convolution_select_fusion.9), channel_id=1, source_target_pairs={{0,8},{4,12},{8,16},{12,20},{16,24},{20,28},{24,32},{28,36},{32,40... | collective-permute-start | bytes 786440 | tf_op jit(solution)/shard_map/ppermute | solution.py:17
  62.1 11.8 %collective-permute-start.6 = (f32[16,256]{1,0:T(8,128)S(1)}, f32[16,256]{1,0:T(8,128)S(1)}, u32[]{:S(2)}, u32[]{:S(2)}) collective-permute-start(f32[16,256]{1,0:T(8,128)S(1)} %fusion.13), channel_id=1, source_target_pairs={{0,16},{4,20},{8,24},{12,28},{16,32},{20,36},{24,40},{28,44},{32,4... | collective-permute-start | bytes 49160 | tf_op jit(solution)/shard_map/ppermute | solution.py:17
  67.7 12.4 %collective-permute-start.9 = (f32[256,256]{1,0:T(8,128)S(1)}, f32[256,256]{1,0:T(8,128)S(1)}, u32[]{:S(2)}, u32[]{:S(2)}) collective-permute-start(f32[256,256]{1,0:T(8,128)S(1)} %convolution_select_fusion.8), channel_id=1, source_target_pairs={{0,16},{4,20},{8,24},{12,28},{16,32},{20,36},{24,40},{28,44},{32,4... | collective-permute-start | bytes 786440 | tf_op jit(solution)/shard_map/ppermute | solution.py:17
  74.1 11.9 %collective-permute-start.8 = (f32[16,256]{1,0:T(8,128)S(1)}, f32[16,256]{1,0:T(8,128)S(1)}, u32[]{:S(2)}, u32[]{:S(2)}) collective-permute-start(f32[16,256]{1,0:T(8,128)S(1)} %fusion.12), channel_id=1, source_target_pairs={{0,32},{4,36},{8,40},{12,44},{16,48},{20,52},{24,56},{28,60},{32,6... | collective-permute-start | bytes 49160 | tf_op jit(solution)/shard_map/ppermute | solution.py:17
  80.5 9.0 %collective-permute-start.11 = (f32[256,256]{1,0:T(8,128)S(1)}, f32[256,256]{1,0:T(8,128)S(1)}, u32[]{:S(2)}, u32[]{:S(2)}) collective-permute-start(f32[256,256]{1,0:T(8,128)S(1)} %convolution_select_fusion.7), channel_id=1, source_target_pairs={{0,32},{4,36},{8,40},{12,44},{16,48},{20,52},{24,56},{28,60},{32,6... | collective-permute-start | bytes 786440 | tf_op jit(solution)/shard_map/ppermute | solution.py:17
  86.3 23.6 %collective-permute-start.10 = (f32[16,256]{1,0:T(8,128)S(1)}, f32[16,256]{1,0:T(8,128)S(1)}, u32[]{:S(2)}, u32[]{:S(2)}) collective-permute-start(f32[16,256]{1,0:T(8,128)S(1)} %fusion.11), channel_id=1, source_target_pairs={{0,64},{4,68},{8,72},{12,76},{16,80},{20,84},{24,88},{28,92},{32,9... | collective-permute-start | bytes 49160 | tf_op jit(solution)/shard_map/ppermute | solution.py:17
  89.9 24.1 %collective-permute-start.13 = (f32[256,256]{1,0:T(8,128)S(1)}, f32[256,256]{1,0:T(8,128)S(1)}, u32[]{:S(2)}, u32[]{:S(2)}) collective-permute-start(f32[256,256]{1,0:T(8,128)S(1)} %convolution_select_fusion.6), channel_id=1, source_target_pairs={{0,64},{4,68},{8,72},{12,76},{16,80},{20,84},{24,88},{28,92},{32,9... | collective-permute-start | bytes 786440 | tf_op jit(solution)/shard_map/ppermute | solution.py:17
  98.6 24.3 %collective-permute-start.21 = (f32[256,256]{1,0:T(8,128)S(1)}, f32[256,256]{1,0:T(8,128)S(1)}, u32[]{:S(2)}, u32[]{:S(2)}) collective-permute-start(f32[256,256]{1,0:T(8,128)S(1)} %constant_dynamic-update-slice_fusion), channel_id=1, source_target_pairs={{4,0},{8,4},{12,8},{16,12},{20,16},{24,20},{28,24},{32,28},{36,32}... | collective-permute-start | bytes 786440 | tf_op jit(solution)/shard_map/ppermute | solution.py:17
  110.2 4.6 %collective-permute-start.12 = (f32[16,256]{1,0:T(8,128)S(1)}, f32[16,256]{1,0:T(8,128)S(1)}, u32[]{:S(2)}, u32[]{:S(2)}) collective-permute-start(f32[16,256]{1,0:T(8,128)S(1)} %fusion.10), channel_id=1, source_target_pairs={{0,128},{4,132},{8,136},{12,140},{16,144},{20,148},{24,152},{28,15... | collective-permute-start | bytes 49160 | tf_op jit(solution)/shard_map/ppermute | solution.py:17
  115.1 9.5 %collective-permute-start.14 = (f32[16,256]{1,0:T(8,128)S(1)}, f32[16,256]{1,0:T(8,128)S(1)}, u32[]{:S(2)}, u32[]{:S(2)}) collective-permute-start(f32[16,256]{1,0:T(8,128)S(1)} %fusion.9), channel_id=1, source_target_pairs={{0,4},{4,8},{8,12},{12,16},{16,20},{20,24},{24,28},{28,32},{32,36}... | collective-permute-start | bytes 49160 | tf_op jit(solution)/shard_map/ppermute | solution.py:17
  123.3 12.5 %collective-permute-start.23 = (f32[256,256]{1,0:T(8,128)S(1)}, f32[256,256]{1,0:T(8,128)S(1)}, u32[]{:S(2)}, u32[]{:S(2)}) collective-permute-start(f32[256,256]{1,0:T(8,128)S(1)} %convolution_select_fusion.4), channel_id=1, source_target_pairs={{8,0},{12,4},{16,8},{20,12},{24,16},{28,20},{32,24},{36,28},{40,32... | collective-permute-start | bytes 786440 | tf_op jit(solution)/shard_map/ppermute | solution.py:17
  125.2 13.7 %copy-start.1 = (f32[4,256,256]{2,1,0:T(8,128)S(1)}, f32[4,256,256]{2,1,0:T(8,128)}, u32[]{:S(2)}) copy-start(f32[4,256,256]{2,1,0:T(8,128)} %param.12) | copy-start | bytes 3145732
  133.1 6.9 %copy-start.3 = (f32[16,16,256]{2,1,0:T(8,128)S(1)}, f32[16,16,256]{2,1,0:T(8,128)}, u32[]{:S(2)}) copy-start(f32[16,16,256]{2,1,0:T(8,128)} %get-tuple-element.2) | copy-start | bytes 786436
  133.9 5.0 %collective-permute-start.15 = (f32[16,256]{1,0:T(8,128)S(1)}, f32[16,256]{1,0:T(8,128)S(1)}, u32[]{:S(2)}, u32[]{:S(2)}) collective-permute-start(f32[16,256]{1,0:T(8,128)S(1)} %slice_bitcast_fusion), channel_id=1, source_target_pairs={{4,0},{8,4},{12,8},{16,12},{20,16},{24,20},{28,24},{32,28},{36,32}... | collective-permute-start | bytes 49160 | tf_op jit(solution)/shard_map/ppermute | solution.py:17
  136.2 19.4 %collective-permute-start.25 = (f32[256,256]{1,0:T(8,128)S(1)}, f32[256,256]{1,0:T(8,128)S(1)}, u32[]{:S(2)}, u32[]{:S(2)}) collective-permute-start(f32[256,256]{1,0:T(8,128)S(1)} %convolution_select_fusion.3), channel_id=1, source_target_pairs={{16,0},{20,4},{24,8},{28,12},{32,16},{36,20},{40,24},{44,28},{48,3... | collective-permute-start | bytes 786440 | tf_op jit(solution)/shard_map/ppermute | solution.py:17
  147.5 5.9 %collective-permute-start.16 = (f32[16,256]{1,0:T(8,128)}, f32[16,256]{1,0:T(8,128)S(1)}, u32[]{:S(2)}, u32[]{:S(2)}) collective-permute-start(f32[16,256]{1,0:T(8,128)} %shard_map.89), channel_id=1, source_target_pairs={{4,0},{8,4},{12,8},{16,12},{20,16},{24,20},{28,24},{32,28},{36,32}... | collective-permute-start | bytes 49160 | tf_op jit(solution)/shard_map/ppermute | solution.py:17
  154.3 5.2 %collective-permute-start.20 = (f32[16,256]{1,0:T(8,128)S(1)}, f32[16,256]{1,0:T(8,128)S(1)}, u32[]{:S(2)}, u32[]{:S(2)}) collective-permute-start(f32[16,256]{1,0:T(8,128)S(1)} %fusion.8), channel_id=1, source_target_pairs={{8,0},{12,4},{16,8},{20,12},{24,16},{28,20},{32,24},{36,28},{40,32... | collective-permute-start | bytes 49160 | tf_op jit(solution)/shard_map/ppermute | solution.py:17
  156.0 15.6 %collective-permute-start.27 = (f32[256,256]{1,0:T(8,128)S(1)}, f32[256,256]{1,0:T(8,128)S(1)}, u32[]{:S(2)}, u32[]{:S(2)}) collective-permute-start(f32[256,256]{1,0:T(8,128)S(1)} %convolution_select_fusion.2), channel_id=1, source_target_pairs={{32,0},{36,4},{40,8},{44,12},{48,16},{52,20},{56,24},{60,28},{64,3... | collective-permute-start | bytes 786440 | tf_op jit(solution)/shard_map/ppermute | solution.py:17
  159.7 7.8 %collective-permute-start.22 = (f32[16,256]{1,0:T(8,128)S(1)}, f32[16,256]{1,0:T(8,128)S(1)}, u32[]{:S(2)}, u32[]{:S(2)}) collective-permute-start(f32[16,256]{1,0:T(8,128)S(1)} %fusion.7), channel_id=1, source_target_pairs={{16,0},{20,4},{24,8},{28,12},{32,16},{36,20},{40,24},{44,28},{48,3... | collective-permute-start | bytes 49160 | tf_op jit(solution)/shard_map/ppermute | solution.py:17
  167.8 11.1 %collective-permute-start.24 = (f32[16,256]{1,0:T(8,128)S(1)}, f32[16,256]{1,0:T(8,128)S(1)}, u32[]{:S(2)}, u32[]{:S(2)}) collective-permute-start(f32[16,256]{1,0:T(8,128)S(1)} %fusion.6), channel_id=1, source_target_pairs={{32,0},{36,4},{40,8},{44,12},{48,16},{52,20},{56,24},{60,28},{64,3... | collective-permute-start | bytes 49160 | tf_op jit(solution)/shard_map/ppermute | solution.py:17
  172.0 22.5 %collective-permute-start.29 = (f32[256,256]{1,0:T(8,128)S(1)}, f32[256,256]{1,0:T(8,128)S(1)}, u32[]{:S(2)}, u32[]{:S(2)}) collective-permute-start(f32[256,256]{1,0:T(8,128)S(1)} %convolution_select_fusion.1), channel_id=1, source_target_pairs={{64,0},{68,4},{72,8},{76,12},{80,16},{84,20},{88,24},{92,28},{96,3... | collective-permute-start | bytes 786440 | tf_op jit(solution)/shard_map/ppermute | solution.py:17
  179.1 13.8 %collective-permute-start.26 = (f32[16,256]{1,0:T(8,128)S(1)}, f32[16,256]{1,0:T(8,128)S(1)}, u32[]{:S(2)}, u32[]{:S(2)}) collective-permute-start(f32[16,256]{1,0:T(8,128)S(1)} %fusion.5), channel_id=1, source_target_pairs={{64,0},{68,4},{72,8},{76,12},{80,16},{84,20},{88,24},{92,28},{96,3... | collective-permute-start | bytes 49160 | tf_op jit(solution)/shard_map/ppermute | solution.py:17
  193.2 6.0 %collective-permute-start.28 = (f32[16,256]{1,0:T(8,128)S(1)}, f32[16,256]{1,0:T(8,128)S(1)}, u32[]{:S(2)}, u32[]{:S(2)}) collective-permute-start(f32[16,256]{1,0:T(8,128)S(1)} %fusion.4), channel_id=1, source_target_pairs={{128,0},{132,4},{136,8},{140,12},{144,16},{148,20},{152,24},{156,2... | collective-permute-start | bytes 49160 | tf_op jit(solution)/shard_map/ppermute | solution.py:17
  199.4 7.3 %collective-permute-start.30 = (f32[16,256]{1,0:T(8,128)S(1)}, f32[16,256]{1,0:T(8,128)S(1)}, u32[]{:S(2)}, u32[]{:S(2)}) collective-permute-start(f32[16,256]{1,0:T(8,128)S(1)} %fusion.3), channel_id=1, source_target_pairs={{4,0},{8,4},{12,8},{16,12},{20,16},{24,20},{28,24},{32,28},{36,32}... | collective-permute-start | bytes 49160 | tf_op jit(solution)/shard_map/ppermute | solution.py:17
  206.7 0.6 copy-start.7

commit v5 on v4

--- a/solution.py
+++ b/solution.py
@@ -35,32 +35,99 @@
     return jnp.dot(first_factor, second_factor, precision=lax.Precision.HIGHEST)
 
 
-def doubling_maps(matrix, axis, reverse):
+def doubling_kernel(matrix_ref, records_ref, out_ref, maps, sums, map_in, sum_in, map_sems, sum_sems,
+                    *, axis, reverse):
     peers, index = (lax.axis_size(axis), lax.axis_index(axis))
-    maps = [matrix]
-    distance = 1
-    while 2 * distance < peers:
-        step = -distance if reverse else distance
-        reached = index + distance < peers if reverse else index >= distance
-        got_matrix = passed_along(matrix, axis, step)
-        matrix = jnp.where(reached, accurate_matmul_result(got_matrix, matrix), matrix)
-        maps.append(matrix)
-        distance *= 2
-    return maps
-
-
-def doubling_records(maps, records, axis, reverse):
-    peers, index = (lax.axis_size(axis), lax.axis_index(axis))
-    distance = 1
-    for matrix in maps:
-        step = -distance if reverse else distance
-        reached = index + distance < peers if reverse else index >= distance
-        got_records = passed_along(records, axis, step)
-        records = jnp.where(
-            reached, accurate_matmul_result(got_records, matrix) + records, records
-        )
-        distance *= 2
-    return records
+    other = lax.axis_index("col")
+    rounds = max(1, (peers - 1).bit_length())
+    barrier = pltpu.get_barrier_semaphore()
+    for r in range(rounds):
+        distance = 1 << r
+        for partner, exists in ((index + distance, index + distance < peers),
+                                (index - distance, index - distance >= 0)):
+            @pl.when(exists)
+            def _():
+                pl.semaphore_signal(barrier, inc=1, device_id=(partner, other),
+                                    device_id_type=pl.DeviceIdType.MESH)
+    partners = 0
+    for r in range(rounds):
+        distance = 1 << r
+        partners = partners + jnp.where(index + distance < peers, 1, 0)
+        partners = partners + jnp.where(index - distance >= 0, 1, 0)
+    pl.semaphore_wait(barrier, partners)
+
+    for r in range(rounds):
+        distance = 1 << r
+        if reverse:
+            target, sends = index - distance, index - distance >= 0
+            receives = index + distance < peers
+        else:
+            target, sends = index + distance, index + distance < peers
+            receives = index - distance >= 0
+        own_map = matrix_ref if r == 0 else maps.at[r]
+        own_sum = records_ref if r == 0 else sums.at[r]
+        sum_copy = pltpu.make_async_remote_copy(
+            src_ref=own_sum, dst_ref=sum_in.at[r], send_sem=sum_sems.at[0, r],
+            recv_sem=sum_sems.at[1, r], device_id=(target, other),
+            device_id_type=pl.DeviceIdType.MESH)
+        map_copy = None
+        if r + 1 < rounds:
+            map_copy = pltpu.make_async_remote_copy(
+                src_ref=own_map, dst_ref=map_in.at[r], send_sem=map_sems.at[0, r],
+                recv_sem=map_sems.at[1, r], device_id=(target, other),
+                device_id_type=pl.DeviceIdType.MESH)
+
+        @pl.when(sends)
+        def _():
+            sum_copy.start()
+            if map_copy is not None:
+                map_copy.start()
+
+        @pl.when(receives)
+        def _():
+            sum_copy.wait_recv()
+            sums[r + 1] = jnp.dot(sum_in[r], own_map[...], precision=lax.Precision.HIGHEST,
+                                  preferred_element_type=jnp.float32) + own_sum[...]
+            if map_copy is not None:
+                map_copy.wait_recv()
+                maps[r + 1] = jnp.dot(map_in[r], own_map[...], precision=lax.Precision.HIGHEST,
+                                      preferred_element_type=jnp.float32)
+
+        @pl.when(jnp.logical_not(receives))
+        def _():
+            sums[r + 1] = own_sum[...]
+            if map_copy is not None:
+                maps[r + 1] = own_map[...]
+
+        @pl.when(sends)
+        def _():
+            sum_copy.wait_send()
+            if map_copy is not None:
+                map_copy.wait_send()
+
+    out_ref[...] = sums[rounds]
+
+
+def doubling_scan(matrix, records, axis, reverse, collective_id):
+    peers = lax.axis_size(axis)
+    rounds = max(1, (peers - 1).bit_length())
+    states = matrix.shape[0]
+    vmem = pl.BlockSpec(memory_space=pltpu.VMEM)
+    return pl.pallas_call(
+        functools.partial(doubling_kernel, axis=axis, reverse=reverse),
+        out_shape=jax.ShapeDtypeStruct(records.shape, jnp.float32),
+        in_specs=[vmem, vmem],
+        out_specs=vmem,
+        scratch_shapes=[
+            pltpu.VMEM((rounds, states, states), jnp.float32),
+            pltpu.VMEM((rounds + 1,) + records.shape, jnp.float32),
+            pltpu.VMEM((max(1, rounds - 1), states, states), jnp.float32),
+            pltpu.VMEM((rounds,) + records.shape, jnp.float32),
+            pltpu.SemaphoreType.DMA((2, max(1, rounds - 1))),
+            pltpu.SemaphoreType.DMA((2, rounds)),
+        ],
+        compiler_params=pltpu.CompilerParams(collective_id=collective_id, has_side_effects=True),
+    )(matrix, records)
 
 
 def diffusion_matrices(diffusivity, side_cells):
@@ -188,9 +255,6 @@
     )
     whole_matrix = gathered_rows(forward_rows, "col")
     first_block = time_index == 0
-    forward_maps = doubling_maps(
-        jnp.where(first_block, jnp.zeros_like(whole_matrix), whole_matrix), "tm", False
-    )
 
     final_here = (time_index == time_devices - 1) & (jnp.arange(steps_dev) == steps_dev - 1)
     backward = jnp.transpose(mode_backward_factors, (0, 2, 1))
@@ -200,7 +264,6 @@
         backward_pick, own_identity, backward_table, blank_columns, True, False
     )
     whole_back = gathered_rows(backward_rows, "col")
-    backward_maps = doubling_maps(whole_back, "tm", True)
 
     block_records = recurrence(
         forward_pick, blank_records, forward_table, measured, False, False
@@ -210,7 +273,8 @@
         accurate_matmul_result(initial_mean[None, :], whole_matrix) + block_records,
         block_records,
     )
-    ending_records = doubling_records(forward_maps, folded_records, "tm", False)
+    folded_matrix = jnp.where(first_block, jnp.zeros_like(whole_matrix), whole_matrix)
+    ending_records = doubling_scan(folded_matrix, folded_records, "tm", False, 0)
     start_rows = jnp.where(
         first_block,
         jnp.broadcast_to(initial_mean[None, :], (record_rows, states)),
@@ -233,7 +297,7 @@
     shift = filtered - per_band_products(next_predicted, backward, live_weights)
 
     back_records = recurrence(backward_pick, blank_records, backward_table, shift, True, False)
-    opening_records = doubling_records(backward_maps, back_records, "tm", True)
+    opening_records = doubling_scan(whole_back, back_records, "tm", True, 1)
     after_records = passed_along(opening_records, "tm", -1)
 
     smoothed = recurrence(backward_pick, after_records, backward_table, shift, True, True)

time: 215 us -> 208 us (0.967)
  Pallas kernels: 43.2 us -> 159 us
  starting transfers between devices: 95 us -> 20.1 us
  waiting for transfers between devices: 47.2 us -> 4.62 us
  matrix products: 11.3 us -> 4.37 us
    pallas_call x0 -> x2, Pallas kernels: none -> 115 us  [doubling_scan(): pl.pallas_call(functools.partial(doubling_kernel, axis=axis, reverse=reve...]
    ppermute x25 -> x3, starting transfers between devices: 86.3 us -> 11.4 us  [passed_along(): return lax.ppermute(block, axis, route)]
    ppermute x25 -> x3, waiting for transfers between devices: 47.2 us -> 4.6 us  [passed_along(): return lax.ppermute(block, axis, route)]
    dot_general x25 -> x3, matrix products: 9.98 us -> 3.05 us  [accurate_matmul_result(): return jnp.dot(first_factor, second_factor, precision=lax.Precision.HIGHEST)]
  transfers between devices with their start and end apart: 31 -> 9, of which waited for: 12 -> 3; matrix products, arithmetic and copies ran while one was open for 9% -> 6% of each run, Pallas kernels for 13% -> 35%
where the time goes in v5:
time: 208 us; the launch traced here: 206 us
  Pallas kernels  159 us (76%)
  starting transfers between devices  20.1 us (10%)
  local copies, waits for them, and re-layouts  9.14 us (4%)
  other arithmetic  7.96 us (4%)
  waiting for transfers between devices  4.62 us (2%)
  matrix products  4.37 us (2%)
    pallas_call x2, Pallas kernels, doubling_scan(): pl.pallas_call(functools.partial(doubling_kernel, axis=axis, reverse=reve...  115 us
    pallas_call x6, Pallas kernels, recurrence(): pl.pallas_call(functools.partial(recurrence_kernel, steps=steps, reverse=...  43.3 us
    ppermute x3, starting transfers between devices, passed_along(): return lax.ppermute(block, axis, route)  11.4 us
    ppermute x6, starting transfers between devices, gathered_rows(): lax.ppermute(part, axis, [(i, (i + shift) % peers) for i in range(peers)])  8.69 us
    ppermute x3, waiting for transfers between devices, passed_along(): return lax.ppermute(block, axis, route)  4.6 us
  transfers between devices with their start and end apart: 9, of which 3 were waited for; matrix products, arithmetic and copies ran while one was open for 6% of the time, Pallas kernels for 35%

profile of v5, /device:TPU:1, one launch (start us, length us, event | category | flops | bytes accessed | tf_op | source)
XLA Modules:
  0.0 205.8 jit_solution(10501274890191345659)
XLA Ops:
  0.6 0.0 copy-start
  0.6 0.0 copy-start.3
  0.7 0.2 fusion.9
  0.9 1.2 fusion.5
  2.1 1.1 multiply_add_fusion.1
  3.2 0.0 copy-done
  3.2 0.0 copy-done.3
  3.2 1.3 fusion
  4.5 0.1 pad_maximum_fusion
  4.7 0.0 copy-start.9
  4.7 0.0 copy-start.11
  4.7 1.5 copy.10
  6.2 0.6 constant_dynamic-slice_fusion.refs_1_
  6.8 0.0 copy-done.9
  6.8 0.0 copy-done.11
  6.8 0.5 broadcast_select_fusion.2
  7.3 1.1 broadcast_in_dim.12.refs_3_
  8.4 7.5 %shard_map.86 = f32[64,256]{1,0:T(8,128)} custom-call(s32[16]{0:T(128)} %get-tuple-element.9.refs_0_, f32[64,256]{1,0:T(8,128)} %constant_dynamic-slice_fusion.refs_1_, f32[8,256,256]{2,1,0:T(8,128)} %bitcast.42, f32[16,64,256]{2,1,0:T(8,128)} %broadcast_in_dim.12.refs_3_), custom_call_target="tpu_custom_call" | custom-call | tf_op jit(solution)/shard_map/pallas_call | solution.py:197
  15.9 2.1 %collective-permute-start = (f32[64,256]{1,0:T(8,128)}, f32[64,256]{1,0:T(8,128)S(1)}, u32[]{:S(2)}, u32[]{:S(2)}) collective-permute-start(f32[64,256]{1,0:T(8,128)} %shard_map.86), channel_id=1, source_target_pairs={{0,1},{1,2},{2,3},{3,0},{4,5},{5,6},{6,7},{7,4},{8,9},{9,10},{10,1... | collective-permute-start | bytes 196616 | tf_op jit(solution)/shard_map/ppermute | solution.py:28
  18.0 2.6 %collective-permute-start.1 = (f32[64,256]{1,0:T(8,128)}, f32[64,256]{1,0:T(8,128)S(1)}, u32[]{:S(2)}, u32[]{:S(2)}) collective-permute-start(f32[64,256]{1,0:T(8,128)} %shard_map.86), channel_id=1, source_target_pairs={{0,2},{1,3},{2,0},{3,1},{4,6},{5,7},{6,4},{7,5},{8,10},{9,11},{10,... | collective-permute-start | bytes 196616 | tf_op jit(solution)/shard_map/ppermute | solution.py:28
  20.6 1.1 collective-permute-start.2
  21.7 1.6 copy.11
  23.3 1.2 concatenate.6.refs_2_
  24.5 7.3 %shard_map.90 = f32[64,256]{1,0:T(8,128)} custom-call(s32[16]{0:T(128)} %get-tuple-element.8.refs_0_, f32[64,256]{1,0:T(8,128)} %constant_dynamic-slice_fusion.refs_1_, f32[5,256,256]{2,1,0:T(8,128)} %concatenate.6.refs_2_, f32[16,64,256]{2,1,0:T(8,128)} %broadcast_in_dim.12.refs_3_), custom_call_target="tpu_custom_call" | custom-call | tf_op jit(solution)/shard_map/pallas_call | solution.py:197
  31.8 0.4 collective-permute-start.4
  32.2 0.8 collective-permute-start.5
  33.0 1.3 multiply_add_fusion.refs_4_
  34.3 0.0 copy-done.6
  34.3 0.1 fusion.11
  34.4 0.0 copy-done.7
  34.4 0.0 copy-start.10
  34.4 1.8 fusion.1.refs_3_.refs_5_
  36.2 0.6 broadcast_in_dim.13.refs_1_
  36.8 7.0 %shard_map.87 = f32[16,256]{1,0:T(8,128)} custom-call(s32[16]{0:T(128)} %get-tuple-element.9.refs_0_, f32[16,256]{1,0:T(8,128)} %broadcast_in_dim.13.refs_1_, f32[8,256,256]{2,1,0:T(8,128)} %bitcast.43, f32[16,16,256]{2,1,0:T(8,128)} %fusion.1.refs_3_.refs_5_), custom_call_target="tpu_custom_call" | custom-call | tf_op jit(solution)/shard_map/pallas_call | solution.py:197
  43.8 0.0 copy-done.5
  43.8 0.0 collective-permute-done
  43.9 1.7 collective-permute-start.6
  45.6 0.0 collective-permute-done.1
  45.6 0.0 collective-permute-done.2
  45.6 0.0 copy-done.10
  45.6 0.2 fusion.16
  45.8 0.8 broadcast_select_fusion.matrix_ref
  46.6 1.3 add_select_fusion.records_ref
  47.9 49.3 %shard_map.88 = f32[16,256]{1,0:T(8,128)} custom-call(f32[256,256]{1,0:T(8,128)} %broadcast_select_fusion.matrix_ref, f32[16,256]{1,0:T(8,128)} %add_select_fusion.records_ref), custom_call_target="tpu_custom_call" | custom-call | tf_op jit(solution)/shard_map/pallas_call | solution.py:116
  97.2 3.7 %collective-permute-start.3 = (f32[16,256]{1,0:T(8,128)}, f32[16,256]{1,0:T(8,128)S(1)}, u32[]{:S(2)}, u32[]{:S(2)}) collective-permute-start(f32[16,256]{1,0:T(8,128)} %shard_map.88), channel_id=1, source_target_pairs={{0,4},{4,8},{8,12},{12,16},{16,20},{20,24},{24,28},{28,32},{32,36}... | collective-permute-start | bytes 49160 | tf_op jit(solution)/shard_map/ppermute | solution.py:17
  100.9 0.0 collective-permute-done.4
  101.0 0.0 copy-start.1
  101.0 0.0 collective-permute-done.5
  101.0 1.0 collective-permute-done.3
  102.0 0.6 broadcast_select_fusion.1.refs_2_
  102.6 7.9 %shard_map.89 = (f32[16,16,256]{2,1,0:T(8,128)}, f32[16,16,256]{2,1,0:T(8,128)}) custom-call(s32[16]{0:T(128)} %get-tuple-element.9.refs_0_, s32[16]{0:T(128)} %refs_1_.1, f32[16,256]{1,0:T(8,128)} %broadcast_select_fusion.1.refs_2_, f32[8,256,256]{2,1,0:T(8,128)} %bitcast.44, f32[4,256,256]{2,1,0:T(8,128)} %multiply_add_fusion.refs_4_, ...), custom_call_target="tpu_custom_call" | custom-call | tf_op jit(solution)/shard_map/pallas_call | solution.py:197
  110.5 0.8 slice_bitcast_fusion
  111.3 1.9 collective-permute-start.7
  113.2 0.0 collective-permute-done.6
  113.2 1.1 slice.6
  114.3 2.6 %collective-permute-done.7 = f32[16,256]{1,0:T(8,128)S(1)} collective-permute-done((f32[16,256]{1,0:T(8,128)S(1)}, f32[16,256]{1,0:T(8,128)S(1)}, u32[]{:S(2)}, u32[]{:S(2)}) %collective-permute-start.7) | collective-permute-done | bytes 16416 | tf_op jit(solution)/shard_map/ppermute | solution.py:17
  116.9 1.1 fusion.2
  118.0 0.7 sub.94.refs_3_
  118.7 6.8 %shard_map.91.records_ref = f32[16,256]{1,0:T(8,128)} custom-call(s32[16]{0:T(128)} %get-tuple-element.8.refs_0_, f32[16,256]{1,0:T(8,128)} %broadcast_in_dim.13.refs_1_, f32[5,256,256]{2,1,0:T(8,128)} %concatenate.6.refs_2_, f32[16,16,256]{2,1,0:T(8,128)} %sub.94.refs_3_), custom_call_target="tpu_custom_call" | custom-call | tf_op jit(solution)/shard_map/pallas_call | solution.py:197
  125.5 66.0 %shard_map.92 = f32[16,256]{1,0:T(8,128)} custom-call(f32[256,256]{1,0:T(8,128)} %copy-done.2, f32[16,256]{1,0:T(8,128)} %shard_map.91.records_ref), custom_call_target="tpu_custom_call" | custom-call | tf_op jit(solution)/shard_map/pallas_call | solution.py:116
  191.5 5.8 %collective-permute-start.8 = (f32[16,256]{1,0:T(8,128)}, f32[16,256]{1,0:T(8,128)S(1)}, u32[]{:S(2)}, u32[]{:S(2)}) collective-permute-start(f32[16,256]{1,0:T(8,128)} %shard_map.92), channel_id=1, source_target_pairs={{4,0},{8,4},{12,8},{16,12},{20,16},{24,20},{28,24},{32,28},{36,32}... | collective-permute-start | bytes 49160 | tf_op jit(solution)/shard_map/ppermute | solution.py:17
  197.4 1.0 collective-permute-done.8.refs_1_
  198.4 0.6 copy-done.8
  199.0 6.9 %shard_map.93 = f32[16,16,256]{2,1,0:T(8,128)} custom-call(s32[16]{0:T(128)} %get-tuple-element.8.refs_0_, f32[16,256]{1,0:T(8,128)} %copy-done.8, f32[5,256,256]{2,1,0:T(8,128)} %concatenate.6.refs_2_, f32[16,16,256]{2,1,0:T(8,128)} %sub.94.refs_3_), custom_call_target="tpu_custom_call" | custom-call | tf_op jit(solution)/shard_map/pallas_call | solution.py:197
  (23 shorter events, 0.2 us)
Async XLA Ops:
  0.6 2.5 %copy-start = (f32[4,256,256]{2,1,0:T(8,128)S(1)}, f32[4,256,256]{2,1,0:T(8,128)}, u32[]{:S(2)}) copy-start(f32[4,256,256]{2,1,0:T(8,128)} %param.11) | copy-start | bytes 3145732
  0.6 2.5 %copy-start.3 = (f32[4,256]{1,0:T(4,128)S(1)}, f32[4,256]{1,0:T(4,128)}, u32[]{:S(2)}) copy-start(f32[4,256]{1,0:T(4,128)} %param.10) | copy-start | bytes 12292
  4.7 2.1 %copy-start.9 = (s32[16]{0:T(128)S(1)}, s32[16]{0:T(128)}, u32[]{:S(2)}) copy-start(s32[16]{0:T(128)} %refs_1_.1) | copy-start | bytes 196
  4.7 2.1 %copy-start.11 = (s32[16]{0:T(128)S(1)}, s32[16]{0:T(128)}, u32[]{:S(2)}) copy-start(s32[16]{0:T(128)} %param.9) | copy-start | bytes 196
  15.9 28.0 %collective-permute-start = (f32[64,256]{1,0:T(8,128)}, f32[64,256]{1,0:T(8,128)S(1)}, u32[]{:S(2)}, u32[]{:S(2)}) collective-permute-start(f32[64,256]{1,0:T(8,128)} %shard_map.86), channel_id=1, source_target_pairs={{0,1},{1,2},{2,3},{3,0},{4,5},{5,6},{6,7},{7,4},{8,9},{9,10},{10,1... | collective-permute-start | bytes 196616 | tf_op jit(solution)/shard_map/ppermute | solution.py:28
  18.0 27.5 %collective-permute-start.1 = (f32[64,256]{1,0:T(8,128)}, f32[64,256]{1,0:T(8,128)S(1)}, u32[]{:S(2)}, u32[]{:S(2)}) collective-permute-start(f32[64,256]{1,0:T(8,128)} %shard_map.86), channel_id=1, source_target_pairs={{0,2},{1,3},{2,0},{3,1},{4,6},{5,7},{6,4},{7,5},{8,10},{9,11},{10,... | collective-permute-start | bytes 196616 | tf_op jit(solution)/shard_map/ppermute | solution.py:28
  20.6 25.0 %collective-permute-start.2 = (f32[64,256]{1,0:T(8,128)}, f32[64,256]{1,0:T(8,128)S(1)}, u32[]{:S(2)}, u32[]{:S(2)}) collective-permute-start(f32[64,256]{1,0:T(8,128)} %shard_map.86), channel_id=1, source_target_pairs={{0,3},{1,0},{2,1},{3,2},{4,7},{5,4},{6,5},{7,6},{8,11},{9,8},{10,9... | collective-permute-start | bytes 196616 | tf_op jit(solution)/shard_map/ppermute | solution.py:28
  24.4 9.8 %copy-start.6 = (f32[64,256]{1,0:T(8,128)S(1)}, f32[64,256]{1,0:T(8,128)}, u32[]{:S(2)}) copy-start(f32[64,256]{1,0:T(8,128)} %shard_map.86) | copy-start | bytes 196612
  24.5 10.0 %copy-start.7 = (f32[16,16,256]{2,1,0:T(8,128)S(1)}, f32[16,16,256]{2,1,0:T(8,128)}, u32[]{:S(2)}) copy-start(f32[16,16,256]{2,1,0:T(8,128)} %param.7) | copy-start | bytes 786436
  31.8 69.2 %collective-permute-start.4 = (f32[64,256]{1,0:T(8,128)}, f32[64,256]{1,0:T(8,128)S(1)}, u32[]{:S(2)}, u32[]{:S(2)}) collective-permute-start(f32[64,256]{1,0:T(8,128)} %shard_map.90), channel_id=1, source_target_pairs={{0,1},{1,2},{2,3},{3,0},{4,5},{5,6},{6,7},{7,4},{8,9},{9,10},{10,1... | collective-permute-start | bytes 196616 | tf_op jit(solution)/shard_map/ppermute | solution.py:28
  32.2 68.8 %collective-permute-start.5 = (f32[64,256]{1,0:T(8,128)}, f32[64,256]{1,0:T(8,128)S(1)}, u32[]{:S(2)}, u32[]{:S(2)}) collective-permute-start(f32[64,256]{1,0:T(8,128)} %shard_map.90), channel_id=1, source_target_pairs={{0,2},{1,3},{2,0},{3,1},{4,6},{5,7},{6,4},{7,5},{8,10},{9,11},{10,... | collective-permute-start | bytes 196616 | tf_op jit(solution)/shard_map/ppermute | solution.py:28
  34.4 9.4 %copy-start.5 = (f32[64,256]{1,0:T(8,128)S(1)}, f32[64,256]{1,0:T(8,128)}, u32[]{:S(2)}) copy-start(f32[64,256]{1,0:T(8,128)} %shard_map.90) | copy-start | bytes 196612
  34.4 11.2 %copy-start.10 = (f32[256]{0:T(256)S(1)}, f32[256]{0:T(256)}, u32[]{:S(2)}) copy-start(f32[256]{0:T(256)} %param.13) | copy-start | bytes 3076
  43.9 69.3 %collective-permute-start.6 = (f32[64,256]{1,0:T(8,128)S(1)}, f32[64,256]{1,0:T(8,128)S(1)}, u32[]{:S(2)}, u32[]{:S(2)}) collective-permute-start(f32[64,256]{1,0:T(8,128)S(1)} %copy-done.5), channel_id=1, source_target_pairs={{0,3},{1,0},{2,1},{3,2},{4,7},{5,4},{6,5},{7,6},{8,11},{9,8},{10,9... | collective-permute-start | bytes 196616 | tf_op jit(solution)/shard_map/ppermute | solution.py:28
  97.2 4.7 %collective-permute-start.3 = (f32[16,256]{1,0:T(8,128)}, f32[16,256]{1,0:T(8,128)S(1)}, u32[]{:S(2)}, u32[]{:S(2)}) collective-permute-start(f32[16,256]{1,0:T(8,128)} %shard_map.88), channel_id=1, source_target_pairs={{0,4},{4,8},{8,12},{12,16},{16,20},{20,24},{24,28},{28,32},{32,36}... | collective-permute-start | bytes 49160 | tf_op jit(solution)/shard_map/ppermute | solution.py:17
  101.0 15.9 %copy-start.1 = (f32[4,256,256]{2,1,0:T(8,128)S(1)}, f32[4,256,256]{2,1,0:T(8,128)}, u32[]{:S(2)}) copy-start(f32[4,256,256]{2,1,0:T(8,128)} %param.12) | copy-start | bytes 3145732
  110.5 7.4 %copy-start.4 = (f32[16,16,256]{2,1,0:T(8,128)S(1)}, f32[16,16,256]{2,1,0:T(8,128)}, u32[]{:S(2)}) copy-start(f32[16,16,256]{2,1,0:T(8,128)} %get-tuple-element.2) | copy-start | bytes 786436
  111.3 5.6 %collective-permute-start.7 = (f32[16,256]{1,0:T(8,128)S(1)}, f32[16,256]{1,0:T(8,128)S(1)}, u32[]{:S(2)}, u32[]{:S(2)}) collective-permute-start(f32[16,256]{1,0:T(8,128)S(1)} %slice_bitcast_fusion), channel_id=1, source_target_pairs={{4,0},{8,4},{12,8},{16,12},{20,16},{24,20},{28,24},{32,28},{36,32}... | collective-permute-start | bytes 49160 | tf_op jit(solution)/shard_map/ppermute | solution.py:17
  113.2 12.2 %copy-start.2 = (f32[256,256]{1,0:T(8,128)}, f32[256,256]{1,0:T(8,128)S(1)}, u32[]{:S(2)}) copy-start(f32[256,256]{1,0:T(8,128)S(1)} %constant_dynamic-update-slice_fusion.matrix_ref) | copy-start | bytes 786436
  191.5 6.9 %collective-permute-start.8 = (f32[16,256]{1,0:T(8,128)}, f32[16,256]{1,0:T(8,128)S(1)}, u32[]{:S(2)}, u32[]{:S(2)}) collective-permute-start(f32[16,256]{1,0:T(8,128)} %shard_map.92), channel_id=1, source_target_pairs={{4,0},{8,4},{12,8},{16,12},{20,16},{24,20},{28,24},{32,28},{36,32}... | collective-permute-start | bytes 49160 | tf_op jit(solution)/shard_map/ppermute | solution.py:17
  198.4 0.6 copy-start.8

commit v6 on v5

--- a/solution.py
+++ b/solution.py
@@ -35,12 +35,9 @@
     return jnp.dot(first_factor, second_factor, precision=lax.Precision.HIGHEST)
 
 
-def doubling_kernel(matrix_ref, records_ref, out_ref, maps, sums, map_in, sum_in, map_sems, sum_sems,
-                    *, axis, reverse):
-    peers, index = (lax.axis_size(axis), lax.axis_index(axis))
-    other = lax.axis_index("col")
-    rounds = max(1, (peers - 1).bit_length())
+def greet_partners(index, peers, other, rounds):
     barrier = pltpu.get_barrier_semaphore()
+    partners = 0
     for r in range(rounds):
         distance = 1 << r
         for partner, exists in ((index + distance, index + distance < peers),
@@ -49,13 +46,98 @@
             def _():
                 pl.semaphore_signal(barrier, inc=1, device_id=(partner, other),
                                     device_id_type=pl.DeviceIdType.MESH)
-    partners = 0
-    for r in range(rounds):
+
+            partners = partners + jnp.where(exists, 1, 0)
+    pl.semaphore_wait(barrier, partners)
+
+
+def exact_dot(first, second):
+    return jnp.dot(first, second, precision=lax.Precision.HIGHEST,
+                   preferred_element_type=jnp.float32)
+
+
+def maps_kernel(ahead_ref, behind_ref, ahead_out, behind_out, ahead_in, behind_in, sems, *, axis):
+    peers, index = (lax.axis_size(axis), lax.axis_index(axis))
+    other = lax.axis_index("col")
+    rounds = ahead_out.shape[0]
+    greet_partners(index, peers, other, max(1, rounds - 1))
+    ahead_out[0] = ahead_ref[...]
+    behind_out[0] = behind_ref[...]
+    for r in range(rounds - 1):
         distance = 1 << r
-        partners = partners + jnp.where(index + distance < peers, 1, 0)
-        partners = partners + jnp.where(index - distance >= 0, 1, 0)
-    pl.semaphore_wait(barrier, partners)
-
+        up, has_up = index + distance, index + distance < peers
+        down, has_down = index - distance, index - distance >= 0
+        own_ahead = ahead_ref if r == 0 else ahead_out.at[r]
+        own_behind = behind_ref if r == 0 else behind_out.at[r]
+        ahead_copy = pltpu.make_async_remote_copy(
+            src_ref=own_ahead, dst_ref=ahead_in.at[r], send_sem=sems.at[0, 0, r],
+            recv_sem=sems.at[0, 1, r], device_id=(up, other),
+            device_id_type=pl.DeviceIdType.MESH)
+        behind_copy = pltpu.make_async_remote_copy(
+            src_ref=own_behind, dst_ref=behind_in.at[r], send_sem=sems.at[1, 0, r],
+            recv_sem=sems.at[1, 1, r], device_id=(down, other),
+            device_id_type=pl.DeviceIdType.MESH)
+
+        @pl.when(has_up)
+        def _():
+            ahead_copy.start()
+
+        @pl.when(has_down)
+        def _():
+            behind_copy.start()
+
+        @pl.when(has_down)
+        def _():
+            ahead_copy.wait_recv()
+            ahead_out[r + 1] = exact_dot(ahead_in[r], own_ahead[...])
+
+        @pl.when(jnp.logical_not(has_down))
+        def _():
+            ahead_out[r + 1] = own_ahead[...]
+
+        @pl.when(has_up)
+        def _():
+            behind_copy.wait_recv()
+            behind_out[r + 1] = exact_dot(behind_in[r], own_behind[...])
+
+        @pl.when(jnp.logical_not(has_up))
+        def _():
+            behind_out[r + 1] = own_behind[...]
+
+        @pl.when(has_up)
+        def _():
+            ahead_copy.wait_send()
+
+        @pl.when(has_down)
+        def _():
+            behind_copy.wait_send()
+
+
+def doubling_maps(ahead, behind, axis, collective_id):
+    peers = lax.axis_size(axis)
+    rounds = max(1, (peers - 1).bit_length())
+    states = ahead.shape[0]
+    vmem = pl.BlockSpec(memory_space=pltpu.VMEM)
+    stack = jax.ShapeDtypeStruct((rounds, states, states), jnp.float32)
+    return pl.pallas_call(
+        functools.partial(maps_kernel, axis=axis),
+        out_shape=(stack, stack),
+        in_specs=[vmem, vmem],
+        out_specs=(vmem, vmem),
+        scratch_shapes=[
+            pltpu.VMEM((max(1, rounds - 1), states, states), jnp.float32),
+            pltpu.VMEM((max(1, rounds - 1), states, states), jnp.float32),
+            pltpu.SemaphoreType.DMA((2, 2, max(1, rounds - 1))),
+        ],
+        compiler_params=pltpu.CompilerParams(collective_id=collective_id, has_side_effects=True),
+    )(ahead, behind)
+
+
+def records_kernel(maps_ref, records_ref, out_ref, sums, sum_in, sems, *, axis, reverse):
+    peers, index = (lax.axis_size(axis), lax.axis_index(axis))
+    other = lax.axis_index("col")
+    rounds = maps_ref.shape[0]
+    greet_partners(index, peers, other, rounds)
     for r in range(rounds):
         distance = 1 << r
         if reverse:
@@ -64,70 +146,47 @@
         else:
             target, sends = index + distance, index + distance < peers
             receives = index - distance >= 0
-        own_map = matrix_ref if r == 0 else maps.at[r]
         own_sum = records_ref if r == 0 else sums.at[r]
         sum_copy = pltpu.make_async_remote_copy(
-            src_ref=own_sum, dst_ref=sum_in.at[r], send_sem=sum_sems.at[0, r],
-            recv_sem=sum_sems.at[1, r], device_id=(target, other),
+            src_ref=own_sum, dst_ref=sum_in.at[r], send_sem=sems.at[0, r],
+            recv_sem=sems.at[1, r], device_id=(target, other),
             device_id_type=pl.DeviceIdType.MESH)
-        map_copy = None
-        if r + 1 < rounds:
-            map_copy = pltpu.make_async_remote_copy(
-                src_ref=own_map, dst_ref=map_in.at[r], send_sem=map_sems.at[0, r],
-                recv_sem=map_sems.at[1, r], device_id=(target, other),
-                device_id_type=pl.DeviceIdType.MESH)
 
         @pl.when(sends)
         def _():
             sum_copy.start()
-            if map_copy is not None:
-                map_copy.start()
 
         @pl.when(receives)
         def _():
             sum_copy.wait_recv()
-            sums[r + 1] = jnp.dot(sum_in[r], own_map[...], precision=lax.Precision.HIGHEST,
-                                  preferred_element_type=jnp.float32) + own_sum[...]
-            if map_copy is not None:
-                map_copy.wait_recv()
-                maps[r + 1] = jnp.dot(map_in[r], own_map[...], precision=lax.Precision.HIGHEST,
-                                      preferred_element_type=jnp.float32)
+            sums[r + 1] = exact_dot(sum_in[r], maps_ref[r]) + own_sum[...]
 
         @pl.when(jnp.logical_not(receives))
         def _():
             sums[r + 1] = own_sum[...]
-            if map_copy is not None:
-                maps[r + 1] = own_map[...]
 
         @pl.when(sends)
         def _():
             sum_copy.wait_send()
-            if map_copy is not None:
-                map_copy.wait_send()
 
     out_ref[...] = sums[rounds]
 
 
-def doubling_scan(matrix, records, axis, reverse, collective_id):
-    peers = lax.axis_size(axis)
-    rounds = max(1, (peers - 1).bit_length())
-    states = matrix.shape[0]
+def doubling_records(maps, records, axis, reverse, collective_id):
+    rounds = maps.shape[0]
     vmem = pl.BlockSpec(memory_space=pltpu.VMEM)
     return pl.pallas_call(
-        functools.partial(doubling_kernel, axis=axis, reverse=reverse),
+        functools.partial(records_kernel, axis=axis, reverse=reverse),
         out_shape=jax.ShapeDtypeStruct(records.shape, jnp.float32),
         in_specs=[vmem, vmem],
         out_specs=vmem,
         scratch_shapes=[
-            pltpu.VMEM((rounds, states, states), jnp.float32),
             pltpu.VMEM((rounds + 1,) + records.shape, jnp.float32),
-            pltpu.VMEM((max(1, rounds - 1), states, states), jnp.float32),
             pltpu.VMEM((rounds,) + records.shape, jnp.float32),
-            pltpu.SemaphoreType.DMA((2, max(1, rounds - 1))),
             pltpu.SemaphoreType.DMA((2, rounds)),
         ],
         compiler_params=pltpu.CompilerParams(collective_id=collective_id, has_side_effects=True),
-    )(matrix, records)
+    )(maps, records)
 
 
 def diffusion_matrices(diffusivity, side_cells):
@@ -264,6 +323,9 @@
         backward_pick, own_identity, backward_table, blank_columns, True, False
     )
     whole_back = gathered_rows(backward_rows, "col")
+    forward_maps, backward_maps = doubling_maps(
+        jnp.where(first_block, jnp.zeros_like(whole_matrix), whole_matrix), whole_back, "tm", 0
+    )
 
     block_records = recurrence(
         forward_pick, blank_records, forward_table, measured, False, False
@@ -273,8 +335,7 @@
         accurate_matmul_result(initial_mean[None, :], whole_matrix) + block_records,
         block_records,
     )
-    folded_matrix = jnp.where(first_block, jnp.zeros_like(whole_matrix), whole_matrix)
-    ending_records = doubling_scan(folded_matrix, folded_records, "tm", False, 0)
+    ending_records = doubling_records(forward_maps, folded_records, "tm", False, 1)
     start_rows = jnp.where(
         first_block,
         jnp.broadcast_to(initial_mean[None, :], (record_rows, states)),
@@ -297,7 +358,7 @@
     shift = filtered - per_band_products(next_predicted, backward, live_weights)
 
     back_records = recurrence(backward_pick, blank_records, backward_table, shift, True, False)
-    opening_records = doubling_scan(whole_back, back_records, "tm", True, 1)
+    opening_records = doubling_records(backward_maps, back_records, "tm", True, 2)
     after_records = passed_along(opening_records, "tm", -1)
 
     smoothed = recurrence(backward_pick, after_records, backward_table, shift, True, True)

time: 208 us -> 214 us (1.029)
  starting transfers between devices: 20.1 us -> 23.9 us
    ppermute x3, starting transfers between devices: 11.4 us -> 15.2 us  [passed_along(): return lax.ppermute(block, axis, route)]
    pallas_call x2 -> x3, Pallas kernels: 115 us -> 117 us  [the longest x1 60.5 us: doubling_maps(): pl.pallas_call(functools.partial(maps_kernel, axis=axis), out_shape=(stac...]
  transfers between devices with their start and end apart: 9 -> 9, of which waited for: 3 -> 3; matrix products, arithmetic and copies ran while one was open for 6% -> 4% of each run, Pallas kernels for 35% -> 7%
where the time goes in v6:
time: 214 us
  Pallas kernels  161 us (75%)
  starting transfers between devices  23.9 us (11%)
  local copies, waits for them, and re-layouts  9.81 us (5%)
  other arithmetic  7.29 us (3%)
  waiting for transfers between devices  6.45 us (3%)
  matrix products  4.42 us (2%)
    pallas_call x1, Pallas kernels, doubling_maps(): pl.pallas_call(functools.partial(maps_kernel, axis=axis), out_shape=(stac...  60.5 us
    pallas_call x2, Pallas kernels, doubling_records(): pl.pallas_call(functools.partial(records_kernel, axis=axis, reverse=rever...  57 us
    pallas_call x6, Pallas kernels, recurrence(): pl.pallas_call(functools.partial(recurrence_kernel, steps=steps, reverse=...  43.2 us
    ppermute x3, starting transfers between devices, passed_along(): return lax.ppermute(block, axis, route)  15.2 us
    ppermute x6, starting transfers between devices, gathered_rows(): lax.ppermute(part, axis, [(i, (i + shift) % peers) for i in range(peers)])  8.68 us
    ppermute x3, waiting for transfers between devices, passed_along(): return lax.ppermute(block, axis, route)  5.4 us
  transfers between devices with their start and end apart: 9, of which 3 were waited for; matrix products, arithmetic and copies ran while one was open for 4% of the time, Pallas kernels for 7%

profile of v6, /device:TPU:1, one launch (start us, length us, event | category | flops | bytes accessed | tf_op | source)
XLA Modules:
  0.0 213.5 jit_solution(17285644732634312443)
XLA Ops:
  0.6 0.0 copy-start
  0.6 0.0 copy-start.3
  0.7 0.2 fusion.9
  0.9 1.2 fusion.5
  2.1 0.6 constant_dynamic-slice_fusion.refs_1_
  2.7 1.1 multiply_add_fusion.1
  3.8 0.0 copy-done
  3.8 0.0 copy-done.3
  3.8 1.4 fusion
  5.2 0.1 pad_maximum_fusion
  5.3 0.0 copy-start.10
  5.4 0.0 copy-start.12
  5.4 1.5 copy.10
  6.9 0.0 copy-done.10
  6.9 0.0 copy-done.12
  6.9 0.6 fusion.16
  7.5 1.1 broadcast_in_dim.12.refs_3_
  8.5 7.5 %shard_map.86 = f32[64,256]{1,0:T(8,128)} custom-call(s32[16]{0:T(128)} %get-tuple-element.13.refs_0_, f32[64,256]{1,0:T(8,128)} %constant_dynamic-slice_fusion.refs_1_, f32[8,256,256]{2,1,0:T(8,128)} %bitcast.42, f32[16,64,256]{2,1,0:T(8,128)} %broadcast_in_dim.12.refs_3_), custom_call_target="tpu_custom_call" | custom-call | tf_op jit(solution)/shard_map/pallas_call | solution.py:256
  16.0 2.1 collective-permute-start
  18.1 2.6 %collective-permute-start.1 = (f32[64,256]{1,0:T(8,128)}, f32[64,256]{1,0:T(8,128)S(1)}, u32[]{:S(2)}, u32[]{:S(2)}) collective-permute-start(f32[64,256]{1,0:T(8,128)} %shard_map.86), channel_id=1, source_target_pairs={{0,2},{1,3},{2,0},{3,1},{4,6},{5,7},{6,4},{7,5},{8,10},{9,11},{10,... | collective-permute-start | bytes 196616 | tf_op jit(solution)/shard_map/ppermute | solution.py:28
  20.8 1.1 collective-permute-start.2
  21.8 1.6 copy.11
  23.4 0.0 copy-start.6
  23.4 0.0 copy-start.7
  23.4 1.2 concatenate.6.refs_2_
  24.6 7.3 %shard_map.87 = f32[64,256]{1,0:T(8,128)} custom-call(s32[16]{0:T(128)} %get-tuple-element.14.refs_0_, f32[64,256]{1,0:T(8,128)} %constant_dynamic-slice_fusion.refs_1_, f32[5,256,256]{2,1,0:T(8,128)} %concatenate.6.refs_2_, f32[16,64,256]{2,1,0:T(8,128)} %broadcast_in_dim.12.refs_3_), custom_call_target="tpu_custom_call" | custom-call | tf_op jit(solution)/shard_map/pallas_call | solution.py:256
  31.9 0.4 collective-permute-start.3
  32.3 0.8 collective-permute-start.4
  33.1 0.0 copy-done.6
  33.2 0.1 fusion.11
  33.2 1.8 fusion.1.refs_3_.refs_5_
  35.0 0.6 broadcast_in_dim.14.refs_1_
  35.6 7.0 %shard_map.89 = f32[16,256]{1,0:T(8,128)} custom-call(s32[16]{0:T(128)} %get-tuple-element.13.refs_0_, f32[16,256]{1,0:T(8,128)} %broadcast_in_dim.14.refs_1_, f32[8,256,256]{2,1,0:T(8,128)} %bitcast.43, f32[16,16,256]{2,1,0:T(8,128)} %fusion.1.refs_3_.refs_5_), custom_call_target="tpu_custom_call" | custom-call | tf_op jit(solution)/shard_map/pallas_call | solution.py:256
  42.7 0.0 collective-permute-done
  42.7 1.7 collective-permute-start.5
  44.4 0.0 collective-permute-done.1
  44.4 0.0 collective-permute-done.2
  44.4 0.7 broadcast_select_fusion.ahead_ref
  45.2 0.2 fusion.17
  45.4 0.0 collective-permute-done.3
  45.4 0.0 collective-permute-done.4
  45.5 1.0 collective-permute-done.5
  46.5 0.0 copy-start.2
  46.5 0.7 copy-done.2
  47.2 60.5 %shard_map.88 = (f32[6,256,256]{2,1,0:T(8,128)}, f32[6,256,256]{2,1,0:T(8,128)}) custom-call(f32[256,256]{1,0:T(8,128)} %broadcast_select_fusion.ahead_ref, f32[256,256]{1,0:T(8,128)} %copy-done.2), custom_call_target="tpu_custom_call" | custom-call | tf_op jit(solution)/shard_map/pallas_call | solution.py:122
  107.7 0.6 add_select_fusion.records_ref
  108.3 22.8 %shard_map.90 = f32[16,256]{1,0:T(8,128)} custom-call(f32[6,256,256]{2,1,0:T(8,128)} %get-tuple-element.6.maps_ref, f32[16,256]{1,0:T(8,128)} %add_select_fusion.records_ref), custom_call_target="tpu_custom_call" | custom-call | tf_op jit(solution)/shard_map/pallas_call | solution.py:178
  131.1 9.0 %collective-permute-start.6 = (f32[16,256]{1,0:T(8,128)}, f32[16,256]{1,0:T(8,128)S(1)}, u32[]{:S(2)}, u32[]{:S(2)}) collective-permute-start(f32[16,256]{1,0:T(8,128)} %shard_map.90), channel_id=1, source_target_pairs={{0,4},{4,8},{8,12},{12,16},{16,20},{20,24},{24,28},{28,32},{32,36}... | collective-permute-start | bytes 49160 | tf_op jit(solution)/shard_map/ppermute | solution.py:17
  140.1 1.3 multiply_add_fusion.refs_4_
  141.5 0.0 collective-permute-done.6
  141.5 0.6 broadcast_select_fusion.1.refs_2_
  142.1 7.9 %shard_map.91 = (f32[16,16,256]{2,1,0:T(8,128)}, f32[16,16,256]{2,1,0:T(8,128)}) custom-call(s32[16]{0:T(128)} %get-tuple-element.13.refs_0_, s32[16]{0:T(128)} %refs_1_.1, f32[16,256]{1,0:T(8,128)} %broadcast_select_fusion.1.refs_2_, f32[8,256,256]{2,1,0:T(8,128)} %bitcast.44, f32[4,256,256]{2,1,0:T(8,128)} %multiply_add_fusion.refs_4_, ...), custom_call_target="tpu_custom_call" | custom-call | tf_op jit(solution)/shard_map/pallas_call | solution.py:256
  150.0 0.8 slice_bitcast_fusion
  150.7 1.9 collective-permute-start.7
  152.7 1.0 slice.6
  153.6 2.5 %collective-permute-done.7 = f32[16,256]{1,0:T(8,128)S(1)} collective-permute-done((f32[16,256]{1,0:T(8,128)S(1)}, f32[16,256]{1,0:T(8,128)S(1)}, u32[]{:S(2)}, u32[]{:S(2)}) %collective-permute-start.7) | collective-permute-done | bytes 16416 | tf_op jit(solution)/shard_map/ppermute | solution.py:17
  156.1 1.1 fusion.2
  157.2 0.7 sub.94.refs_3_
  157.9 6.8 %shard_map.92.records_ref = f32[16,256]{1,0:T(8,128)} custom-call(s32[16]{0:T(128)} %get-tuple-element.14.refs_0_, f32[16,256]{1,0:T(8,128)} %broadcast_in_dim.14.refs_1_, f32[5,256,256]{2,1,0:T(8,128)} %concatenate.6.refs_2_, f32[16,16,256]{2,1,0:T(8,128)} %sub.94.refs_3_), custom_call_target="tpu_custom_call" | custom-call | tf_op jit(solution)/shard_map/pallas_call | solution.py:256
  164.7 34.2 %shard_map.93 = f32[16,256]{1,0:T(8,128)} custom-call(f32[6,256,256]{2,1,0:T(8,128)} %get-tuple-element.8.maps_ref, f32[16,256]{1,0:T(8,128)} %shard_map.92.records_ref), custom_call_target="tpu_custom_call" | custom-call | tf_op jit(solution)/shard_map/pallas_call | solution.py:178
  198.9 4.3 %collective-permute-start.8 = (f32[16,256]{1,0:T(8,128)}, f32[16,256]{1,0:T(8,128)S(1)}, u32[]{:S(2)}, u32[]{:S(2)}) collective-permute-start(f32[16,256]{1,0:T(8,128)} %shard_map.93), channel_id=1, source_target_pairs={{4,0},{8,4},{12,8},{16,12},{20,16},{24,20},{28,24},{32,28},{36,32}... | collective-permute-start | bytes 49160 | tf_op jit(solution)/shard_map/ppermute | solution.py:17
  203.1 2.9 %collective-permute-done.8.refs_1_ = f32[16,256]{1,0:T(8,128)S(1)} collective-permute-done((f32[16,256]{1,0:T(8,128)}, f32[16,256]{1,0:T(8,128)S(1)}, u32[]{:S(2)}, u32[]{:S(2)}) %collective-permute-start.8) | collective-permute-done | bytes 16416 | tf_op jit(solution)/shard_map/ppermute | solution.py:17
  206.1 0.6 copy-done.9
  206.7 6.9 %shard_map.94 = f32[16,16,256]{2,1,0:T(8,128)} custom-call(s32[16]{0:T(128)} %get-tuple-element.14.refs_0_, f32[16,256]{1,0:T(8,128)} %copy-done.9, f32[5,256,256]{2,1,0:T(8,128)} %concatenate.6.refs_2_, f32[16,16,256]{2,1,0:T(8,128)} %sub.94.refs_3_), custom_call_target="tpu_custom_call" | custom-call | tf_op jit(solution)/shard_map/pallas_call | solution.py:256
  (26 shorter events, 0.2 us)
Async XLA Ops:
  0.6 3.2 %copy-start = (f32[4,256,256]{2,1,0:T(8,128)S(1)}, f32[4,256,256]{2,1,0:T(8,128)}, u32[]{:S(2)}) copy-start(f32[4,256,256]{2,1,0:T(8,128)} %param.11) | copy-start | bytes 3145732
  0.6 3.2 %copy-start.3 = (f32[4,256]{1,0:T(4,128)S(1)}, f32[4,256]{1,0:T(4,128)}, u32[]{:S(2)}) copy-start(f32[4,256]{1,0:T(4,128)} %param.10) | copy-start | bytes 12292
  5.3 1.5 copy-start.10
  5.4 1.5 copy-start.12
  16.0 26.7 %collective-permute-start = (f32[64,256]{1,0:T(8,128)}, f32[64,256]{1,0:T(8,128)S(1)}, u32[]{:S(2)}, u32[]{:S(2)}) collective-permute-start(f32[64,256]{1,0:T(8,128)} %shard_map.86), channel_id=1, source_target_pairs={{0,1},{1,2},{2,3},{3,0},{4,5},{5,6},{6,7},{7,4},{8,9},{9,10},{10,1... | collective-permute-start | bytes 196616 | tf_op jit(solution)/shard_map/ppermute | solution.py:28
  18.1 26.2 %collective-permute-start.1 = (f32[64,256]{1,0:T(8,128)}, f32[64,256]{1,0:T(8,128)S(1)}, u32[]{:S(2)}, u32[]{:S(2)}) collective-permute-start(f32[64,256]{1,0:T(8,128)} %shard_map.86), channel_id=1, source_target_pairs={{0,2},{1,3},{2,0},{3,1},{4,6},{5,7},{6,4},{7,5},{8,10},{9,11},{10,... | collective-permute-start | bytes 196616 | tf_op jit(solution)/shard_map/ppermute | solution.py:28
  20.8 23.6 %collective-permute-start.2 = (f32[64,256]{1,0:T(8,128)}, f32[64,256]{1,0:T(8,128)S(1)}, u32[]{:S(2)}, u32[]{:S(2)}) collective-permute-start(f32[64,256]{1,0:T(8,128)} %shard_map.86), channel_id=1, source_target_pairs={{0,3},{1,0},{2,1},{3,2},{4,7},{5,4},{6,5},{7,6},{8,11},{9,8},{10,9... | collective-permute-start | bytes 196616 | tf_op jit(solution)/shard_map/ppermute | solution.py:28
  23.4 9.7 %copy-start.6 = (f32[64,256]{1,0:T(8,128)S(1)}, f32[64,256]{1,0:T(8,128)}, u32[]{:S(2)}) copy-start(f32[64,256]{1,0:T(8,128)} %shard_map.86) | copy-start | bytes 196612
  23.4 9.8 %copy-start.7 = (f32[16,16,256]{2,1,0:T(8,128)S(1)}, f32[16,16,256]{2,1,0:T(8,128)}, u32[]{:S(2)}) copy-start(f32[16,16,256]{2,1,0:T(8,128)} %param.7) | copy-start | bytes 786436
  31.9 13.5 %collective-permute-start.3 = (f32[64,256]{1,0:T(8,128)}, f32[64,256]{1,0:T(8,128)S(1)}, u32[]{:S(2)}, u32[]{:S(2)}) collective-permute-start(f32[64,256]{1,0:T(8,128)} %shard_map.87), channel_id=1, source_target_pairs={{0,1},{1,2},{2,3},{3,0},{4,5},{5,6},{6,7},{7,4},{8,9},{9,10},{10,1... | collective-permute-start | bytes 196616 | tf_op jit(solution)/shard_map/ppermute | solution.py:28
  32.3 13.1 %collective-permute-start.4 = (f32[64,256]{1,0:T(8,128)}, f32[64,256]{1,0:T(8,128)S(1)}, u32[]{:S(2)}, u32[]{:S(2)}) collective-permute-start(f32[64,256]{1,0:T(8,128)} %shard_map.87), channel_id=1, source_target_pairs={{0,2},{1,3},{2,0},{3,1},{4,6},{5,7},{6,4},{7,5},{8,10},{9,11},{10,... | collective-permute-start | bytes 196616 | tf_op jit(solution)/shard_map/ppermute | solution.py:28
  33.2 9.4 %copy-start.5 = (f32[64,256]{1,0:T(8,128)S(1)}, f32[64,256]{1,0:T(8,128)}, u32[]{:S(2)}) copy-start(f32[64,256]{1,0:T(8,128)} %shard_map.87) | copy-start | bytes 196612
  35.0 10.1 %copy-start.11 = (f32[256]{0:T(256)S(1)}, f32[256]{0:T(256)}, u32[]{:S(2)}) copy-start(f32[256]{0:T(256)} %param.13) | copy-start | bytes 3076
  42.6 65.1 %copy-start.8 = (f32[16,256]{1,0:T(8,128)S(1)}, f32[16,256]{1,0:T(8,128)}, u32[]{:S(2)}) copy-start(f32[16,256]{1,0:T(8,128)} %shard_map.89) | copy-start | bytes 49156
  42.7 3.8 %collective-permute-start.5 = (f32[64,256]{1,0:T(8,128)S(1)}, f32[64,256]{1,0:T(8,128)S(1)}, u32[]{:S(2)}, u32[]{:S(2)}) collective-permute-start(f32[64,256]{1,0:T(8,128)S(1)} %copy-done.5), channel_id=1, source_target_pairs={{0,3},{1,0},{2,1},{3,2},{4,7},{5,4},{6,5},{7,6},{8,11},{9,8},{10,9... | collective-permute-start | bytes 196616 | tf_op jit(solution)/shard_map/ppermute | solution.py:28
  46.5 0.7 copy-start.2
  131.1 10.4 %collective-permute-start.6 = (f32[16,256]{1,0:T(8,128)}, f32[16,256]{1,0:T(8,128)S(1)}, u32[]{:S(2)}, u32[]{:S(2)}) collective-permute-start(f32[16,256]{1,0:T(8,128)} %shard_map.90), channel_id=1, source_target_pairs={{0,4},{4,8},{8,12},{12,16},{16,20},{20,24},{24,28},{28,32},{32,36}... | collective-permute-start | bytes 49160 | tf_op jit(solution)/shard_map/ppermute | solution.py:17
  141.5 14.6 %copy-start.1 = (f32[4,256,256]{2,1,0:T(8,128)S(1)}, f32[4,256,256]{2,1,0:T(8,128)}, u32[]{:S(2)}) copy-start(f32[4,256,256]{2,1,0:T(8,128)} %param.12) | copy-start | bytes 3145732
  150.0 7.2 %copy-start.4 = (f32[16,16,256]{2,1,0:T(8,128)S(1)}, f32[16,16,256]{2,1,0:T(8,128)}, u32[]{:S(2)}) copy-start(f32[16,16,256]{2,1,0:T(8,128)} %get-tuple-element.4) | copy-start | bytes 786436
  150.7 5.3 %collective-permute-start.7 = (f32[16,256]{1,0:T(8,128)S(1)}, f32[16,256]{1,0:T(8,128)S(1)}, u32[]{:S(2)}, u32[]{:S(2)}) collective-permute-start(f32[16,256]{1,0:T(8,128)S(1)} %slice_bitcast_fusion), channel_id=1, source_target_pairs={{4,0},{8,4},{12,8},{16,12},{20,16},{24,20},{28,24},{32,28},{36,32}... | collective-permute-start | bytes 49160 | tf_op jit(solution)/shard_map/ppermute | solution.py:17
  198.9 7.2 %collective-permute-start.8 = (f32[16,256]{1,0:T(8,128)}, f32[16,256]{1,0:T(8,128)S(1)}, u32[]{:S(2)}, u32[]{:S(2)}) collective-permute-start(f32[16,256]{1,0:T(8,128)} %shard_map.93), channel_id=1, source_target_pairs={{4,0},{8,4},{12,8},{16,12},{20,16},{24,20},{28,24},{32,28},{36,32}... | collective-permute-start | bytes 49160 | tf_op jit(solution)/shard_map/ppermute | solution.py:17
  206.1 0.6 copy-start.9

commit v7 on v6

--- a/solution.py
+++ b/solution.py
@@ -56,18 +56,44 @@
                    preferred_element_type=jnp.float32)
 
 
-def maps_kernel(ahead_ref, behind_ref, ahead_out, behind_out, ahead_in, behind_in, sems, *, axis):
+def maps_kernel(ahead_ref, behind_ref, records_ref, ahead_out, behind_out, records_out,
+                ahead_in, behind_in, sums, sum_in, sems, sum_sems, *, axis):
     peers, index = (lax.axis_size(axis), lax.axis_index(axis))
     other = lax.axis_index("col")
     rounds = ahead_out.shape[0]
-    greet_partners(index, peers, other, max(1, rounds - 1))
+    greet_partners(index, peers, other, rounds)
     ahead_out[0] = ahead_ref[...]
     behind_out[0] = behind_ref[...]
-    for r in range(rounds - 1):
+    for r in range(rounds):
         distance = 1 << r
         up, has_up = index + distance, index + distance < peers
         down, has_down = index - distance, index - distance >= 0
         own_ahead = ahead_ref if r == 0 else ahead_out.at[r]
+        own_sum = records_ref if r == 0 else sums.at[r]
+        sum_copy = pltpu.make_async_remote_copy(
+            src_ref=own_sum, dst_ref=sum_in.at[r], send_sem=sum_sems.at[0, r],
+            recv_sem=sum_sems.at[1, r], device_id=(up, other),
+            device_id_type=pl.DeviceIdType.MESH)
+
+        @pl.when(has_up)
+        def _():
+            sum_copy.start()
+
+        if r == rounds - 1:
+            @pl.when(has_down)
+            def _():
+                sum_copy.wait_recv()
+                sums[r + 1] = exact_dot(sum_in[r], own_ahead[...]) + own_sum[...]
+
+            @pl.when(jnp.logical_not(has_down))
+            def _():
+                sums[r + 1] = own_sum[...]
+
+            @pl.when(has_up)
+            def _():
+                sum_copy.wait_send()
+
+            break
         own_behind = behind_ref if r == 0 else behind_out.at[r]
         ahead_copy = pltpu.make_async_remote_copy(
             src_ref=own_ahead, dst_ref=ahead_in.at[r], send_sem=sems.at[0, 0, r],
@@ -88,6 +114,15 @@
 
         @pl.when(has_down)
         def _():
+            sum_copy.wait_recv()
+            sums[r + 1] = exact_dot(sum_in[r], own_ahead[...]) + own_sum[...]
+
+        @pl.when(jnp.logical_not(has_down))
+        def _():
+            sums[r + 1] = own_sum[...]
+
+        @pl.when(has_down)
+        def _():
             ahead_copy.wait_recv()
             ahead_out[r + 1] = exact_dot(ahead_in[r], own_ahead[...])
 
@@ -107,13 +142,16 @@
         @pl.when(has_up)
         def _():
             ahead_copy.wait_send()
+            sum_copy.wait_send()
 
         @pl.when(has_down)
         def _():
             behind_copy.wait_send()
 
-
-def doubling_maps(ahead, behind, axis, collective_id):
+    records_out[...] = sums[rounds]
+
+
+def doubling_maps(ahead, behind, records, axis, collective_id):
     peers = lax.axis_size(axis)
     rounds = max(1, (peers - 1).bit_length())
     states = ahead.shape[0]
@@ -121,16 +159,19 @@
     stack = jax.ShapeDtypeStruct((rounds, states, states), jnp.float32)
     return pl.pallas_call(
         functools.partial(maps_kernel, axis=axis),
-        out_shape=(stack, stack),
-        in_specs=[vmem, vmem],
-        out_specs=(vmem, vmem),
+        out_shape=(stack, stack, jax.ShapeDtypeStruct(records.shape, jnp.float32)),
+        in_specs=[vmem, vmem, vmem],
+        out_specs=(vmem, vmem, vmem),
         scratch_shapes=[
             pltpu.VMEM((max(1, rounds - 1), states, states), jnp.float32),
             pltpu.VMEM((max(1, rounds - 1), states, states), jnp.float32),
+            pltpu.VMEM((rounds + 1,) + records.shape, jnp.float32),
+            pltpu.VMEM((rounds,) + records.shape, jnp.float32),
             pltpu.SemaphoreType.DMA((2, 2, max(1, rounds - 1))),
+            pltpu.SemaphoreType.DMA((2, rounds)),
         ],
         compiler_params=pltpu.CompilerParams(collective_id=collective_id, has_side_effects=True),
-    )(ahead, behind)
+    )(ahead, behind, records)
 
 
 def records_kernel(maps_ref, records_ref, out_ref, sums, sum_in, sems, *, axis, reverse):
@@ -323,10 +364,6 @@
         backward_pick, own_identity, backward_table, blank_columns, True, False
     )
     whole_back = gathered_rows(backward_rows, "col")
-    forward_maps, backward_maps = doubling_maps(
-        jnp.where(first_block, jnp.zeros_like(whole_matrix), whole_matrix), whole_back, "tm", 0
-    )
-
     block_records = recurrence(
         forward_pick, blank_records, forward_table, measured, False, False
     )
@@ -335,7 +372,13 @@
         accurate_matmul_result(initial_mean[None, :], whole_matrix) + block_records,
         block_records,
     )
-    ending_records = doubling_records(forward_maps, folded_records, "tm", False, 1)
+    _, backward_maps, ending_records = doubling_maps(
+        jnp.where(first_block, jnp.zeros_like(whole_matrix), whole_matrix),
+        whole_back,
+        folded_records,
+        "tm",
+        0,
+    )
     start_rows = jnp.where(
         first_block,
         jnp.broadcast_to(initial_mean[None, :], (record_rows, states)),
@@ -358,7 +401,7 @@
     shift = filtered - per_band_products(next_predicted, backward, live_weights)
 
     back_records = recurrence(backward_pick, blank_records, backward_table, shift, True, False)
-    opening_records = doubling_records(backward_maps, back_records, "tm", True, 2)
+    opening_records = doubling_records(backward_maps, back_records, "tm", True, 1)
     after_records = passed_along(opening_records, "tm", -1)
 
     smoothed = recurrence(backward_pick, after_records, backward_table, shift, True, True)

time: 214 us -> 194 us (0.907)
  Pallas kernels: 161 us -> 142 us
    pallas_call x2 -> x1, Pallas kernels: 57 us -> 24 us  [doubling_records(): pl.pallas_call(functools.partial(records_kernel, axis=axis, reverse=rever...]
    pallas_call x1, Pallas kernels: 60.5 us -> 74.9 us  [doubling_maps(): pl.pallas_call(functools.partial(maps_kernel, axis=axis), out_shape=(stac...]
  transfers between devices with their start and end apart: 9 -> 9, of which waited for: 3 -> 2; matrix products, arithmetic and copies ran while one was open for 4% -> 5% of each run, Pallas kernels for 7% -> 7%
where the time goes in v7:
time: 194 us; the launch traced here: 193 us
  Pallas kernels  142 us (73%)
  starting transfers between devices  22.8 us (12%)
  local copies, waits for them, and re-layouts  9.8 us (5%)
  other arithmetic  8.02 us (4%)
  waiting for transfers between devices  4.86 us (3%)
  matrix products  4.43 us (2%)
    pallas_call x1, Pallas kernels, doubling_maps(): pl.pallas_call(functools.partial(maps_kernel, axis=axis), out_shape=(stac...  74.9 us
    pallas_call x6, Pallas kernels, recurrence(): pl.pallas_call(functools.partial(recurrence_kernel, steps=steps, reverse=...  43.2 us
    pallas_call x1, Pallas kernels, doubling_records(): pl.pallas_call(functools.partial(records_kernel, axis=axis, reverse=rever...  24 us
    ppermute x3, starting transfers between devices, passed_along(): return lax.ppermute(block, axis, route)  14.1 us
    ppermute x6, starting transfers between devices, gathered_rows(): lax.ppermute(part, axis, [(i, (i + shift) % peers) for i in range(peers)])  8.68 us
    ppermute x3, waiting for transfers between devices, passed_along(): return lax.ppermute(block, axis, route)  4.85 us
  transfers between devices with their start and end apart: 9, of which 2 were waited for; matrix products, arithmetic and copies ran while one was open for 5% of the time, Pallas kernels for 7%

profile of v7, /device:TPU:1, one launch (start us, length us, event | category | flops | bytes accessed | tf_op | source)
XLA Modules:
  0.0 193.0 jit_solution(8289526409889017402)
XLA Ops:
  0.6 0.0 copy-start
  0.6 0.0 copy-start.3
  0.7 0.2 fusion.9
  0.9 1.2 fusion.5
  2.1 1.1 multiply_add_fusion.1
  3.2 0.0 copy-done
  3.2 0.0 copy-done.3
  3.2 1.4 fusion
  4.6 0.1 pad_maximum_fusion
  4.7 0.0 copy-start.9
  4.7 0.0 copy-start.11
  4.7 1.5 copy.10
  6.2 0.6 constant_dynamic-slice_fusion.refs_1_
  6.9 0.0 copy-done.9
  6.9 0.0 copy-done.11
  6.9 0.6 fusion.16
  7.5 1.1 broadcast_in_dim.12.refs_3_
  8.5 7.5 %shard_map.86 = f32[64,256]{1,0:T(8,128)} custom-call(s32[16]{0:T(128)} %get-tuple-element.13.refs_0_, f32[64,256]{1,0:T(8,128)} %constant_dynamic-slice_fusion.refs_1_, f32[8,256,256]{2,1,0:T(8,128)} %bitcast.42, f32[16,64,256]{2,1,0:T(8,128)} %broadcast_in_dim.12.refs_3_), custom_call_target="tpu_custom_call" | custom-call | tf_op jit(solution)/shard_map/pallas_call | solution.py:297
  16.0 2.1 %collective-permute-start = (f32[64,256]{1,0:T(8,128)}, f32[64,256]{1,0:T(8,128)S(1)}, u32[]{:S(2)}, u32[]{:S(2)}) collective-permute-start(f32[64,256]{1,0:T(8,128)} %shard_map.86), channel_id=1, source_target_pairs={{0,1},{1,2},{2,3},{3,0},{4,5},{5,6},{6,7},{7,4},{8,9},{9,10},{10,1... | collective-permute-start | bytes 196616 | tf_op jit(solution)/shard_map/ppermute | solution.py:28
  18.1 2.6 %collective-permute-start.1 = (f32[64,256]{1,0:T(8,128)}, f32[64,256]{1,0:T(8,128)S(1)}, u32[]{:S(2)}, u32[]{:S(2)}) collective-permute-start(f32[64,256]{1,0:T(8,128)} %shard_map.86), channel_id=1, source_target_pairs={{0,2},{1,3},{2,0},{3,1},{4,6},{5,7},{6,4},{7,5},{8,10},{9,11},{10,... | collective-permute-start | bytes 196616 | tf_op jit(solution)/shard_map/ppermute | solution.py:28
  20.7 1.1 collective-permute-start.2
  21.8 1.6 copy.11
  23.4 0.0 copy-start.6
  23.4 0.0 copy-start.7
  23.4 1.2 concatenate.6.refs_2_
  24.6 7.3 %shard_map.87 = f32[64,256]{1,0:T(8,128)} custom-call(s32[16]{0:T(128)} %get-tuple-element.14.refs_0_, f32[64,256]{1,0:T(8,128)} %constant_dynamic-slice_fusion.refs_1_, f32[5,256,256]{2,1,0:T(8,128)} %concatenate.6.refs_2_, f32[16,64,256]{2,1,0:T(8,128)} %broadcast_in_dim.12.refs_3_), custom_call_target="tpu_custom_call" | custom-call | tf_op jit(solution)/shard_map/pallas_call | solution.py:297
  31.9 0.4 collective-permute-start.3
  32.3 0.8 collective-permute-start.4
  33.1 0.1 fusion.11
  33.2 0.0 copy-start.10
  33.2 1.8 fusion.1.refs_3_.refs_5_
  35.0 0.6 broadcast_in_dim.14.refs_1_
  35.6 7.0 %shard_map.88 = f32[16,256]{1,0:T(8,128)} custom-call(s32[16]{0:T(128)} %get-tuple-element.13.refs_0_, f32[16,256]{1,0:T(8,128)} %broadcast_in_dim.14.refs_1_, f32[8,256,256]{2,1,0:T(8,128)} %bitcast.43, f32[16,16,256]{2,1,0:T(8,128)} %fusion.1.refs_3_.refs_5_), custom_call_target="tpu_custom_call" | custom-call | tf_op jit(solution)/shard_map/pallas_call | solution.py:297
  42.7 0.0 collective-permute-done
  42.7 1.7 collective-permute-start.5
  44.4 0.0 collective-permute-done.1
  44.4 0.0 collective-permute-done.2
  44.4 0.2 fusion.17
  44.7 0.8 broadcast_select_fusion.ahead_ref
  45.4 1.3 add_select_fusion.records_ref
  46.7 0.0 collective-permute-done.3
  46.7 0.0 collective-permute-done.4
  46.8 0.0 collective-permute-done.5
  46.8 0.0 copy-start.2
  46.8 0.7 copy-done.2
  47.5 74.9 %shard_map.89 = (f32[6,256,256]{2,1,0:T(8,128)}, f32[6,256,256]{2,1,0:T(8,128)}, f32[16,256]{1,0:T(8,128)}) custom-call(f32[256,256]{1,0:T(8,128)} %broadcast_select_fusion.ahead_ref, f32[256,256]{1,0:T(8,128)} %copy-done.2, f32[16,256]{1,0:T(8,128)} %add_select_fusion.records_ref), custom_call_target="tpu_custom_call" | custom-call | tf_op jit(solution)/shard_map/pallas_call | solution.py:160
  122.4 6.6 %collective-permute-start.6 = (f32[16,256]{1,0:T(8,128)}, f32[16,256]{1,0:T(8,128)S(1)}, u32[]{:S(2)}, u32[]{:S(2)}) collective-permute-start(f32[16,256]{1,0:T(8,128)} %get-tuple-element.6), channel_id=1, source_target_pairs={{0,4},{4,8},{8,12},{12,16},{16,20},{20,24},{24,28},{28,32},{32,36}... | collective-permute-start | bytes 49160 | tf_op jit(solution)/shard_map/ppermute | solution.py:17
  129.0 1.3 multiply_add_fusion.refs_4_
  130.3 0.0 collective-permute-done.6
  130.3 0.6 broadcast_select_fusion.1.refs_2_
  130.9 7.9 %shard_map.90 = (f32[16,16,256]{2,1,0:T(8,128)}, f32[16,16,256]{2,1,0:T(8,128)}) custom-call(s32[16]{0:T(128)} %get-tuple-element.13.refs_0_, s32[16]{0:T(128)} %refs_1_.1, f32[16,256]{1,0:T(8,128)} %broadcast_select_fusion.1.refs_2_, f32[8,256,256]{2,1,0:T(8,128)} %bitcast.44, f32[4,256,256]{2,1,0:T(8,128)} %multiply_add_fusion.refs_4_, ...), custom_call_target="tpu_custom_call" | custom-call | tf_op jit(solution)/shard_map/pallas_call | solution.py:297
  138.8 0.8 slice_bitcast_fusion
  139.6 1.9 collective-permute-start.7
  141.5 1.0 slice.6
  142.5 2.5 %collective-permute-done.7 = f32[16,256]{1,0:T(8,128)S(1)} collective-permute-done((f32[16,256]{1,0:T(8,128)S(1)}, f32[16,256]{1,0:T(8,128)S(1)}, u32[]{:S(2)}, u32[]{:S(2)}) %collective-permute-start.7) | collective-permute-done | bytes 16416 | tf_op jit(solution)/shard_map/ppermute | solution.py:17
  145.0 1.1 fusion.2
  146.0 0.0 copy-done.4
  146.0 0.7 sub.94.refs_3_
  146.8 6.8 %shard_map.91.records_ref = f32[16,256]{1,0:T(8,128)} custom-call(s32[16]{0:T(128)} %get-tuple-element.14.refs_0_, f32[16,256]{1,0:T(8,128)} %broadcast_in_dim.14.refs_1_, f32[5,256,256]{2,1,0:T(8,128)} %concatenate.6.refs_2_, f32[16,16,256]{2,1,0:T(8,128)} %sub.94.refs_3_), custom_call_target="tpu_custom_call" | custom-call | tf_op jit(solution)/shard_map/pallas_call | solution.py:297
  153.5 24.0 %shard_map.92 = f32[16,256]{1,0:T(8,128)} custom-call(f32[6,256,256]{2,1,0:T(8,128)} %get-tuple-element.8.maps_ref, f32[16,256]{1,0:T(8,128)} %shard_map.91.records_ref), custom_call_target="tpu_custom_call" | custom-call | tf_op jit(solution)/shard_map/pallas_call | solution.py:219
  177.5 5.6 %collective-permute-start.8 = (f32[16,256]{1,0:T(8,128)}, f32[16,256]{1,0:T(8,128)S(1)}, u32[]{:S(2)}, u32[]{:S(2)}) collective-permute-start(f32[16,256]{1,0:T(8,128)} %shard_map.92), channel_id=1, source_target_pairs={{4,0},{8,4},{12,8},{16,12},{20,16},{24,20},{28,24},{32,28},{36,32}... | collective-permute-start | bytes 49160 | tf_op jit(solution)/shard_map/ppermute | solution.py:17
  183.2 2.4 %collective-permute-done.8.refs_1_ = f32[16,256]{1,0:T(8,128)S(1)} collective-permute-done((f32[16,256]{1,0:T(8,128)}, f32[16,256]{1,0:T(8,128)S(1)}, u32[]{:S(2)}, u32[]{:S(2)}) %collective-permute-start.8) | collective-permute-done | bytes 16416 | tf_op jit(solution)/shard_map/ppermute | solution.py:17
  185.6 0.6 copy-done.8
  186.2 6.9 %shard_map.93 = f32[16,16,256]{2,1,0:T(8,128)} custom-call(s32[16]{0:T(128)} %get-tuple-element.14.refs_0_, f32[16,256]{1,0:T(8,128)} %copy-done.8, f32[5,256,256]{2,1,0:T(8,128)} %concatenate.6.refs_2_, f32[16,16,256]{2,1,0:T(8,128)} %sub.94.refs_3_), custom_call_target="tpu_custom_call" | custom-call | tf_op jit(solution)/shard_map/pallas_call | solution.py:297
  (23 shorter events, 0.2 us)
Async XLA Ops:
  0.6 2.5 %copy-start = (f32[4,256,256]{2,1,0:T(8,128)S(1)}, f32[4,256,256]{2,1,0:T(8,128)}, u32[]{:S(2)}) copy-start(f32[4,256,256]{2,1,0:T(8,128)} %param.11) | copy-start | bytes 3145732
  0.6 2.5 %copy-start.3 = (f32[4,256]{1,0:T(4,128)S(1)}, f32[4,256]{1,0:T(4,128)}, u32[]{:S(2)}) copy-start(f32[4,256]{1,0:T(4,128)} %param.10) | copy-start | bytes 12292
  4.7 2.2 %copy-start.9 = (s32[16]{0:T(128)S(1)}, s32[16]{0:T(128)}, u32[]{:S(2)}) copy-start(s32[16]{0:T(128)} %refs_1_.1) | copy-start | bytes 196
  4.7 2.1 %copy-start.11 = (s32[16]{0:T(128)S(1)}, s32[16]{0:T(128)}, u32[]{:S(2)}) copy-start(s32[16]{0:T(128)} %param.9) | copy-start | bytes 196
  16.0 26.7 %collective-permute-start = (f32[64,256]{1,0:T(8,128)}, f32[64,256]{1,0:T(8,128)S(1)}, u32[]{:S(2)}, u32[]{:S(2)}) collective-permute-start(f32[64,256]{1,0:T(8,128)} %shard_map.86), channel_id=1, source_target_pairs={{0,1},{1,2},{2,3},{3,0},{4,5},{5,6},{6,7},{7,4},{8,9},{9,10},{10,1... | collective-permute-start | bytes 196616 | tf_op jit(solution)/shard_map/ppermute | solution.py:28
  18.1 26.2 %collective-permute-start.1 = (f32[64,256]{1,0:T(8,128)}, f32[64,256]{1,0:T(8,128)S(1)}, u32[]{:S(2)}, u32[]{:S(2)}) collective-permute-start(f32[64,256]{1,0:T(8,128)} %shard_map.86), channel_id=1, source_target_pairs={{0,2},{1,3},{2,0},{3,1},{4,6},{5,7},{6,4},{7,5},{8,10},{9,11},{10,... | collective-permute-start | bytes 196616 | tf_op jit(solution)/shard_map/ppermute | solution.py:28
  20.7 23.7 %collective-permute-start.2 = (f32[64,256]{1,0:T(8,128)}, f32[64,256]{1,0:T(8,128)S(1)}, u32[]{:S(2)}, u32[]{:S(2)}) collective-permute-start(f32[64,256]{1,0:T(8,128)} %shard_map.86), channel_id=1, source_target_pairs={{0,3},{1,0},{2,1},{3,2},{4,7},{5,4},{6,5},{7,6},{8,11},{9,8},{10,9... | collective-permute-start | bytes 196616 | tf_op jit(solution)/shard_map/ppermute | solution.py:28
  23.4 9.7 %copy-start.6 = (f32[64,256]{1,0:T(8,128)S(1)}, f32[64,256]{1,0:T(8,128)}, u32[]{:S(2)}) copy-start(f32[64,256]{1,0:T(8,128)} %shard_map.86) | copy-start | bytes 196612
  23.4 9.8 %copy-start.7 = (f32[16,16,256]{2,1,0:T(8,128)S(1)}, f32[16,16,256]{2,1,0:T(8,128)}, u32[]{:S(2)}) copy-start(f32[16,16,256]{2,1,0:T(8,128)} %param.7) | copy-start | bytes 786436
  31.9 14.8 %collective-permute-start.3 = (f32[64,256]{1,0:T(8,128)}, f32[64,256]{1,0:T(8,128)S(1)}, u32[]{:S(2)}, u32[]{:S(2)}) collective-permute-start(f32[64,256]{1,0:T(8,128)} %shard_map.87), channel_id=1, source_target_pairs={{0,1},{1,2},{2,3},{3,0},{4,5},{5,6},{6,7},{7,4},{8,9},{9,10},{10,1... | collective-permute-start | bytes 196616 | tf_op jit(solution)/shard_map/ppermute | solution.py:28
  32.3 14.5 %collective-permute-start.4 = (f32[64,256]{1,0:T(8,128)}, f32[64,256]{1,0:T(8,128)S(1)}, u32[]{:S(2)}, u32[]{:S(2)}) collective-permute-start(f32[64,256]{1,0:T(8,128)} %shard_map.87), channel_id=1, source_target_pairs={{0,2},{1,3},{2,0},{3,1},{4,6},{5,7},{6,4},{7,5},{8,10},{9,11},{10,... | collective-permute-start | bytes 196616 | tf_op jit(solution)/shard_map/ppermute | solution.py:28
  33.2 9.4 %copy-start.5 = (f32[64,256]{1,0:T(8,128)S(1)}, f32[64,256]{1,0:T(8,128)}, u32[]{:S(2)}) copy-start(f32[64,256]{1,0:T(8,128)} %shard_map.87) | copy-start | bytes 196612
  33.2 11.2 %copy-start.10 = (f32[256]{0:T(256)S(1)}, f32[256]{0:T(256)}, u32[]{:S(2)}) copy-start(f32[256]{0:T(256)} %param.13) | copy-start | bytes 3076
  42.7 4.1 %collective-permute-start.5 = (f32[64,256]{1,0:T(8,128)S(1)}, f32[64,256]{1,0:T(8,128)S(1)}, u32[]{:S(2)}, u32[]{:S(2)}) collective-permute-start(f32[64,256]{1,0:T(8,128)S(1)} %copy-done.5), channel_id=1, source_target_pairs={{0,3},{1,0},{2,1},{3,2},{4,7},{5,4},{6,5},{7,6},{8,11},{9,8},{10,9... | collective-permute-start | bytes 196616 | tf_op jit(solution)/shard_map/ppermute | solution.py:28
  46.8 0.7 copy-start.2
  122.4 7.9 %collective-permute-start.6 = (f32[16,256]{1,0:T(8,128)}, f32[16,256]{1,0:T(8,128)S(1)}, u32[]{:S(2)}, u32[]{:S(2)}) collective-permute-start(f32[16,256]{1,0:T(8,128)} %get-tuple-element.6), channel_id=1, source_target_pairs={{0,4},{4,8},{8,12},{12,16},{16,20},{20,24},{24,28},{28,32},{32,36}... | collective-permute-start | bytes 49160 | tf_op jit(solution)/shard_map/ppermute | solution.py:17
  130.3 14.6 %copy-start.1 = (f32[4,256,256]{2,1,0:T(8,128)S(1)}, f32[4,256,256]{2,1,0:T(8,128)}, u32[]{:S(2)}) copy-start(f32[4,256,256]{2,1,0:T(8,128)} %param.12) | copy-start | bytes 3145732
  138.8 7.2 %copy-start.4 = (f32[16,16,256]{2,1,0:T(8,128)S(1)}, f32[16,16,256]{2,1,0:T(8,128)}, u32[]{:S(2)}) copy-start(f32[16,16,256]{2,1,0:T(8,128)} %get-tuple-element.4) | copy-start | bytes 786436
  139.6 5.3 %collective-permute-start.7 = (f32[16,256]{1,0:T(8,128)S(1)}, f32[16,256]{1,0:T(8,128)S(1)}, u32[]{:S(2)}, u32[]{:S(2)}) collective-permute-start(f32[16,256]{1,0:T(8,128)S(1)} %slice_bitcast_fusion), channel_id=1, source_target_pairs={{4,0},{8,4},{12,8},{16,12},{20,16},{24,20},{28,24},{32,28},{36,32}... | collective-permute-start | bytes 49160 | tf_op jit(solution)/shard_map/ppermute | solution.py:17
  177.5 8.0 %collective-permute-start.8 = (f32[16,256]{1,0:T(8,128)}, f32[16,256]{1,0:T(8,128)S(1)}, u32[]{:S(2)}, u32[]{:S(2)}) collective-permute-start(f32[16,256]{1,0:T(8,128)} %shard_map.92), channel_id=1, source_target_pairs={{4,0},{8,4},{12,8},{16,12},{20,16},{24,20},{28,24},{32,28},{36,32}... | collective-permute-start | bytes 49160 | tf_op jit(solution)/shard_map/ppermute | solution.py:17
  185.6 0.6 copy-start.8

commit v8 on v7

--- a/solution.py
+++ b/solution.py
@@ -308,6 +308,38 @@
     )(*operands)
 
 
+def paired_kernel(ahead_pick_ref, behind_pick_ref, ahead_start_ref, behind_start_ref,
+                  ahead_table_ref, behind_table_ref, ahead_source_ref, ahead_out, behind_out,
+                  *, steps):
+    def advance(i, carry):
+        ahead, behind = carry
+        back = steps - 1 - i
+        ahead = exact_dot(ahead, ahead_table_ref[ahead_pick_ref[i]]) + ahead_source_ref[i]
+        behind = exact_dot(behind, behind_table_ref[behind_pick_ref[back]])
+        return ahead, behind
+
+    ahead, behind = lax.fori_loop(
+        0, steps, advance, (ahead_start_ref[...], behind_start_ref[...]), unroll=UNROLL
+    )
+    ahead_out[...] = ahead
+    behind_out[...] = behind
+
+
+def paired_maps(ahead_pick, behind_pick, ahead_start, behind_start, ahead_table, behind_table,
+                ahead_source):
+    smem = pl.BlockSpec(memory_space=pltpu.SMEM)
+    vmem = pl.BlockSpec(memory_space=pltpu.VMEM)
+    return pl.pallas_call(
+        functools.partial(paired_kernel, steps=ahead_source.shape[0]),
+        out_shape=(
+            jax.ShapeDtypeStruct(ahead_start.shape, jnp.float32),
+            jax.ShapeDtypeStruct(behind_start.shape, jnp.float32),
+        ),
+        in_specs=[smem, smem, vmem, vmem, vmem, vmem, vmem],
+        out_specs=(vmem, vmem),
+    )(ahead_pick, behind_pick, ahead_start, behind_start, ahead_table, behind_table, ahead_source)
+
+
 def per_band_products(lines, factors, weights):
     steps, rows, states = lines.shape
     bands = factors.shape[0]
@@ -350,23 +382,23 @@
     measured = per_band_products(observations, gain, observed_weights)
 
     blank_records = jnp.zeros((record_rows, states), jnp.float32)
-    forward_rows = recurrence(
-        forward_pick, own_identity, forward_table, blank_columns, False, False
-    )
-    whole_matrix = gathered_rows(forward_rows, "col")
     first_block = time_index == 0
-
     final_here = (time_index == time_devices - 1) & (jnp.arange(steps_dev) == steps_dev - 1)
     backward = jnp.transpose(mode_backward_factors, (0, 2, 1))
     backward_table = jnp.concatenate([backward, jnp.zeros_like(backward[:1])], axis=0)
     backward_pick = jnp.where(final_here, bands, band_index)
-    backward_rows = recurrence(
-        backward_pick, own_identity, backward_table, blank_columns, True, False
-    )
+    forward_rows, backward_rows = paired_maps(
+        forward_pick,
+        backward_pick,
+        jnp.concatenate([own_identity, blank_records], axis=0),
+        own_identity,
+        forward_table,
+        backward_table,
+        jnp.concatenate([blank_columns, measured], axis=1),
+    )
+    whole_matrix = gathered_rows(forward_rows[:column_share], "col")
     whole_back = gathered_rows(backward_rows, "col")
-    block_records = recurrence(
-        forward_pick, blank_records, forward_table, measured, False, False
-    )
+    block_records = forward_rows[column_share:]
     folded_records = jnp.where(
         first_block,
         accurate_matmul_result(initial_mean[None, :], whole_matrix) + block_records,

time: 194 us -> 183 us (0.943)
  Pallas kernels: 142 us -> 131 us
    pallas_call x6 -> x3, Pallas kernels: 43.2 us -> 21.4 us  [recurrence(): pl.pallas_call(functools.partial(recurrence_kernel, steps=steps, reverse=...]
    pallas_call x0 -> x1, Pallas kernels: none -> 9.12 us  [paired_maps(): pl.pallas_call(functools.partial(paired_kernel, steps=ahead_source.shape[...]
  transfers between devices with their start and end apart: 9 -> 9, of which waited for: 2 -> 3; matrix products, arithmetic and copies ran while one was open for 5% -> 3% of each run, Pallas kernels for 7% -> 0%
where the time goes in v8:
time: 183 us; the launch traced here: 182 us
  Pallas kernels  131 us (72%)
  starting transfers between devices  21.9 us (12%)
  local copies, waits for them, and re-layouts  11.7 us (6%)
  other arithmetic  8 us (4%)
  waiting for transfers between devices  5.13 us (3%)
  matrix products  3.7 us (2%)
    pallas_call x1, Pallas kernels, doubling_maps(): pl.pallas_call(functools.partial(maps_kernel, axis=axis), out_shape=(stac...  75.1 us
    pallas_call x1, Pallas kernels, doubling_records(): pl.pallas_call(functools.partial(records_kernel, axis=axis, reverse=rever...  25 us
    pallas_call x3, Pallas kernels, recurrence(): pl.pallas_call(functools.partial(recurrence_kernel, steps=steps, reverse=...  21.4 us
    ppermute x3, starting transfers between devices, passed_along(): return lax.ppermute(block, axis, route)  13.1 us
    pallas_call x1, Pallas kernels, paired_maps(): pl.pallas_call(functools.partial(paired_kernel, steps=ahead_source.shape[...  9.12 us
    ppermute x6, starting transfers between devices, gathered_rows(): lax.ppermute(part, axis, [(i, (i + shift) % peers) for i in range(peers)])  8.76 us
    ppermute x3, waiting for transfers between devices, passed_along(): return lax.ppermute(block, axis, route)  4.91 us
  transfers between devices with their start and end apart: 9, of which 3 were waited for; matrix products, arithmetic and copies ran while one was open for 3% of the time, Pallas kernels for 0%

profile of v8, /device:TPU:1, one launch (start us, length us, event | category | flops | bytes accessed | tf_op | source)
XLA Modules:
  0.0 182.0 jit_solution(7604187474034076284)
XLA Ops:
  0.6 0.0 copy-start
  0.6 0.0 copy-start.5
  0.7 0.2 fusion.9
  0.9 1.2 fusion.5
  2.1 1.1 multiply_add_fusion.1
  3.2 0.0 copy-done
  3.2 0.0 copy-done.5
  3.2 1.4 fusion
  4.6 0.1 pad_maximum_fusion
  4.7 1.5 copy.10
  6.2 0.0 copy-start.4
  6.2 1.6 copy.11
  7.9 0.6 concatenate.12.ahead_start_ref
  8.5 0.0 copy-done.9
  8.5 0.0 copy-done.11
  8.5 0.6 fusion.17
  9.1 0.1 fusion.11
  9.2 0.0 copy-done.7
  9.2 1.1 fusion.1.refs_5_
  10.3 0.0 copy-start.2
  10.3 1.2 concatenate.14.ahead_source_ref
  11.5 0.0 copy-done.4
  11.5 1.2 concatenate.13.behind_table_ref.refs_2_
  12.7 9.1 %shard_map.86 = (f32[80,256]{1,0:T(8,128)}, f32[64,256]{1,0:T(8,128)}) custom-call(s32[16]{0:T(128)} %get-tuple-element.19.ahead_pick_ref.refs_0_, s32[16]{0:T(128)} %get-tuple-element.20.behind_pick_ref.refs_0_, f32[80,256]{1,0:T(8,128)} %concatenate.12.ahead_start_ref, f32[64,256]{1,0:T(8,128)} %copy-done.4, f32[8,256,256]{2,1,0:T(8,128)} %bitcast.42, ...), custom_call_target="tpu_custom_call" | custom-call | tf_op jit(solution)/shard_map/pallas_call | solution.py:332
  21.8 0.0 copy-done.2
  21.9 0.9 fusion.16
  22.7 2.2 %collective-permute-start = (f32[64,256]{1,0:T(8,128)S(1)}, f32[64,256]{1,0:T(8,128)S(1)}, u32[]{:S(2)}, u32[]{:S(2)}) collective-permute-start(f32[64,256]{1,0:T(8,128)S(1)} %get-tuple-element.14), channel_id=1, source_target_pairs={{0,1},{1,2},{2,3},{3,0},{4,5},{5,6},{6,7},{7,4},{8,9},{9,10},{10,1... | collective-permute-start | bytes 196616 | tf_op jit(solution)/shard_map/ppermute | solution.py:28
  24.9 2.6 %collective-permute-start.1 = (f32[64,256]{1,0:T(8,128)S(1)}, f32[64,256]{1,0:T(8,128)S(1)}, u32[]{:S(2)}, u32[]{:S(2)}) collective-permute-start(f32[64,256]{1,0:T(8,128)S(1)} %get-tuple-element.14), channel_id=1, source_target_pairs={{0,2},{1,3},{2,0},{3,1},{4,6},{5,7},{6,4},{7,5},{8,10},{9,11},{10,... | collective-permute-start | bytes 196616 | tf_op jit(solution)/shard_map/ppermute | solution.py:28
  27.5 1.1 collective-permute-start.2
  28.6 0.4 collective-permute-start.3
  29.0 0.8 collective-permute-start.4
  29.8 0.9 constant_dynamic-update-slice_fusion.3
  30.7 0.0 collective-permute-done
  30.7 1.7 collective-permute-start.5
  32.4 0.0 collective-permute-done.1
  32.4 0.0 collective-permute-done.2
  32.4 0.0 copy-done.10
  32.4 0.2 fusion.18
  32.7 0.8 broadcast_select_fusion.ahead_ref
  33.4 1.3 add_select_fusion.records_ref
  34.7 0.0 collective-permute-done.3
  34.7 0.0 collective-permute-done.4
  34.8 0.2 collective-permute-done.5
  35.0 0.0 copy-start.3
  35.0 0.7 copy-done.3
  35.7 75.1 %shard_map.87 = (f32[6,256,256]{2,1,0:T(8,128)}, f32[6,256,256]{2,1,0:T(8,128)}, f32[16,256]{1,0:T(8,128)}) custom-call(f32[256,256]{1,0:T(8,128)} %broadcast_select_fusion.ahead_ref, f32[256,256]{1,0:T(8,128)} %copy-done.3, f32[16,256]{1,0:T(8,128)} %add_select_fusion.records_ref), custom_call_target="tpu_custom_call" | custom-call | tf_op jit(solution)/shard_map/pallas_call | solution.py:160
  110.8 6.6 %collective-permute-start.6 = (f32[16,256]{1,0:T(8,128)}, f32[16,256]{1,0:T(8,128)S(1)}, u32[]{:S(2)}, u32[]{:S(2)}) collective-permute-start(f32[16,256]{1,0:T(8,128)} %get-tuple-element.10), channel_id=1, source_target_pairs={{0,4},{4,8},{8,12},{12,16},{16,20},{20,24},{24,28},{28,32},{32,36}... | collective-permute-start | bytes 49160 | tf_op jit(solution)/shard_map/ppermute | solution.py:17
  117.4 1.3 multiply_add_fusion.refs_4_
  118.7 0.0 collective-permute-done.6
  118.7 0.6 broadcast_select_fusion.1.refs_2_
  119.3 7.8 %shard_map.88 = (f32[16,16,256]{2,1,0:T(8,128)}, f32[16,16,256]{2,1,0:T(8,128)}) custom-call(s32[16]{0:T(128)} %get-tuple-element.19.ahead_pick_ref.refs_0_, s32[16]{0:T(128)} %refs_1_.1, f32[16,256]{1,0:T(8,128)} %broadcast_select_fusion.1.refs_2_, f32[8,256,256]{2,1,0:T(8,128)} %bitcast.43, f32[4,256,256]{2,1,0:T(8,128)} %multiply_add_fusion.refs_4_, ...), custom_call_target="tpu_custom_call" | custom-call | tf_op jit(solution)/shard_map/pallas_call | solution.py:297
  127.2 0.8 slice_bitcast_fusion
  127.9 1.9 %collective-permute-start.7 = (f32[16,256]{1,0:T(8,128)S(1)}, f32[16,256]{1,0:T(8,128)S(1)}, u32[]{:S(2)}, u32[]{:S(2)}) collective-permute-start(f32[16,256]{1,0:T(8,128)S(1)} %slice_bitcast_fusion), channel_id=1, source_target_pairs={{4,0},{8,4},{12,8},{16,12},{20,16},{24,20},{28,24},{32,28},{36,32}... | collective-permute-start | bytes 49160 | tf_op jit(solution)/shard_map/ppermute | solution.py:17
  129.9 1.0 slice.14
  130.8 2.5 %collective-permute-done.7 = f32[16,256]{1,0:T(8,128)S(1)} collective-permute-done((f32[16,256]{1,0:T(8,128)S(1)}, f32[16,256]{1,0:T(8,128)S(1)}, u32[]{:S(2)}, u32[]{:S(2)}) %collective-permute-start.7) | collective-permute-done | bytes 16416 | tf_op jit(solution)/shard_map/ppermute | solution.py:17
  133.3 1.1 fusion.2
  134.4 0.7 sub.94.refs_3_
  135.1 0.6 broadcast_in_dim.11.refs_1_
  135.7 6.7 %shard_map.89.records_ref = f32[16,256]{1,0:T(8,128)} custom-call(s32[16]{0:T(128)} %get-tuple-element.20.behind_pick_ref.refs_0_, f32[16,256]{1,0:T(8,128)} %broadcast_in_dim.11.refs_1_, f32[5,256,256]{2,1,0:T(8,128)} %concatenate.13.behind_table_ref.refs_2_, f32[16,16,256]{2,1,0:T(8,128)} %sub.94.refs_3_), custom_call_target="tpu_custom_call" | custom-call | tf_op jit(solution)/shard_map/pallas_call | solution.py:297
  142.5 25.0 %shard_map.90 = f32[16,256]{1,0:T(8,128)} custom-call(f32[6,256,256]{2,1,0:T(8,128)} %get-tuple-element.12.maps_ref, f32[16,256]{1,0:T(8,128)} %shard_map.89.records_ref), custom_call_target="tpu_custom_call" | custom-call | tf_op jit(solution)/shard_map/pallas_call | solution.py:219
  167.5 4.6 %collective-permute-start.8 = (f32[16,256]{1,0:T(8,128)}, f32[16,256]{1,0:T(8,128)S(1)}, u32[]{:S(2)}, u32[]{:S(2)}) collective-permute-start(f32[16,256]{1,0:T(8,128)} %shard_map.90), channel_id=1, source_target_pairs={{4,0},{8,4},{12,8},{16,12},{20,16},{24,20},{28,24},{32,28},{36,32}... | collective-permute-start | bytes 49160 | tf_op jit(solution)/shard_map/ppermute | solution.py:17
  172.1 2.4 %collective-permute-done.8.refs_1_ = f32[16,256]{1,0:T(8,128)S(1)} collective-permute-done((f32[16,256]{1,0:T(8,128)}, f32[16,256]{1,0:T(8,128)S(1)}, u32[]{:S(2)}, u32[]{:S(2)}) %collective-permute-start.8) | collective-permute-done | bytes 16416 | tf_op jit(solution)/shard_map/ppermute | solution.py:17
  174.6 0.6 copy-done.8
  175.2 6.9 %shard_map.91 = f32[16,16,256]{2,1,0:T(8,128)} custom-call(s32[16]{0:T(128)} %get-tuple-element.20.behind_pick_ref.refs_0_, f32[16,256]{1,0:T(8,128)} %copy-done.8, f32[5,256,256]{2,1,0:T(8,128)} %concatenate.13.behind_table_ref.refs_2_, f32[16,16,256]{2,1,0:T(8,128)} %sub.94.refs_3_), custom_call_target="tpu_custom_call" | custom-call | tf_op jit(solution)/shard_map/pallas_call | solution.py:297
  (22 shorter events, 0.2 us)
Async XLA Ops:
  0.6 2.5 %copy-start = (f32[4,256,256]{2,1,0:T(8,128)S(1)}, f32[4,256,256]{2,1,0:T(8,128)}, u32[]{:S(2)}) copy-start(f32[4,256,256]{2,1,0:T(8,128)} %param.11) | copy-start | bytes 3145732
  0.6 2.5 %copy-start.5 = (f32[4,256]{1,0:T(4,128)S(1)}, f32[4,256]{1,0:T(4,128)}, u32[]{:S(2)}) copy-start(f32[4,256]{1,0:T(4,128)} %param.10) | copy-start | bytes 12292
  6.2 2.3 %copy-start.9 = (s32[16]{0:T(128)S(1)}, s32[16]{0:T(128)}, u32[]{:S(2)}) copy-start(s32[16]{0:T(128)} %refs_1_.1) | copy-start | bytes 196
  6.2 2.3 %copy-start.11 = (s32[16]{0:T(128)S(1)}, s32[16]{0:T(128)}, u32[]{:S(2)}) copy-start(s32[16]{0:T(128)} %param.9) | copy-start | bytes 196
  6.2 3.0 %copy-start.7 = (f32[16,16,256]{2,1,0:T(8,128)S(1)}, f32[16,16,256]{2,1,0:T(8,128)}, u32[]{:S(2)}) copy-start(f32[16,16,256]{2,1,0:T(8,128)} %param.7) | copy-start | bytes 786436
  6.2 5.3 %copy-start.4 = (f32[64,256]{1,0:T(8,128)}, f32[64,256]{1,0:T(8,128)S(1)}, u32[]{:S(2)}) copy-start(f32[64,256]{1,0:T(8,128)S(1)} %constant_dynamic-slice_fusion.behind_start_ref) | copy-start | bytes 196612
  10.3 11.6 %copy-start.2 = (f32[16,16,256]{2,1,0:T(8,128)}, f32[16,16,256]{2,1,0:T(8,128)S(1)}, u32[]{:S(2)}) copy-start(f32[16,16,256]{2,1,0:T(8,128)S(1)} %fusion.1.refs_5_) | copy-start | bytes 786436
  12.7 19.7 %copy-start.10 = (f32[256]{0:T(256)S(1)}, f32[256]{0:T(256)}, u32[]{:S(2)}) copy-start(f32[256]{0:T(256)} %param.13) | copy-start | bytes 3076
  22.7 8.0 %collective-permute-start = (f32[64,256]{1,0:T(8,128)S(1)}, f32[64,256]{1,0:T(8,128)S(1)}, u32[]{:S(2)}, u32[]{:S(2)}) collective-permute-start(f32[64,256]{1,0:T(8,128)S(1)} %get-tuple-element.14), channel_id=1, source_target_pairs={{0,1},{1,2},{2,3},{3,0},{4,5},{5,6},{6,7},{7,4},{8,9},{9,10},{10,1... | collective-permute-start | bytes 196616 | tf_op jit(solution)/shard_map/ppermute | solution.py:28
  24.9 7.5 %collective-permute-start.1 = (f32[64,256]{1,0:T(8,128)S(1)}, f32[64,256]{1,0:T(8,128)S(1)}, u32[]{:S(2)}, u32[]{:S(2)}) collective-permute-start(f32[64,256]{1,0:T(8,128)S(1)} %get-tuple-element.14), channel_id=1, source_target_pairs={{0,2},{1,3},{2,0},{3,1},{4,6},{5,7},{6,4},{7,5},{8,10},{9,11},{10,... | collective-permute-start | bytes 196616 | tf_op jit(solution)/shard_map/ppermute | solution.py:28
  27.5 4.9 %collective-permute-start.2 = (f32[64,256]{1,0:T(8,128)S(1)}, f32[64,256]{1,0:T(8,128)S(1)}, u32[]{:S(2)}, u32[]{:S(2)}) collective-permute-start(f32[64,256]{1,0:T(8,128)S(1)} %get-tuple-element.14), channel_id=1, source_target_pairs={{0,3},{1,0},{2,1},{3,2},{4,7},{5,4},{6,5},{7,6},{8,11},{9,8},{10,9... | collective-permute-start | bytes 196616 | tf_op jit(solution)/shard_map/ppermute | solution.py:28
  28.6 6.1 %collective-permute-start.3 = (f32[64,256]{1,0:T(8,128)}, f32[64,256]{1,0:T(8,128)S(1)}, u32[]{:S(2)}, u32[]{:S(2)}) collective-permute-start(f32[64,256]{1,0:T(8,128)} %get-tuple-element.9), channel_id=1, source_target_pairs={{0,1},{1,2},{2,3},{3,0},{4,5},{5,6},{6,7},{7,4},{8,9},{9,10},{10,1... | collective-permute-start | bytes 196616 | tf_op jit(solution)/shard_map/ppermute | solution.py:28
  29.0 5.7 %collective-permute-start.4 = (f32[64,256]{1,0:T(8,128)}, f32[64,256]{1,0:T(8,128)S(1)}, u32[]{:S(2)}, u32[]{:S(2)}) collective-permute-start(f32[64,256]{1,0:T(8,128)} %get-tuple-element.9), channel_id=1, source_target_pairs={{0,2},{1,3},{2,0},{3,1},{4,6},{5,7},{6,4},{7,5},{8,10},{9,11},{10,... | collective-permute-start | bytes 196616 | tf_op jit(solution)/shard_map/ppermute | solution.py:28
  30.7 4.3 %collective-permute-start.5 = (f32[64,256]{1,0:T(8,128)}, f32[64,256]{1,0:T(8,128)S(1)}, u32[]{:S(2)}, u32[]{:S(2)}) collective-permute-start(f32[64,256]{1,0:T(8,128)} %get-tuple-element.9), channel_id=1, source_target_pairs={{0,3},{1,0},{2,1},{3,2},{4,7},{5,4},{6,5},{7,6},{8,11},{9,8},{10,9... | collective-permute-start | bytes 196616 | tf_op jit(solution)/shard_map/ppermute | solution.py:28
  35.0 0.7 copy-start.3
  110.8 7.9 %collective-permute-start.6 = (f32[16,256]{1,0:T(8,128)}, f32[16,256]{1,0:T(8,128)S(1)}, u32[]{:S(2)}, u32[]{:S(2)}) collective-permute-start(f32[16,256]{1,0:T(8,128)} %get-tuple-element.10), channel_id=1, source_target_pairs={{0,4},{4,8},{8,12},{12,16},{16,20},{20,24},{24,28},{28,32},{32,36}... | collective-permute-start | bytes 49160 | tf_op jit(solution)/shard_map/ppermute | solution.py:17
  118.7 14.6 %copy-start.1 = (f32[4,256,256]{2,1,0:T(8,128)S(1)}, f32[4,256,256]{2,1,0:T(8,128)}, u32[]{:S(2)}) copy-start(f32[4,256,256]{2,1,0:T(8,128)} %param.12) | copy-start | bytes 3145732
  127.2 7.2 %copy-start.6 = (f32[16,16,256]{2,1,0:T(8,128)S(1)}, f32[16,16,256]{2,1,0:T(8,128)}, u32[]{:S(2)}) copy-start(f32[16,16,256]{2,1,0:T(8,128)} %get-tuple-element.6) | copy-start | bytes 786436
  127.9 5.3 %collective-permute-start.7 = (f32[16,256]{1,0:T(8,128)S(1)}, f32[16,256]{1,0:T(8,128)S(1)}, u32[]{:S(2)}, u32[]{:S(2)}) collective-permute-start(f32[16,256]{1,0:T(8,128)S(1)} %slice_bitcast_fusion), channel_id=1, source_target_pairs={{4,0},{8,4},{12,8},{16,12},{20,16},{24,20},{28,24},{32,28},{36,32}... | collective-permute-start | bytes 49160 | tf_op jit(solution)/shard_map/ppermute | solution.py:17
  167.5 7.1 %collective-permute-start.8 = (f32[16,256]{1,0:T(8,128)}, f32[16,256]{1,0:T(8,128)S(1)}, u32[]{:S(2)}, u32[]{:S(2)}) collective-permute-start(f32[16,256]{1,0:T(8,128)} %shard_map.90), channel_id=1, source_target_pairs={{4,0},{8,4},{12,8},{16,12},{20,16},{24,20},{28,24},{32,28},{36,32}... | collective-permute-start | bytes 49160 | tf_op jit(solution)/shard_map/ppermute | solution.py:17
  174.6 0.6 copy-start.8

commit v9 on v8

--- a/solution.py
+++ b/solution.py
@@ -49,6 +49,11 @@
 
             partners = partners + jnp.where(exists, 1, 0)
     pl.semaphore_wait(barrier, partners)
+
+
+def map_dot(first, second):
+    return jnp.dot(first, second, precision=lax.Precision.HIGH,
+                   preferred_element_type=jnp.float32)
 
 
 def exact_dot(first, second):
@@ -124,7 +129,7 @@
         @pl.when(has_down)
         def _():
             ahead_copy.wait_recv()
-            ahead_out[r + 1] = exact_dot(ahead_in[r], own_ahead[...])
+            ahead_out[r + 1] = map_dot(ahead_in[r], own_ahead[...])
 
         @pl.when(jnp.logical_not(has_down))
         def _():
@@ -133,7 +138,7 @@
         @pl.when(has_up)
         def _():
             behind_copy.wait_recv()
-            behind_out[r + 1] = exact_dot(behind_in[r], own_behind[...])
+            behind_out[r + 1] = map_dot(behind_in[r], own_behind[...])
 
         @pl.when(jnp.logical_not(has_up))
         def _():

time: 183 us -> 182 us (level)
  Pallas kernels: 131 us -> 129 us
where the time goes in v9:
time: 182 us
  Pallas kernels  129 us (71%)
  starting transfers between devices  23.4 us (13%)
  local copies, waits for them, and re-layouts  11.7 us (6%)
  other arithmetic  8 us (4%)
  waiting for transfers between devices  5.19 us (3%)
  matrix products  3.7 us (2%)
    pallas_call x1, Pallas kernels, doubling_maps(): pl.pallas_call(functools.partial(maps_kernel, axis=axis), out_shape=(stac...  74.5 us
    pallas_call x1, Pallas kernels, doubling_records(): pl.pallas_call(functools.partial(records_kernel, axis=axis, reverse=rever...  23.5 us
    pallas_call x3, Pallas kernels, recurrence(): pl.pallas_call(functools.partial(recurrence_kernel, steps=steps, reverse=...  21.4 us
    ppermute x3, starting transfers between devices, passed_along(): return lax.ppermute(block, axis, route)  14.6 us
    pallas_call x1, Pallas kernels, paired_maps(): pl.pallas_call(functools.partial(paired_kernel, steps=ahead_source.shape[...  9.12 us
    ppermute x6, starting transfers between devices, gathered_rows(): lax.ppermute(part, axis, [(i, (i + shift) % peers) for i in range(peers)])  8.76 us
    ppermute x3, waiting for transfers between devices, passed_along(): return lax.ppermute(block, axis, route)  4.97 us
  transfers between devices with their start and end apart: 9, of which 3 were waited for; matrix products, arithmetic and copies ran while one was open for 3% of the time, Pallas kernels for 0%

profile of v9, /device:TPU:1, one launch (start us, length us, event | category | flops | bytes accessed | tf_op | source)
XLA Modules:
  0.0 181.5 jit_solution(2663939325693514896)
XLA Ops:
  0.6 0.0 copy-start
  0.6 0.0 copy-start.5
  0.7 0.2 fusion.9
  0.9 1.2 fusion.5
  2.1 1.1 multiply_add_fusion.1
  3.2 0.0 copy-done
  3.2 0.0 copy-done.5
  3.2 1.4 fusion
  4.6 0.1 pad_maximum_fusion
  4.7 1.5 copy.10
  6.2 0.0 copy-start.4
  6.2 1.6 copy.11
  7.9 0.6 concatenate.12.ahead_start_ref
  8.5 0.0 copy-done.9
  8.5 0.0 copy-done.11
  8.5 0.6 fusion.17
  9.1 0.1 fusion.11
  9.2 0.0 copy-done.7
  9.2 1.1 fusion.1.refs_5_
  10.3 0.0 copy-start.2
  10.3 1.2 concatenate.14.ahead_source_ref
  11.5 0.0 copy-done.4
  11.5 1.2 concatenate.13.behind_table_ref.refs_2_
  12.7 9.1 %shard_map.86 = (f32[80,256]{1,0:T(8,128)}, f32[64,256]{1,0:T(8,128)}) custom-call(s32[16]{0:T(128)} %get-tuple-element.19.ahead_pick_ref.refs_0_, s32[16]{0:T(128)} %get-tuple-element.20.behind_pick_ref.refs_0_, f32[80,256]{1,0:T(8,128)} %concatenate.12.ahead_start_ref, f32[64,256]{1,0:T(8,128)} %copy-done.4, f32[8,256,256]{2,1,0:T(8,128)} %bitcast.42, ...), custom_call_target="tpu_custom_call" | custom-call | tf_op jit(solution)/shard_map/pallas_call | solution.py:337
  21.8 0.0 copy-done.2
  21.9 0.9 fusion.16
  22.7 2.2 %collective-permute-start = (f32[64,256]{1,0:T(8,128)S(1)}, f32[64,256]{1,0:T(8,128)S(1)}, u32[]{:S(2)}, u32[]{:S(2)}) collective-permute-start(f32[64,256]{1,0:T(8,128)S(1)} %get-tuple-element.14), channel_id=1, source_target_pairs={{0,1},{1,2},{2,3},{3,0},{4,5},{5,6},{6,7},{7,4},{8,9},{9,10},{10,1... | collective-permute-start | bytes 196616 | tf_op jit(solution)/shard_map/ppermute | solution.py:28
  24.9 2.6 %collective-permute-start.1 = (f32[64,256]{1,0:T(8,128)S(1)}, f32[64,256]{1,0:T(8,128)S(1)}, u32[]{:S(2)}, u32[]{:S(2)}) collective-permute-start(f32[64,256]{1,0:T(8,128)S(1)} %get-tuple-element.14), channel_id=1, source_target_pairs={{0,2},{1,3},{2,0},{3,1},{4,6},{5,7},{6,4},{7,5},{8,10},{9,11},{10,... | collective-permute-start | bytes 196616 | tf_op jit(solution)/shard_map/ppermute | solution.py:28
  27.5 1.1 collective-permute-start.2
  28.6 0.4 collective-permute-start.3
  29.0 0.8 collective-permute-start.4
  29.8 0.9 constant_dynamic-update-slice_fusion.3
  30.7 0.0 collective-permute-done
  30.7 1.7 collective-permute-start.5
  32.4 0.0 collective-permute-done.1
  32.4 0.0 collective-permute-done.2
  32.4 0.0 copy-done.10
  32.4 0.2 fusion.18
  32.7 0.8 broadcast_select_fusion.ahead_ref
  33.4 1.3 add_select_fusion.records_ref
  34.7 0.0 collective-permute-done.3
  34.7 0.0 collective-permute-done.4
  34.8 0.2 collective-permute-done.5
  35.0 0.0 copy-start.3
  35.0 0.7 copy-done.3
  35.7 74.5 %shard_map.87 = (f32[6,256,256]{2,1,0:T(8,128)}, f32[6,256,256]{2,1,0:T(8,128)}, f32[16,256]{1,0:T(8,128)}) custom-call(f32[256,256]{1,0:T(8,128)} %broadcast_select_fusion.ahead_ref, f32[256,256]{1,0:T(8,128)} %copy-done.3, f32[16,256]{1,0:T(8,128)} %add_select_fusion.records_ref), custom_call_target="tpu_custom_call" | custom-call | tf_op jit(solution)/shard_map/pallas_call | solution.py:165
  110.2 6.1 %collective-permute-start.6 = (f32[16,256]{1,0:T(8,128)}, f32[16,256]{1,0:T(8,128)S(1)}, u32[]{:S(2)}, u32[]{:S(2)}) collective-permute-start(f32[16,256]{1,0:T(8,128)} %get-tuple-element.10), channel_id=1, source_target_pairs={{0,4},{4,8},{8,12},{12,16},{16,20},{20,24},{24,28},{28,32},{32,36}... | collective-permute-start | bytes 49160 | tf_op jit(solution)/shard_map/ppermute | solution.py:17
  116.3 1.3 multiply_add_fusion.refs_4_
  117.7 0.0 collective-permute-done.6
  117.7 0.6 broadcast_select_fusion.1.refs_2_
  118.3 7.8 %shard_map.88 = (f32[16,16,256]{2,1,0:T(8,128)}, f32[16,16,256]{2,1,0:T(8,128)}) custom-call(s32[16]{0:T(128)} %get-tuple-element.19.ahead_pick_ref.refs_0_, s32[16]{0:T(128)} %refs_1_.1, f32[16,256]{1,0:T(8,128)} %broadcast_select_fusion.1.refs_2_, f32[8,256,256]{2,1,0:T(8,128)} %bitcast.43, f32[4,256,256]{2,1,0:T(8,128)} %multiply_add_fusion.refs_4_, ...), custom_call_target="tpu_custom_call" | custom-call | tf_op jit(solution)/shard_map/pallas_call | solution.py:302
  126.1 0.8 slice_bitcast_fusion
  126.9 1.9 %collective-permute-start.7 = (f32[16,256]{1,0:T(8,128)S(1)}, f32[16,256]{1,0:T(8,128)S(1)}, u32[]{:S(2)}, u32[]{:S(2)}) collective-permute-start(f32[16,256]{1,0:T(8,128)S(1)} %slice_bitcast_fusion), channel_id=1, source_target_pairs={{4,0},{8,4},{12,8},{16,12},{20,16},{24,20},{28,24},{32,28},{36,32}... | collective-permute-start | bytes 49160 | tf_op jit(solution)/shard_map/ppermute | solution.py:17
  128.8 1.0 slice.14
  129.8 2.5 %collective-permute-done.7 = f32[16,256]{1,0:T(8,128)S(1)} collective-permute-done((f32[16,256]{1,0:T(8,128)S(1)}, f32[16,256]{1,0:T(8,128)S(1)}, u32[]{:S(2)}, u32[]{:S(2)}) %collective-permute-start.7) | collective-permute-done | bytes 16416 | tf_op jit(solution)/shard_map/ppermute | solution.py:17
  132.2 1.1 fusion.2
  133.3 0.7 sub.94.refs_3_
  134.0 0.6 broadcast_in_dim.11.refs_1_
  134.6 6.7 %shard_map.89.records_ref = f32[16,256]{1,0:T(8,128)} custom-call(s32[16]{0:T(128)} %get-tuple-element.20.behind_pick_ref.refs_0_, f32[16,256]{1,0:T(8,128)} %broadcast_in_dim.11.refs_1_, f32[5,256,256]{2,1,0:T(8,128)} %concatenate.13.behind_table_ref.refs_2_, f32[16,16,256]{2,1,0:T(8,128)} %sub.94.refs_3_), custom_call_target="tpu_custom_call" | custom-call | tf_op jit(solution)/shard_map/pallas_call | solution.py:302
  141.4 23.5 %shard_map.90 = f32[16,256]{1,0:T(8,128)} custom-call(f32[6,256,256]{2,1,0:T(8,128)} %get-tuple-element.12.maps_ref, f32[16,256]{1,0:T(8,128)} %shard_map.89.records_ref), custom_call_target="tpu_custom_call" | custom-call | tf_op jit(solution)/shard_map/pallas_call | solution.py:224
  164.9 6.6 %collective-permute-start.8 = (f32[16,256]{1,0:T(8,128)}, f32[16,256]{1,0:T(8,128)S(1)}, u32[]{:S(2)}, u32[]{:S(2)}) collective-permute-start(f32[16,256]{1,0:T(8,128)} %shard_map.90), channel_id=1, source_target_pairs={{4,0},{8,4},{12,8},{16,12},{20,16},{24,20},{28,24},{32,28},{36,32}... | collective-permute-start | bytes 49160 | tf_op jit(solution)/shard_map/ppermute | solution.py:17
  171.5 2.5 %collective-permute-done.8.refs_1_ = f32[16,256]{1,0:T(8,128)S(1)} collective-permute-done((f32[16,256]{1,0:T(8,128)}, f32[16,256]{1,0:T(8,128)S(1)}, u32[]{:S(2)}, u32[]{:S(2)}) %collective-permute-start.8) | collective-permute-done | bytes 16416 | tf_op jit(solution)/shard_map/ppermute | solution.py:17
  174.1 0.6 copy-done.8
  174.7 6.9 %shard_map.91 = f32[16,16,256]{2,1,0:T(8,128)} custom-call(s32[16]{0:T(128)} %get-tuple-element.20.behind_pick_ref.refs_0_, f32[16,256]{1,0:T(8,128)} %copy-done.8, f32[5,256,256]{2,1,0:T(8,128)} %concatenate.13.behind_table_ref.refs_2_, f32[16,16,256]{2,1,0:T(8,128)} %sub.94.refs_3_), custom_call_target="tpu_custom_call" | custom-call | tf_op jit(solution)/shard_map/pallas_call | solution.py:302
  (22 shorter events, 0.2 us)
Async XLA Ops:
  0.6 2.5 %copy-start = (f32[4,256,256]{2,1,0:T(8,128)S(1)}, f32[4,256,256]{2,1,0:T(8,128)}, u32[]{:S(2)}) copy-start(f32[4,256,256]{2,1,0:T(8,128)} %param.11) | copy-start | bytes 3145732
  0.6 2.5 %copy-start.5 = (f32[4,256]{1,0:T(4,128)S(1)}, f32[4,256]{1,0:T(4,128)}, u32[]{:S(2)}) copy-start(f32[4,256]{1,0:T(4,128)} %param.10) | copy-start | bytes 12292
  6.2 2.3 %copy-start.9 = (s32[16]{0:T(128)S(1)}, s32[16]{0:T(128)}, u32[]{:S(2)}) copy-start(s32[16]{0:T(128)} %refs_1_.1) | copy-start | bytes 196
  6.2 2.3 %copy-start.11 = (s32[16]{0:T(128)S(1)}, s32[16]{0:T(128)}, u32[]{:S(2)}) copy-start(s32[16]{0:T(128)} %param.9) | copy-start | bytes 196
  6.2 3.0 %copy-start.7 = (f32[16,16,256]{2,1,0:T(8,128)S(1)}, f32[16,16,256]{2,1,0:T(8,128)}, u32[]{:S(2)}) copy-start(f32[16,16,256]{2,1,0:T(8,128)} %param.7) | copy-start | bytes 786436
  6.2 5.3 %copy-start.4 = (f32[64,256]{1,0:T(8,128)}, f32[64,256]{1,0:T(8,128)S(1)}, u32[]{:S(2)}) copy-start(f32[64,256]{1,0:T(8,128)S(1)} %constant_dynamic-slice_fusion.behind_start_ref) | copy-start | bytes 196612
  10.3 11.6 %copy-start.2 = (f32[16,16,256]{2,1,0:T(8,128)}, f32[16,16,256]{2,1,0:T(8,128)S(1)}, u32[]{:S(2)}) copy-start(f32[16,16,256]{2,1,0:T(8,128)S(1)} %fusion.1.refs_5_) | copy-start | bytes 786436
  12.7 19.7 %copy-start.10 = (f32[256]{0:T(256)S(1)}, f32[256]{0:T(256)}, u32[]{:S(2)}) copy-start(f32[256]{0:T(256)} %param.13) | copy-start | bytes 3076
  22.7 8.0 %collective-permute-start = (f32[64,256]{1,0:T(8,128)S(1)}, f32[64,256]{1,0:T(8,128)S(1)}, u32[]{:S(2)}, u32[]{:S(2)}) collective-permute-start(f32[64,256]{1,0:T(8,128)S(1)} %get-tuple-element.14), channel_id=1, source_target_pairs={{0,1},{1,2},{2,3},{3,0},{4,5},{5,6},{6,7},{7,4},{8,9},{9,10},{10,1... | collective-permute-start | bytes 196616 | tf_op jit(solution)/shard_map/ppermute | solution.py:28
  24.9 7.5 %collective-permute-start.1 = (f32[64,256]{1,0:T(8,128)S(1)}, f32[64,256]{1,0:T(8,128)S(1)}, u32[]{:S(2)}, u32[]{:S(2)}) collective-permute-start(f32[64,256]{1,0:T(8,128)S(1)} %get-tuple-element.14), channel_id=1, source_target_pairs={{0,2},{1,3},{2,0},{3,1},{4,6},{5,7},{6,4},{7,5},{8,10},{9,11},{10,... | collective-permute-start | bytes 196616 | tf_op jit(solution)/shard_map/ppermute | solution.py:28
  27.5 4.9 %collective-permute-start.2 = (f32[64,256]{1,0:T(8,128)S(1)}, f32[64,256]{1,0:T(8,128)S(1)}, u32[]{:S(2)}, u32[]{:S(2)}) collective-permute-start(f32[64,256]{1,0:T(8,128)S(1)} %get-tuple-element.14), channel_id=1, source_target_pairs={{0,3},{1,0},{2,1},{3,2},{4,7},{5,4},{6,5},{7,6},{8,11},{9,8},{10,9... | collective-permute-start | bytes 196616 | tf_op jit(solution)/shard_map/ppermute | solution.py:28
  28.6 6.1 %collective-permute-start.3 = (f32[64,256]{1,0:T(8,128)}, f32[64,256]{1,0:T(8,128)S(1)}, u32[]{:S(2)}, u32[]{:S(2)}) collective-permute-start(f32[64,256]{1,0:T(8,128)} %get-tuple-element.9), channel_id=1, source_target_pairs={{0,1},{1,2},{2,3},{3,0},{4,5},{5,6},{6,7},{7,4},{8,9},{9,10},{10,1... | collective-permute-start | bytes 196616 | tf_op jit(solution)/shard_map/ppermute | solution.py:28
  29.0 5.7 %collective-permute-start.4 = (f32[64,256]{1,0:T(8,128)}, f32[64,256]{1,0:T(8,128)S(1)}, u32[]{:S(2)}, u32[]{:S(2)}) collective-permute-start(f32[64,256]{1,0:T(8,128)} %get-tuple-element.9), channel_id=1, source_target_pairs={{0,2},{1,3},{2,0},{3,1},{4,6},{5,7},{6,4},{7,5},{8,10},{9,11},{10,... | collective-permute-start | bytes 196616 | tf_op jit(solution)/shard_map/ppermute | solution.py:28
  30.7 4.3 %collective-permute-start.5 = (f32[64,256]{1,0:T(8,128)}, f32[64,256]{1,0:T(8,128)S(1)}, u32[]{:S(2)}, u32[]{:S(2)}) collective-permute-start(f32[64,256]{1,0:T(8,128)} %get-tuple-element.9), channel_id=1, source_target_pairs={{0,3},{1,0},{2,1},{3,2},{4,7},{5,4},{6,5},{7,6},{8,11},{9,8},{10,9... | collective-permute-start | bytes 196616 | tf_op jit(solution)/shard_map/ppermute | solution.py:28
  35.0 0.7 copy-start.3
  110.2 7.4 %collective-permute-start.6 = (f32[16,256]{1,0:T(8,128)}, f32[16,256]{1,0:T(8,128)S(1)}, u32[]{:S(2)}, u32[]{:S(2)}) collective-permute-start(f32[16,256]{1,0:T(8,128)} %get-tuple-element.10), channel_id=1, source_target_pairs={{0,4},{4,8},{8,12},{12,16},{16,20},{20,24},{24,28},{28,32},{32,36}... | collective-permute-start | bytes 49160 | tf_op jit(solution)/shard_map/ppermute | solution.py:17
  117.7 14.6 %copy-start.1 = (f32[4,256,256]{2,1,0:T(8,128)S(1)}, f32[4,256,256]{2,1,0:T(8,128)}, u32[]{:S(2)}) copy-start(f32[4,256,256]{2,1,0:T(8,128)} %param.12) | copy-start | bytes 3145732
  126.1 7.2 %copy-start.6 = (f32[16,16,256]{2,1,0:T(8,128)S(1)}, f32[16,16,256]{2,1,0:T(8,128)}, u32[]{:S(2)}) copy-start(f32[16,16,256]{2,1,0:T(8,128)} %get-tuple-element.6) | copy-start | bytes 786436
  126.9 5.3 %collective-permute-start.7 = (f32[16,256]{1,0:T(8,128)S(1)}, f32[16,256]{1,0:T(8,128)S(1)}, u32[]{:S(2)}, u32[]{:S(2)}) collective-permute-start(f32[16,256]{1,0:T(8,128)S(1)} %slice_bitcast_fusion), channel_id=1, source_target_pairs={{4,0},{8,4},{12,8},{16,12},{20,16},{24,20},{28,24},{32,28},{36,32}... | collective-permute-start | bytes 49160 | tf_op jit(solution)/shard_map/ppermute | solution.py:17
  164.9 9.1 %collective-permute-start.8 = (f32[16,256]{1,0:T(8,128)}, f32[16,256]{1,0:T(8,128)S(1)}, u32[]{:S(2)}, u32[]{:S(2)}) collective-permute-start(f32[16,256]{1,0:T(8,128)} %shard_map.90), channel_id=1, source_target_pairs={{4,0},{8,4},{12,8},{16,12},{20,16},{24,20},{28,24},{32,28},{36,32}... | collective-permute-start | bytes 49160 | tf_op jit(solution)/shard_map/ppermute | solution.py:17
  174.1 0.6 copy-start.8

commit v10 on v8

--- a/solution.py
+++ b/solution.py
@@ -35,7 +35,7 @@
     return jnp.dot(first_factor, second_factor, precision=lax.Precision.HIGHEST)
 
 
-def greet_partners(index, peers, other, rounds):
+def greet_partners(index, peers, other, rounds, columns=1):
     barrier = pltpu.get_barrier_semaphore()
     partners = 0
     for r in range(rounds):
@@ -48,6 +48,10 @@
                                     device_id_type=pl.DeviceIdType.MESH)
 
             partners = partners + jnp.where(exists, 1, 0)
+    for shift in range(1, columns):
+        pl.semaphore_signal(barrier, inc=1, device_id=(index, lax.rem(other + shift, columns)),
+                            device_id_type=pl.DeviceIdType.MESH)
+        partners = partners + 1
     pl.semaphore_wait(barrier, partners)
 
 
@@ -56,19 +60,40 @@
                    preferred_element_type=jnp.float32)
 
 
-def maps_kernel(ahead_ref, behind_ref, records_ref, ahead_out, behind_out, records_out,
-                ahead_in, behind_in, sums, sum_in, sems, sum_sems, *, axis):
+def share_rows(full, slot, mine, index, other, columns, sems):
+    copies = []
+    for shift in range(1, columns):
+        copy = pltpu.make_async_remote_copy(
+            src_ref=full.at[slot, mine], dst_ref=full.at[slot, mine],
+            send_sem=sems.at[0, shift - 1], recv_sem=sems.at[1, shift - 1],
+            device_id=(index, lax.rem(other + shift, columns)),
+            device_id_type=pl.DeviceIdType.MESH)
+        copy.start()
+        copies.append(copy)
+    for copy in copies:
+        copy.wait_recv()
+    for copy in copies:
+        copy.wait_send()
+
+
+def maps_kernel(ahead_ref, behind_ref, records_ref, behind_out, records_out, fulls,
+                ahead_in, behind_in, sums, sum_in, sems, sum_sems, col_sems, *, axis):
     peers, index = (lax.axis_size(axis), lax.axis_index(axis))
     other = lax.axis_index("col")
-    rounds = ahead_out.shape[0]
-    greet_partners(index, peers, other, rounds)
-    ahead_out[0] = ahead_ref[...]
-    behind_out[0] = behind_ref[...]
+    columns = lax.axis_size("col")
+    rounds = behind_out.shape[0]
+    share = ahead_ref.shape[0] // columns
+    mine = pl.ds(pl.multiple_of(other * share, share), share)
+    greet_partners(index, peers, other, rounds, columns)
+    fulls[0, 0] = ahead_ref[...]
+    fulls[1, 0] = behind_ref[...]
+    ahead_full = fulls.at[0]
+    behind_full = fulls.at[1]
     for r in range(rounds):
         distance = 1 << r
         up, has_up = index + distance, index + distance < peers
         down, has_down = index - distance, index - distance >= 0
-        own_ahead = ahead_ref if r == 0 else ahead_out.at[r]
+        own_ahead = ahead_full.at[r]
         own_sum = records_ref if r == 0 else sums.at[r]
         sum_copy = pltpu.make_async_remote_copy(
             src_ref=own_sum, dst_ref=sum_in.at[r], send_sem=sum_sems.at[0, r],
@@ -94,13 +119,13 @@
                 sum_copy.wait_send()
 
             break
-        own_behind = behind_ref if r == 0 else behind_out.at[r]
+        own_behind = behind_full.at[r]
         ahead_copy = pltpu.make_async_remote_copy(
-            src_ref=own_ahead, dst_ref=ahead_in.at[r], send_sem=sems.at[0, 0, r],
+            src_ref=own_ahead.at[mine], dst_ref=ahead_in.at[r], send_sem=sems.at[0, 0, r],
             recv_sem=sems.at[0, 1, r], device_id=(up, other),
             device_id_type=pl.DeviceIdType.MESH)
         behind_copy = pltpu.make_async_remote_copy(
-            src_ref=own_behind, dst_ref=behind_in.at[r], send_sem=sems.at[1, 0, r],
+            src_ref=own_behind.at[mine], dst_ref=behind_in.at[r], send_sem=sems.at[1, 0, r],
             recv_sem=sems.at[1, 1, r], device_id=(down, other),
             device_id_type=pl.DeviceIdType.MESH)
 
@@ -124,20 +149,22 @@
         @pl.when(has_down)
         def _():
             ahead_copy.wait_recv()
-            ahead_out[r + 1] = exact_dot(ahead_in[r], own_ahead[...])
+            ahead_full[r + 1, mine] = exact_dot(ahead_in[r], own_ahead[...])
+            share_rows(ahead_full, r + 1, mine, index, other, columns, col_sems.at[0, r])
 
         @pl.when(jnp.logical_not(has_down))
         def _():
-            ahead_out[r + 1] = own_ahead[...]
+            ahead_full[r + 1] = own_ahead[...]
 
         @pl.when(has_up)
         def _():
             behind_copy.wait_recv()
-            behind_out[r + 1] = exact_dot(behind_in[r], own_behind[...])
+            behind_full[r + 1, mine] = exact_dot(behind_in[r], own_behind[...])
+            share_rows(behind_full, r + 1, mine, index, other, columns, col_sems.at[1, r])
 
         @pl.when(jnp.logical_not(has_up))
         def _():
-            behind_out[r + 1] = own_behind[...]
+            behind_full[r + 1] = own_behind[...]
 
         @pl.when(has_up)
         def _():
@@ -148,27 +175,31 @@
         def _():
             behind_copy.wait_send()
 
+    behind_out[...] = behind_full[...]
     records_out[...] = sums[rounds]
 
 
 def doubling_maps(ahead, behind, records, axis, collective_id):
     peers = lax.axis_size(axis)
+    columns = lax.axis_size("col")
     rounds = max(1, (peers - 1).bit_length())
     states = ahead.shape[0]
     vmem = pl.BlockSpec(memory_space=pltpu.VMEM)
     stack = jax.ShapeDtypeStruct((rounds, states, states), jnp.float32)
     return pl.pallas_call(
         functools.partial(maps_kernel, axis=axis),
-        out_shape=(stack, stack, jax.ShapeDtypeStruct(records.shape, jnp.float32)),
+        out_shape=(stack, jax.ShapeDtypeStruct(records.shape, jnp.float32)),
         in_specs=[vmem, vmem, vmem],
-        out_specs=(vmem, vmem, vmem),
+        out_specs=(vmem, vmem),
         scratch_shapes=[
-            pltpu.VMEM((max(1, rounds - 1), states, states), jnp.float32),
-            pltpu.VMEM((max(1, rounds - 1), states, states), jnp.float32),
+            pltpu.VMEM((2, rounds, states, states), jnp.float32),
+            pltpu.VMEM((max(1, rounds - 1), states // columns, states), jnp.float32),
+            pltpu.VMEM((max(1, rounds - 1), states // columns, states), jnp.float32),
             pltpu.VMEM((rounds + 1,) + records.shape, jnp.float32),
             pltpu.VMEM((rounds,) + records.shape, jnp.float32),
             pltpu.SemaphoreType.DMA((2, 2, max(1, rounds - 1))),
             pltpu.SemaphoreType.DMA((2, rounds)),
+            pltpu.SemaphoreType.DMA((2, max(1, rounds - 1), 2, max(1, columns - 1))),
         ],
         compiler_params=pltpu.CompilerParams(collective_id=collective_id, has_side_effects=True),
     )(ahead, behind, records)
@@ -404,7 +435,7 @@
         accurate_matmul_result(initial_mean[None, :], whole_matrix) + block_records,
         block_records,
     )
-    _, backward_maps, ending_records = doubling_maps(
+    backward_maps, ending_records = doubling_maps(
         jnp.where(first_block, jnp.zeros_like(whole_matrix), whole_matrix),
         whole_back,
         folded_records,

time: 183 us -> 189 us (1.033)
  starting transfers between devices: 21.9 us -> 32.5 us
  Pallas kernels: 131 us -> 127 us
    ppermute x3, starting transfers between devices: 13.1 us -> 23.7 us  [passed_along(): return lax.ppermute(block, axis, route)]
    pallas_call x1, Pallas kernels: 75.1 us -> 69.9 us  [doubling_maps(): pl.pallas_call(functools.partial(maps_kernel, axis=axis), out_shape=(stac...]
where the time goes in v10:
time: 189 us
  Pallas kernels  127 us (67%)
  starting transfers between devices  32.5 us (17%)
  local copies, waits for them, and re-layouts  11.7 us (6%)
  other arithmetic  7.98 us (4%)
  waiting for transfers between devices  5.5 us (3%)
  matrix products  3.7 us (2%)
    pallas_call x1, Pallas kernels, doubling_maps(): pl.pallas_call(functools.partial(maps_kernel, axis=axis), out_shape=(stac...  69.9 us
    pallas_call x1, Pallas kernels, doubling_records(): pl.pallas_call(functools.partial(records_kernel, axis=axis, reverse=rever...  26 us
    ppermute x3, starting transfers between devices, passed_along(): return lax.ppermute(block, axis, route)  23.7 us
    pallas_call x3, Pallas kernels, recurrence(): pl.pallas_call(functools.partial(recurrence_kernel, steps=steps, reverse=...  21.4 us
    pallas_call x1, Pallas kernels, paired_maps(): pl.pallas_call(functools.partial(paired_kernel, steps=ahead_source.shape[...  9.12 us
    ppermute x6, starting transfers between devices, gathered_rows(): lax.ppermute(part, axis, [(i, (i + shift) % peers) for i in range(peers)])  8.76 us
    ppermute x3, waiting for transfers between devices, passed_along(): return lax.ppermute(block, axis, route)  5.28 us
  transfers between devices with their start and end apart: 9, of which 3 were waited for; matrix products, arithmetic and copies ran while one was open for 3% of the time, Pallas kernels for 0%

profile of v10, /device:TPU:1, one launch (start us, length us, event | category | flops | bytes accessed | tf_op | source)
XLA Modules:
  0.0 188.8 jit_solution(9327481912258158219)
XLA Ops:
  0.6 0.0 copy-start
  0.6 0.0 copy-start.5
  0.7 0.2 fusion.9
  0.9 1.2 fusion.5
  2.1 1.1 multiply_add_fusion.1
  3.2 0.0 copy-done
  3.2 0.0 copy-done.5
  3.2 1.4 fusion
  4.6 0.1 pad_maximum_fusion
  4.7 1.5 copy.10
  6.2 0.0 copy-start.4
  6.2 1.6 copy.11
  7.9 0.6 concatenate.12.ahead_start_ref
  8.5 0.0 copy-done.9
  8.5 0.0 copy-done.11
  8.5 0.6 fusion.17
  9.1 0.1 fusion.11
  9.2 0.0 copy-done.7
  9.2 1.1 fusion.1.refs_5_
  10.2 0.0 copy-start.2
  10.2 1.2 concatenate.14.ahead_source_ref
  11.5 0.0 copy-done.4
  11.5 1.2 concatenate.13.behind_table_ref.refs_2_
  12.6 9.1 %shard_map.86 = (f32[80,256]{1,0:T(8,128)}, f32[64,256]{1,0:T(8,128)}) custom-call(s32[16]{0:T(128)} %get-tuple-element.19.ahead_pick_ref.refs_0_, s32[16]{0:T(128)} %get-tuple-element.20.behind_pick_ref.refs_0_, f32[80,256]{1,0:T(8,128)} %concatenate.12.ahead_start_ref, f32[64,256]{1,0:T(8,128)} %copy-done.4, f32[8,256,256]{2,1,0:T(8,128)} %bitcast.42, ...), custom_call_target="tpu_custom_call" | custom-call | tf_op jit(solution)/shard_map/pallas_call | solution.py:363
  21.8 0.0 copy-done.2
  21.8 0.9 fusion.16
  22.7 2.2 %collective-permute-start = (f32[64,256]{1,0:T(8,128)S(1)}, f32[64,256]{1,0:T(8,128)S(1)}, u32[]{:S(2)}, u32[]{:S(2)}) collective-permute-start(f32[64,256]{1,0:T(8,128)S(1)} %get-tuple-element.14), channel_id=1, source_target_pairs={{0,1},{1,2},{2,3},{3,0},{4,5},{5,6},{6,7},{7,4},{8,9},{9,10},{10,1... | collective-permute-start | bytes 196616 | tf_op jit(solution)/shard_map/ppermute | solution.py:28
  24.9 2.6 %collective-permute-start.1 = (f32[64,256]{1,0:T(8,128)S(1)}, f32[64,256]{1,0:T(8,128)S(1)}, u32[]{:S(2)}, u32[]{:S(2)}) collective-permute-start(f32[64,256]{1,0:T(8,128)S(1)} %get-tuple-element.14), channel_id=1, source_target_pairs={{0,2},{1,3},{2,0},{3,1},{4,6},{5,7},{6,4},{7,5},{8,10},{9,11},{10,... | collective-permute-start | bytes 196616 | tf_op jit(solution)/shard_map/ppermute | solution.py:28
  27.5 1.1 collective-permute-start.2
  28.6 0.4 collective-permute-start.3
  28.9 0.8 collective-permute-start.4
  29.8 0.9 constant_dynamic-update-slice_fusion.3
  30.6 0.0 collective-permute-done
  30.6 1.7 collective-permute-start.5
  32.3 0.0 collective-permute-done.1
  32.3 0.0 collective-permute-done.2
  32.4 0.0 copy-done.10
  32.4 0.2 fusion.18
  32.6 0.8 broadcast_select_fusion.ahead_ref
  33.4 1.3 add_select_fusion.records_ref
  34.7 0.0 collective-permute-done.3
  34.7 0.0 collective-permute-done.4
  34.7 0.2 collective-permute-done.5
  34.9 0.0 copy-start.3
  34.9 0.7 copy-done.3
  35.6 69.9 %shard_map.87 = (f32[6,256,256]{2,1,0:T(8,128)}, f32[16,256]{1,0:T(8,128)}) custom-call(f32[256,256]{1,0:T(8,128)} %broadcast_select_fusion.ahead_ref, f32[256,256]{1,0:T(8,128)} %copy-done.3, f32[16,256]{1,0:T(8,128)} %add_select_fusion.records_ref), custom_call_target="tpu_custom_call" | custom-call | tf_op jit(solution)/shard_map/pallas_call | solution.py:189
  105.6 17.3 %collective-permute-start.6 = (f32[16,256]{1,0:T(8,128)}, f32[16,256]{1,0:T(8,128)S(1)}, u32[]{:S(2)}, u32[]{:S(2)}) collective-permute-start(f32[16,256]{1,0:T(8,128)} %get-tuple-element.10), channel_id=1, source_target_pairs={{0,4},{4,8},{8,12},{12,16},{16,20},{20,24},{24,28},{28,32},{32,36}... | collective-permute-start | bytes 49160 | tf_op jit(solution)/shard_map/ppermute | solution.py:17
  122.9 1.3 multiply_add_fusion.refs_4_
  124.2 0.0 collective-permute-done.6
  124.2 0.6 broadcast_select_fusion.1.refs_2_
  124.9 7.8 %shard_map.88 = (f32[16,16,256]{2,1,0:T(8,128)}, f32[16,16,256]{2,1,0:T(8,128)}) custom-call(s32[16]{0:T(128)} %get-tuple-element.19.ahead_pick_ref.refs_0_, s32[16]{0:T(128)} %refs_1_.1, f32[16,256]{1,0:T(8,128)} %broadcast_select_fusion.1.refs_2_, f32[8,256,256]{2,1,0:T(8,128)} %bitcast.43, f32[4,256,256]{2,1,0:T(8,128)} %multiply_add_fusion.refs_4_, ...), custom_call_target="tpu_custom_call" | custom-call | tf_op jit(solution)/shard_map/pallas_call | solution.py:328
  132.7 0.8 slice_bitcast_fusion
  133.5 1.9 %collective-permute-start.7 = (f32[16,256]{1,0:T(8,128)S(1)}, f32[16,256]{1,0:T(8,128)S(1)}, u32[]{:S(2)}, u32[]{:S(2)}) collective-permute-start(f32[16,256]{1,0:T(8,128)S(1)} %slice_bitcast_fusion), channel_id=1, source_target_pairs={{4,0},{8,4},{12,8},{16,12},{20,16},{24,20},{28,24},{32,28},{36,32}... | collective-permute-start | bytes 49160 | tf_op jit(solution)/shard_map/ppermute | solution.py:17
  135.4 1.0 slice.14
  136.3 2.4 %collective-permute-done.7 = f32[16,256]{1,0:T(8,128)S(1)} collective-permute-done((f32[16,256]{1,0:T(8,128)S(1)}, f32[16,256]{1,0:T(8,128)S(1)}, u32[]{:S(2)}, u32[]{:S(2)}) %collective-permute-start.7) | collective-permute-done | bytes 16416 | tf_op jit(solution)/shard_map/ppermute | solution.py:17
  138.8 1.1 fusion.2
  139.9 0.7 sub.94.refs_3_
  140.6 0.6 broadcast_in_dim.11.refs_1_
  141.2 6.7 %shard_map.89.records_ref = f32[16,256]{1,0:T(8,128)} custom-call(s32[16]{0:T(128)} %get-tuple-element.20.behind_pick_ref.refs_0_, f32[16,256]{1,0:T(8,128)} %broadcast_in_dim.11.refs_1_, f32[5,256,256]{2,1,0:T(8,128)} %concatenate.13.behind_table_ref.refs_2_, f32[16,16,256]{2,1,0:T(8,128)} %sub.94.refs_3_), custom_call_target="tpu_custom_call" | custom-call | tf_op jit(solution)/shard_map/pallas_call | solution.py:328
  147.9 26.0 %shard_map.90 = f32[16,256]{1,0:T(8,128)} custom-call(f32[6,256,256]{2,1,0:T(8,128)} %get-tuple-element.12.maps_ref, f32[16,256]{1,0:T(8,128)} %shard_map.89.records_ref), custom_call_target="tpu_custom_call" | custom-call | tf_op jit(solution)/shard_map/pallas_call | solution.py:250
  174.0 4.5 %collective-permute-start.8 = (f32[16,256]{1,0:T(8,128)}, f32[16,256]{1,0:T(8,128)S(1)}, u32[]{:S(2)}, u32[]{:S(2)}) collective-permute-start(f32[16,256]{1,0:T(8,128)} %shard_map.90), channel_id=1, source_target_pairs={{4,0},{8,4},{12,8},{16,12},{20,16},{24,20},{28,24},{32,28},{36,32}... | collective-permute-start | bytes 49160 | tf_op jit(solution)/shard_map/ppermute | solution.py:17
  178.5 2.8 %collective-permute-done.8.refs_1_ = f32[16,256]{1,0:T(8,128)S(1)} collective-permute-done((f32[16,256]{1,0:T(8,128)}, f32[16,256]{1,0:T(8,128)S(1)}, u32[]{:S(2)}, u32[]{:S(2)}) %collective-permute-start.8) | collective-permute-done | bytes 16416 | tf_op jit(solution)/shard_map/ppermute | solution.py:17
  181.3 0.6 copy-done.8
  181.9 6.9 %shard_map.91 = f32[16,16,256]{2,1,0:T(8,128)} custom-call(s32[16]{0:T(128)} %get-tuple-element.20.behind_pick_ref.refs_0_, f32[16,256]{1,0:T(8,128)} %copy-done.8, f32[5,256,256]{2,1,0:T(8,128)} %concatenate.13.behind_table_ref.refs_2_, f32[16,16,256]{2,1,0:T(8,128)} %sub.94.refs_3_), custom_call_target="tpu_custom_call" | custom-call | tf_op jit(solution)/shard_map/pallas_call | solution.py:328
  (22 shorter events, 0.2 us)
Async XLA Ops:
  0.6 2.5 %copy-start = (f32[4,256,256]{2,1,0:T(8,128)S(1)}, f32[4,256,256]{2,1,0:T(8,128)}, u32[]{:S(2)}) copy-start(f32[4,256,256]{2,1,0:T(8,128)} %param.11) | copy-start | bytes 3145732
  0.6 2.5 %copy-start.5 = (f32[4,256]{1,0:T(4,128)S(1)}, f32[4,256]{1,0:T(4,128)}, u32[]{:S(2)}) copy-start(f32[4,256]{1,0:T(4,128)} %param.10) | copy-start | bytes 12292
  6.2 2.3 %copy-start.9 = (s32[16]{0:T(128)S(1)}, s32[16]{0:T(128)}, u32[]{:S(2)}) copy-start(s32[16]{0:T(128)} %refs_1_.1) | copy-start | bytes 196
  6.2 2.3 %copy-start.11 = (s32[16]{0:T(128)S(1)}, s32[16]{0:T(128)}, u32[]{:S(2)}) copy-start(s32[16]{0:T(128)} %param.9) | copy-start | bytes 196
  6.2 3.0 %copy-start.7 = (f32[16,16,256]{2,1,0:T(8,128)S(1)}, f32[16,16,256]{2,1,0:T(8,128)}, u32[]{:S(2)}) copy-start(f32[16,16,256]{2,1,0:T(8,128)} %param.7) | copy-start | bytes 786436
  6.2 5.3 %copy-start.4 = (f32[64,256]{1,0:T(8,128)}, f32[64,256]{1,0:T(8,128)S(1)}, u32[]{:S(2)}) copy-start(f32[64,256]{1,0:T(8,128)S(1)} %constant_dynamic-slice_fusion.behind_start_ref) | copy-start | bytes 196612
  10.2 11.5 %copy-start.2 = (f32[16,16,256]{2,1,0:T(8,128)}, f32[16,16,256]{2,1,0:T(8,128)S(1)}, u32[]{:S(2)}) copy-start(f32[16,16,256]{2,1,0:T(8,128)S(1)} %fusion.1.refs_5_) | copy-start | bytes 786436
  12.6 19.7 %copy-start.10 = (f32[256]{0:T(256)S(1)}, f32[256]{0:T(256)}, u32[]{:S(2)}) copy-start(f32[256]{0:T(256)} %param.13) | copy-start | bytes 3076
  22.7 8.0 %collective-permute-start = (f32[64,256]{1,0:T(8,128)S(1)}, f32[64,256]{1,0:T(8,128)S(1)}, u32[]{:S(2)}, u32[]{:S(2)}) collective-permute-start(f32[64,256]{1,0:T(8,128)S(1)} %get-tuple-element.14), channel_id=1, source_target_pairs={{0,1},{1,2},{2,3},{3,0},{4,5},{5,6},{6,7},{7,4},{8,9},{9,10},{10,1... | collective-permute-start | bytes 196616 | tf_op jit(solution)/shard_map/ppermute | solution.py:28
  24.9 7.5 %collective-permute-start.1 = (f32[64,256]{1,0:T(8,128)S(1)}, f32[64,256]{1,0:T(8,128)S(1)}, u32[]{:S(2)}, u32[]{:S(2)}) collective-permute-start(f32[64,256]{1,0:T(8,128)S(1)} %get-tuple-element.14), channel_id=1, source_target_pairs={{0,2},{1,3},{2,0},{3,1},{4,6},{5,7},{6,4},{7,5},{8,10},{9,11},{10,... | collective-permute-start | bytes 196616 | tf_op jit(solution)/shard_map/ppermute | solution.py:28
  27.5 4.9 %collective-permute-start.2 = (f32[64,256]{1,0:T(8,128)S(1)}, f32[64,256]{1,0:T(8,128)S(1)}, u32[]{:S(2)}, u32[]{:S(2)}) collective-permute-start(f32[64,256]{1,0:T(8,128)S(1)} %get-tuple-element.14), channel_id=1, source_target_pairs={{0,3},{1,0},{2,1},{3,2},{4,7},{5,4},{6,5},{7,6},{8,11},{9,8},{10,9... | collective-permute-start | bytes 196616 | tf_op jit(solution)/shard_map/ppermute | solution.py:28
  28.6 6.1 %collective-permute-start.3 = (f32[64,256]{1,0:T(8,128)}, f32[64,256]{1,0:T(8,128)S(1)}, u32[]{:S(2)}, u32[]{:S(2)}) collective-permute-start(f32[64,256]{1,0:T(8,128)} %get-tuple-element.9), channel_id=1, source_target_pairs={{0,1},{1,2},{2,3},{3,0},{4,5},{5,6},{6,7},{7,4},{8,9},{9,10},{10,1... | collective-permute-start | bytes 196616 | tf_op jit(solution)/shard_map/ppermute | solution.py:28
  28.9 5.7 %collective-permute-start.4 = (f32[64,256]{1,0:T(8,128)}, f32[64,256]{1,0:T(8,128)S(1)}, u32[]{:S(2)}, u32[]{:S(2)}) collective-permute-start(f32[64,256]{1,0:T(8,128)} %get-tuple-element.9), channel_id=1, source_target_pairs={{0,2},{1,3},{2,0},{3,1},{4,6},{5,7},{6,4},{7,5},{8,10},{9,11},{10,... | collective-permute-start | bytes 196616 | tf_op jit(solution)/shard_map/ppermute | solution.py:28
  30.6 4.3 %collective-permute-start.5 = (f32[64,256]{1,0:T(8,128)}, f32[64,256]{1,0:T(8,128)S(1)}, u32[]{:S(2)}, u32[]{:S(2)}) collective-permute-start(f32[64,256]{1,0:T(8,128)} %get-tuple-element.9), channel_id=1, source_target_pairs={{0,3},{1,0},{2,1},{3,2},{4,7},{5,4},{6,5},{7,6},{8,11},{9,8},{10,9... | collective-permute-start | bytes 196616 | tf_op jit(solution)/shard_map/ppermute | solution.py:28
  34.9 0.7 copy-start.3
  105.6 18.7 %collective-permute-start.6 = (f32[16,256]{1,0:T(8,128)}, f32[16,256]{1,0:T(8,128)S(1)}, u32[]{:S(2)}, u32[]{:S(2)}) collective-permute-start(f32[16,256]{1,0:T(8,128)} %get-tuple-element.10), channel_id=1, source_target_pairs={{0,4},{4,8},{8,12},{12,16},{16,20},{20,24},{24,28},{28,32},{32,36}... | collective-permute-start | bytes 49160 | tf_op jit(solution)/shard_map/ppermute | solution.py:17
  124.2 14.5 %copy-start.1 = (f32[4,256,256]{2,1,0:T(8,128)S(1)}, f32[4,256,256]{2,1,0:T(8,128)}, u32[]{:S(2)}) copy-start(f32[4,256,256]{2,1,0:T(8,128)} %param.12) | copy-start | bytes 3145732
  132.7 7.2 %copy-start.6 = (f32[16,16,256]{2,1,0:T(8,128)S(1)}, f32[16,16,256]{2,1,0:T(8,128)}, u32[]{:S(2)}) copy-start(f32[16,16,256]{2,1,0:T(8,128)} %get-tuple-element.6) | copy-start | bytes 786436
  133.5 5.3 %collective-permute-start.7 = (f32[16,256]{1,0:T(8,128)S(1)}, f32[16,256]{1,0:T(8,128)S(1)}, u32[]{:S(2)}, u32[]{:S(2)}) collective-permute-start(f32[16,256]{1,0:T(8,128)S(1)} %slice_bitcast_fusion), channel_id=1, source_target_pairs={{4,0},{8,4},{12,8},{16,12},{20,16},{24,20},{28,24},{32,28},{36,32}... | collective-permute-start | bytes 49160 | tf_op jit(solution)/shard_map/ppermute | solution.py:17
  174.0 7.4 %collective-permute-start.8 = (f32[16,256]{1,0:T(8,128)}, f32[16,256]{1,0:T(8,128)S(1)}, u32[]{:S(2)}, u32[]{:S(2)}) collective-permute-start(f32[16,256]{1,0:T(8,128)} %shard_map.90), channel_id=1, source_target_pairs={{4,0},{8,4},{12,8},{16,12},{20,16},{24,20},{28,24},{32,28},{36,32}... | collective-permute-start | bytes 49160 | tf_op jit(solution)/shard_map/ppermute | solution.py:17
  181.3 0.6 copy-start.8

commit v11 on v8

--- a/solution.py
+++ b/solution.py
@@ -64,6 +64,7 @@
     greet_partners(index, peers, other, rounds)
     ahead_out[0] = ahead_ref[...]
     behind_out[0] = behind_ref[...]
+    pending = []
     for r in range(rounds):
         distance = 1 << r
         up, has_up = index + distance, index + distance < peers
@@ -89,10 +90,7 @@
             def _():
                 sums[r + 1] = own_sum[...]
 
-            @pl.when(has_up)
-            def _():
-                sum_copy.wait_send()
-
+            pending.append((has_up, sum_copy))
             break
         own_behind = behind_ref if r == 0 else behind_out.at[r]
         ahead_copy = pltpu.make_async_remote_copy(
@@ -139,14 +137,12 @@
         def _():
             behind_out[r + 1] = own_behind[...]
 
-        @pl.when(has_up)
-        def _():
-            ahead_copy.wait_send()
-            sum_copy.wait_send()
-
-        @pl.when(has_down)
-        def _():
-            behind_copy.wait_send()
+        pending += [(has_up, ahead_copy), (has_up, sum_copy), (has_down, behind_copy)]
+
+    for sent, copy in pending:
+        @pl.when(sent)
+        def _():
+            copy.wait_send()
 
     records_out[...] = sums[rounds]
 
@@ -179,6 +175,7 @@
     other = lax.axis_index("col")
     rounds = maps_ref.shape[0]
     greet_partners(index, peers, other, rounds)
+    pending = []
     for r in range(rounds):
         distance = 1 << r
         if reverse:
@@ -206,9 +203,12 @@
         def _():
             sums[r + 1] = own_sum[...]
 
-        @pl.when(sends)
-        def _():
-            sum_copy.wait_send()
+        pending.append((sends, sum_copy))
+
+    for sent, copy in pending:
+        @pl.when(sent)
+        def _():
+            copy.wait_send()
 
     out_ref[...] = sums[rounds]
 

time: 183 us -> 181 us (0.989)
  Pallas kernels: 131 us -> 128 us
  starting transfers between devices: 21.9 us -> 23.9 us
    ppermute x3, starting transfers between devices: 13.1 us -> 15.2 us  [passed_along(): return lax.ppermute(block, axis, route)]
where the time goes in v11:
time: 181 us; the launch traced here: 180 us
  Pallas kernels  128 us (71%)
  starting transfers between devices  23.9 us (13%)
  local copies, waits for them, and re-layouts  11.7 us (6%)
  other arithmetic  8 us (4%)
  waiting for transfers between devices  3.74 us (2%)
  matrix products  3.7 us (2%)
    pallas_call x1, Pallas kernels, doubling_maps(): pl.pallas_call(functools.partial(maps_kernel, axis=axis), out_shape=(stac...  73.6 us
    pallas_call x1, Pallas kernels, doubling_records(): pl.pallas_call(functools.partial(records_kernel, axis=axis, reverse=rever...  24.3 us
    pallas_call x3, Pallas kernels, recurrence(): pl.pallas_call(functools.partial(recurrence_kernel, steps=steps, reverse=...  21.4 us
    ppermute x3, starting transfers between devices, passed_along(): return lax.ppermute(block, axis, route)  15.2 us
    pallas_call x1, Pallas kernels, paired_maps(): pl.pallas_call(functools.partial(paired_kernel, steps=ahead_source.shape[...  9.12 us
    ppermute x6, starting transfers between devices, gathered_rows(): lax.ppermute(part, axis, [(i, (i + shift) % peers) for i in range(peers)])  8.76 us
  transfers between devices with their start and end apart: 9, of which 3 were waited for; matrix products, arithmetic and copies ran while one was open for 3% of the time, Pallas kernels for 0%

profile of v11, /device:TPU:1, one launch (start us, length us, event | category | flops | bytes accessed | tf_op | source)
XLA Modules:
  0.0 180.5 jit_solution(15419257034633285296)
XLA Ops:
  0.6 0.0 copy-start
  0.6 0.0 copy-start.5
  0.7 0.2 fusion.9
  0.9 1.2 fusion.5
  2.1 1.1 multiply_add_fusion.1
  3.2 0.0 copy-done
  3.2 0.0 copy-done.5
  3.2 1.4 fusion
  4.6 0.1 pad_maximum_fusion
  4.7 1.5 copy.10
  6.2 0.0 copy-start.4
  6.2 1.6 copy.11
  7.9 0.6 concatenate.12.ahead_start_ref
  8.5 0.0 copy-done.9
  8.5 0.0 copy-done.11
  8.5 0.6 fusion.17
  9.1 0.1 fusion.11
  9.2 0.0 copy-done.7
  9.2 1.1 fusion.1.refs_5_
  10.3 0.0 copy-start.2
  10.3 1.2 concatenate.14.ahead_source_ref
  11.5 0.0 copy-done.4
  11.5 1.2 concatenate.13.behind_table_ref.refs_2_
  12.7 9.1 %shard_map.86 = (f32[80,256]{1,0:T(8,128)}, f32[64,256]{1,0:T(8,128)}) custom-call(s32[16]{0:T(128)} %get-tuple-element.19.ahead_pick_ref.refs_0_, s32[16]{0:T(128)} %get-tuple-element.20.behind_pick_ref.refs_0_, f32[80,256]{1,0:T(8,128)} %concatenate.12.ahead_start_ref, f32[64,256]{1,0:T(8,128)} %copy-done.4, f32[8,256,256]{2,1,0:T(8,128)} %bitcast.42, ...), custom_call_target="tpu_custom_call" | custom-call | tf_op jit(solution)/shard_map/pallas_call | solution.py:332
  21.8 0.0 copy-done.2
  21.9 0.9 fusion.16
  22.7 2.2 %collective-permute-start = (f32[64,256]{1,0:T(8,128)S(1)}, f32[64,256]{1,0:T(8,128)S(1)}, u32[]{:S(2)}, u32[]{:S(2)}) collective-permute-start(f32[64,256]{1,0:T(8,128)S(1)} %get-tuple-element.14), channel_id=1, source_target_pairs={{0,1},{1,2},{2,3},{3,0},{4,5},{5,6},{6,7},{7,4},{8,9},{9,10},{10,1... | collective-permute-start | bytes 196616 | tf_op jit(solution)/shard_map/ppermute | solution.py:28
  24.9 2.6 %collective-permute-start.1 = (f32[64,256]{1,0:T(8,128)S(1)}, f32[64,256]{1,0:T(8,128)S(1)}, u32[]{:S(2)}, u32[]{:S(2)}) collective-permute-start(f32[64,256]{1,0:T(8,128)S(1)} %get-tuple-element.14), channel_id=1, source_target_pairs={{0,2},{1,3},{2,0},{3,1},{4,6},{5,7},{6,4},{7,5},{8,10},{9,11},{10,... | collective-permute-start | bytes 196616 | tf_op jit(solution)/shard_map/ppermute | solution.py:28
  27.5 1.1 collective-permute-start.2
  28.6 0.4 collective-permute-start.3
  29.0 0.8 collective-permute-start.4
  29.8 0.9 constant_dynamic-update-slice_fusion.3
  30.7 0.0 collective-permute-done
  30.7 1.7 collective-permute-start.5
  32.4 0.0 collective-permute-done.1
  32.4 0.0 collective-permute-done.2
  32.4 0.0 copy-done.10
  32.4 0.2 fusion.18
  32.7 0.8 broadcast_select_fusion.ahead_ref
  33.4 1.3 add_select_fusion.records_ref
  34.7 0.0 collective-permute-done.3
  34.7 0.0 collective-permute-done.4
  34.8 0.2 collective-permute-done.5
  35.0 0.0 copy-start.3
  35.0 0.7 copy-done.3
  35.7 73.6 %shard_map.87 = (f32[6,256,256]{2,1,0:T(8,128)}, f32[6,256,256]{2,1,0:T(8,128)}, f32[16,256]{1,0:T(8,128)}) custom-call(f32[256,256]{1,0:T(8,128)} %broadcast_select_fusion.ahead_ref, f32[256,256]{1,0:T(8,128)} %copy-done.3, f32[16,256]{1,0:T(8,128)} %add_select_fusion.records_ref), custom_call_target="tpu_custom_call" | custom-call | tf_op jit(solution)/shard_map/pallas_call | solution.py:156
  109.3 6.2 %collective-permute-start.6 = (f32[16,256]{1,0:T(8,128)}, f32[16,256]{1,0:T(8,128)S(1)}, u32[]{:S(2)}, u32[]{:S(2)}) collective-permute-start(f32[16,256]{1,0:T(8,128)} %get-tuple-element.10), channel_id=1, source_target_pairs={{0,4},{4,8},{8,12},{12,16},{16,20},{20,24},{24,28},{28,32},{32,36}... | collective-permute-start | bytes 49160 | tf_op jit(solution)/shard_map/ppermute | solution.py:17
  115.5 1.3 multiply_add_fusion.refs_4_
  116.8 0.0 collective-permute-done.6
  116.8 0.6 broadcast_select_fusion.1.refs_2_
  117.4 7.8 %shard_map.88 = (f32[16,16,256]{2,1,0:T(8,128)}, f32[16,16,256]{2,1,0:T(8,128)}) custom-call(s32[16]{0:T(128)} %get-tuple-element.19.ahead_pick_ref.refs_0_, s32[16]{0:T(128)} %refs_1_.1, f32[16,256]{1,0:T(8,128)} %broadcast_select_fusion.1.refs_2_, f32[8,256,256]{2,1,0:T(8,128)} %bitcast.43, f32[4,256,256]{2,1,0:T(8,128)} %multiply_add_fusion.refs_4_, ...), custom_call_target="tpu_custom_call" | custom-call | tf_op jit(solution)/shard_map/pallas_call | solution.py:297
  125.3 0.8 slice_bitcast_fusion
  126.1 1.9 %collective-permute-start.7 = (f32[16,256]{1,0:T(8,128)S(1)}, f32[16,256]{1,0:T(8,128)S(1)}, u32[]{:S(2)}, u32[]{:S(2)}) collective-permute-start(f32[16,256]{1,0:T(8,128)S(1)} %slice_bitcast_fusion), channel_id=1, source_target_pairs={{4,0},{8,4},{12,8},{16,12},{20,16},{24,20},{28,24},{32,28},{36,32}... | collective-permute-start | bytes 49160 | tf_op jit(solution)/shard_map/ppermute | solution.py:17
  128.0 1.0 slice.14
  128.9 2.5 %collective-permute-done.7 = f32[16,256]{1,0:T(8,128)S(1)} collective-permute-done((f32[16,256]{1,0:T(8,128)S(1)}, f32[16,256]{1,0:T(8,128)S(1)}, u32[]{:S(2)}, u32[]{:S(2)}) %collective-permute-start.7) | collective-permute-done | bytes 16416 | tf_op jit(solution)/shard_map/ppermute | solution.py:17
  131.4 1.1 fusion.2
  132.5 0.7 sub.94.refs_3_
  133.2 0.6 broadcast_in_dim.11.refs_1_
  133.8 6.7 %shard_map.89.records_ref = f32[16,256]{1,0:T(8,128)} custom-call(s32[16]{0:T(128)} %get-tuple-element.20.behind_pick_ref.refs_0_, f32[16,256]{1,0:T(8,128)} %broadcast_in_dim.11.refs_1_, f32[5,256,256]{2,1,0:T(8,128)} %concatenate.13.behind_table_ref.refs_2_, f32[16,16,256]{2,1,0:T(8,128)} %sub.94.refs_3_), custom_call_target="tpu_custom_call" | custom-call | tf_op jit(solution)/shard_map/pallas_call | solution.py:297
  140.6 24.3 %shard_map.90 = f32[16,256]{1,0:T(8,128)} custom-call(f32[6,256,256]{2,1,0:T(8,128)} %get-tuple-element.12.maps_ref, f32[16,256]{1,0:T(8,128)} %shard_map.89.records_ref), custom_call_target="tpu_custom_call" | custom-call | tf_op jit(solution)/shard_map/pallas_call | solution.py:219
  164.9 7.1 %collective-permute-start.8 = (f32[16,256]{1,0:T(8,128)}, f32[16,256]{1,0:T(8,128)S(1)}, u32[]{:S(2)}, u32[]{:S(2)}) collective-permute-start(f32[16,256]{1,0:T(8,128)} %shard_map.90), channel_id=1, source_target_pairs={{4,0},{8,4},{12,8},{16,12},{20,16},{24,20},{28,24},{32,28},{36,32}... | collective-permute-start | bytes 49160 | tf_op jit(solution)/shard_map/ppermute | solution.py:17
  172.0 1.1 collective-permute-done.8.refs_1_
  173.0 0.6 copy-done.8
  173.6 6.9 %shard_map.91 = f32[16,16,256]{2,1,0:T(8,128)} custom-call(s32[16]{0:T(128)} %get-tuple-element.20.behind_pick_ref.refs_0_, f32[16,256]{1,0:T(8,128)} %copy-done.8, f32[5,256,256]{2,1,0:T(8,128)} %concatenate.13.behind_table_ref.refs_2_, f32[16,16,256]{2,1,0:T(8,128)} %sub.94.refs_3_), custom_call_target="tpu_custom_call" | custom-call | tf_op jit(solution)/shard_map/pallas_call | solution.py:297
  (22 shorter events, 0.2 us)
Async XLA Ops:
  0.6 2.5 %copy-start = (f32[4,256,256]{2,1,0:T(8,128)S(1)}, f32[4,256,256]{2,1,0:T(8,128)}, u32[]{:S(2)}) copy-start(f32[4,256,256]{2,1,0:T(8,128)} %param.11) | copy-start | bytes 3145732
  0.6 2.5 %copy-start.5 = (f32[4,256]{1,0:T(4,128)S(1)}, f32[4,256]{1,0:T(4,128)}, u32[]{:S(2)}) copy-start(f32[4,256]{1,0:T(4,128)} %param.10) | copy-start | bytes 12292
  6.2 2.3 %copy-start.9 = (s32[16]{0:T(128)S(1)}, s32[16]{0:T(128)}, u32[]{:S(2)}) copy-start(s32[16]{0:T(128)} %refs_1_.1) | copy-start | bytes 196
  6.2 2.3 %copy-start.11 = (s32[16]{0:T(128)S(1)}, s32[16]{0:T(128)}, u32[]{:S(2)}) copy-start(s32[16]{0:T(128)} %param.9) | copy-start | bytes 196
  6.2 3.0 %copy-start.7 = (f32[16,16,256]{2,1,0:T(8,128)S(1)}, f32[16,16,256]{2,1,0:T(8,128)}, u32[]{:S(2)}) copy-start(f32[16,16,256]{2,1,0:T(8,128)} %param.7) | copy-start | bytes 786436
  6.2 5.3 %copy-start.4 = (f32[64,256]{1,0:T(8,128)}, f32[64,256]{1,0:T(8,128)S(1)}, u32[]{:S(2)}) copy-start(f32[64,256]{1,0:T(8,128)S(1)} %constant_dynamic-slice_fusion.behind_start_ref) | copy-start | bytes 196612
  10.3 11.6 %copy-start.2 = (f32[16,16,256]{2,1,0:T(8,128)}, f32[16,16,256]{2,1,0:T(8,128)S(1)}, u32[]{:S(2)}) copy-start(f32[16,16,256]{2,1,0:T(8,128)S(1)} %fusion.1.refs_5_) | copy-start | bytes 786436
  12.7 19.7 %copy-start.10 = (f32[256]{0:T(256)S(1)}, f32[256]{0:T(256)}, u32[]{:S(2)}) copy-start(f32[256]{0:T(256)} %param.13) | copy-start | bytes 3076
  22.7 8.0 %collective-permute-start = (f32[64,256]{1,0:T(8,128)S(1)}, f32[64,256]{1,0:T(8,128)S(1)}, u32[]{:S(2)}, u32[]{:S(2)}) collective-permute-start(f32[64,256]{1,0:T(8,128)S(1)} %get-tuple-element.14), channel_id=1, source_target_pairs={{0,1},{1,2},{2,3},{3,0},{4,5},{5,6},{6,7},{7,4},{8,9},{9,10},{10,1... | collective-permute-start | bytes 196616 | tf_op jit(solution)/shard_map/ppermute | solution.py:28
  24.9 7.5 %collective-permute-start.1 = (f32[64,256]{1,0:T(8,128)S(1)}, f32[64,256]{1,0:T(8,128)S(1)}, u32[]{:S(2)}, u32[]{:S(2)}) collective-permute-start(f32[64,256]{1,0:T(8,128)S(1)} %get-tuple-element.14), channel_id=1, source_target_pairs={{0,2},{1,3},{2,0},{3,1},{4,6},{5,7},{6,4},{7,5},{8,10},{9,11},{10,... | collective-permute-start | bytes 196616 | tf_op jit(solution)/shard_map/ppermute | solution.py:28
  27.5 4.9 %collective-permute-start.2 = (f32[64,256]{1,0:T(8,128)S(1)}, f32[64,256]{1,0:T(8,128)S(1)}, u32[]{:S(2)}, u32[]{:S(2)}) collective-permute-start(f32[64,256]{1,0:T(8,128)S(1)} %get-tuple-element.14), channel_id=1, source_target_pairs={{0,3},{1,0},{2,1},{3,2},{4,7},{5,4},{6,5},{7,6},{8,11},{9,8},{10,9... | collective-permute-start | bytes 196616 | tf_op jit(solution)/shard_map/ppermute | solution.py:28
  28.6 6.1 %collective-permute-start.3 = (f32[64,256]{1,0:T(8,128)}, f32[64,256]{1,0:T(8,128)S(1)}, u32[]{:S(2)}, u32[]{:S(2)}) collective-permute-start(f32[64,256]{1,0:T(8,128)} %get-tuple-element.9), channel_id=1, source_target_pairs={{0,1},{1,2},{2,3},{3,0},{4,5},{5,6},{6,7},{7,4},{8,9},{9,10},{10,1... | collective-permute-start | bytes 196616 | tf_op jit(solution)/shard_map/ppermute | solution.py:28
  29.0 5.7 %collective-permute-start.4 = (f32[64,256]{1,0:T(8,128)}, f32[64,256]{1,0:T(8,128)S(1)}, u32[]{:S(2)}, u32[]{:S(2)}) collective-permute-start(f32[64,256]{1,0:T(8,128)} %get-tuple-element.9), channel_id=1, source_target_pairs={{0,2},{1,3},{2,0},{3,1},{4,6},{5,7},{6,4},{7,5},{8,10},{9,11},{10,... | collective-permute-start | bytes 196616 | tf_op jit(solution)/shard_map/ppermute | solution.py:28
  30.7 4.3 %collective-permute-start.5 = (f32[64,256]{1,0:T(8,128)}, f32[64,256]{1,0:T(8,128)S(1)}, u32[]{:S(2)}, u32[]{:S(2)}) collective-permute-start(f32[64,256]{1,0:T(8,128)} %get-tuple-element.9), channel_id=1, source_target_pairs={{0,3},{1,0},{2,1},{3,2},{4,7},{5,4},{6,5},{7,6},{8,11},{9,8},{10,9... | collective-permute-start | bytes 196616 | tf_op jit(solution)/shard_map/ppermute | solution.py:28
  35.0 0.7 copy-start.3
  109.3 7.5 %collective-permute-start.6 = (f32[16,256]{1,0:T(8,128)}, f32[16,256]{1,0:T(8,128)S(1)}, u32[]{:S(2)}, u32[]{:S(2)}) collective-permute-start(f32[16,256]{1,0:T(8,128)} %get-tuple-element.10), channel_id=1, source_target_pairs={{0,4},{4,8},{8,12},{12,16},{16,20},{20,24},{24,28},{28,32},{32,36}... | collective-permute-start | bytes 49160 | tf_op jit(solution)/shard_map/ppermute | solution.py:17
  116.8 14.6 %copy-start.1 = (f32[4,256,256]{2,1,0:T(8,128)S(1)}, f32[4,256,256]{2,1,0:T(8,128)}, u32[]{:S(2)}) copy-start(f32[4,256,256]{2,1,0:T(8,128)} %param.12) | copy-start | bytes 3145732
  125.3 7.2 %copy-start.6 = (f32[16,16,256]{2,1,0:T(8,128)S(1)}, f32[16,16,256]{2,1,0:T(8,128)}, u32[]{:S(2)}) copy-start(f32[16,16,256]{2,1,0:T(8,128)} %get-tuple-element.6) | copy-start | bytes 786436
  126.1 5.3 %collective-permute-start.7 = (f32[16,256]{1,0:T(8,128)S(1)}, f32[16,256]{1,0:T(8,128)S(1)}, u32[]{:S(2)}, u32[]{:S(2)}) collective-permute-start(f32[16,256]{1,0:T(8,128)S(1)} %slice_bitcast_fusion), channel_id=1, source_target_pairs={{4,0},{8,4},{12,8},{16,12},{20,16},{24,20},{28,24},{32,28},{36,32}... | collective-permute-start | bytes 49160 | tf_op jit(solution)/shard_map/ppermute | solution.py:17
  164.9 8.1 %collective-permute-start.8 = (f32[16,256]{1,0:T(8,128)}, f32[16,256]{1,0:T(8,128)S(1)}, u32[]{:S(2)}, u32[]{:S(2)}) collective-permute-start(f32[16,256]{1,0:T(8,128)} %shard_map.90), channel_id=1, source_target_pairs={{4,0},{8,4},{12,8},{16,12},{20,16},{24,20},{28,24},{32,28},{36,32}... | collective-permute-start | bytes 49160 | tf_op jit(solution)/shard_map/ppermute | solution.py:17
  173.0 0.6 copy-start.8

commit v12 on v11

--- a/solution.py
+++ b/solution.py
@@ -305,6 +305,11 @@
         out_shape=out_shape,
         in_specs=in_specs,
         out_specs=out_specs,
+        cost_estimate=pl.CostEstimate(
+            flops=2 * steps * start.shape[0] * table.shape[1] * table.shape[2] * (2 if side else 1),
+            bytes_accessed=4 * (table.size + 3 * source.size),
+            transcendentals=0,
+        ),
     )(*operands)
 
 
@@ -417,6 +422,7 @@
         passed_along(ending_records, "tm", 1),
     )
 
+    first_prediction = accurate_matmul_result(start_rows, dynamics[band_index[0]])
     filtered, predicted = recurrence(
         forward_pick,
         start_rows,
@@ -426,7 +432,7 @@
         True,
         side=(band_index, dynamics),
     )
-    following = passed_along(predicted[0], "tm", -1)
+    following = passed_along(first_prediction, "tm", -1)
     next_predicted = jnp.concatenate([predicted[1:], following[None]], axis=0)
 
     live_weights = band_weights * (1.0 - final_here.astype(jnp.float32))[:, None]

time: 181 us -> 179 us (0.989)
  Pallas kernels: 128 us -> 131 us
    pallas_call x1, Pallas kernels: 24.3 us -> 26.7 us  [doubling_records(): pl.pallas_call(functools.partial(records_kernel, axis=axis, reverse=rever...]
    dot_general x3 -> x4, matrix products: 2.34 us -> 3.77 us  [accurate_matmul_result(): return jnp.dot(first_factor, second_factor, precision=lax.Precision.HIGHEST)]
  transfers between devices with their start and end apart: 9 -> 9, of which waited for: 3 -> 3; matrix products, arithmetic and copies ran while one was open for 3% -> 3% of each run, Pallas kernels for 0% -> 4%
where the time goes in v12:
time: 179 us
  Pallas kernels  131 us (73%)
  starting transfers between devices  22.2 us (12%)
  local copies, waits for them, and re-layouts  11 us (6%)
  other arithmetic  6.42 us (4%)
  matrix products  5.14 us (3%)
  waiting for transfers between devices  2.29 us (1%)
    pallas_call x1, Pallas kernels, doubling_maps(): pl.pallas_call(functools.partial(maps_kernel, axis=axis), out_shape=(stac...  73.6 us
    pallas_call x1, Pallas kernels, doubling_records(): pl.pallas_call(functools.partial(records_kernel, axis=axis, reverse=rever...  26.7 us
    pallas_call x3, Pallas kernels, recurrence(): pl.pallas_call(functools.partial(recurrence_kernel, steps=steps, reverse=...  21.4 us
    ppermute x3, starting transfers between devices, passed_along(): return lax.ppermute(block, axis, route)  13.4 us
    pallas_call x1, Pallas kernels, paired_maps(): pl.pallas_call(functools.partial(paired_kernel, steps=ahead_source.shape[...  9.11 us
    ppermute x6, starting transfers between devices, gathered_rows(): lax.ppermute(part, axis, [(i, (i + shift) % peers) for i in range(peers)])  8.76 us
    dot_general x4, matrix products, accurate_matmul_result(): return jnp.dot(first_factor, second_factor, precision=lax.Precision.HIGHEST)  3.77 us
  transfers between devices with their start and end apart: 9, of which 3 were waited for; matrix products, arithmetic and copies ran while one was open for 3% of the time, Pallas kernels for 4%

profile of v12, /device:TPU:1, one launch (start us, length us, event | category | flops | bytes accessed | tf_op | source)
XLA Modules:
  0.0 178.9 jit_solution(18121801562859622289)
XLA Ops:
  0.6 0.0 copy-start
  0.6 0.0 copy-start.5
  0.7 0.2 fusion.12
  0.9 1.2 fusion.5
  2.1 1.1 multiply_add_fusion.1
  3.2 0.0 copy-done
  3.2 0.0 copy-done.5
  3.2 1.4 fusion
  4.6 0.1 pad_maximum_fusion
  4.7 1.5 copy.10
  6.2 0.0 copy-start.4
  6.2 1.6 copy.11
  7.9 0.6 concatenate.12.ahead_start_ref
  8.5 0.0 copy-done.10
  8.5 0.0 copy-done.12
  8.5 0.6 fusion.21
  9.1 0.1 fusion.14
  9.2 0.0 copy-done.7
  9.2 1.1 fusion.1.refs_5_
  10.3 0.0 copy-start.2
  10.3 1.2 concatenate.14.ahead_source_ref
  11.5 0.0 copy-done.4
  11.5 1.2 concatenate.13.behind_table_ref.refs_2_
  12.7 9.1 %shard_map.86 = (f32[80,256]{1,0:T(8,128)}, f32[64,256]{1,0:T(8,128)}) custom-call(s32[16]{0:T(128)} %get-tuple-element.19.ahead_pick_ref.refs_0_, s32[16]{0:T(128)} %get-tuple-element.20.behind_pick_ref.refs_0_, f32[80,256]{1,0:T(8,128)} %concatenate.12.ahead_start_ref, f32[64,256]{1,0:T(8,128)} %copy-done.4, f32[8,256,256]{2,1,0:T(8,128)} %bitcast.46, ...), custom_call_target="tpu_custom_call" | custom-call | tf_op jit(solution)/shard_map/pallas_call | solution.py:337
  21.8 0.0 copy-done.2
  21.8 0.9 fusion.20
  22.7 2.2 %collective-permute-start = (f32[64,256]{1,0:T(8,128)S(1)}, f32[64,256]{1,0:T(8,128)S(1)}, u32[]{:S(2)}, u32[]{:S(2)}) collective-permute-start(f32[64,256]{1,0:T(8,128)S(1)} %get-tuple-element.14), channel_id=1, source_target_pairs={{0,1},{1,2},{2,3},{3,0},{4,5},{5,6},{6,7},{7,4},{8,9},{9,10},{10,1... | collective-permute-start | bytes 196616 | tf_op jit(solution)/shard_map/ppermute | solution.py:28
  24.9 2.6 %collective-permute-start.1 = (f32[64,256]{1,0:T(8,128)S(1)}, f32[64,256]{1,0:T(8,128)S(1)}, u32[]{:S(2)}, u32[]{:S(2)}) collective-permute-start(f32[64,256]{1,0:T(8,128)S(1)} %get-tuple-element.14), channel_id=1, source_target_pairs={{0,2},{1,3},{2,0},{3,1},{4,6},{5,7},{6,4},{7,5},{8,10},{9,11},{10,... | collective-permute-start | bytes 196616 | tf_op jit(solution)/shard_map/ppermute | solution.py:28
  27.5 1.1 collective-permute-start.2
  28.6 0.4 collective-permute-start.3
  29.0 0.8 collective-permute-start.4
  29.8 0.9 constant_dynamic-update-slice_fusion.3
  30.7 0.0 collective-permute-done
  30.7 1.7 collective-permute-start.5
  32.4 0.0 collective-permute-done.1
  32.4 0.0 collective-permute-done.2
  32.4 0.0 copy-done.11
  32.4 0.2 fusion.22
  32.6 0.8 broadcast_select_fusion.ahead_ref
  33.4 1.3 add_select_fusion.records_ref
  34.7 0.0 collective-permute-done.3
  34.7 0.0 collective-permute-done.4
  34.8 0.2 collective-permute-done.5
  35.0 0.0 copy-start.3
  35.0 0.7 copy-done.3
  35.7 73.6 %shard_map.87 = (f32[6,256,256]{2,1,0:T(8,128)}, f32[6,256,256]{2,1,0:T(8,128)}, f32[16,256]{1,0:T(8,128)}) custom-call(f32[256,256]{1,0:T(8,128)} %broadcast_select_fusion.ahead_ref, f32[256,256]{1,0:T(8,128)} %copy-done.3, f32[16,256]{1,0:T(8,128)} %add_select_fusion.records_ref), custom_call_target="tpu_custom_call" | custom-call | tf_op jit(solution)/shard_map/pallas_call | solution.py:156
  109.3 6.2 %collective-permute-start.6 = (f32[16,256]{1,0:T(8,128)}, f32[16,256]{1,0:T(8,128)S(1)}, u32[]{:S(2)}, u32[]{:S(2)}) collective-permute-start(f32[16,256]{1,0:T(8,128)} %get-tuple-element.10), channel_id=1, source_target_pairs={{0,4},{4,8},{8,12},{12,16},{16,20},{20,24},{24,28},{28,32},{32,36}... | collective-permute-start | bytes 49160 | tf_op jit(solution)/shard_map/ppermute | solution.py:17
  115.5 0.3 multiply_add_fusion.refs_4_
  115.9 0.0 copy-start.1
  116.0 0.6 collective-permute-done.6
  116.6 0.2 fusion.9
  116.8 1.9 %collective-permute-start.7 = (f32[16,256]{1,0:T(8,128)S(1)}, f32[16,256]{1,0:T(8,128)S(1)}, u32[]{:S(2)}, u32[]{:S(2)}) collective-permute-start(f32[16,256]{1,0:T(8,128)S(1)} %fusion.9), channel_id=1, source_target_pairs={{4,0},{8,4},{12,8},{16,12},{20,16},{24,20},{28,24},{32,28},{36,32}... | collective-permute-start | bytes 49160 | tf_op jit(solution)/shard_map/ppermute | solution.py:17
  118.8 7.8 %shard_map.88 = (f32[16,16,256]{2,1,0:T(8,128)}, f32[16,16,256]{2,1,0:T(8,128)}) custom-call(s32[16]{0:T(128)} %get-tuple-element.19.ahead_pick_ref.refs_0_, s32[16]{0:T(128)} %refs_1_.1, f32[16,256]{1,0:T(8,128)} %copy-done.8, f32[8,256,256]{2,1,0:T(8,128)} %bitcast.47, f32[4,256,256]{2,1,0:T(8,128)} %copy-done.1, f32[16,16,256]{2,1,0:T(8,128)} %copy-done.2), custom_call_target="tpu_custom_call" | custom-call | flops 67108864 | bytes 2883584 | tf_op jit(solution)/shard_map/pallas_call | solution.py:297
  126.6 1.0 slice.14
  127.6 0.0 collective-permute-done.7
  127.6 2.3 %fusion.2 = f32[16,16,256]{2,1,0:T(8,128)S(1)} fusion(f32[4,256,256]{2,1,0:T(8,128)} %param.12, f32[16,4]{1,0:T(8,128)S(1)} %get-tuple-element.16, f32[1,16,256]{2,1,0:T(8,128)S(1)} %bitcast.49, f32[15,16,256]{2,1,0:T(8,128)S(1)} %slice.14), kind=kOutput, calls=%fused_computation.6 | convolution fusion | flops 805830656 | bytes 1573120 | tf_op jit(solution)/shard_map/dot_general | solution.py:35
  130.0 0.7 sub.94.refs_3_
  130.7 0.6 broadcast_in_dim.11.refs_1_
  131.3 6.7 %shard_map.89.records_ref = f32[16,256]{1,0:T(8,128)} custom-call(s32[16]{0:T(128)} %get-tuple-element.20.behind_pick_ref.refs_0_, f32[16,256]{1,0:T(8,128)} %broadcast_in_dim.11.refs_1_, f32[5,256,256]{2,1,0:T(8,128)} %concatenate.13.behind_table_ref.refs_2_, f32[16,16,256]{2,1,0:T(8,128)} %sub.94.refs_3_), custom_call_target="tpu_custom_call" | custom-call | flops 33554432 | bytes 2097152 | tf_op jit(solution)/shard_map/pallas_call | solution.py:297
  138.0 26.7 %shard_map.90 = f32[16,256]{1,0:T(8,128)} custom-call(f32[6,256,256]{2,1,0:T(8,128)} %get-tuple-element.12.maps_ref, f32[16,256]{1,0:T(8,128)} %shard_map.89.records_ref), custom_call_target="tpu_custom_call" | custom-call | tf_op jit(solution)/shard_map/pallas_call | solution.py:219
  164.8 5.3 %collective-permute-start.8 = (f32[16,256]{1,0:T(8,128)}, f32[16,256]{1,0:T(8,128)S(1)}, u32[]{:S(2)}, u32[]{:S(2)}) collective-permute-start(f32[16,256]{1,0:T(8,128)} %shard_map.90), channel_id=1, source_target_pairs={{4,0},{8,4},{12,8},{16,12},{20,16},{24,20},{28,24},{32,28},{36,32}... | collective-permute-start | bytes 49160 | tf_op jit(solution)/shard_map/ppermute | solution.py:17
  170.0 1.5 collective-permute-done.8.refs_1_
  171.5 0.6 copy-done.9
  172.1 6.9 %shard_map.91 = f32[16,16,256]{2,1,0:T(8,128)} custom-call(s32[16]{0:T(128)} %get-tuple-element.20.behind_pick_ref.refs_0_, f32[16,256]{1,0:T(8,128)} %copy-done.9, f32[5,256,256]{2,1,0:T(8,128)} %concatenate.13.behind_table_ref.refs_2_, f32[16,16,256]{2,1,0:T(8,128)} %sub.94.refs_3_), custom_call_target="tpu_custom_call" | custom-call | flops 33554432 | bytes 2097152 | tf_op jit(solution)/shard_map/pallas_call | solution.py:297
  (24 shorter events, 0.2 us)
Async XLA Ops:
  0.6 2.5 %copy-start = (f32[4,256,256]{2,1,0:T(8,128)S(1)}, f32[4,256,256]{2,1,0:T(8,128)}, u32[]{:S(2)}) copy-start(f32[4,256,256]{2,1,0:T(8,128)} %param.11) | copy-start | bytes 3145732
  0.6 2.5 %copy-start.5 = (f32[4,256]{1,0:T(4,128)S(1)}, f32[4,256]{1,0:T(4,128)}, u32[]{:S(2)}) copy-start(f32[4,256]{1,0:T(4,128)} %param.10) | copy-start | bytes 12292
  6.2 2.3 %copy-start.10 = (s32[16]{0:T(128)S(1)}, s32[16]{0:T(128)}, u32[]{:S(2)}) copy-start(s32[16]{0:T(128)} %refs_1_.1) | copy-start | bytes 196
  6.2 2.3 %copy-start.12 = (s32[16]{0:T(128)S(1)}, s32[16]{0:T(128)}, u32[]{:S(2)}) copy-start(s32[16]{0:T(128)} %param.9) | copy-start | bytes 196
  6.2 3.0 %copy-start.7 = (f32[16,16,256]{2,1,0:T(8,128)S(1)}, f32[16,16,256]{2,1,0:T(8,128)}, u32[]{:S(2)}) copy-start(f32[16,16,256]{2,1,0:T(8,128)} %param.7) | copy-start | bytes 786436
  6.2 5.3 %copy-start.4 = (f32[64,256]{1,0:T(8,128)}, f32[64,256]{1,0:T(8,128)S(1)}, u32[]{:S(2)}) copy-start(f32[64,256]{1,0:T(8,128)S(1)} %constant_dynamic-slice_fusion.behind_start_ref) | copy-start | bytes 196612
  10.3 11.6 %copy-start.2 = (f32[16,16,256]{2,1,0:T(8,128)}, f32[16,16,256]{2,1,0:T(8,128)S(1)}, u32[]{:S(2)}) copy-start(f32[16,16,256]{2,1,0:T(8,128)S(1)} %fusion.1.refs_5_) | copy-start | bytes 786436
  12.7 19.7 %copy-start.11 = (f32[256]{0:T(256)S(1)}, f32[256]{0:T(256)}, u32[]{:S(2)}) copy-start(f32[256]{0:T(256)} %param.13) | copy-start | bytes 3076
  22.7 8.0 %collective-permute-start = (f32[64,256]{1,0:T(8,128)S(1)}, f32[64,256]{1,0:T(8,128)S(1)}, u32[]{:S(2)}, u32[]{:S(2)}) collective-permute-start(f32[64,256]{1,0:T(8,128)S(1)} %get-tuple-element.14), channel_id=1, source_target_pairs={{0,1},{1,2},{2,3},{3,0},{4,5},{5,6},{6,7},{7,4},{8,9},{9,10},{10,1... | collective-permute-start | bytes 196616 | tf_op jit(solution)/shard_map/ppermute | solution.py:28
  24.9 7.5 %collective-permute-start.1 = (f32[64,256]{1,0:T(8,128)S(1)}, f32[64,256]{1,0:T(8,128)S(1)}, u32[]{:S(2)}, u32[]{:S(2)}) collective-permute-start(f32[64,256]{1,0:T(8,128)S(1)} %get-tuple-element.14), channel_id=1, source_target_pairs={{0,2},{1,3},{2,0},{3,1},{4,6},{5,7},{6,4},{7,5},{8,10},{9,11},{10,... | collective-permute-start | bytes 196616 | tf_op jit(solution)/shard_map/ppermute | solution.py:28
  27.5 4.9 %collective-permute-start.2 = (f32[64,256]{1,0:T(8,128)S(1)}, f32[64,256]{1,0:T(8,128)S(1)}, u32[]{:S(2)}, u32[]{:S(2)}) collective-permute-start(f32[64,256]{1,0:T(8,128)S(1)} %get-tuple-element.14), channel_id=1, source_target_pairs={{0,3},{1,0},{2,1},{3,2},{4,7},{5,4},{6,5},{7,6},{8,11},{9,8},{10,9... | collective-permute-start | bytes 196616 | tf_op jit(solution)/shard_map/ppermute | solution.py:28
  28.6 6.1 %collective-permute-start.3 = (f32[64,256]{1,0:T(8,128)}, f32[64,256]{1,0:T(8,128)S(1)}, u32[]{:S(2)}, u32[]{:S(2)}) collective-permute-start(f32[64,256]{1,0:T(8,128)} %get-tuple-element.9), channel_id=1, source_target_pairs={{0,1},{1,2},{2,3},{3,0},{4,5},{5,6},{6,7},{7,4},{8,9},{9,10},{10,1... | collective-permute-start | bytes 196616 | tf_op jit(solution)/shard_map/ppermute | solution.py:28
  29.0 5.7 %collective-permute-start.4 = (f32[64,256]{1,0:T(8,128)}, f32[64,256]{1,0:T(8,128)S(1)}, u32[]{:S(2)}, u32[]{:S(2)}) collective-permute-start(f32[64,256]{1,0:T(8,128)} %get-tuple-element.9), channel_id=1, source_target_pairs={{0,2},{1,3},{2,0},{3,1},{4,6},{5,7},{6,4},{7,5},{8,10},{9,11},{10,... | collective-permute-start | bytes 196616 | tf_op jit(solution)/shard_map/ppermute | solution.py:28
  30.7 4.3 %collective-permute-start.5 = (f32[64,256]{1,0:T(8,128)}, f32[64,256]{1,0:T(8,128)S(1)}, u32[]{:S(2)}, u32[]{:S(2)}) collective-permute-start(f32[64,256]{1,0:T(8,128)} %get-tuple-element.9), channel_id=1, source_target_pairs={{0,3},{1,0},{2,1},{3,2},{4,7},{5,4},{6,5},{7,6},{8,11},{9,8},{10,9... | collective-permute-start | bytes 196616 | tf_op jit(solution)/shard_map/ppermute | solution.py:28
  35.0 0.7 copy-start.3
  109.3 7.3 %collective-permute-start.6 = (f32[16,256]{1,0:T(8,128)}, f32[16,256]{1,0:T(8,128)S(1)}, u32[]{:S(2)}, u32[]{:S(2)}) collective-permute-start(f32[16,256]{1,0:T(8,128)} %get-tuple-element.10), channel_id=1, source_target_pairs={{0,4},{4,8},{8,12},{12,16},{16,20},{20,24},{24,28},{28,32},{32,36}... | collective-permute-start | bytes 49160 | tf_op jit(solution)/shard_map/ppermute | solution.py:17
  115.9 2.9 %copy-start.1 = (f32[4,256,256]{2,1,0:T(8,128)}, f32[4,256,256]{2,1,0:T(8,128)S(1)}, u32[]{:S(2)}) copy-start(f32[4,256,256]{2,1,0:T(8,128)S(1)} %multiply_add_fusion.refs_4_) | copy-start | bytes 3145732
  116.6 2.2 %copy-start.8 = (f32[16,256]{1,0:T(8,128)}, f32[16,256]{1,0:T(8,128)S(1)}, u32[]{:S(2)}) copy-start(f32[16,256]{1,0:T(8,128)S(1)} %broadcast_select_fusion.1.refs_2_) | copy-start | bytes 49156
  116.8 10.8 %collective-permute-start.7 = (f32[16,256]{1,0:T(8,128)S(1)}, f32[16,256]{1,0:T(8,128)S(1)}, u32[]{:S(2)}, u32[]{:S(2)}) collective-permute-start(f32[16,256]{1,0:T(8,128)S(1)} %fusion.9), channel_id=1, source_target_pairs={{4,0},{8,4},{12,8},{16,12},{20,16},{24,20},{28,24},{32,28},{36,32}... | collective-permute-start | bytes 49160 | tf_op jit(solution)/shard_map/ppermute | solution.py:17
  126.6 3.3 %copy-start.6 = (f32[16,16,256]{2,1,0:T(8,128)S(1)}, f32[16,16,256]{2,1,0:T(8,128)}, u32[]{:S(2)}) copy-start(f32[16,16,256]{2,1,0:T(8,128)} %get-tuple-element.6) | copy-start | bytes 786436
  164.8 6.7 %collective-permute-start.8 = (f32[16,256]{1,0:T(8,128)}, f32[16,256]{1,0:T(8,128)S(1)}, u32[]{:S(2)}, u32[]{:S(2)}) collective-permute-start(f32[16,256]{1,0:T(8,128)} %shard_map.90), channel_id=1, source_target_pairs={{4,0},{8,4},{12,8},{16,12},{20,16},{24,20},{28,24},{32,28},{36,32}... | collective-permute-start | bytes 49160 | tf_op jit(solution)/shard_map/ppermute | solution.py:17
  171.5 0.6 copy-start.9

commit v13 on v12

--- a/solution.py
+++ b/solution.py
@@ -170,7 +170,8 @@
     )(ahead, behind, records)
 
 
-def records_kernel(maps_ref, records_ref, out_ref, sums, sum_in, sems, *, axis, reverse):
+def records_kernel(maps_ref, records_ref, out_ref, sums, sum_in, handed, hand_sems, sems, *,
+                   axis, reverse):
     peers, index = (lax.axis_size(axis), lax.axis_index(axis))
     other = lax.axis_index("col")
     rounds = maps_ref.shape[0]
@@ -205,12 +206,33 @@
 
         pending.append((sends, sum_copy))
 
+    if reverse:
+        target, sends, receives = index - 1, index - 1 >= 0, index + 1 < peers
+    else:
+        target, sends, receives = index + 1, index + 1 < peers, index - 1 >= 0
+    hand_copy = pltpu.make_async_remote_copy(
+        src_ref=sums.at[rounds], dst_ref=handed, send_sem=hand_sems.at[0],
+        recv_sem=hand_sems.at[1], device_id=(target, other),
+        device_id_type=pl.DeviceIdType.MESH)
+
+    @pl.when(sends)
+    def _():
+        hand_copy.start()
+
+    @pl.when(receives)
+    def _():
+        hand_copy.wait_recv()
+        out_ref[...] = handed[...]
+
+    @pl.when(jnp.logical_not(receives))
+    def _():
+        out_ref[...] = jnp.zeros_like(handed)
+
+    pending.append((sends, hand_copy))
     for sent, copy in pending:
         @pl.when(sent)
         def _():
             copy.wait_send()
-
-    out_ref[...] = sums[rounds]
 
 
 def doubling_records(maps, records, axis, reverse, collective_id):
@@ -224,6 +246,8 @@
         scratch_shapes=[
             pltpu.VMEM((rounds + 1,) + records.shape, jnp.float32),
             pltpu.VMEM((rounds,) + records.shape, jnp.float32),
+            pltpu.VMEM(records.shape, jnp.float32),
+            pltpu.SemaphoreType.DMA((2,)),
             pltpu.SemaphoreType.DMA((2, rounds)),
         ],
         compiler_params=pltpu.CompilerParams(collective_id=collective_id, has_side_effects=True),
@@ -439,8 +463,7 @@
     shift = filtered - per_band_products(next_predicted, backward, live_weights)
 
     back_records = recurrence(backward_pick, blank_records, backward_table, shift, True, False)
-    opening_records = doubling_records(backward_maps, back_records, "tm", True, 1)
-    after_records = passed_along(opening_records, "tm", -1)
+    after_records = doubling_records(backward_maps, back_records, "tm", True, 1)
 
     smoothed = recurrence(backward_pick, after_records, backward_table, shift, True, True)
     return (filtered, smoothed)

time: 179 us -> 177 us (0.989)
  starting transfers between devices: 22.2 us -> 16.9 us
  Pallas kernels: 131 us -> 136 us
    ppermute x3 -> x2, starting transfers between devices: 13.4 us -> 8.14 us  [passed_along(): return lax.ppermute(block, axis, route)]
    pallas_call x1, Pallas kernels: 26.7 us -> 31.3 us  [doubling_records(): pl.pallas_call(functools.partial(records_kernel, axis=axis, reverse=rever...]
  transfers between devices with their start and end apart: 9 -> 8, of which waited for: 3 -> 2; matrix products, arithmetic and copies ran while one was open for 3% -> 3% of each run, Pallas kernels for 4% -> 4%
where the time goes in v13:
time: 177 us; the launch traced here: 176 us
  Pallas kernels  136 us (77%)
  starting transfers between devices  16.9 us (10%)
  local copies, waits for them, and re-layouts  10.4 us (6%)
  other arithmetic  6.44 us (4%)
  matrix products  5.14 us (3%)
    pallas_call x1, Pallas kernels, doubling_maps(): pl.pallas_call(functools.partial(maps_kernel, axis=axis), out_shape=(stac...  73.6 us
    pallas_call x1, Pallas kernels, doubling_records(): pl.pallas_call(functools.partial(records_kernel, axis=axis, reverse=rever...  31.3 us
    pallas_call x3, Pallas kernels, recurrence(): pl.pallas_call(functools.partial(recurrence_kernel, steps=steps, reverse=...  21.4 us
    pallas_call x1, Pallas kernels, paired_maps(): pl.pallas_call(functools.partial(paired_kernel, steps=ahead_source.shape[...  9.12 us
    ppermute x6, starting transfers between devices, gathered_rows(): lax.ppermute(part, axis, [(i, (i + shift) % peers) for i in range(peers)])  8.76 us
    ppermute x2, starting transfers between devices, passed_along(): return lax.ppermute(block, axis, route)  8.14 us
    dot_general x4, matrix products, accurate_matmul_result(): return jnp.dot(first_factor, second_factor, precision=lax.Precision.HIGHEST)  3.78 us
  transfers between devices with their start and end apart: 8, of which 2 were waited for; matrix products, arithmetic and copies ran while one was open for 3% of the time, Pallas kernels for 4%

profile of v13, /device:TPU:1, one launch (start us, length us, event | category | flops | bytes accessed | tf_op | source)
XLA Modules:
  0.0 176.3 jit_solution(16445025626623262305)
XLA Ops:
  0.6 0.0 copy-start
  0.6 0.0 copy-start.5
  0.7 0.2 fusion.12
  0.9 1.2 fusion.5
  2.1 1.1 multiply_add_fusion.1
  3.2 0.0 copy-done
  3.2 0.0 copy-done.5
  3.2 1.4 fusion
  4.6 0.1 pad_maximum_fusion
  4.7 1.5 copy.10
  6.2 0.0 copy-start.4
  6.2 1.6 copy.11
  7.9 0.6 concatenate.12.ahead_start_ref
  8.5 0.0 copy-done.9
  8.5 0.0 copy-done.11
  8.5 0.6 fusion.21
  9.1 0.1 fusion.14
  9.2 0.0 copy-done.7
  9.2 1.1 fusion.1.refs_5_
  10.3 0.0 copy-start.2
  10.3 1.2 concatenate.14.ahead_source_ref
  11.5 0.0 copy-done.4
  11.5 1.2 concatenate.13.behind_table_ref.refs_2_
  12.7 9.1 %shard_map.86 = (f32[80,256]{1,0:T(8,128)}, f32[64,256]{1,0:T(8,128)}) custom-call(s32[16]{0:T(128)} %get-tuple-element.19.ahead_pick_ref.refs_0_, s32[16]{0:T(128)} %get-tuple-element.20.behind_pick_ref.refs_0_, f32[80,256]{1,0:T(8,128)} %concatenate.12.ahead_start_ref, f32[64,256]{1,0:T(8,128)} %copy-done.4, f32[8,256,256]{2,1,0:T(8,128)} %bitcast.46, ...), custom_call_target="tpu_custom_call" | custom-call | tf_op jit(solution)/shard_map/pallas_call | solution.py:361
  21.8 0.0 copy-done.2
  21.9 0.9 fusion.20
  22.7 2.2 %collective-permute-start = (f32[64,256]{1,0:T(8,128)S(1)}, f32[64,256]{1,0:T(8,128)S(1)}, u32[]{:S(2)}, u32[]{:S(2)}) collective-permute-start(f32[64,256]{1,0:T(8,128)S(1)} %get-tuple-element.14), channel_id=1, source_target_pairs={{0,1},{1,2},{2,3},{3,0},{4,5},{5,6},{6,7},{7,4},{8,9},{9,10},{10,1... | collective-permute-start | bytes 196616 | tf_op jit(solution)/shard_map/ppermute | solution.py:28
  24.9 2.6 %collective-permute-start.1 = (f32[64,256]{1,0:T(8,128)S(1)}, f32[64,256]{1,0:T(8,128)S(1)}, u32[]{:S(2)}, u32[]{:S(2)}) collective-permute-start(f32[64,256]{1,0:T(8,128)S(1)} %get-tuple-element.14), channel_id=1, source_target_pairs={{0,2},{1,3},{2,0},{3,1},{4,6},{5,7},{6,4},{7,5},{8,10},{9,11},{10,... | collective-permute-start | bytes 196616 | tf_op jit(solution)/shard_map/ppermute | solution.py:28
  27.6 1.1 collective-permute-start.2
  28.6 0.4 collective-permute-start.3
  29.0 0.8 collective-permute-start.4
  29.8 0.9 constant_dynamic-update-slice_fusion.3
  30.7 0.0 collective-permute-done
  30.7 1.7 collective-permute-start.5
  32.4 0.0 collective-permute-done.1
  32.4 0.0 collective-permute-done.2
  32.4 0.0 copy-done.10
  32.5 0.2 fusion.22
  32.7 0.8 broadcast_select_fusion.ahead_ref
  33.4 1.3 add_select_fusion.records_ref
  34.8 0.0 collective-permute-done.3
  34.8 0.0 collective-permute-done.4
  34.8 0.2 collective-permute-done.5
  35.0 0.0 copy-start.3
  35.0 0.7 copy-done.3
  35.7 73.6 %shard_map.87 = (f32[6,256,256]{2,1,0:T(8,128)}, f32[6,256,256]{2,1,0:T(8,128)}, f32[16,256]{1,0:T(8,128)}) custom-call(f32[256,256]{1,0:T(8,128)} %broadcast_select_fusion.ahead_ref, f32[256,256]{1,0:T(8,128)} %copy-done.3, f32[16,256]{1,0:T(8,128)} %add_select_fusion.records_ref), custom_call_target="tpu_custom_call" | custom-call | tf_op jit(solution)/shard_map/pallas_call | solution.py:156
  109.3 6.2 %collective-permute-start.6 = (f32[16,256]{1,0:T(8,128)}, f32[16,256]{1,0:T(8,128)S(1)}, u32[]{:S(2)}, u32[]{:S(2)}) collective-permute-start(f32[16,256]{1,0:T(8,128)} %get-tuple-element.10), channel_id=1, source_target_pairs={{0,4},{4,8},{8,12},{12,16},{16,20},{20,24},{24,28},{28,32},{32,36}... | collective-permute-start | bytes 49160 | tf_op jit(solution)/shard_map/ppermute | solution.py:17
  115.5 0.3 multiply_add_fusion.refs_4_
  115.9 0.0 copy-start.1
  116.0 0.6 collective-permute-done.6
  116.6 0.2 fusion.9
  116.8 1.9 %collective-permute-start.7 = (f32[16,256]{1,0:T(8,128)S(1)}, f32[16,256]{1,0:T(8,128)S(1)}, u32[]{:S(2)}, u32[]{:S(2)}) collective-permute-start(f32[16,256]{1,0:T(8,128)S(1)} %fusion.9), channel_id=1, source_target_pairs={{4,0},{8,4},{12,8},{16,12},{20,16},{24,20},{28,24},{32,28},{36,32}... | collective-permute-start | bytes 49160 | tf_op jit(solution)/shard_map/ppermute | solution.py:17
  118.8 0.0 copy-done.1
  118.8 0.0 copy-done.8
  118.8 7.8 %shard_map.88 = (f32[16,16,256]{2,1,0:T(8,128)}, f32[16,16,256]{2,1,0:T(8,128)}) custom-call(s32[16]{0:T(128)} %get-tuple-element.19.ahead_pick_ref.refs_0_, s32[16]{0:T(128)} %refs_1_.1, f32[16,256]{1,0:T(8,128)} %copy-done.8, f32[8,256,256]{2,1,0:T(8,128)} %bitcast.47, f32[4,256,256]{2,1,0:T(8,128)} %copy-done.1, f32[16,16,256]{2,1,0:T(8,128)} %copy-done.2), custom_call_target="tpu_custom_call" | custom-call | flops 67108864 | bytes 2883584 | tf_op jit(solution)/shard_map/pallas_call | solution.py:321
  126.6 1.0 slice.14
  127.6 0.0 collective-permute-done.7
  127.6 2.3 %fusion.2 = f32[16,16,256]{2,1,0:T(8,128)S(1)} fusion(f32[4,256,256]{2,1,0:T(8,128)} %param.12, f32[16,4]{1,0:T(8,128)S(1)} %get-tuple-element.16, f32[1,16,256]{2,1,0:T(8,128)S(1)} %bitcast.49, f32[15,16,256]{2,1,0:T(8,128)S(1)} %slice.14), kind=kOutput, calls=%fused_computation.6 | convolution fusion | flops 805830656 | bytes 1573120 | tf_op jit(solution)/shard_map/dot_general | solution.py:35
  130.0 0.0 copy-done.6
  130.0 0.7 sub.94.refs_3_
  130.7 0.6 broadcast_in_dim.11.refs_1_
  131.3 6.7 %shard_map.89.records_ref = f32[16,256]{1,0:T(8,128)} custom-call(s32[16]{0:T(128)} %get-tuple-element.20.behind_pick_ref.refs_0_, f32[16,256]{1,0:T(8,128)} %broadcast_in_dim.11.refs_1_, f32[5,256,256]{2,1,0:T(8,128)} %concatenate.13.behind_table_ref.refs_2_, f32[16,16,256]{2,1,0:T(8,128)} %sub.94.refs_3_), custom_call_target="tpu_custom_call" | custom-call | flops 33554432 | bytes 2097152 | tf_op jit(solution)/shard_map/pallas_call | solution.py:321
  138.1 31.3 %shard_map.90.refs_1_ = f32[16,256]{1,0:T(8,128)} custom-call(f32[6,256,256]{2,1,0:T(8,128)} %get-tuple-element.12.maps_ref, f32[16,256]{1,0:T(8,128)} %shard_map.89.records_ref), custom_call_target="tpu_custom_call" | custom-call | tf_op jit(solution)/shard_map/pallas_call | solution.py:241
  169.4 6.9 %shard_map.91 = f32[16,16,256]{2,1,0:T(8,128)} custom-call(s32[16]{0:T(128)} %get-tuple-element.20.behind_pick_ref.refs_0_, f32[16,256]{1,0:T(8,128)} %shard_map.90.refs_1_, f32[5,256,256]{2,1,0:T(8,128)} %concatenate.13.behind_table_ref.refs_2_, f32[16,16,256]{2,1,0:T(8,128)} %sub.94.refs_3_), custom_call_target="tpu_custom_call" | custom-call | flops 33554432 | bytes 2097152 | tf_op jit(solution)/shard_map/pallas_call | solution.py:321
  (20 shorter events, 0.1 us)
Async XLA Ops:
  0.6 2.5 %copy-start = (f32[4,256,256]{2,1,0:T(8,128)S(1)}, f32[4,256,256]{2,1,0:T(8,128)}, u32[]{:S(2)}) copy-start(f32[4,256,256]{2,1,0:T(8,128)} %param.11) | copy-start | bytes 3145732
  0.6 2.5 %copy-start.5 = (f32[4,256]{1,0:T(4,128)S(1)}, f32[4,256]{1,0:T(4,128)}, u32[]{:S(2)}) copy-start(f32[4,256]{1,0:T(4,128)} %param.10) | copy-start | bytes 12292
  6.2 2.3 %copy-start.9 = (s32[16]{0:T(128)S(1)}, s32[16]{0:T(128)}, u32[]{:S(2)}) copy-start(s32[16]{0:T(128)} %refs_1_.1) | copy-start | bytes 196
  6.2 2.3 %copy-start.11 = (s32[16]{0:T(128)S(1)}, s32[16]{0:T(128)}, u32[]{:S(2)}) copy-start(s32[16]{0:T(128)} %param.9) | copy-start | bytes 196
  6.2 3.0 %copy-start.7 = (f32[16,16,256]{2,1,0:T(8,128)S(1)}, f32[16,16,256]{2,1,0:T(8,128)}, u32[]{:S(2)}) copy-start(f32[16,16,256]{2,1,0:T(8,128)} %param.7) | copy-start | bytes 786436
  6.2 5.3 %copy-start.4 = (f32[64,256]{1,0:T(8,128)}, f32[64,256]{1,0:T(8,128)S(1)}, u32[]{:S(2)}) copy-start(f32[64,256]{1,0:T(8,128)S(1)} %constant_dynamic-slice_fusion.behind_start_ref) | copy-start | bytes 196612
  10.3 11.6 %copy-start.2 = (f32[16,16,256]{2,1,0:T(8,128)}, f32[16,16,256]{2,1,0:T(8,128)S(1)}, u32[]{:S(2)}) copy-start(f32[16,16,256]{2,1,0:T(8,128)S(1)} %fusion.1.refs_5_) | copy-start | bytes 786436
  12.7 19.7 %copy-start.10 = (f32[256]{0:T(256)S(1)}, f32[256]{0:T(256)}, u32[]{:S(2)}) copy-start(f32[256]{0:T(256)} %param.13) | copy-start | bytes 3076
  22.7 8.0 %collective-permute-start = (f32[64,256]{1,0:T(8,128)S(1)}, f32[64,256]{1,0:T(8,128)S(1)}, u32[]{:S(2)}, u32[]{:S(2)}) collective-permute-start(f32[64,256]{1,0:T(8,128)S(1)} %get-tuple-element.14), channel_id=1, source_target_pairs={{0,1},{1,2},{2,3},{3,0},{4,5},{5,6},{6,7},{7,4},{8,9},{9,10},{10,1... | collective-permute-start | bytes 196616 | tf_op jit(solution)/shard_map/ppermute | solution.py:28
  24.9 7.5 %collective-permute-start.1 = (f32[64,256]{1,0:T(8,128)S(1)}, f32[64,256]{1,0:T(8,128)S(1)}, u32[]{:S(2)}, u32[]{:S(2)}) collective-permute-start(f32[64,256]{1,0:T(8,128)S(1)} %get-tuple-element.14), channel_id=1, source_target_pairs={{0,2},{1,3},{2,0},{3,1},{4,6},{5,7},{6,4},{7,5},{8,10},{9,11},{10,... | collective-permute-start | bytes 196616 | tf_op jit(solution)/shard_map/ppermute | solution.py:28
  27.6 4.9 %collective-permute-start.2 = (f32[64,256]{1,0:T(8,128)S(1)}, f32[64,256]{1,0:T(8,128)S(1)}, u32[]{:S(2)}, u32[]{:S(2)}) collective-permute-start(f32[64,256]{1,0:T(8,128)S(1)} %get-tuple-element.14), channel_id=1, source_target_pairs={{0,3},{1,0},{2,1},{3,2},{4,7},{5,4},{6,5},{7,6},{8,11},{9,8},{10,9... | collective-permute-start | bytes 196616 | tf_op jit(solution)/shard_map/ppermute | solution.py:28
  28.6 6.1 %collective-permute-start.3 = (f32[64,256]{1,0:T(8,128)}, f32[64,256]{1,0:T(8,128)S(1)}, u32[]{:S(2)}, u32[]{:S(2)}) collective-permute-start(f32[64,256]{1,0:T(8,128)} %get-tuple-element.9), channel_id=1, source_target_pairs={{0,1},{1,2},{2,3},{3,0},{4,5},{5,6},{6,7},{7,4},{8,9},{9,10},{10,1... | collective-permute-start | bytes 196616 | tf_op jit(solution)/shard_map/ppermute | solution.py:28
  29.0 5.7 %collective-permute-start.4 = (f32[64,256]{1,0:T(8,128)}, f32[64,256]{1,0:T(8,128)S(1)}, u32[]{:S(2)}, u32[]{:S(2)}) collective-permute-start(f32[64,256]{1,0:T(8,128)} %get-tuple-element.9), channel_id=1, source_target_pairs={{0,2},{1,3},{2,0},{3,1},{4,6},{5,7},{6,4},{7,5},{8,10},{9,11},{10,... | collective-permute-start | bytes 196616 | tf_op jit(solution)/shard_map/ppermute | solution.py:28
  30.7 4.3 %collective-permute-start.5 = (f32[64,256]{1,0:T(8,128)}, f32[64,256]{1,0:T(8,128)S(1)}, u32[]{:S(2)}, u32[]{:S(2)}) collective-permute-start(f32[64,256]{1,0:T(8,128)} %get-tuple-element.9), channel_id=1, source_target_pairs={{0,3},{1,0},{2,1},{3,2},{4,7},{5,4},{6,5},{7,6},{8,11},{9,8},{10,9... | collective-permute-start | bytes 196616 | tf_op jit(solution)/shard_map/ppermute | solution.py:28
  35.0 0.7 copy-start.3
  109.3 7.3 %collective-permute-start.6 = (f32[16,256]{1,0:T(8,128)}, f32[16,256]{1,0:T(8,128)S(1)}, u32[]{:S(2)}, u32[]{:S(2)}) collective-permute-start(f32[16,256]{1,0:T(8,128)} %get-tuple-element.10), channel_id=1, source_target_pairs={{0,4},{4,8},{8,12},{12,16},{16,20},{20,24},{24,28},{28,32},{32,36}... | collective-permute-start | bytes 49160 | tf_op jit(solution)/shard_map/ppermute | solution.py:17
  115.9 2.9 %copy-start.1 = (f32[4,256,256]{2,1,0:T(8,128)}, f32[4,256,256]{2,1,0:T(8,128)S(1)}, u32[]{:S(2)}) copy-start(f32[4,256,256]{2,1,0:T(8,128)S(1)} %multiply_add_fusion.refs_4_) | copy-start | bytes 3145732
  116.6 2.2 %copy-start.8 = (f32[16,256]{1,0:T(8,128)}, f32[16,256]{1,0:T(8,128)S(1)}, u32[]{:S(2)}) copy-start(f32[16,256]{1,0:T(8,128)S(1)} %broadcast_select_fusion.1.refs_2_) | copy-start | bytes 49156
  116.8 10.8 %collective-permute-start.7 = (f32[16,256]{1,0:T(8,128)S(1)}, f32[16,256]{1,0:T(8,128)S(1)}, u32[]{:S(2)}, u32[]{:S(2)}) collective-permute-start(f32[16,256]{1,0:T(8,128)S(1)} %fusion.9), channel_id=1, source_target_pairs={{4,0},{8,4},{12,8},{16,12},{20,16},{24,20},{28,24},{32,28},{36,32}... | collective-permute-start | bytes 49160 | tf_op jit(solution)/shard_map/ppermute | solution.py:17
  126.6 3.3 %copy-start.6 = (f32[16,16,256]{2,1,0:T(8,128)S(1)}, f32[16,16,256]{2,1,0:T(8,128)}, u32[]{:S(2)}) copy-start(f32[16,16,256]{2,1,0:T(8,128)} %get-tuple-element.6) | copy-start | bytes 786436

commit v14 on v13

--- a/solution.py
+++ b/solution.py
@@ -57,7 +57,7 @@
 
 
 def maps_kernel(ahead_ref, behind_ref, records_ref, ahead_out, behind_out, records_out,
-                ahead_in, behind_in, sums, sum_in, sems, sum_sems, *, axis):
+                ahead_in, behind_in, sums, sum_in, handed, hand_sems, sems, sum_sems, *, axis):
     peers, index = (lax.axis_size(axis), lax.axis_index(axis))
     other = lax.axis_index("col")
     rounds = ahead_out.shape[0]
@@ -139,12 +139,30 @@
 
         pending += [(has_up, ahead_copy), (has_up, sum_copy), (has_down, behind_copy)]
 
+    sends, receives = index + 1 < peers, index - 1 >= 0
+    hand_copy = pltpu.make_async_remote_copy(
+        src_ref=sums.at[rounds], dst_ref=handed, send_sem=hand_sems.at[0],
+        recv_sem=hand_sems.at[1], device_id=(index + 1, other),
+        device_id_type=pl.DeviceIdType.MESH)
+
+    @pl.when(sends)
+    def _():
+        hand_copy.start()
+
+    @pl.when(receives)
+    def _():
+        hand_copy.wait_recv()
+        records_out[...] = handed[...]
+
+    @pl.when(jnp.logical_not(receives))
+    def _():
+        records_out[...] = jnp.zeros_like(handed)
+
+    pending.append((sends, hand_copy))
     for sent, copy in pending:
         @pl.when(sent)
         def _():
             copy.wait_send()
-
-    records_out[...] = sums[rounds]
 
 
 def doubling_maps(ahead, behind, records, axis, collective_id):
@@ -163,6 +181,8 @@
             pltpu.VMEM((max(1, rounds - 1), states, states), jnp.float32),
             pltpu.VMEM((rounds + 1,) + records.shape, jnp.float32),
             pltpu.VMEM((rounds,) + records.shape, jnp.float32),
+            pltpu.VMEM(records.shape, jnp.float32),
+            pltpu.SemaphoreType.DMA((2,)),
             pltpu.SemaphoreType.DMA((2, 2, max(1, rounds - 1))),
             pltpu.SemaphoreType.DMA((2, rounds)),
         ],
@@ -443,7 +463,7 @@
     start_rows = jnp.where(
         first_block,
         jnp.broadcast_to(initial_mean[None, :], (record_rows, states)),
-        passed_along(ending_records, "tm", 1),
+        ending_records,
     )
 
     first_prediction = accurate_matmul_result(start_rows, dynamics[band_index[0]])

time: 177 us -> 172 us (0.972)
  starting transfers between devices: 16.9 us -> 10.7 us
    ppermute x2 -> x1, starting transfers between devices: 8.14 us -> 1.96 us  [passed_along(): return lax.ppermute(block, axis, route)]
  transfers between devices with their start and end apart: 8 -> 7, of which waited for: 2 -> 1; matrix products, arithmetic and copies ran while one was open for 3% -> 2% of each run, Pallas kernels for 4% -> 5%
where the time goes in v14:
time: 172 us; the launch traced here: 171 us
  Pallas kernels  137 us (80%)
  starting transfers between devices  10.7 us (6%)
  local copies, waits for them, and re-layouts  9.53 us (6%)
  other arithmetic  7.09 us (4%)
  matrix products  5.14 us (3%)
    pallas_call x1, Pallas kernels, doubling_maps(): pl.pallas_call(functools.partial(maps_kernel, axis=axis), out_shape=(stac...  74.5 us
    pallas_call x1, Pallas kernels, doubling_records(): pl.pallas_call(functools.partial(records_kernel, axis=axis, reverse=rever...  32.3 us
    pallas_call x3, Pallas kernels, recurrence(): pl.pallas_call(functools.partial(recurrence_kernel, steps=steps, reverse=...  21.4 us
    pallas_call x1, Pallas kernels, paired_maps(): pl.pallas_call(functools.partial(paired_kernel, steps=ahead_source.shape[...  9.1 us
    ppermute x6, starting transfers between devices, gathered_rows(): lax.ppermute(part, axis, [(i, (i + shift) % peers) for i in range(peers)])  8.77 us
    dot_general x4, matrix products, accurate_matmul_result(): return jnp.dot(first_factor, second_factor, precision=lax.Precision.HIGHEST)  3.78 us
  transfers between devices with their start and end apart: 7, of which 1 were waited for; matrix products, arithmetic and copies ran while one was open for 2% of the time, Pallas kernels for 5%

profile of v14, /device:TPU:1, one launch (start us, length us, event | category | flops | bytes accessed | tf_op | source)
XLA Modules:
  0.0 171.3 jit_solution(1400937448379915376)
XLA Ops:
  0.6 0.0 copy-start
  0.6 0.0 copy-start.5
  0.7 0.2 fusion.12
  0.9 1.2 fusion.5
  2.1 1.1 multiply_add_fusion.1
  3.2 0.0 copy-done
  3.2 0.0 copy-done.5
  3.2 1.4 fusion
  4.6 0.1 pad_maximum_fusion
  4.7 1.5 copy.10
  6.2 0.0 copy-start.10
  6.2 0.0 copy-start.4
  6.2 1.6 copy.11
  7.9 0.6 concatenate.12.ahead_start_ref
  8.5 0.0 copy-done.10
  8.5 0.0 copy-done.12
  8.5 0.5 fusion.21
  9.0 0.1 fusion.14
  9.1 0.0 copy-done.7
  9.1 1.1 fusion.1.refs_5_
  10.2 0.0 copy-start.2
  10.2 1.2 concatenate.14.ahead_source_ref
  11.4 0.0 copy-done.4
  11.4 1.2 concatenate.13.behind_table_ref.refs_2_
  12.6 9.1 %shard_map.86 = (f32[80,256]{1,0:T(8,128)}, f32[64,256]{1,0:T(8,128)}) custom-call(s32[16]{0:T(128)} %get-tuple-element.19.ahead_pick_ref.refs_0_, s32[16]{0:T(128)} %get-tuple-element.20.behind_pick_ref.refs_0_, f32[80,256]{1,0:T(8,128)} %concatenate.12.ahead_start_ref, f32[64,256]{1,0:T(8,128)} %copy-done.4, f32[8,256,256]{2,1,0:T(8,128)} %bitcast.46, ...), custom_call_target="tpu_custom_call" | custom-call | tf_op jit(solution)/shard_map/pallas_call | solution.py:381
  21.7 0.0 copy-done.2
  21.8 0.9 fusion.20
  22.6 2.2 %collective-permute-start = (f32[64,256]{1,0:T(8,128)S(1)}, f32[64,256]{1,0:T(8,128)S(1)}, u32[]{:S(2)}, u32[]{:S(2)}) collective-permute-start(f32[64,256]{1,0:T(8,128)S(1)} %get-tuple-element.14), channel_id=1, source_target_pairs={{0,1},{1,2},{2,3},{3,0},{4,5},{5,6},{6,7},{7,4},{8,9},{9,10},{10,1... | collective-permute-start | bytes 196616 | tf_op jit(solution)/shard_map/ppermute | solution.py:28
  24.9 2.6 %collective-permute-start.1 = (f32[64,256]{1,0:T(8,128)S(1)}, f32[64,256]{1,0:T(8,128)S(1)}, u32[]{:S(2)}, u32[]{:S(2)}) collective-permute-start(f32[64,256]{1,0:T(8,128)S(1)} %get-tuple-element.14), channel_id=1, source_target_pairs={{0,2},{1,3},{2,0},{3,1},{4,6},{5,7},{6,4},{7,5},{8,10},{9,11},{10,... | collective-permute-start | bytes 196616 | tf_op jit(solution)/shard_map/ppermute | solution.py:28
  27.5 1.1 collective-permute-start.2
  28.5 0.4 collective-permute-start.3
  28.9 0.8 collective-permute-start.4
  29.7 0.3 multiply_add_fusion.refs_4_
  30.1 0.0 copy-start.1
  30.2 0.0 copy-done.9
  30.3 0.0 collective-permute-done
  30.3 1.7 collective-permute-start.5
  32.0 0.0 collective-permute-done.1
  32.0 0.0 collective-permute-done.2
  32.0 0.0 copy-done.11
  32.0 0.2 fusion.22
  32.2 0.8 broadcast_select_fusion.ahead_ref
  33.0 1.3 add_select_fusion.records_ref
  34.3 0.0 collective-permute-done.3
  34.3 0.0 collective-permute-done.4
  34.4 0.3 collective-permute-done.5
  34.7 0.0 copy-start.3
  34.7 0.7 copy-done.3
  35.4 74.5 %shard_map.87 = (f32[6,256,256]{2,1,0:T(8,128)}, f32[6,256,256]{2,1,0:T(8,128)}, f32[16,256]{1,0:T(8,128)}) custom-call(f32[256,256]{1,0:T(8,128)} %broadcast_select_fusion.ahead_ref, f32[256,256]{1,0:T(8,128)} %copy-done.3, f32[16,256]{1,0:T(8,128)} %add_select_fusion.records_ref), custom_call_target="tpu_custom_call" | custom-call | tf_op jit(solution)/shard_map/pallas_call | solution.py:174
  109.9 0.7 broadcast_select_fusion.1.refs_2_
  110.6 0.2 fusion.9
  110.9 2.0 %collective-permute-start.6 = (f32[16,256]{1,0:T(8,128)S(1)}, f32[16,256]{1,0:T(8,128)S(1)}, u32[]{:S(2)}, u32[]{:S(2)}) collective-permute-start(f32[16,256]{1,0:T(8,128)S(1)} %fusion.9), channel_id=1, source_target_pairs={{4,0},{8,4},{12,8},{16,12},{20,16},{24,20},{28,24},{32,28},{36,32}... | collective-permute-start | bytes 49160 | tf_op jit(solution)/shard_map/ppermute | solution.py:17
  112.8 0.0 copy-done.1
  112.8 0.0 copy-done.8
  112.8 7.8 %shard_map.88 = (f32[16,16,256]{2,1,0:T(8,128)}, f32[16,16,256]{2,1,0:T(8,128)}) custom-call(s32[16]{0:T(128)} %get-tuple-element.19.ahead_pick_ref.refs_0_, s32[16]{0:T(128)} %refs_1_.1, f32[16,256]{1,0:T(8,128)} %copy-done.8, f32[8,256,256]{2,1,0:T(8,128)} %bitcast.47, f32[4,256,256]{2,1,0:T(8,128)} %copy-done.1, f32[16,16,256]{2,1,0:T(8,128)} %copy-done.2), custom_call_target="tpu_custom_call" | custom-call | flops 67108864 | bytes 2883584 | tf_op jit(solution)/shard_map/pallas_call | solution.py:341
  120.7 1.0 slice.14
  121.7 0.0 collective-permute-done.6
  121.7 2.3 %fusion.2 = f32[16,16,256]{2,1,0:T(8,128)S(1)} fusion(f32[4,256,256]{2,1,0:T(8,128)} %param.12, f32[16,4]{1,0:T(8,128)S(1)} %get-tuple-element.16, f32[1,16,256]{2,1,0:T(8,128)S(1)} %bitcast.49, f32[15,16,256]{2,1,0:T(8,128)S(1)} %slice.14), kind=kOutput, calls=%fused_computation.6 | convolution fusion | flops 805830656 | bytes 1573120 | tf_op jit(solution)/shard_map/dot_general | solution.py:35
  124.0 0.0 copy-done.6
  124.0 0.7 sub.94.refs_3_
  124.8 0.6 broadcast_in_dim.11.refs_1_
  125.4 6.7 %shard_map.89.records_ref = f32[16,256]{1,0:T(8,128)} custom-call(s32[16]{0:T(128)} %get-tuple-element.20.behind_pick_ref.refs_0_, f32[16,256]{1,0:T(8,128)} %broadcast_in_dim.11.refs_1_, f32[5,256,256]{2,1,0:T(8,128)} %concatenate.13.behind_table_ref.refs_2_, f32[16,16,256]{2,1,0:T(8,128)} %sub.94.refs_3_), custom_call_target="tpu_custom_call" | custom-call | flops 33554432 | bytes 2097152 | tf_op jit(solution)/shard_map/pallas_call | solution.py:341
  132.1 32.3 %shard_map.90.refs_1_ = f32[16,256]{1,0:T(8,128)} custom-call(f32[6,256,256]{2,1,0:T(8,128)} %get-tuple-element.12.maps_ref, f32[16,256]{1,0:T(8,128)} %shard_map.89.records_ref), custom_call_target="tpu_custom_call" | custom-call | tf_op jit(solution)/shard_map/pallas_call | solution.py:261
  164.4 6.9 %shard_map.91 = f32[16,16,256]{2,1,0:T(8,128)} custom-call(s32[16]{0:T(128)} %get-tuple-element.20.behind_pick_ref.refs_0_, f32[16,256]{1,0:T(8,128)} %shard_map.90.refs_1_, f32[5,256,256]{2,1,0:T(8,128)} %concatenate.13.behind_table_ref.refs_2_, f32[16,16,256]{2,1,0:T(8,128)} %sub.94.refs_3_), custom_call_target="tpu_custom_call" | custom-call | flops 33554432 | bytes 2097152 | tf_op jit(solution)/shard_map/pallas_call | solution.py:341
  (20 shorter events, 0.2 us)
Async XLA Ops:
  0.6 2.5 %copy-start = (f32[4,256,256]{2,1,0:T(8,128)S(1)}, f32[4,256,256]{2,1,0:T(8,128)}, u32[]{:S(2)}) copy-start(f32[4,256,256]{2,1,0:T(8,128)} %param.11) | copy-start | bytes 3145732
  0.6 2.5 %copy-start.5 = (f32[4,256]{1,0:T(4,128)S(1)}, f32[4,256]{1,0:T(4,128)}, u32[]{:S(2)}) copy-start(f32[4,256]{1,0:T(4,128)} %param.10) | copy-start | bytes 12292
  6.2 2.3 %copy-start.10 = (s32[16]{0:T(128)S(1)}, s32[16]{0:T(128)}, u32[]{:S(2)}) copy-start(s32[16]{0:T(128)} %refs_1_.1) | copy-start | bytes 196
  6.2 2.3 %copy-start.12 = (s32[16]{0:T(128)S(1)}, s32[16]{0:T(128)}, u32[]{:S(2)}) copy-start(s32[16]{0:T(128)} %param.9) | copy-start | bytes 196
  6.2 2.9 %copy-start.7 = (f32[16,16,256]{2,1,0:T(8,128)S(1)}, f32[16,16,256]{2,1,0:T(8,128)}, u32[]{:S(2)}) copy-start(f32[16,16,256]{2,1,0:T(8,128)} %param.7) | copy-start | bytes 786436
  6.2 5.2 %copy-start.4 = (f32[64,256]{1,0:T(8,128)}, f32[64,256]{1,0:T(8,128)S(1)}, u32[]{:S(2)}) copy-start(f32[64,256]{1,0:T(8,128)S(1)} %constant_dynamic-slice_fusion.behind_start_ref) | copy-start | bytes 196612
  10.2 11.5 %copy-start.2 = (f32[16,16,256]{2,1,0:T(8,128)}, f32[16,16,256]{2,1,0:T(8,128)S(1)}, u32[]{:S(2)}) copy-start(f32[16,16,256]{2,1,0:T(8,128)S(1)} %fusion.1.refs_5_) | copy-start | bytes 786436
  21.7 8.5 %copy-start.9 = (f32[64,256]{1,0:T(8,128)S(1)}, f32[64,256]{1,0:T(8,128)}, u32[]{:S(2)}) copy-start(f32[64,256]{1,0:T(8,128)} %get-tuple-element.9) | copy-start | bytes 196612
  21.7 10.3 %copy-start.11 = (f32[256]{0:T(256)S(1)}, f32[256]{0:T(256)}, u32[]{:S(2)}) copy-start(f32[256]{0:T(256)} %param.13) | copy-start | bytes 3076
  22.6 7.6 %collective-permute-start = (f32[64,256]{1,0:T(8,128)S(1)}, f32[64,256]{1,0:T(8,128)S(1)}, u32[]{:S(2)}, u32[]{:S(2)}) collective-permute-start(f32[64,256]{1,0:T(8,128)S(1)} %get-tuple-element.14), channel_id=1, source_target_pairs={{0,1},{1,2},{2,3},{3,0},{4,5},{5,6},{6,7},{7,4},{8,9},{9,10},{10,1... | collective-permute-start | bytes 196616 | tf_op jit(solution)/shard_map/ppermute | solution.py:28
  24.9 7.1 %collective-permute-start.1 = (f32[64,256]{1,0:T(8,128)S(1)}, f32[64,256]{1,0:T(8,128)S(1)}, u32[]{:S(2)}, u32[]{:S(2)}) collective-permute-start(f32[64,256]{1,0:T(8,128)S(1)} %get-tuple-element.14), channel_id=1, source_target_pairs={{0,2},{1,3},{2,0},{3,1},{4,6},{5,7},{6,4},{7,5},{8,10},{9,11},{10,... | collective-permute-start | bytes 196616 | tf_op jit(solution)/shard_map/ppermute | solution.py:28
  27.5 4.5 %collective-permute-start.2 = (f32[64,256]{1,0:T(8,128)S(1)}, f32[64,256]{1,0:T(8,128)S(1)}, u32[]{:S(2)}, u32[]{:S(2)}) collective-permute-start(f32[64,256]{1,0:T(8,128)S(1)} %get-tuple-element.14), channel_id=1, source_target_pairs={{0,3},{1,0},{2,1},{3,2},{4,7},{5,4},{6,5},{7,6},{8,11},{9,8},{10,9... | collective-permute-start | bytes 196616 | tf_op jit(solution)/shard_map/ppermute | solution.py:28
  28.5 5.8 %collective-permute-start.3 = (f32[64,256]{1,0:T(8,128)}, f32[64,256]{1,0:T(8,128)S(1)}, u32[]{:S(2)}, u32[]{:S(2)}) collective-permute-start(f32[64,256]{1,0:T(8,128)} %get-tuple-element.9), channel_id=1, source_target_pairs={{0,1},{1,2},{2,3},{3,0},{4,5},{5,6},{6,7},{7,4},{8,9},{9,10},{10,1... | collective-permute-start | bytes 196616 | tf_op jit(solution)/shard_map/ppermute | solution.py:28
  28.9 5.4 %collective-permute-start.4 = (f32[64,256]{1,0:T(8,128)}, f32[64,256]{1,0:T(8,128)S(1)}, u32[]{:S(2)}, u32[]{:S(2)}) collective-permute-start(f32[64,256]{1,0:T(8,128)} %get-tuple-element.9), channel_id=1, source_target_pairs={{0,2},{1,3},{2,0},{3,1},{4,6},{5,7},{6,4},{7,5},{8,10},{9,11},{10,... | collective-permute-start | bytes 196616 | tf_op jit(solution)/shard_map/ppermute | solution.py:28
  30.1 82.7 %copy-start.1 = (f32[4,256,256]{2,1,0:T(8,128)}, f32[4,256,256]{2,1,0:T(8,128)S(1)}, u32[]{:S(2)}) copy-start(f32[4,256,256]{2,1,0:T(8,128)S(1)} %multiply_add_fusion.refs_4_) | copy-start | bytes 3145732
  30.3 4.4 %collective-permute-start.5 = (f32[64,256]{1,0:T(8,128)S(1)}, f32[64,256]{1,0:T(8,128)S(1)}, u32[]{:S(2)}, u32[]{:S(2)}) collective-permute-start(f32[64,256]{1,0:T(8,128)S(1)} %copy-done.9), channel_id=1, source_target_pairs={{0,3},{1,0},{2,1},{3,2},{4,7},{5,4},{6,5},{7,6},{8,11},{9,8},{10,9... | collective-permute-start | bytes 196616 | tf_op jit(solution)/shard_map/ppermute | solution.py:28
  34.7 0.7 copy-start.3
  110.6 2.2 %copy-start.8 = (f32[16,256]{1,0:T(8,128)}, f32[16,256]{1,0:T(8,128)S(1)}, u32[]{:S(2)}) copy-start(f32[16,256]{1,0:T(8,128)S(1)} %broadcast_select_fusion.1.refs_2_) | copy-start | bytes 49156
  110.9 10.8 %collective-permute-start.6 = (f32[16,256]{1,0:T(8,128)S(1)}, f32[16,256]{1,0:T(8,128)S(1)}, u32[]{:S(2)}, u32[]{:S(2)}) collective-permute-start(f32[16,256]{1,0:T(8,128)S(1)} %fusion.9), channel_id=1, source_target_pairs={{4,0},{8,4},{12,8},{16,12},{20,16},{24,20},{28,24},{32,28},{36,32}... | collective-permute-start | bytes 49160 | tf_op jit(solution)/shard_map/ppermute | solution.py:17
  120.7 3.3 %copy-start.6 = (f32[16,16,256]{2,1,0:T(8,128)S(1)}, f32[16,16,256]{2,1,0:T(8,128)}, u32[]{:S(2)}) copy-start(f32[16,16,256]{2,1,0:T(8,128)} %get-tuple-element.6) | copy-start | bytes 786436
